TPU v7x, 32 devices: a whole 2x2x4 slice. The times are simulated.
32 devices in a mesh: dp: 4 (over y, x), depth: 4 (over z), mp: 2 (over core).
Axes of the slice: x: 2, y: 2, z: 4, core: 2. Of those that a mesh axis runs over, the one named last changes fastest.
Arguments:
- history: bfloat16 [20, 8192, 2048], P('depth', 'dp', 'mp'), may hold values from -6 to 6
- slot_layer: int32 [20], P('depth'), may hold values from 0 to 18, as said below
- current: bfloat16 [8192, 2048], P(('dp', 'depth')), may hold values from -6 to 6
- positions: int32 [8192], P(('dp', 'depth')), may hold values from 0 to 1023, as said below
- doc_ids: int32 [8192], P('dp'), may hold values from 0 to 8191, as said below
- cotangent: bfloat16 [8192, 2048], P(('dp', 'depth'), 'mp'), may hold values from -6 to 6
- norm_gains: bfloat16 [5, 2048], P(None, ('dp', 'depth')), may hold values from 0.5 to 1.5
- generator_in: bfloat16 [2048, 72], P(('dp', 'depth')), may hold values from -0.125 to 0.125
- generator_out: bfloat16 [5184], P(('dp', 'depth')), may hold values from -0.75 to 0.75
- query_weight: bfloat16 [2048, 2048], P(('dp', 'depth'), 'mp'), may hold values from -0.125 to 0.125
- key_weight: bfloat16 [2048, 2048], P(('dp', 'depth'), 'mp'), may hold values from -0.125 to 0.125
- value_weight: bfloat16 [2048, 2048], P(('dp', 'depth'), 'mp'), may hold values from -0.125 to 0.125
- out_weight: bfloat16 [2048, 2048], P('mp', ('dp', 'depth')), may hold values from -0.75 to 0.75
- up_weight: bfloat16 [2048, 8192], P(('dp', 'depth'), 'mp'), may hold values from -0.125 to 0.125
- down_weight: bfloat16 [8192, 2048], P('mp', ('dp', 'depth')), may hold values from -0.0625 to 0.0625
Outputs:
- layer_out: bfloat16 [8192, 2048], P(('dp', 'depth'), 'mp')
- history_grad: bfloat16 [20, 8192, 2048], P('depth', 'dp', 'mp')
- current_grad: float32 [8192, 2048], P(('dp', 'depth'), 'mp')
- gains_grad: float32 [5, 2048], P(None, ('dp', 'depth'))
- gen_in_grad: float32 [2048, 72], P(('dp', 'depth'))
- gen_out_grad: float32 [5184], P(('dp', 'depth'))
- query_grad: float32 [2048, 2048], P(('dp', 'depth'), 'mp')
- key_grad: float32 [2048, 2048], P(('dp', 'depth'), 'mp')
- value_grad: float32 [2048, 2048], P(('dp', 'depth'), 'mp')
- out_grad: float32 [2048, 2048], P('mp', ('dp', 'depth'))
- up_grad: float32 [2048, 8192], P(('dp', 'depth'), 'mp')
- down_grad: float32 [8192, 2048], P('mp', ('dp', 'depth'))
Inputs may be any that keep to these rules, and one draw needn't show every extreme that they name: `slot_layer`: each of the 17 history states sits in exactly one slot; the other slots hold 18 and are empty. `positions`: a token's place within its document; documents never cross sequences, and some sequence is one whole document. `doc_ids`: the tokens of one document stand consecutively within one sequence and share one number; different documents have different numbers.
All inputs are finite; a program needn't handle non-finite values.
Results may differ from a plain program's by a relative error of at most 0.012.
The roundings to bfloat16 on the way count: a program that leaves them out, or rounds other values in their place, can miss the bound.
Values may be sent and summed in bfloat16 or wider, within the bound.
No kernel may reach another device: no remote copies, remote signals or barrier semaphores. Data moves between devices by JAX's collectives and lax.ppermute only.
A program may use at most 704 MiB of HBM per device.

v0:
```python
import math

import jax
import jax.numpy as jnp
from jax import lax
from jax.sharding import PartitionSpec as P

HDIM = 128
ROT = 32
GEN = 72
MB = 2
MIX = 18


PRECISE = lax.Precision.HIGHEST
NORM_EPSILON = 1e-05
RMS_EPSILON = 1e-06
MASKED = -1e30


def dot_bulk(left_op, right_op):
    return jnp.dot(left_op, right_op, preferred_element_type=jnp.float32)


def dot_exact(left_op, right_op):
    return jnp.dot(left_op, right_op, precision=PRECISE, preferred_element_type=jnp.float32)


def gelu_exact(values):
    return jax.nn.gelu(values, approximate=False)


def gelu_slope(values):
    result, pullback = jax.vjp(gelu_exact, values)
    return pullback(jnp.ones_like(result))[0]


def rotary_tables(places):
    half_rot = ROT // 2
    inverse = jnp.exp(jnp.arange(half_rot, dtype=jnp.float32) * (-2.0 * math.log(10000.0) / ROT))
    angles = places.astype(jnp.float32)[:, None] * inverse[None, :]
    return (jnp.cos(angles)[:, None, :], jnp.sin(angles)[:, None, :])


def rotate(values, cosine, sine_part):
    half_rot = ROT // 2
    first_half = values[..., :half_rot]
    second_half = values[..., half_rot:ROT]
    return jnp.concatenate(
        [
            first_half * cosine - second_half * sine_part,
            second_half * cosine + first_half * sine_part,
            values[..., ROT:],
        ],
        axis=-1,
    )


def unrotate(values, cosine, sine_part):
    half_rot = ROT // 2
    first_half = values[..., :half_rot]
    second_half = values[..., half_rot:ROT]
    return jnp.concatenate(
        [
            first_half * cosine + second_half * sine_part,
            second_half * cosine - first_half * sine_part,
            values[..., ROT:],
        ],
        axis=-1,
    )


def generate(current_rows, gain_vec, gen_first, second_low):
    mean_square = jnp.mean(current_rows * current_rows, axis=-1, keepdims=True)
    inverse_rms = lax.rsqrt(mean_square + RMS_EPSILON)
    scaled = current_rows * inverse_rms
    normed = (scaled * gain_vec).astype(jnp.bfloat16)
    pre_act = dot_bulk(normed, gen_first)
    gen_hidden = gelu_exact(pre_act).astype(jnp.bfloat16)
    last_col = (jnp.arange(MIX) == MIX - 1).astype(jnp.float32)
    mixing = (dot_bulk(gen_hidden, second_low).reshape(-1, 4, MIX) + last_col).astype(jnp.bfloat16)
    return (mixing, (scaled, inverse_rms, normed, pre_act, gen_hidden))


def generate_back(grad_mixing, gen_parts, gain_vec, first_float, second_float):
    scaled, inverse_rms, normed, pre_act, gen_hidden = gen_parts
    grad_flat = grad_mixing.reshape(grad_mixing.shape[0], 4 * MIX)
    grad_second = dot_exact(gen_hidden.astype(jnp.float32).T, grad_flat)
    grad_pre = dot_exact(grad_flat, second_float.T) * gelu_slope(pre_act)
    grad_first = dot_exact(normed.astype(jnp.float32).T, grad_pre)
    grad_normed = dot_exact(grad_pre, first_float.T)
    grad_gain = jnp.sum(grad_normed * scaled, axis=0)
    grad_scaled = grad_normed * gain_vec
    grad_current = inverse_rms * (
        grad_scaled - scaled * jnp.mean(grad_scaled * scaled, axis=-1, keepdims=True)
    )
    return (grad_current, grad_gain, grad_first, grad_second.reshape(-1))


def local(
    history,
    slot_layer,
    current,
    positions,
    doc_ids,
    cotangent,
    norm_gains,
    generator_in,
    generator_out,
    query_weight,
    key_weight,
    value_weight,
    out_weight,
    up_weight,
    down_weight,
):
    gain_rows, gen_first, gen_second, query_w, key_w, value_w, out_w, up_w, down_w = (
        lax.all_gather(norm_gains, ("dp", "depth"), axis=1, tiled=True),
        lax.all_gather(generator_in, ("dp", "depth"), axis=0, tiled=True),
        lax.all_gather(generator_out, ("dp", "depth"), axis=0, tiled=True),
        lax.all_gather(query_weight, ("dp", "depth"), axis=0, tiled=True),
        lax.all_gather(key_weight, ("dp", "depth"), axis=0, tiled=True),
        lax.all_gather(value_weight, ("dp", "depth"), axis=0, tiled=True),
        lax.all_gather(out_weight, ("dp", "depth"), axis=1, tiled=True),
        lax.all_gather(up_weight, ("dp", "depth"), axis=0, tiled=True),
        lax.all_gather(down_weight, ("dp", "depth"), axis=1, tiled=True),
    )
    gain_float = gain_rows.astype(jnp.float32)
    first_float = gen_first.astype(jnp.float32)
    second_low = gen_second.reshape(GEN, 4 * MIX)
    second_float = second_low.astype(jnp.float32)
    depth_count = lax.axis_size("depth")
    depth_at = lax.axis_index("depth")
    model_at = lax.axis_index("mp")
    slot_count = history.shape[0]
    width_local = history.shape[2]
    rows_mb = current.shape[0] // MB
    length = depth_count * rows_mb
    head_count = query_w.shape[1] // HDIM
    score_scale = HDIM ** (-0.5)
    last_col = (jnp.arange(MIX) == MIX - 1).astype(jnp.float32)
    resid_mask = (jnp.arange(4) == 3).astype(jnp.float32)
    select = (slot_layer[:, None] == jnp.arange(MIX)[None, :]).astype(jnp.float32)
    history_view = history.reshape(slot_count, depth_count, MB, rows_mb, width_local)
    document_view = doc_ids.reshape(depth_count, MB, rows_mb)
    ordinal = jnp.arange(length)
    query_places = depth_at * rows_mb + jnp.arange(rows_mb)

    def masked_scores(queries, key_rows, allowed):
        raw_scores = (
            jnp.einsum("qhd,khd->hqk", queries, key_rows, preferred_element_type=jnp.float32)
            * score_scale
        )
        return jnp.where(allowed[None], raw_scores, MASKED)

    saved = []
    outputs = []
    for micro_at in range(MB):
        row_start = micro_at * rows_mb
        current_rows = current[row_start : row_start + rows_mb].astype(jnp.float32)
        current_part = lax.dynamic_slice_in_dim(
            current_rows, model_at * width_local, width_local, 1
        )
        mixing, gen_parts = generate(current_rows, gain_float[4], gen_first, second_low)
        mix_float = mixing.astype(jnp.float32)
        mix_all = lax.all_gather(mixing, "depth", axis=0, tiled=True)
        slot_mix = jnp.sum(
            mix_all.astype(jnp.float32)[:, :, None, :] * select[None, None], axis=-1
        ).astype(jnp.bfloat16)
        history_mb = history_view[:, :, micro_at].reshape(slot_count, length, width_local)
        streams = lax.psum_scatter(
            jnp.einsum("rsk,krd->rsd", slot_mix, history_mb, preferred_element_type=jnp.float32),
            "depth",
            scatter_dimension=0,
            tiled=True,
        )
        streams = streams + mix_float[:, :, MIX - 1 : MIX] * current_part[:, None, :]
        full_streams = lax.all_gather(
            streams.astype(jnp.bfloat16), "mp", axis=2, tiled=True
        ).astype(jnp.float32)
        average = jnp.mean(full_streams, axis=-1, keepdims=True)
        centred = full_streams - average
        inverse_dev = lax.rsqrt(jnp.mean(centred * centred, axis=-1, keepdims=True) + NORM_EPSILON)
        scaled = centred * inverse_dev
        normed = (scaled * gain_float[None, :4]).astype(jnp.bfloat16)
        cosine, sine_part = rotary_tables(positions[row_start : row_start + rows_mb])
        queries = rotate(
            dot_bulk(normed[:, 0], query_w).reshape(rows_mb, head_count, HDIM), cosine, sine_part
        ).astype(jnp.bfloat16)
        key_local = (
            rotate(
                dot_bulk(normed[:, 1], key_w).reshape(rows_mb, head_count, HDIM), cosine, sine_part
            )
            .astype(jnp.bfloat16)
            .reshape(rows_mb, head_count * HDIM)
        )
        value_local = dot_bulk(normed[:, 2], value_w).astype(jnp.bfloat16)
        key_all, value_all = (
            lax.all_gather(key_local, "depth", axis=0, tiled=True),
            lax.all_gather(value_local, "depth", axis=0, tiled=True),
        )
        key_rows = key_all.reshape(length, head_count, HDIM)
        value_rows = value_all.reshape(length, head_count, HDIM)
        documents = document_view[:, micro_at].reshape(length)
        query_docs = lax.dynamic_slice_in_dim(documents, depth_at * rows_mb, rows_mb, 0)
        allowed = (query_docs[:, None] == documents[None, :]) & (
            query_places[:, None] >= ordinal[None, :]
        )
        scores = masked_scores(queries, key_rows, allowed)
        highest = jnp.max(scores, axis=-1, keepdims=True)
        exponent = jnp.exp(scores - highest)
        totals = jnp.sum(exponent, axis=-1, keepdims=True)
        attention = exponent / totals
        log_total = highest + jnp.log(totals)
        attended = (
            jnp.einsum(
                "hqk,khd->qhd",
                attention.astype(jnp.bfloat16),
                value_rows,
                preferred_element_type=jnp.float32,
            )
            .reshape(rows_mb, head_count * HDIM)
            .astype(jnp.bfloat16)
        )
        up_pre = dot_bulk(normed[:, 3], up_w)
        hidden = gelu_exact(up_pre).astype(jnp.bfloat16)
        branch_sum = lax.psum_scatter(
            dot_bulk(attended, out_w) + dot_bulk(hidden, down_w),
            "mp",
            scatter_dimension=1,
            tiled=True,
        )
        outputs.append((streams[:, 3] + branch_sum).astype(jnp.bfloat16))
        saved.append(
            (
                current_part,
                mix_float,
                gen_parts,
                slot_mix,
                history_mb,
                normed,
                scaled,
                inverse_dev,
                cosine,
                sine_part,
                queries,
                key_rows,
                value_rows,
                allowed,
                log_total,
                attended,
                up_pre,
                hidden,
            )
        )
    history_grads = []
    current_grads = []
    operand_pairs = [([], []) for index in range(9)]
    small_grads = None
    finished = [None] * 9

    def summed(index):
        left_rows = jnp.concatenate(operand_pairs[index][0], axis=0)
        right_rows = jnp.concatenate(operand_pairs[index][1], axis=0)
        return dot_bulk(left_rows.T, right_rows)

    for micro_at in range(MB):
        (
            current_part,
            mix_float,
            gen_parts,
            slot_mix,
            history_mb,
            normed,
            scaled,
            inverse_dev,
            cosine,
            sine_part,
            queries,
            key_rows,
            value_rows,
            allowed,
            log_total,
            attended,
            up_pre,
            hidden,
        ) = saved[micro_at]
        row_start = micro_at * rows_mb
        grad_rows_out = cotangent[row_start : row_start + rows_mb]
        grad_full = lax.all_gather(grad_rows_out, "mp", axis=1, tiled=True)
        grad_up = (dot_bulk(grad_full, down_w.T) * gelu_slope(up_pre)).astype(jnp.bfloat16)
        grad_resid_norm = dot_bulk(grad_up, up_w.T)
        operand_pairs[6][0].append(attended)
        operand_pairs[6][1].append(grad_full)
        operand_pairs[7][0].append(normed[:, 3])
        operand_pairs[7][1].append(grad_up)
        operand_pairs[8][0].append(hidden)
        operand_pairs[8][1].append(grad_full)
        grad_attended = (
            dot_bulk(grad_full, out_w.T).astype(jnp.bfloat16).reshape(rows_mb, head_count, HDIM)
        )
        attention = jnp.exp(masked_scores(queries, key_rows, allowed) - log_total)
        grad_attention = (
            jnp.einsum(
                "qhd,khd->hqk", grad_attended, value_rows, preferred_element_type=jnp.float32
            )
            .astype(jnp.bfloat16)
            .astype(jnp.float32)
        )
        grad_scores = (
            attention
            * (grad_attention - jnp.sum(attention * grad_attention, axis=-1, keepdims=True))
        ).astype(jnp.bfloat16)
        grad_queries = (
            jnp.einsum("hqk,khd->qhd", grad_scores, key_rows, preferred_element_type=jnp.float32)
            * score_scale
        )
        grad_key_seq = (
            jnp.einsum("hqk,qhd->khd", grad_scores, queries, preferred_element_type=jnp.float32)
            * score_scale
        ).reshape(length, head_count * HDIM)
        grad_value_seq = jnp.einsum(
            "hqk,qhd->khd",
            attention.astype(jnp.bfloat16),
            grad_attended,
            preferred_element_type=jnp.float32,
        ).reshape(length, head_count * HDIM)
        grad_key_own, grad_value_own = (
            lax.psum_scatter(grad_key_seq, "depth", scatter_dimension=0, tiled=True),
            lax.psum_scatter(grad_value_seq, "depth", scatter_dimension=0, tiled=True),
        )
        grad_query_pre = (
            unrotate(grad_queries, cosine, sine_part)
            .reshape(rows_mb, head_count * HDIM)
            .astype(jnp.bfloat16)
        )
        grad_key_pre = (
            unrotate(grad_key_own.reshape(rows_mb, head_count, HDIM), cosine, sine_part)
            .reshape(rows_mb, head_count * HDIM)
            .astype(jnp.bfloat16)
        )
        grad_value_pre = grad_value_own.astype(jnp.bfloat16)
        operand_pairs[3][0].append(normed[:, 0])
        operand_pairs[3][1].append(grad_query_pre)
        operand_pairs[4][0].append(normed[:, 1])
        operand_pairs[4][1].append(grad_key_pre)
        operand_pairs[5][0].append(normed[:, 2])
        operand_pairs[5][1].append(grad_value_pre)
        grad_normed = jnp.stack(
            [
                dot_bulk(grad_query_pre, query_w.T),
                dot_bulk(grad_key_pre, key_w.T),
                dot_bulk(grad_value_pre, value_w.T),
                grad_resid_norm,
            ],
            axis=1,
        )
        gain_part = jnp.sum(grad_normed * scaled, axis=0)
        grad_scaled = grad_normed * gain_float[None, :4]
        grad_stream_part = inverse_dev * (
            grad_scaled
            - jnp.mean(grad_scaled, axis=-1, keepdims=True)
            - scaled * jnp.mean(grad_scaled * scaled, axis=-1, keepdims=True)
        )
        grad_streams = lax.psum_scatter(grad_stream_part, "mp", scatter_dimension=2, tiled=True)
        grad_streams = (
            grad_streams + resid_mask[None, :, None] * grad_rows_out.astype(jnp.float32)[:, None, :]
        )
        grad_low = grad_streams.astype(jnp.bfloat16)
        grad_low_float = grad_low.astype(jnp.float32)
        grad_current_mix = jnp.sum(mix_float[:, :, MIX - 1 : MIX] * grad_low_float, axis=1)
        grad_last = jnp.sum(grad_low_float * current_part[:, None, :], axis=-1)
        grad_gathered = lax.all_gather(grad_low, "depth", axis=0, tiled=True)
        history_grads.append(
            jnp.einsum("rsk,rsd->krd", slot_mix, grad_gathered, preferred_element_type=jnp.float32)
            .astype(jnp.bfloat16)
            .reshape(slot_count, depth_count, rows_mb, width_local)
        )
        grad_slot = jnp.einsum(
            "rsd,krd->rsk", grad_gathered, history_mb, preferred_element_type=jnp.float32
        )
        grad_mix_part = jnp.sum(grad_slot[..., None] * select[None, None], axis=2)
        grad_mixing = (
            lax.psum_scatter(grad_mix_part, "depth", scatter_dimension=0, tiled=True)
            + grad_last[:, :, None] * last_col
        )
        grad_mixing, gain_sum = lax.psum((grad_mixing, gain_part), "mp")
        grad_current_gen, grad_gain_gen, first_part, second_part = generate_back(
            grad_mixing, gen_parts, gain_float[4], first_float, second_float
        )
        current_grads.append(
            grad_current_mix
            + lax.dynamic_slice_in_dim(grad_current_gen, model_at * width_local, width_local, 1)
        )
        micro_small = (
            jnp.concatenate([gain_sum, grad_gain_gen[None]], axis=0),
            first_part,
            second_part,
        )
        small_grads = (
            micro_small
            if small_grads is None
            else tuple(
                (
                    first_term + second_term
                    for first_term, second_term in zip(small_grads, micro_small)
                )
            )
        )
    finished = (
        lax.psum_scatter(small_grads[0], ("dp", "depth"), scatter_dimension=1, tiled=True),
        lax.psum_scatter(small_grads[1], ("dp", "depth"), scatter_dimension=0, tiled=True),
        lax.psum_scatter(small_grads[2], ("dp", "depth"), scatter_dimension=0, tiled=True),
        lax.psum_scatter(summed(3), ("dp", "depth"), scatter_dimension=0, tiled=True),
        lax.psum_scatter(summed(4), ("dp", "depth"), scatter_dimension=0, tiled=True),
        lax.psum_scatter(summed(5), ("dp", "depth"), scatter_dimension=0, tiled=True),
        lax.psum_scatter(summed(6), ("dp", "depth"), scatter_dimension=1, tiled=True),
        lax.psum_scatter(summed(7), ("dp", "depth"), scatter_dimension=0, tiled=True),
        lax.psum_scatter(summed(8), ("dp", "depth"), scatter_dimension=1, tiled=True),
    )
    layer_out = jnp.concatenate(outputs, axis=0)
    history_grad = jnp.stack(history_grads, axis=2).reshape(
        slot_count, depth_count * MB * rows_mb, width_local
    )
    current_grad = jnp.concatenate(current_grads, axis=0)
    return (
        layer_out,
        history_grad,
        current_grad,
        finished[0],
        finished[1],
        finished[2],
        finished[3],
        finished[4],
        finished[5],
        finished[6],
        finished[7],
        finished[8],
    )


def solution(mesh):
    return jax.shard_map(
        local,
        mesh=mesh,
        in_specs=(
            P("depth", "dp", "mp"),
            P("depth"),
            P(("dp", "depth"), None),
            P(("dp", "depth")),
            P("dp"),
            P(("dp", "depth"), "mp"),
            P(None, ("dp", "depth")),
            P(("dp", "depth"), None),
            P(("dp", "depth")),
            P(("dp", "depth"), "mp"),
            P(("dp", "depth"), "mp"),
            P(("dp", "depth"), "mp"),
            P("mp", ("dp", "depth")),
            P(("dp", "depth"), "mp"),
            P("mp", ("dp", "depth")),
        ),
        out_specs=(
            P(("dp", "depth"), "mp"),
            P("depth", "dp", "mp"),
            P(("dp", "depth"), "mp"),
            P(None, ("dp", "depth")),
            P(("dp", "depth"), None),
            P(("dp", "depth")),
            P(("dp", "depth"), "mp"),
            P(("dp", "depth"), "mp"),
            P(("dp", "depth"), "mp"),
            P("mp", ("dp", "depth")),
            P(("dp", "depth"), "mp"),
            P("mp", ("dp", "depth")),
        ),
        check_vma=False,
    )
```

profile of v0, /device:TPU:0, one launch (start us, length us, event | category | flops | bytes accessed | tf_op | source)
XLA Modules:
  0.0 6561.6 jit_solution(14194698363981784941)
XLA Ops:
  14.3 78.9 %all-reduce = bf16[5184]{0:T(1024)(128)(2,1)S(1)} all-reduce(bf16[5184]{0:T(1024)(128)(2,1)S(1)} %dynamic-update-slice), channel_id=1, replica_groups=mesh['dp'=4,'depth'=4,'mp'=2] {'dp','depth'}, use_global_device_ids=true, to_apply=%add | all-reduce | flops 5184 | bytes 20736
  251.4 619.0 %all-reduce.11.cloned.1.call-done = f32[1024,4,1024]{2,1,0:T(4,128)} async-done(((f32[1024,4,1024]{2,1,0:T(4,128)}), f32[1024,4,1024]{2,1,0:T(4,128)}) %all-reduce.11.cloned.1.call-update) | async-done | bytes 16777232
  982.0 92.9 %all-gather.29.cloned.1.call-done = bf16[1024,2048]{1,0:T(8,128)(2,1)} async-done(((bf16[1024,128]{1,0:T(8,128)(2,1)}), bf16[1024,2048]{1,0:T(8,128)(2,1)}) %all-gather.29.cloned.1.call-update) | async-done | bytes 4194320 | tf_op jit(solution)/shard_map/all_gather | solution.py:124
  1192.0 283.2 %all-gather.31.cloned.1.call-done = bf16[2048,4096]{1,0:T(8,128)(2,1)} async-done(((bf16[128,4096]{1,0:T(8,128)(2,1)}), bf16[2048,4096]{1,0:T(8,128)(2,1)}) %all-gather.31.cloned.1.call-update) | async-done | bytes 16777232 | tf_op jit(solution)/shard_map/all_gather | solution.py:125
  1493.8 233.5 %all-gather.33.cloned.1.call-done = bf16[4096,2048]{1,0:T(8,128)(2,1)} async-done(((bf16[4096,128]{1,0:T(8,128)(2,1)}), bf16[4096,2048]{1,0:T(8,128)(2,1)}) %all-gather.33.cloned.1.call-update) | async-done | bytes 16777232 | tf_op jit(solution)/shard_map/all_gather | solution.py:126
  1780.0 129.4 %copy.254 = f32[256,4,2048]{1,0,2:T(8,128)} copy(f32[256,4,2048]{2,0,1:T(8,128)} %fusion.21) | data formatting | bytes 16777216
  1909.4 218.9 %reshape.465 = f32[2048,1024]{1,0:T(8,128)} reshape(f32[2048,256,4]{2,1,0:T(8,128)} %bitcast.69) | data formatting | bytes 16777216
  2143.4 140.7 %reshape.466 = f32[1024,256,4]{2,1,0:T(8,128)} reshape(f32[1024,1024]{1,0:T(8,128)} %reduce-scatter.55.cloned.1.call-done) | data formatting | bytes 8388608
  2284.1 75.0 %copy.231 = f32[256,4,1024]{2,0,1:T(8,128)} copy(f32[256,4,1024]{1,0,2:T(8,128)} %bitcast.70) | data formatting | bytes 8388608 | tf_op jit(solution)/shard_map/reduce_scatter | solution.py:365
  2398.4 119.6 %all-gather.43.cloned.1.call-done = bf16[1024,4,1024]{2,1,0:T(4,128)(2,1)} async-done(((bf16[256,4,1024]{2,1,0:T(4,128)(2,1)}), bf16[1024,4,1024]{2,1,0:T(4,128)(2,1)}) %all-gather.43.cloned.1.call-update) | async-done | bytes 8388624 | tf_op jit(solution)/shard_map/all_gather | solution.py:373
  2558.3 559.2 %all-reduce.13.cloned.1.call-done = f32[1024,4,1024]{2,1,0:T(4,128)} async-done(((f32[1024,4,1024]{2,1,0:T(4,128)}), f32[1024,4,1024]{2,1,0:T(4,128)}) %all-reduce.13.cloned.1.call-update) | async-done | bytes 16777232
  3336.7 77.2 %reduce-scatter.33.cloned.1.call-done = f32[256,1024]{0,1:T(8,128)} async-done(((f32[1024,1024]{0,1:T(8,128)}), f32[256,1024]{0,1:T(8,128)}) %reduce-scatter.33.cloned.1.call-update) | async-done | bytes 1048592 | tf_op jit(solution)/shard_map/reduce_scatter | solution.py:330
  3434.8 129.4 %copy.256 = f32[256,4,2048]{1,0,2:T(8,128)} copy(f32[256,4,2048]{2,0,1:T(8,128)} %fusion.15) | data formatting | bytes 16777216
  3564.2 219.3 %reshape.467 = f32[2048,1024]{1,0:T(8,128)} reshape(f32[2048,256,4]{2,1,0:T(8,128)} %bitcast.71) | data formatting | bytes 16777216
  3800.9 140.7 %reshape.468 = f32[1024,256,4]{2,1,0:T(8,128)} reshape(f32[1024,1024]{1,0:T(8,128)} %reduce-scatter.57.cloned.1.call-done) | data formatting | bytes 8388608
  4025.1 150.0 %all-gather.47.cloned.1.call-done = bf16[1024,4,1024]{2,1,0:T(4,128)(2,1)} async-done(((bf16[256,4,1024]{2,1,0:T(4,128)(2,1)}), bf16[1024,4,1024]{2,1,0:T(4,128)(2,1)}) %all-gather.47.cloned.1.call-update) | async-done | bytes 8388624 | tf_op jit(solution)/shard_map/all_gather | solution.py:373
  4419.1 79.1 %all-reduce.3 = f32[5184]{0:T(1024)S(1)} all-reduce(f32[5184]{0:T(1024)S(1)} %add.246), channel_id=16, replica_groups=mesh['dp'=4,'depth'=4,'mp'=2] {'dp','depth'}, use_global_device_ids=true, to_apply=%region_48.49.clone | all-reduce | flops 5184 | bytes 41472
  4502.9 150.5 %reduce-scatter.45.cloned.1.call-done = f32[128,1024]{1,0:T(8,128)} async-done(((f32[2048,1024]{1,0:T(8,128)}), f32[128,1024]{1,0:T(8,128)}) %reduce-scatter.45.cloned.1.call-update) | async-done | bytes 524304 | tf_op jit(solution)/shard_map/reduce_scatter | solution.py:415
  4653.4 182.5 %reduce-scatter.43.cloned.1.call-done = f32[128,1024]{1,0:T(8,128)} async-done(((f32[2048,1024]{1,0:T(8,128)}), f32[128,1024]{1,0:T(8,128)}) %reduce-scatter.43.cloned.1.call-update) | async-done | bytes 524304 | tf_op jit(solution)/shard_map/reduce_scatter | solution.py:414
  4835.9 182.7 %reduce-scatter.47.cloned.1.call-done = f32[128,1024]{1,0:T(8,128)} async-done(((f32[2048,1024]{1,0:T(8,128)}), f32[128,1024]{1,0:T(8,128)}) %reduce-scatter.47.cloned.1.call-update) | async-done | bytes 524304 | tf_op jit(solution)/shard_map/reduce_scatter | solution.py:416
  5018.6 78.1 %reduce-scatter.39.cloned.1.call-done = f32[5,128]{1,0:T(8,128)} async-done(((f32[5,2048]{1,0:T(8,128)}), f32[5,128]{1,0:T(8,128)}) %reduce-scatter.39.cloned.1.call-update) | async-done | bytes 2576 | tf_op jit(solution)/shard_map/reduce_scatter | solution.py:411
  5096.7 76.8 %reduce-scatter.41.cloned.1.call-done = f32[128,72]{0,1:T(8,128)} async-done(((f32[2048,72]{0,1:T(8,128)}), f32[128,72]{0,1:T(8,128)}) %reduce-scatter.41.cloned.1.call-update) | async-done | bytes 36880 | tf_op jit(solution)/shard_map/reduce_scatter | solution.py:412
  5173.5 689.1 %reduce-scatter.53.cloned.1.call-done = f32[4096,128]{1,0:T(8,128)} async-done(((f32[4096,2048]{1,0:T(8,128)}), f32[4096,128]{1,0:T(8,128)}) %reduce-scatter.53.cloned.1.call-update) | async-done | bytes 2097168 | tf_op jit(solution)/shard_map/reduce_scatter | solution.py:419
  5862.6 691.4 %reduce-scatter.51.cloned.1.call-done = f32[128,4096]{1,0:T(8,128)} async-done(((f32[2048,4096]{1,0:T(8,128)}), f32[128,4096]{1,0:T(8,128)}) %reduce-scatter.51.cloned.1.call-update) | async-done | bytes 2097168 | tf_op jit(solution)/shard_map/reduce_scatter | solution.py:418
  (513 shorter events, 1144.5 us)
Async XLA Ops:
  8.0 862.4 %all-reduce.11.cloned.1.call-start = ((), (), s32[]{:S(2)}) async-start(), calls=%async_computation.52 | async-start | bytes 33554432
  246.9 636.5 %all-gather.25.cloned.1.call-start = ((), (), s32[]{:S(2)}) async-start(), calls=%async_computation.22 | async-start | bytes 4456448 | tf_op jit(solution)/shard_map/all_gather | solution.py:122
  247.5 642.7 %all-gather.23.cloned.1.call-start = ((), (), s32[]{:S(2)}) async-start(), calls=%async_computation.21 | async-start | bytes 4456448 | tf_op jit(solution)/shard_map/all_gather | solution.py:121
  248.1 648.5 %all-gather.17.cloned.1.call-start = ((), (), s32[]{:S(2)}) async-start(), calls=%async_computation.18 | async-start | bytes 6291456 | tf_op jit(solution)/shard_map/all_gather | solution.py:178
  882.6 238.5 %all-gather.27.cloned.1.call-start = ((), (), s32[]{:S(2)}) async-start(), calls=%async_computation.23 | async-start | bytes 2621440 | tf_op jit(solution)/shard_map/all_gather | solution.py:199
  909.2 257.8 %all-gather.21.cloned.1.call-start = ((), (), s32[]{:S(2)}) async-start(), calls=%async_computation.20 | async-start | bytes 2621440 | tf_op jit(solution)/shard_map/all_gather | solution.py:200
  976.8 498.4 %all-gather.31.cloned.1.call-start = ((), (), s32[]{:S(2)}) async-start(), calls=%async_computation.25 | async-start | bytes 17825792 | tf_op jit(solution)/shard_map/all_gather | solution.py:125
  977.4 749.9 %all-gather.33.cloned.1.call-start = ((), (), s32[]{:S(2)}) async-start(), calls=%async_computation.26 | async-start | bytes 17825792 | tf_op jit(solution)/shard_map/all_gather | solution.py:126
  978.2 777.1 %reduce-scatter.27.cloned.1.call-start = ((), (), s32[]{:S(2)}) async-start(), calls=%async_computation.33 | async-start | bytes 5242880 | tf_op jit(solution)/shard_map/reduce_scatter | solution.py:329
  1179.1 580.2 %reduce-scatter.29.cloned.1.call-start = ((), (), s32[]{:S(2)}) async-start(), calls=%async_computation.34 | async-start | bytes 5242880 | tf_op jit(solution)/shard_map/reduce_scatter | solution.py:330
  1191.8 951.6 %reduce-scatter.55.cloned.1.call-start = ((), (), s32[]{:S(2)}) async-start(), calls=%async_computation.50 | async-start | bytes 12582912
  2128.3 389.6 %all-gather.43.cloned.1.call-start = ((), (), s32[]{:S(2)}) async-start(), calls=%async_computation.35 | async-start | bytes 10485760 | tf_op jit(solution)/shard_map/all_gather | solution.py:373
  2366.6 750.9 %all-reduce.13.cloned.1.call-start = ((), (), s32[]{:S(2)}) async-start(), calls=%async_computation.53 | async-start | bytes 33554432
  2556.6 582.3 %all-gather.35.cloned.1.call-start = ((), (), s32[]{:S(2)}) async-start(), calls=%async_computation.28 | async-start | bytes 6291456 | tf_op jit(solution)/shard_map/all_gather | solution.py:178
  3265.8 535.1 %reduce-scatter.57.cloned.1.call-start = ((), (), s32[]{:S(2)}) async-start(), calls=%async_computation.51 | async-start | bytes 12582912
  3783.5 391.6 %all-gather.47.cloned.1.call-start = ((), (), s32[]{:S(2)}) async-start(), calls=%async_computation.39 | async-start | bytes 10485760 | tf_op jit(solution)/shard_map/all_gather | solution.py:373
  4251.9 251.0 %reduce-scatter.49.cloned.1.call-start = ((), (), s32[]{:S(2)}) async-start(), calls=%async_computation.47 | async-start | bytes 8912896 | tf_op jit(solution)/shard_map/reduce_scatter | solution.py:417
  4260.2 393.2 %reduce-scatter.45.cloned.1.call-start = ((), (), s32[]{:S(2)}) async-start(), calls=%async_computation.45 | async-start | bytes 8912896 | tf_op jit(solution)/shard_map/reduce_scatter | solution.py:415
  4272.1 563.9 %reduce-scatter.43.cloned.1.call-start = ((), (), s32[]{:S(2)}) async-start(), calls=%async_computation.44 | async-start | bytes 8912896 | tf_op jit(solution)/shard_map/reduce_scatter | solution.py:414
  4279.6 739.0 %reduce-scatter.47.cloned.1.call-start = ((), (), s32[]{:S(2)}) async-start(), calls=%async_computation.46 | async-start | bytes 8912896 | tf_op jit(solution)/shard_map/reduce_scatter | solution.py:416
  4286.6 810.1 %reduce-scatter.39.cloned.1.call-start = ((), (), s32[]{:S(2)}) async-start(), calls=%async_computation.42 | async-start | bytes 69632 | tf_op jit(solution)/shard_map/reduce_scatter | solution.py:411
  4300.1 873.4 %reduce-scatter.41.cloned.1.call-start = ((), (), s32[]{:S(2)}) async-start(), calls=%async_computation.43 | async-start | bytes 626688 | tf_op jit(solution)/shard_map/reduce_scatter | solution.py:412
  4302.9 1559.6 %reduce-scatter.53.cloned.1.call-start = ((), (), s32[]{:S(2)}) async-start(), calls=%async_computation.49 | async-start | bytes 35651584 | tf_op jit(solution)/shard_map/reduce_scatter | solution.py:419
  4320.7 2233.2 %reduce-scatter.51.cloned.1.call-start = ((), (), s32[]{:S(2)}) async-start(), calls=%async_computation.48 | async-start | bytes 35651584 | tf_op jit(solution)/shard_map/reduce_scatter | solution.py:418
  (127 other events, 8881.8 us)
Sparse Core Ops, SparseCore 0:
  247.1 623.3 all-reduce.10
  1179.2 92.8 reduce-scatter.26
  1274.5 110.2 reduce-scatter.28
  2366.7 151.2 all-gather.42
  2556.7 560.7 all-reduce.12
  3258.7 75.5 reduce-scatter.30
  3336.7 77.2 reduce-scatter.32
  4024.2 150.9 all-gather.46
  4178.0 18.7 reduce-scatter.34
  4199.7 18.8 reduce-scatter.36
Sparse Core Ops, SparseCore 1:
  250.2 313.4 all-gather.24
  566.3 311.7 all-gather.22
  880.0 12.3 all-gather.16
  895.2 77.0 all-gather.18
  984.7 90.1 all-gather.28
  1076.8 44.2 all-gather.26
  1123.1 43.8 all-gather.20
  1169.6 305.6 all-gather.30
  1478.0 249.3 all-gather.32
  2128.4 14.9 reduce-scatter.54
  3126.3 12.5 all-gather.34
  3153.3 47.2 all-gather.38
  3202.9 43.8 all-gather.36
  3783.6 17.2 reduce-scatter.56
  4221.0 15.9 all-reduce.16
  4239.9 18.6 all-reduce.14
  4287.8 182.9 reduce-scatter.48
  4473.5 179.8 reduce-scatter.44
  4656.2 179.7 reduce-scatter.42
  4838.8 179.7 reduce-scatter.46
  5021.3 75.4 reduce-scatter.38
  5099.6 73.8 reduce-scatter.40
  5176.5 686.0 reduce-scatter.52
  5865.4 688.5 reduce-scatter.50
  (4 shorter events, 39.0 us)
where the time goes:
time: 6580 us; the launch traced here: 6560 us
  waiting for transfers between devices  4490 us (68%)
  local copies, waits for them, and re-layouts  1290 us (20%)
  matrix products  387 us (6%)
  blocking collectives  262 us (4%)
  other arithmetic  114 us (2%)
    unnamed x42, waiting for transfers between devices  1220 us
    unnamed x244, local copies, waits for them, and re-layouts  1060 us
    reduce_scatter x1, waiting for transfers between devices, local(): lax.psum_scatter(summed(7), ('dp', 'depth'), scatter_dimension=0, tiled=T...  691 us
    reduce_scatter x1, waiting for transfers between devices, local(): lax.psum_scatter(summed(8), ('dp', 'depth'), scatter_dimension=1, tiled=T...  689 us
    all_gather x1, waiting for transfers between devices, local(): lax.all_gather(up_weight, ('dp', 'depth'), axis=0, tiled=True)  283 us
    all_gather x2, waiting for transfers between devices, local(): grad_gathered = lax.all_gather(grad_low, 'depth', axis=0, tiled=True)  270 us
    all_gather x1, waiting for transfers between devices, local(): lax.all_gather(down_weight, ('dp', 'depth'), axis=1, tiled=True)  233 us
    dot_general x34, matrix products, dot_bulk(): return jnp.dot(left_op, right_op, preferred_element_type=jnp.float32)  220 us
  transfers between devices with their start and end apart: 38, of which 26 were waited for; matrix products, arithmetic and copies ran while one was open for 7% of the time, Pallas kernels for 0%

commit v1 on v0

v1 whole, which is shorter than its diff:
```python
import functools
import math

import jax
import jax.numpy as jnp
from jax import lax
from jax.experimental import pallas as pl
from jax.experimental.pallas import tpu as pltpu
from jax.sharding import PartitionSpec as P

HDIM = 128
ROT = 32
GEN = 72
MB = 2
MIX = 18
STREAMS = 4

PRECISE = lax.Precision.HIGHEST
NORM_EPSILON = 1e-05
RMS_EPSILON = 1e-06
MASKED = -1e30

bf16 = jnp.bfloat16
f32 = jnp.float32


def dot_nn(a, b):
    return lax.dot_general(a, b, (((1,), (0,)), ((), ())), preferred_element_type=f32)


def dot_nt(a, b):
    return lax.dot_general(a, b, (((1,), (1,)), ((), ())), preferred_element_type=f32)


def dot_tn(a, b):
    return lax.dot_general(a, b, (((0,), (0,)), ((), ())), preferred_element_type=f32)


def dot_exact(a, b):
    return jnp.dot(a, b, precision=PRECISE, preferred_element_type=f32)


def gelu_exact(values):
    return jax.nn.gelu(values, approximate=False)


def gelu_slope(values):
    result, pullback = jax.vjp(gelu_exact, values)
    return pullback(jnp.ones_like(result))[0]


def bit_count(size):
    count = size.bit_length() - 1
    assert 1 << count == size
    return count


def swap_mask(values, axis, mask):
    size = lax.axis_size(axis)
    return lax.ppermute(values, axis, [(i, i ^ mask) for i in range(size)])


def gather_masked(values, axis, order):
    pieces = {0: values}
    for bit in order:
        arrived = {m | (1 << bit): swap_mask(v, axis, 1 << bit) for m, v in pieces.items()}
        pieces.update(arrived)
    return [pieces[m] for m in range(len(pieces))]


def scatter_masked(pieces, axis, order, link=bf16):
    pieces = dict(enumerate(pieces))
    for bit in order:
        flag = 1 << bit
        for m in [m for m in pieces if m & flag]:
            arrived = swap_mask(pieces.pop(m).astype(link), axis, flag)
            pieces[m ^ flag] = pieces[m ^ flag].astype(f32) + arrived.astype(f32)
    return pieces[0]


def reorder_masked(stacked, axis):
    count = bit_count(stacked.shape[0])
    here = lax.axis_index(axis)
    shape = stacked.shape
    values = stacked.reshape((2,) * count + shape[1:])
    for bit in range(count):
        turned = jnp.flip(values, count - 1 - bit)
        values = jnp.where(((here >> bit) & 1) == 1, turned, values)
    return values.reshape(shape)


def gather_small(values, axes):
    shape = values.shape
    values = values[None]
    for axis in reversed(axes):
        order = range(bit_count(lax.axis_size(axis)))
        stacked = jnp.stack(gather_masked(values, axis, order))
        values = reorder_masked(stacked, axis)
        values = values.reshape((-1,) + shape)
    return values


def scatter_small(values, axes):
    for axis in axes:
        size = lax.axis_size(axis)
        values = values.reshape((size, values.shape[0] // size) + values.shape[1:])
        turned = reorder_masked(values, axis)
        order = reversed(range(bit_count(size)))
        values = scatter_masked([turned[m] for m in range(size)], axis, order, f32)
    return values[0]


def other_core(values):
    return swap_mask(values, "mp", 1)


def join_kernel(model_ref, own_ref, other_ref, out_ref):
    width = own_ref.shape[1]
    own_at = pl.multiple_of(model_ref[0] * width, width)
    other_at = pl.multiple_of((1 - model_ref[0]) * width, width)
    out_ref[:, pl.ds(own_at, width)] = own_ref[...]
    out_ref[:, pl.ds(other_at, width)] = other_ref[...]


def join_halves(own, other, model_at):
    tall, width = own.shape
    rows = min(256, tall)
    return pl.pallas_call(
        join_kernel,
        grid_spec=pltpu.PrefetchScalarGridSpec(
            num_scalar_prefetch=1,
            grid=(tall // rows,),
            in_specs=[pl.BlockSpec((rows, width), lambda i, m: (i, 0))] * 2,
            out_specs=pl.BlockSpec((rows, 2 * width), lambda i, m: (i, 0)),
        ),
        out_shape=jax.ShapeDtypeStruct((tall, 2 * width), own.dtype),
        cost_estimate=pl.CostEstimate(
            flops=0, bytes_accessed=8 * tall * width, transcendentals=0
        ),
        name="join_halves",
    )(model_at.astype(jnp.int32)[None], own, other)


def mix_kernel(slots, mix_ref, hist_ref, out_ref):
    rows, width = hist_ref.shape[1], hist_ref.shape[2]
    part = 512 if width % 512 == 0 else width

    def step(at, carry):
        r0 = pl.multiple_of(at * 16, 16)
        weights = mix_ref[pl.ds(r0, 16), :]
        for c0 in range(0, width, part):
            sums = [None] * STREAMS
            for k in range(slots):
                state = hist_ref[k, pl.ds(r0, 16), c0 : c0 + part].astype(f32)
                for s in range(STREAMS):
                    term = weights[:, s * slots + k : s * slots + k + 1] * state
                    sums[s] = term if sums[s] is None else sums[s] + term
            for s in range(STREAMS):
                out_ref[pl.ds(r0, 16), s * width + c0 : s * width + c0 + part] = sums[s].astype(bf16)
        return carry

    lax.fori_loop(0, rows // 16, step, 0)


def mix_streams(slot_mix, history, micro_at, depth_count, rows_mb):
    slots, _, width = history.shape
    rows = min(128, rows_mb)
    per = rows_mb // rows

    def row_block(i):
        return ((i // per) * MB + micro_at) * per + i % per

    return pl.pallas_call(
        functools.partial(mix_kernel, slots),
        grid=(depth_count * per,),
        in_specs=[
            pl.BlockSpec((rows, slot_mix.shape[1]), lambda i: (row_block(i), 0)),
            pl.BlockSpec((slots, rows, width), lambda i: (0, row_block(i), 0)),
        ],
        out_specs=pl.BlockSpec((rows, STREAMS * width), lambda i: (i, 0)),
        out_shape=jax.ShapeDtypeStruct((depth_count * rows_mb, STREAMS * width), bf16),
        cost_estimate=pl.CostEstimate(
            flops=2 * slots * STREAMS * depth_count * rows_mb * width,
            bytes_accessed=2 * (slots + STREAMS) * depth_count * rows_mb * width,
            transcendentals=0,
        ),
        name="mix_streams",
    )(slot_mix, history)


def unmix_kernel(slots, mix_ref, hist_ref, grad_ref, *rest):
    hist_grad_ref, slot_grad_ref = rest[-2:]
    rows, width = hist_ref.shape[1], hist_ref.shape[2]
    part = 512 if width % 512 == 0 else width

    def step(at, carry):
        r0 = pl.multiple_of(at * 16, 16)
        weights = mix_ref[pl.ds(r0, 16), :]
        totals = [None] * (STREAMS * slots)
        for c0 in range(0, width, part):
            grads = [
                grad_ref[pl.ds(r0, 16), s * width + c0 : s * width + c0 + part].astype(f32)
                for s in range(STREAMS)
            ]
            for k in range(slots):
                state = hist_ref[k, pl.ds(r0, 16), c0 : c0 + part].astype(f32)
                back = None
                for s in range(STREAMS):
                    at_sk = s * slots + k
                    term = weights[:, at_sk : at_sk + 1] * grads[s]
                    back = term if back is None else back + term
                    product = state * grads[s]
                    folded = product[:, 0:128]
                    for l0 in range(128, part, 128):
                        folded = folded + product[:, l0 : l0 + 128]
                    totals[at_sk] = folded if totals[at_sk] is None else totals[at_sk] + folded
                hist_grad_ref[k, pl.ds(r0, 16), c0 : c0 + part] = back.astype(bf16)
        lane = lax.broadcasted_iota(jnp.int32, (16, 128), 1)
        packed = jnp.zeros((16, 128), f32)
        for at_sk in range(STREAMS * slots):
            column = jnp.sum(totals[at_sk], axis=1, keepdims=True)
            packed = jnp.where(lane == at_sk, column, packed)
        slot_grad_ref[pl.ds(r0, 16), :] = packed
        return carry

    lax.fori_loop(0, rows // 16, step, 0)


def unmix_streams(slot_mix, history, grads, micro_at, depth_count, rows_mb, earlier):
    slots, tokens, width = history.shape
    rows = min(128, rows_mb)
    per = rows_mb // rows

    def row_block(i):
        return ((i // per) * MB + micro_at) * per + i % per

    in_specs = [
        pl.BlockSpec((rows, slot_mix.shape[1]), lambda i: (row_block(i), 0)),
        pl.BlockSpec((slots, rows, width), lambda i: (0, row_block(i), 0)),
        pl.BlockSpec((rows, STREAMS * width), lambda i: (i, 0)),
    ]
    operands = [slot_mix, history, grads]
    aliases = {}
    if earlier is not None:
        in_specs.append(pl.BlockSpec(memory_space=pl.ANY))
        operands.append(earlier)
        aliases = {3: 0}
    return pl.pallas_call(
        functools.partial(unmix_kernel, slots),
        grid=(depth_count * per,),
        in_specs=in_specs,
        out_specs=[
            pl.BlockSpec((slots, rows, width), lambda i: (0, row_block(i), 0)),
            pl.BlockSpec((rows, 128), lambda i: (i, 0)),
        ],
        out_shape=[
            jax.ShapeDtypeStruct((slots, tokens, width), bf16),
            jax.ShapeDtypeStruct((depth_count * rows_mb, 128), f32),
        ],
        input_output_aliases=aliases,
        cost_estimate=pl.CostEstimate(
            flops=4 * slots * STREAMS * depth_count * rows_mb * width,
            bytes_accessed=2 * (2 * slots + STREAMS) * depth_count * rows_mb * width,
            transcendentals=0,
        ),
        name="unmix_streams",
    )(*operands)


def own_spans(model_ref, width):
    own_at = pl.multiple_of(model_ref[0] * width, width)
    other_at = pl.multiple_of((1 - model_ref[0]) * width, width)
    return pl.ds(own_at, width), pl.ds(other_at, width)


def total_kernel(part_ref, cur_ref, last_ref, low_ref, resid_ref):
    width = resid_ref.shape[1]
    current = cur_ref[...].astype(f32)
    for s in range(STREAMS):
        lanes = slice(s * width, (s + 1) * width)
        total = part_ref[0, :, lanes].astype(f32)
        for at in range(1, part_ref.shape[0]):
            total = total + part_ref[at, :, lanes].astype(f32)
        total = total + last_ref[:, s : s + 1] * current
        if s == STREAMS - 1:
            resid_ref[...] = total
        low_ref[:, lanes] = total.astype(bf16)


def total_streams(parts, current_half, last):
    count, tall, wide = parts.shape
    width = wide // STREAMS
    rows = min(64, tall)
    return pl.pallas_call(
        total_kernel,
        grid=(tall // rows,),
        in_specs=[
            pl.BlockSpec((count, rows, wide), lambda i: (0, i, 0)),
            pl.BlockSpec((rows, width), lambda i: (i, 0)),
            pl.BlockSpec((rows, 128), lambda i: (i, 0)),
        ],
        out_specs=[
            pl.BlockSpec((rows, wide), lambda i: (i, 0)),
            pl.BlockSpec((rows, width), lambda i: (i, 0)),
        ],
        out_shape=[
            jax.ShapeDtypeStruct((tall, wide), bf16),
            jax.ShapeDtypeStruct((tall, width), f32),
        ],
        cost_estimate=pl.CostEstimate(
            flops=(count + 2) * tall * wide,
            bytes_accessed=2 * (count + 2) * tall * wide,
            transcendentals=0,
        ),
        name="total_streams",
    )(parts, current_half, last)


def norm_kernel(model_ref, own_ref, other_ref, gain_ref, normed_ref, ff_ref, stat_ref):
    rows, width = ff_ref.shape
    model = 2 * width
    own_span, other_span = own_spans(model_ref, width)
    lane = lax.broadcasted_iota(jnp.int32, (rows, 128), 1)
    stats = jnp.zeros((rows, 128), f32)
    for s in range(STREAMS):
        lanes = slice(s * width, (s + 1) * width)
        own = own_ref[:, lanes].astype(f32)
        other = other_ref[:, lanes].astype(f32)
        average = (
            jnp.sum(own, axis=-1, keepdims=True) + jnp.sum(other, axis=-1, keepdims=True)
        ) / model
        own, other = own - average, other - average
        variance = (
            jnp.sum(own * own, axis=-1, keepdims=True)
            + jnp.sum(other * other, axis=-1, keepdims=True)
        ) / model
        inverse = lax.rsqrt(variance + NORM_EPSILON)
        stats = jnp.where(lane == 2 * s, average, stats)
        stats = jnp.where(lane == 2 * s + 1, inverse, stats)
        norm_own = (own * inverse * gain_ref[s : s + 1, own_span]).astype(bf16)
        if s == STREAMS - 1:
            ff_ref[...] = norm_own
        else:
            normed_ref[s, :, own_span] = norm_own
            norm_other = (other * inverse * gain_ref[s : s + 1, other_span]).astype(bf16)
            normed_ref[s, :, other_span] = norm_other
    stat_ref[...] = stats


def norm_streams(low, low_other, gains, which):
    tall, wide = low.shape
    width = wide // STREAMS
    rows = min(64, tall)
    row = lambda i, m: (i, 0)
    return pl.pallas_call(
        norm_kernel,
        grid_spec=pltpu.PrefetchScalarGridSpec(
            num_scalar_prefetch=1,
            grid=(tall // rows,),
            in_specs=[
                pl.BlockSpec((rows, wide), row),
                pl.BlockSpec((rows, wide), row),
                pl.BlockSpec(gains.shape, lambda i, m: (0, 0)),
            ],
            out_specs=[
                pl.BlockSpec((3, rows, 2 * width), lambda i, m: (0, i, 0)),
                pl.BlockSpec((rows, width), row),
                pl.BlockSpec((rows, 128), row),
            ],
        ),
        out_shape=[
            jax.ShapeDtypeStruct((3, tall, 2 * width), bf16),
            jax.ShapeDtypeStruct((tall, width), bf16),
            jax.ShapeDtypeStruct((tall, 128), f32),
        ],
        cost_estimate=pl.CostEstimate(
            flops=20 * tall * wide, bytes_accessed=8 * tall * wide, transcendentals=0
        ),
        name="norm_streams",
    )(which, low, low_other, gains)


def turn(values, cosine, sine_up, sine_down, sign):
    up = pltpu.roll(values, HDIM - ROT // 2, 1)
    down = pltpu.roll(values, ROT // 2, 1)
    return values * cosine + sign * (up * sine_up + down * sine_down)


def project_kernel(
    x_ref, cot_ref, wq_ref, wk_ref, wv_ref, wo_ref, cos_ref, up_ref, down_ref, out_ref
):
    span = wq_ref.shape[1]
    tables = cos_ref[...], up_ref[...], down_ref[...]
    for kind, w_ref in enumerate((wq_ref, wk_ref, wv_ref, wo_ref)):
        rows = cot_ref[...] if kind == 3 else x_ref[kind]
        product = dot_nn(rows, w_ref[...])
        for begin in range(0, span, HDIM):
            head = product[:, begin : begin + HDIM]
            if kind < 2:
                head = turn(head, *tables, 1.0)
            out_ref[0, :, kind * span + begin : kind * span + begin + HDIM] = head.astype(bf16)


def project_heads(normed, cot, weights, tables, depth_count):
    _, rows, model = normed.shape
    span = weights[0].shape[1] // depth_count
    whole = lambda j: (0, 0)
    return pl.pallas_call(
        project_kernel,
        grid=(depth_count,),
        in_specs=[
            pl.BlockSpec((3, rows, model), lambda j: (0, 0, 0)),
            pl.BlockSpec((rows, model), whole),
        ]
        + [pl.BlockSpec((model, span), lambda j: (0, j))] * 4
        + [pl.BlockSpec((rows, HDIM), whole)] * 3,
        out_specs=pl.BlockSpec((1, rows, 4 * span), lambda j: (j, 0, 0)),
        out_shape=jax.ShapeDtypeStruct((depth_count, rows, 4 * span), bf16),
        compiler_params=pltpu.CompilerParams(vmem_limit_bytes=40 << 20),
        cost_estimate=pl.CostEstimate(
            flops=8 * rows * model * span * depth_count,
            bytes_accessed=8 * model * span * depth_count + 8 * rows * model,
            transcendentals=0,
        ),
        name="project_heads",
    )(normed, cot, *weights, *tables)


def attend_kernel(
    block, q_ref, k_ref, v_ref, g_ref, doc_col_ref, doc_row_ref, cos_ref, up_ref, down_ref,
    out_ref, dk_sum, dv_sum,
):
    length = q_ref.shape[0]
    scale = HDIM**-0.5
    heads_each = out_ref.shape[1] // (4 * HDIM)

    def lanes(kind):
        return pl.ds(pl.multiple_of((kind * heads_each + pl.program_id(0)) * HDIM, HDIM), HDIM)

    for begin in range(0, length, block):
        end = begin + block
        rows = slice(begin, end)
        queries, grads = q_ref[rows, :], g_ref[rows, :]
        keys, values = k_ref[0:end, :], v_ref[0:end, :]
        scores = dot_nt(queries, keys) * scale
        place_q = begin + lax.broadcasted_iota(jnp.int32, scores.shape, 0)
        place_k = lax.broadcasted_iota(jnp.int32, scores.shape, 1)
        allowed = (doc_col_ref[rows, :] == doc_row_ref[:, 0:end]) & (place_q >= place_k)
        scores = jnp.where(allowed, scores, MASKED)
        highest = jnp.max(scores, axis=-1, keepdims=True)
        exponent = jnp.exp(scores - highest)
        totals = jnp.sum(exponent, axis=-1, keepdims=True)
        attention = exponent * (1.0 / totals)
        low = attention.astype(bf16)
        out_ref[rows, lanes(0)] = dot_nn(low, values).astype(bf16)
        grad_att = dot_nt(grads, values).astype(bf16).astype(f32)
        weighted = jnp.sum(attention * grad_att, axis=-1, keepdims=True)
        grad_scores = (attention * (grad_att - weighted)).astype(bf16)
        grad_q = dot_nn(grad_scores, keys) * scale
        out_ref[rows, lanes(1)] = turn(
            grad_q, cos_ref[rows, :], up_ref[rows, :], down_ref[rows, :], -1.0
        ).astype(bf16)
        part_k = dot_tn(grad_scores, queries)
        part_v = dot_tn(low, grads)
        if begin > 0:
            dk_sum[0:begin, :] += part_k[0:begin]
            dv_sum[0:begin, :] += part_v[0:begin]
        dk_sum[begin:end, :] = part_k[begin:end]
        dv_sum[begin:end, :] = part_v[begin:end]
    grad_k = dk_sum[...] * scale
    out_ref[:, lanes(2)] = turn(grad_k, cos_ref[...], up_ref[...], down_ref[...], -1.0).astype(bf16)
    out_ref[:, lanes(3)] = dv_sum[...].astype(bf16)


def attend(packed, documents, tables, heads_each):
    length = packed.shape[0]
    block = min(256, length)
    whole = lambda h: (0, 0)

    def kind(at):
        return pl.BlockSpec((length, HDIM), lambda h: (0, at * heads_each + h))

    return pl.pallas_call(
        functools.partial(attend_kernel, block),
        grid=(heads_each,),
        in_specs=[kind(0), kind(1), kind(2), kind(3)]
        + [pl.BlockSpec((length, 1), whole), pl.BlockSpec((1, length), whole)]
        + [pl.BlockSpec((length, HDIM), whole)] * 3,
        out_specs=pl.BlockSpec((length, 4 * heads_each * HDIM), whole),
        out_shape=jax.ShapeDtypeStruct((length, 4 * heads_each * HDIM), bf16),
        scratch_shapes=[pltpu.VMEM((length, HDIM), f32)] * 2,
        compiler_params=pltpu.CompilerParams(vmem_limit_bytes=48 << 20),
        cost_estimate=pl.CostEstimate(
            flops=9 * heads_each * length * length * HDIM,
            bytes_accessed=16 * length * heads_each * HDIM + 12 * length * HDIM,
            transcendentals=heads_each * length * length,
        ),
        name="attend",
    )(packed, packed, packed, packed, documents[:, None], documents[None, :], *tables)


def gelu_parts(values):
    cdf = 0.5 * (1.0 + lax.erf(values * (0.5**0.5)))
    density = jnp.exp(-0.5 * values * values) * (1.0 / math.sqrt(2.0 * math.pi))
    return values * cdf, cdf + values * density


def ff_kernel(
    model_ref, x_ref, cot_ref, up_ref, down_ref,
    hidden_ref, grad_ref, out_own_ref, out_other_ref, back_own_ref, back_other_ref,
):
    own_span, other_span = own_spans(model_ref, out_own_ref.shape[1])
    up_pre = dot_nn(x_ref[...], up_ref[...])
    hidden, slope = gelu_parts(up_pre)
    hidden = hidden.astype(bf16)
    grad_up = (dot_nn(cot_ref[...], down_ref[...]) * slope).astype(bf16)
    hidden_ref[...] = hidden
    grad_ref[...] = grad_up
    back_other_ref[...] = dot_nt(grad_up, up_ref[other_span, :]).astype(bf16)
    back_own_ref[...] = dot_nt(grad_up, up_ref[own_span, :])
    out_other_ref[...] = dot_nt(hidden, down_ref[other_span, :]).astype(bf16)
    out_own_ref[...] = dot_nt(hidden, down_ref[own_span, :])


def feed_forward(x, cot, up_w, down_wt, which):
    tall, model = x.shape
    part = up_w.shape[1]
    width = model // 2
    rows = min(256, tall)
    row = lambda i, m: (i, 0)
    whole = lambda i, m: (0, 0)
    resident = pl.BlockSpec((model, part), whole, pipeline_mode=pl.Buffered(1))
    return pl.pallas_call(
        ff_kernel,
        grid_spec=pltpu.PrefetchScalarGridSpec(
            num_scalar_prefetch=1,
            grid=(tall // rows,),
            in_specs=[
                pl.BlockSpec((rows, model), row),
                pl.BlockSpec((rows, model), row),
                resident,
                resident,
            ],
            out_specs=[pl.BlockSpec((rows, part), row)] * 2
            + [pl.BlockSpec((rows, width), row)] * 4,
        ),
        out_shape=[jax.ShapeDtypeStruct((tall, part), bf16)] * 2
        + [
            jax.ShapeDtypeStruct((tall, width), f32),
            jax.ShapeDtypeStruct((tall, width), bf16),
            jax.ShapeDtypeStruct((tall, width), f32),
            jax.ShapeDtypeStruct((tall, width), bf16),
        ],
        compiler_params=pltpu.CompilerParams(vmem_limit_bytes=48 << 20),
        cost_estimate=pl.CostEstimate(
            flops=8 * tall * model * part,
            bytes_accessed=4 * model * part + 16 * tall * model,
            transcendentals=2 * tall * part,
        ),
        name="feed_forward",
    )(which, x, cot, up_w, down_wt)


def back_kernel(half_ref, ans_ref, wo_ref, wq_ref, wk_ref, wv_ref, out_ref, *flat):
    count, _, wide = ans_ref.shape
    span = wide // 4
    for kind, w_ref in enumerate((wo_ref, wq_ref, wk_ref, wv_ref)):
        total = None
        for j in range(count):
            term = dot_nt(
                ans_ref[j, :, kind * span : (kind + 1) * span], w_ref[:, j * span : (j + 1) * span]
            )
            total = term if total is None else total + term
        out_ref[kind] = total.astype(out_ref.dtype)
    if flat:

        @pl.when(pl.program_id(0) == 0)
        def _():
            for kind in range(4):
                for j in range(count):
                    flat[0][kind, :, j * span : (j + 1) * span] = ans_ref[
                        j, :, kind * span : (kind + 1) * span
                    ]


def back_project(answer, weights, half, dtype, flat):
    count, rows, wide = answer.shape
    model, heads_width = weights[0].shape
    width = model // 2
    steps = 2
    part = width // steps
    out_specs = [pl.BlockSpec((4, rows, part), lambda i, m: (0, 0, i))]
    out_shape = [jax.ShapeDtypeStruct((4, rows, width), dtype)]
    if flat:
        out_specs.append(pl.BlockSpec((4, rows, heads_width), lambda i, m: (0, 0, 0)))
        out_shape.append(jax.ShapeDtypeStruct((4, rows, heads_width), bf16))
    return pl.pallas_call(
        back_kernel,
        grid_spec=pltpu.PrefetchScalarGridSpec(
            num_scalar_prefetch=1,
            grid=(steps,),
            in_specs=[pl.BlockSpec((count, rows, wide), lambda i, m: (0, 0, 0))]
            + [pl.BlockSpec((part, heads_width), lambda i, m: (m[0] * steps + i, 0))] * 4,
            out_specs=out_specs,
        ),
        out_shape=out_shape,
        compiler_params=pltpu.CompilerParams(vmem_limit_bytes=40 << 20),
        cost_estimate=pl.CostEstimate(
            flops=8 * rows * heads_width * width,
            bytes_accessed=8 * heads_width * width + 20 * rows * width,
            transcendentals=0,
        ),
        name="back_project",
    )(half, answer, *weights)


def slope_kernel(
    model_ref, own_ref, got_ref, ff_ref, low_ref, stat_ref, gain_ref, scaled_ref, sum_ref, gain_out_ref
):
    rows, width = ff_ref.shape
    own_span, _ = own_spans(model_ref, width)
    lane = lax.broadcasted_iota(jnp.int32, (rows, 128), 1)
    packed = jnp.zeros((rows, 128), f32)
    totals = []
    for s in range(STREAMS):
        lanes = slice(s * width, (s + 1) * width)
        if s < 3:
            grad = own_ref[s + 1] + got_ref[s + 1].astype(f32)
        else:
            grad = ff_ref[...]
        average, inverse = stat_ref[:, 2 * s : 2 * s + 1], stat_ref[:, 2 * s + 1 : 2 * s + 2]
        hat = (low_ref[:, lanes].astype(f32) - average) * inverse
        totals.append(jnp.sum(grad * hat, axis=0, keepdims=True))
        scaled = grad * gain_ref[s : s + 1, own_span]
        scaled_ref[:, lanes] = scaled
        packed = jnp.where(lane == 2 * s, jnp.sum(scaled, axis=-1, keepdims=True), packed)
        packed = jnp.where(
            lane == 2 * s + 1, jnp.sum(scaled * hat, axis=-1, keepdims=True), packed
        )
    sum_ref[...] = packed
    totals = jnp.concatenate(totals, axis=0)

    @pl.when(pl.program_id(0) == 0)
    def _():
        gain_out_ref[...] = totals

    @pl.when(pl.program_id(0) > 0)
    def _():
        gain_out_ref[...] += totals


def norm_slopes(own, got, ff_grad, low, stats, gains, which):
    tall, wide = low.shape
    width = wide // STREAMS
    rows = min(64, tall)
    row = lambda i, m: (i, 0)
    cube = pl.BlockSpec((4, rows, width), lambda i, m: (0, i, 0))
    return pl.pallas_call(
        slope_kernel,
        grid_spec=pltpu.PrefetchScalarGridSpec(
            num_scalar_prefetch=1,
            grid=(tall // rows,),
            in_specs=[
                cube,
                cube,
                pl.BlockSpec((rows, width), row),
                pl.BlockSpec((rows, wide), row),
                pl.BlockSpec((rows, 128), row),
                pl.BlockSpec(gains.shape, lambda i, m: (0, 0)),
            ],
            out_specs=[
                pl.BlockSpec((rows, wide), row),
                pl.BlockSpec((rows, 128), row),
                pl.BlockSpec((STREAMS, width), lambda i, m: (0, 0)),
            ],
        ),
        out_shape=[
            jax.ShapeDtypeStruct((tall, wide), f32),
            jax.ShapeDtypeStruct((tall, 128), f32),
            jax.ShapeDtypeStruct((STREAMS, width), f32),
        ],
        cost_estimate=pl.CostEstimate(
            flops=12 * tall * wide, bytes_accessed=12 * tall * wide, transcendentals=0
        ),
        name="norm_slopes",
    )(which, own, got, ff_grad, low, stats, gains)


def grads_kernel(
    scaled_ref, mine_ref, theirs_ref, low_ref, stat_ref, cot_ref, cur_ref, last_ref,
    grad_ref, mix_ref, dot_ref,
):
    rows, width = cot_ref.shape
    lane = lax.broadcasted_iota(jnp.int32, (rows, 128), 1)
    means = (mine_ref[...] + theirs_ref[...]) / (2 * width)
    current = cur_ref[...].astype(f32)
    packed = jnp.zeros((rows, 128), f32)
    mixed = None
    for s in range(STREAMS):
        lanes = slice(s * width, (s + 1) * width)
        average, inverse = stat_ref[:, 2 * s : 2 * s + 1], stat_ref[:, 2 * s + 1 : 2 * s + 2]
        hat = (low_ref[:, lanes].astype(f32) - average) * inverse
        grad = inverse * (
            scaled_ref[:, lanes]
            - means[:, 2 * s : 2 * s + 1]
            - hat * means[:, 2 * s + 1 : 2 * s + 2]
        )
        if s == STREAMS - 1:
            grad = grad + cot_ref[...].astype(f32)
        grad = grad.astype(bf16)
        grad_ref[:, lanes] = grad
        grad = grad.astype(f32)
        term = last_ref[:, s : s + 1] * grad
        mixed = term if mixed is None else mixed + term
        packed = jnp.where(lane == s, jnp.sum(grad * current, axis=-1, keepdims=True), packed)
    mix_ref[...] = mixed
    dot_ref[...] = packed


def stream_grads(scaled, mine, theirs, low, stats, cot, current_half, last):
    tall, wide = low.shape
    width = wide // STREAMS
    rows = min(64, tall)
    row = lambda i: (i, 0)
    return pl.pallas_call(
        grads_kernel,
        grid=(tall // rows,),
        in_specs=[
            pl.BlockSpec((rows, wide), row),
            pl.BlockSpec((rows, 128), row),
            pl.BlockSpec((rows, 128), row),
            pl.BlockSpec((rows, wide), row),
            pl.BlockSpec((rows, 128), row),
            pl.BlockSpec((rows, width), row),
            pl.BlockSpec((rows, width), row),
            pl.BlockSpec((rows, 128), row),
        ],
        out_specs=[
            pl.BlockSpec((rows, wide), row),
            pl.BlockSpec((rows, width), row),
            pl.BlockSpec((rows, 128), row),
        ],
        out_shape=[
            jax.ShapeDtypeStruct((tall, wide), bf16),
            jax.ShapeDtypeStruct((tall, width), f32),
            jax.ShapeDtypeStruct((tall, 128), f32),
        ],
        cost_estimate=pl.CostEstimate(
            flops=12 * tall * wide, bytes_accessed=10 * tall * wide, transcendentals=0
        ),
        name="stream_grads",
    )(scaled, mine, theirs, low, stats, cot, current_half, last)


def turning_tables(places):
    half = ROT // 2
    inverse = jnp.exp(jnp.arange(half, dtype=f32) * (-2.0 * math.log(10000.0) / ROT))
    angles = places.astype(f32)[:, None] * inverse[None, :]
    cosine, sine = jnp.cos(angles), jnp.sin(angles)
    rows = places.shape[0]
    rest = jnp.zeros((rows, HDIM - ROT), f32)
    blank = jnp.zeros((rows, half), f32)
    return (
        jnp.concatenate([cosine, cosine, rest + 1.0], axis=1),
        jnp.concatenate([-sine, blank, rest], axis=1),
        jnp.concatenate([blank, sine, rest], axis=1),
    )


def local(
    history,
    slot_layer,
    current,
    positions,
    doc_ids,
    cotangent,
    norm_gains,
    generator_in,
    generator_out,
    query_weight,
    key_weight,
    value_weight,
    out_weight,
    up_weight,
    down_weight,
):
    dp_count = lax.axis_size("dp")
    depth_count = lax.axis_size("depth")
    dp_at = lax.axis_index("dp")
    model_at = lax.axis_index("mp")
    dp_bits = list(range(bit_count(dp_count)))
    order_one, order_two = dp_bits, dp_bits[1:] + dp_bits[:1]
    back_one, back_two = order_one[::-1], order_two[::-1]
    slots, tokens_held, width = history.shape
    model = current.shape[1]
    rows_mb = current.shape[0] // MB
    length = depth_count * rows_mb
    heads_width = query_weight.shape[1]
    heads_each = heads_width // HDIM // depth_count
    own_rows = query_weight.shape[0]
    ff_width = up_weight.shape[1]
    ff_part = ff_width // dp_count
    both = ("dp", "depth")

    def half_of(values, axis, which):
        return lax.dynamic_slice_in_dim(values, which * width, width, axis)

    small_cols = jnp.concatenate(
        [generator_in, norm_gains.T, jnp.zeros((own_rows, 128 - GEN - 5), bf16)], axis=1
    )
    small_all = gather_small(small_cols, both).reshape(model, 128)
    gen_first = small_all[:, :GEN]
    gain_float = small_all[:, GEN : GEN + 5].astype(f32).T
    second_rows = generator_out.shape[0]
    second_pad = -second_rows % 128
    second_all = gather_small(jnp.pad(generator_out, (0, second_pad))[None], both)
    gen_second = second_all.reshape(-1, second_rows + second_pad)[:, :second_rows]
    second_low = gen_second.reshape(GEN, STREAMS * MIX)

    stacked = jnp.concatenate([query_weight, key_weight, value_weight, out_weight.T], axis=0)
    over_depth = lax.all_gather(stacked, "depth", axis=0, tiled=True)
    over_depth = over_depth.reshape(depth_count, 4, own_rows, heads_width)
    gathered = []
    for at in range(4):
        piece = over_depth[:, at].reshape(depth_count * own_rows, heads_width)
        pieces = gather_masked(piece, "dp", order_one if at % 2 == 0 else order_two)
        gathered.append(reorder_masked(jnp.stack(pieces), "dp").reshape(model, heads_width))
    query_w, key_w, value_w, out_wt = gathered

    current_f = current.astype(f32)
    current_half = half_of(current, 1, model_at)
    mean_square = jnp.mean(current_f * current_f, axis=-1, keepdims=True)
    inverse_rms = lax.rsqrt(mean_square + RMS_EPSILON)
    unit = current_f * inverse_rms
    gen_normed = (unit * gain_float[4]).astype(bf16)
    gen_pre = dot_nn(gen_normed, gen_first)
    gen_hidden = gelu_exact(gen_pre).astype(bf16)
    column = jnp.arange(STREAMS * MIX)
    last_col = (column % MIX == MIX - 1).astype(f32)
    mixing = (dot_nn(gen_hidden, second_low) + last_col).astype(bf16)
    pick_last = (column[:, None] == (jnp.arange(128) * MIX + MIX - 1)[None, :]).astype(bf16)
    last = dot_nn(mixing, pick_last)

    layer_of = jnp.tile(slot_layer, STREAMS)
    stream_of = jnp.repeat(jnp.arange(STREAMS), slots)
    from_col = jnp.where(layer_of < MIX, stream_of * MIX + layer_of, -1)
    pick = (column[:, None] == from_col[None, :]).astype(f32)
    mix_all = gather_small(mixing, ("depth",)).reshape(depth_count * MB * rows_mb, STREAMS * MIX)
    slot_mix = dot_nn(mix_all, pick.astype(bf16))

    ff_local = jnp.stack([up_weight, down_weight.T])
    ff_local, slot_mix = lax.optimization_barrier((ff_local, slot_mix))
    ff_pieces = [
        lax.dynamic_slice_in_dim(ff_local, (dp_at ^ m) * ff_part, ff_part, 2)
        for m in range(dp_count)
    ]
    ff_pieces = [ff_pieces[0]] + [swap_mask(ff_pieces[m], "dp", m) for m in range(1, dp_count)]
    ff_rows = reorder_masked(jnp.stack(ff_pieces), "dp")

    def ff_gather(at):
        flat = ff_rows[:, at].reshape(dp_count * own_rows, ff_part)
        full = lax.all_gather(flat, "depth", axis=0, tiled=True)
        full = full.reshape(depth_count, dp_count, own_rows, ff_part)
        return jnp.swapaxes(full, 0, 1).reshape(model, ff_part)

    up_w, down_wt = ff_gather(0), ff_gather(1)

    cotangent, slot_mix = lax.optimization_barrier((cotangent, slot_mix))
    cot_full = join_halves(cotangent, other_core(cotangent), model_at)
    cot_group = []
    for micro_at in range(MB):
        rows = cotangent[micro_at * rows_mb : (micro_at + 1) * rows_mb]
        order = order_one if micro_at % 2 == 0 else order_two
        mine = jnp.concatenate(gather_masked(rows, "dp", order), axis=0)
        cot_group.append(join_halves(mine, other_core(mine), model_at))

    places_all = gather_small(positions, ("depth",))
    document_view = doc_ids.reshape(depth_count, MB, rows_mb)
    own_tables = turning_tables(positions)
    which = model_at.astype(jnp.int32)[None]
    gains = gain_float

    saved = []
    for micro_at in range(MB):
        span = slice(micro_at * rows_mb, (micro_at + 1) * rows_mb)
        partial = mix_streams(slot_mix, history, micro_at, depth_count, rows_mb)
        parts = partial.reshape(depth_count, rows_mb, STREAMS * width)
        parts = lax.all_to_all(parts, "depth", 0, 0, tiled=True)
        low, resid = total_streams(parts, current_half[span], last[span])
        normed, ff_normed, stats = norm_streams(low, other_core(low), gains, which)

        packed = project_heads(
            normed,
            cot_full[span],
            [query_w, key_w, value_w, out_wt],
            [t[span] for t in own_tables],
            depth_count,
        )
        by_head = lax.all_to_all(packed, "depth", 0, 0, tiled=True)
        by_head = by_head.reshape(length, 4 * heads_each * HDIM)
        documents = document_view[:, micro_at].reshape(length)
        seq_places = places_all[:, span].reshape(length)
        answer = attend(by_head, documents, turning_tables(seq_places), heads_each)
        answer = answer.reshape(depth_count, rows_mb, 4 * heads_each * HDIM)
        answer = lax.all_to_all(answer, "depth", 0, 0, tiled=True)

        order = order_one if micro_at % 2 == 0 else order_two
        back = back_one if micro_at % 2 == 0 else back_two
        mine = jnp.concatenate(gather_masked(ff_normed, "dp", order), axis=0)
        group_normed = join_halves(mine, other_core(mine), model_at)
        hidden, grad_up, out_own, out_other, back_own, back_other = feed_forward(
            group_normed, cot_group[micro_at], up_w, down_wt, which
        )

        def reduce_group(own, other, back=back):
            total = own + other_core(other).astype(f32)
            return scatter_masked(jnp.split(total, dp_count, axis=0), "dp", back)

        grad_norm_ff = reduce_group(back_own, back_other)
        ff_out = reduce_group(out_own, out_other)

        weights = [out_wt, query_w, key_w, value_w]
        (theirs,) = back_project(answer, weights, 1 - which, bf16, False)
        got = other_core(theirs)
        own, flat = back_project(answer, weights, which, f32, True)
        layer_rows = (resid + own[0] + got[0].astype(f32) + ff_out).astype(bf16)
        scaled, sums, gain_part = norm_slopes(own, got, grad_norm_ff, low, stats, gains, which)
        grad_low, current_mix, last_dot = stream_grads(
            scaled, sums, other_core(sums), low, stats, cotangent[span], current_half[span], last[span]
        )
        grad_all = lax.all_gather(grad_low, "depth", axis=0, tiled=True)
        saved.append(
            dict(
                normed=normed,
                group_normed=group_normed,
                hidden=hidden,
                grad_up=grad_up,
                flat=flat,
                grad_all=grad_all,
                grad_low=grad_low,
                layer_rows=layer_rows,
                gain=gain_part,
                current_mix=current_mix,
                last_dot=last_dot,
            )
        )

    def rows_of(name, at=None):
        return jnp.concatenate([s[name] if at is None else s[name][at] for s in saved], axis=0)

    def over_depth_sum(values):
        arrived = lax.all_to_all(values, "depth", 0, 0, tiled=True).astype(f32)
        return jnp.sum(arrived, axis=0)

    left = [rows_of("normed", 0), rows_of("normed", 1), rows_of("normed", 2), cot_full]
    right = [rows_of("flat", 1), rows_of("flat", 2), rows_of("flat", 3), rows_of("flat", 0)]
    scattered = []
    for at in range(4):
        by_dp = dot_tn(left[at], right[at]).reshape(dp_count, model // dp_count, heads_width)
        pieces = [
            lax.dynamic_index_in_dim(by_dp, dp_at ^ m, 0, keepdims=False) for m in range(dp_count)
        ]
        total = scatter_masked(pieces, "dp", back_one if at % 2 == 0 else back_two)
        total = total.astype(bf16).reshape(depth_count, own_rows, heads_width)
        scattered.append(over_depth_sum(total))

    def ff_scatter(left, right):
        grads = dot_tn(left, right).astype(bf16)
        grads = grads.reshape(dp_count, depth_count, own_rows, ff_part)
        return over_depth_sum(jnp.swapaxes(grads, 0, 1))

    cot_group_all = jnp.concatenate(cot_group, axis=0)
    ff_grads = [
        ff_scatter(rows_of("group_normed"), rows_of("grad_up")),
        ff_scatter(cot_group_all, rows_of("hidden")),
    ]
    ff_grads = jnp.stack(ff_grads).astype(bf16)
    ff_pieces = [
        lax.dynamic_index_in_dim(ff_grads, dp_at ^ m, 1, keepdims=False) for m in range(dp_count)
    ]
    ff_pieces = [ff_pieces[0]] + [swap_mask(ff_pieces[m], "dp", m) for m in range(1, dp_count)]
    ff_cols = reorder_masked(jnp.stack(ff_pieces), "dp").astype(f32)
    up_grad = jnp.swapaxes(ff_cols[:, 0], 0, 1).reshape(own_rows, ff_width)
    down_grad = jnp.swapaxes(ff_cols[:, 1], 1, 2).reshape(ff_width, own_rows)

    history_grad = None
    slot_parts = []
    for micro_at in range(MB):
        history_grad, slot_part = unmix_streams(
            slot_mix, history, saved[micro_at]["grad_all"], micro_at, depth_count, rows_mb, history_grad
        )
        slot_parts.append(slot_part.reshape(depth_count, 1, rows_mb, 128))
    slot_grads = jnp.concatenate(slot_parts, axis=1).reshape(-1, 128)[:, : STREAMS * slots]
    mix_grads = dot_exact(slot_grads, pick.T).reshape(depth_count, MB * rows_mb, STREAMS * MIX)
    grad_mixing = scatter_small(mix_grads, ("depth",))
    last_dots = rows_of("last_dot")
    grad_mixing = grad_mixing + dot_exact(last_dots, pick_last.astype(f32).T)
    grad_mixing = grad_mixing + other_core(grad_mixing)

    second_float = second_low.astype(f32)
    grad_second = dot_exact(gen_hidden.astype(f32).T, grad_mixing)
    grad_pre = dot_exact(grad_mixing, second_float.T) * gelu_slope(gen_pre)
    grad_first = dot_exact(gen_normed.astype(f32).T, grad_pre)
    grad_gen_normed = dot_exact(grad_pre, gen_first.astype(f32).T)
    gain_gen = jnp.sum(grad_gen_normed * unit, axis=0)
    grad_unit = grad_gen_normed * gain_float[4]
    shared = jnp.mean(grad_unit * unit, axis=-1, keepdims=True)
    current_gen = half_of(inverse_rms * (grad_unit - unit * shared), 1, model_at)
    current_grad = rows_of("current_mix") + current_gen

    gain_own = sum(s["gain"] for s in saved)
    gain_other = other_core(gain_own)
    gain_all = jnp.where(
        model_at == 0,
        jnp.concatenate([gain_own, gain_other], axis=1),
        jnp.concatenate([gain_other, gain_own], axis=1),
    )
    gain_all = jnp.concatenate([gain_all, gain_gen[None]], axis=0)
    small_grads = jnp.concatenate(
        [grad_first, gain_all.T, jnp.zeros((model, 128 - GEN - 5), f32)], axis=1
    )
    small_grads = scatter_small(small_grads.reshape(-1, own_rows, 128), both)
    second_grads = jnp.pad(grad_second.reshape(-1, second_rows), ((0, 0), (0, second_pad)))
    second_grads = scatter_small(second_grads[:, None], both)

    return (
        rows_of("layer_rows"),
        history_grad,
        current_grad,
        small_grads[:, GEN : GEN + 5].T,
        small_grads[:, :GEN],
        second_grads[0, :second_rows],
        scattered[0],
        scattered[1],
        scattered[2],
        scattered[3].T,
        up_grad,
        down_grad,
    )


def solution(mesh):
    return jax.shard_map(
        local,
        mesh=mesh,
        in_specs=(
            P("depth", "dp", "mp"),
            P("depth"),
            P(("dp", "depth"), None),
            P(("dp", "depth")),
            P("dp"),
            P(("dp", "depth"), "mp"),
            P(None, ("dp", "depth")),
            P(("dp", "depth"), None),
            P(("dp", "depth")),
            P(("dp", "depth"), "mp"),
            P(("dp", "depth"), "mp"),
            P(("dp", "depth"), "mp"),
            P("mp", ("dp", "depth")),
            P(("dp", "depth"), "mp"),
            P("mp", ("dp", "depth")),
        ),
        out_specs=(
            P(("dp", "depth"), "mp"),
            P("depth", "dp", "mp"),
            P(("dp", "depth"), "mp"),
            P(None, ("dp", "depth")),
            P(("dp", "depth"), None),
            P(("dp", "depth")),
            P(("dp", "depth"), "mp"),
            P(("dp", "depth"), "mp"),
            P(("dp", "depth"), "mp"),
            P("mp", ("dp", "depth")),
            P(("dp", "depth"), "mp"),
            P("mp", ("dp", "depth")),
        ),
        check_vma=False,
    )
```

time: 6580 us -> 1790 us (0.27)
  waiting for transfers between devices: 4490 us -> 968 us
  local copies, waits for them, and re-layouts: 1290 us -> 118 us
  matrix products: 387 us -> 47.1 us
  blocking collectives: 262 us -> 0 us
  Pallas kernels: 0 us -> 249 us
  starting transfers between devices: 3.96 us -> 247 us
    reduce_scatter x16 -> x0, waiting for transfers between devices: 2160 us -> none  [the longest x1 691 us: local(): lax.psum_scatter(summed(7), ('dp', 'depth'), scatter_dimension=0, tiled=T...]
    unnamed x42 -> x5, waiting for transfers between devices: 1220 us -> 0.75 us
    unnamed x244 -> x200, local copies, waits for them, and re-layouts: 1060 us -> 58.6 us
    all_gather x16 -> x5, waiting for transfers between devices: 1110 us -> 232 us  [the longest x1 143 us: local(): over_depth = lax.all_gather(stacked, 'depth', axis=0, tiled=True)]
    ppermute x0 -> x104, waiting for transfers between devices: none -> 424 us  [swap_mask(): return lax.ppermute(values, axis, [(i, i ^ mask) for i in range(size)])]
    dot_general x60 -> x16, matrix products: 387 us -> 47.1 us  [the longest x6 34.7 us: dot_tn(): lax.dot_general(a, b, (((0,), (0,)), ((), ())), preferred_element_type=f32)]
    all_to_all x0 -> x12, waiting for transfers between devices: none -> 311 us  [the longest x6 133 us: over_depth_sum(): arrived = lax.all_to_all(values, 'depth', 0, 0, tiled=True).astype(f32)]
    pallas_call x0 -> x27, Pallas kernels: none -> 249 us  [the longest x2 47.6 us: feed_forward(): pl.pallas_call(ff_kernel, grid_spec=pltpu.PrefetchScalarGridSpec(num_scal...]
  transfers between devices with their start and end apart: 38 -> 121, of which waited for: 26 -> 60; matrix products, arithmetic and copies ran while one was open for 7% -> 14% of each run, Pallas kernels for 0% -> 13%
where the time goes in v1:
time: 1790 us; the launch traced here: 1780 us
  waiting for transfers between devices  968 us (54%)
  Pallas kernels  249 us (14%)
  starting transfers between devices  247 us (14%)
  other arithmetic  139 us (8%)
  local copies, waits for them, and re-layouts  118 us (7%)
  matrix products  47.1 us (3%)
    ppermute x104, waiting for transfers between devices, swap_mask(): return lax.ppermute(values, axis, [(i, i ^ mask) for i in range(size)])  424 us
    all_gather x1, waiting for transfers between devices, local(): over_depth = lax.all_gather(stacked, 'depth', axis=0, tiled=True)  143 us
    all_to_all x6, waiting for transfers between devices, over_depth_sum(): arrived = lax.all_to_all(values, 'depth', 0, 0, tiled=True).astype(f32)  133 us
    ppermute x104, starting transfers between devices, swap_mask(): return lax.ppermute(values, axis, [(i, i ^ mask) for i in range(size)])  113 us
    all_gather x2, waiting for transfers between devices, ff_gather(): full = lax.all_gather(flat, 'depth', axis=0, tiled=True)  88.7 us
    all_to_all x2, waiting for transfers between devices, local(): answer = lax.all_to_all(answer, 'depth', 0, 0, tiled=True)  76.9 us
    all_to_all x2, starting transfers between devices, local(): by_head = lax.all_to_all(packed, 'depth', 0, 0, tiled=True)  73.5 us
    unnamed x200, local copies, waits for them, and re-layouts  58.6 us
  transfers between devices with their start and end apart: 121, of which 60 were waited for; matrix products, arithmetic and copies ran while one was open for 14% of the time, Pallas kernels for 13%

profile of v1, /device:TPU:0, one launch (start us, length us, event | category | flops | bytes accessed | tf_op | source)
XLA Modules:
  0.0 1782.9 jit_solution(7090163880735263895)
XLA Ops:
  87.8 143.1 %all-gather.6.cloned.1.call-done = bf16[2048,1024]{1,0:T(8,128)(2,1)} async-done(((bf16[512,1024]{1,0:T(8,128)(2,1)}), bf16[2048,1024]{1,0:T(8,128)(2,1)}) %all-gather.6.cloned.1.call-update) | async-done | bytes 4194320 | tf_op jit(solution)/shard_map/all_gather | solution.py:821
  245.2 16.3 collective-permute-done.24
  264.9 19.1 %collective-permute-done.27 = bf16[512,1024]{1,0:T(8,128)(2,1)} collective-permute-done((bf16[512,1024]{1,0:T(8,128)(2,1)}, bf16[512,1024]{1,0:T(8,128)(2,1)}, u32[]{:S(2)}, u32[]{:S(2)}) %collective-permute-start.27) | collective-permute-done | bytes 1048608 | tf_op jit(solution)/shard_map/ppermute | solution.py:60
  311.4 17.5 collective-permute-done.25
  336.8 16.2 collective-permute-done.20
  353.3 22.2 %collective-permute-done.22 = bf16[512,1024]{1,0:T(8,128)(2,1)S(1)} collective-permute-done((bf16[512,1024]{1,0:T(8,128)(2,1)}, bf16[512,1024]{1,0:T(8,128)(2,1)S(1)}, u32[]{:S(2)}, u32[]{:S(2)}) %collective-permute-start.22) | collective-permute-done | bytes 1048608 | tf_op jit(solution)/shard_map/ppermute | solution.py:60
  435.8 62.4 %all-to-all-start.1 = ((bf16[4,256,1024]{2,1,0:T(8,128)(2,1)}), bf16[4,256,1024]{2,1,0:T(8,128)(2,1)}, u32[]{:S(2)}, u32[]{:S(2)}) async-start(bf16[4,256,1024]{2,1,0:T(8,128)(2,1)} %project_heads.2), calls=%async_computation.1 | async-start | bytes 4194304 | tf_op jit(solution)/shard_map/all_to_all | solution.py:899
  512.8 36.1 %collective-permute-done.29 = s32[1,512]{1,0:T(1,128)S(1)} collective-permute-done((s32[1,512]{1,0:T(1,128)S(1)}, s32[1,512]{1,0:T(1,128)S(1)}, u32[]{:S(2)}, u32[]{:S(2)}) %collective-permute-start.29) | collective-permute-done | bytes 2080 | tf_op jit(solution)/shard_map/ppermute | solution.py:60
  554.0 31.6 %collective-permute-done.30 = s32[1,512]{1,0:T(1,128)S(1)} collective-permute-done((s32[1,512]{1,0:T(1,128)S(1)}, s32[1,512]{1,0:T(1,128)S(1)}, u32[]{:S(2)}, u32[]{:S(2)}) %collective-permute-start.30) | collective-permute-done | bytes 2080 | tf_op jit(solution)/shard_map/ppermute | solution.py:60
  607.1 14.3 mix_streams.3
  621.5 38.1 %all-to-all-done.2.ans_ref = bf16[4,256,1024]{2,1,0:T(8,128)(2,1)S(1)} async-done(((bf16[4,256,1024]{2,1,0:T(8,128)(2,1)}), bf16[4,256,1024]{2,1,0:T(8,128)(2,1)S(1)}, u32[]{:S(2)}, u32[]{:S(2)}) %all-to-all-start.2) | async-done | bytes 2097184 | tf_op jit(solution)/shard_map/all_to_all | solution.py:905
  727.7 88.7 %all-gather.10.cloned.1.call-done = bf16[2048,1024]{1,0:T(8,128)(2,1)} async-done(((bf16[512,1024]{1,0:T(8,128)(2,1)}), bf16[2048,1024]{1,0:T(8,128)(2,1)}) %all-gather.10.cloned.1.call-update) | async-done | bytes 4194320 | tf_op jit(solution)/shard_map/all_gather | solution.py:862
  825.9 23.8 %feed_forward.2 = (bf16[1024,1024]{1,0:T(8,128)(2,1)S(1)}, bf16[1024,1024]{1,0:T(8,128)(2,1)S(1)}, f32[1024,1024]{1,0:T(8,128)}, bf16[1024,1024]{1,0:T(8,128)(2,...) custom-call(s32[1]{0:T(128)} %bitcast.35.model_ref.half_ref, bf16[1024,2048]{1,0:T(8,128)(2,1)} %join_halves.6.x_ref, ...), custom_call_target="tpu_custom_call" | custom-call | flops 17179869184 | bytes 41943040 | tf_op jit(solution)/shard_map/feed_forward/pallas_call | solution.py:533
  862.7 53.5 %all-to-all-done.3.part_ref = bf16[4,256,4096]{2,1,0:T(8,128)(2,1)} async-done(((bf16[4,256,4096]{2,1,0:T(8,128)(2,1)}), bf16[4,256,4096]{2,1,0:T(8,128)(2,1)}, u32[]{:S(2)}, u32[]{:S(2)}) %all-to-all-start.3) | async-done | bytes 8388640 | tf_op jit(solution)/shard_map/all_to_all | solution.py:888
  1043.9 46.9 %all-to-all-done.4 = bf16[4,256,1024]{2,1,0:T(8,128)(2,1)} async-done(((bf16[4,256,1024]{2,1,0:T(8,128)(2,1)}), bf16[4,256,1024]{2,1,0:T(8,128)(2,1)}, u32[]{:S(2)}, u32[]{:S(2)}) %all-to-all-start.4) | async-done | bytes 2097184 | tf_op jit(solution)/shard_map/all_to_all | solution.py:899
  1116.1 23.8 %feed_forward.3 = (bf16[1024,1024]{1,0:T(8,128)(2,1)S(1)}, bf16[1024,1024]{1,0:T(8,128)(2,1)S(1)}, f32[1024,1024]{1,0:T(8,128)}, bf16[1024,1024]{1,0:T(8,128)(2,...) custom-call(s32[1]{0:T(128)} %bitcast.35.model_ref.half_ref, bf16[1024,2048]{1,0:T(8,128)(2,1)} %join_halves.8.x_ref, ...), custom_call_target="tpu_custom_call" | custom-call | flops 17179869184 | bytes 41943040 | tf_op jit(solution)/shard_map/feed_forward/pallas_call | solution.py:533
  1157.6 38.8 %all-to-all-done.5.ans_ref = bf16[4,256,1024]{2,1,0:T(8,128)(2,1)S(1)} async-done(((bf16[4,256,1024]{2,1,0:T(8,128)(2,1)}), bf16[4,256,1024]{2,1,0:T(8,128)(2,1)S(1)}, u32[]{:S(2)}, u32[]{:S(2)}) %all-to-all-start.5) | async-done | bytes 2097184 | tf_op jit(solution)/shard_map/all_to_all | solution.py:905
  1277.2 67.0 %all-to-all-done.10 = bf16[4,4,128,1024]{3,2,1,0:T(8,128)(2,1)} async-done(((bf16[4,4,128,1024]{3,2,1,0:T(8,128)(2,1)}), bf16[4,4,128,1024]{3,2,1,0:T(8,128)(2,1)}, u32[]{:S(2)}, u32[]{:S(2)}) %all-to-all-start.10) | async-done | bytes 4194336 | tf_op jit(solution)/shard_map/all_to_all | solution.py:952
  1384.4 16.0 collective-permute-done.99
  1416.8 14.3 collective-permute-done.98
  1450.4 66.3 %all-to-all-done.11 = bf16[4,4,128,1024]{3,2,1,0:T(8,128)(2,1)} async-done(((bf16[4,4,128,1024]{3,2,1,0:T(8,128)(2,1)}), bf16[4,4,128,1024]{3,2,1,0:T(8,128)(2,1)}, u32[]{:S(2)}, u32[]{:S(2)}) %all-to-all-start.11) | async-done | bytes 4194336 | tf_op jit(solution)/shard_map/all_to_all | solution.py:952
  1646.2 19.5 %unmix_streams.2 = (bf16[5,2048,1024]{2,1,0:T(8,128)(2,1)}, f32[1024,128]{1,0:T(8,128)}) custom-call(f32[2048,20]{1,0:T(8,128)} %copy.175.mix_ref, bf16[5,2048,1024]{2,1,0:T(8,128)(2,1)} %hist_ref.7, bf16[1024,4096]{1,0:T(8,128)(2,1)} %all-gather.14.cloned.1.call-done.grad_ref), custom_call_target="tpu_custom_call" | custom-call | flops 83886080 | bytes 29360128 | tf_op jit(solution)/shard_map/unmix_streams/pallas_call | solution.py:248
  1665.7 19.6 %unmix_streams.3 = (bf16[5,2048,1024]{2,1,0:T(8,128)(2,1)}, f32[1024,128]{1,0:T(8,128)}) custom-call(f32[2048,20]{1,0:T(8,128)} %copy.175.mix_ref, bf16[5,2048,1024]{2,1,0:T(8,128)(2,1)} %hist_ref.7, bf16[1024,4096]{1,0:T(8,128)(2,1)} %all-gather.12.cloned.1.call-done.grad_ref, ...), custom_call_target="tpu_custom_call", output_to_operand_aliasing={{0}: (3, {})} | custom-call | flops 83886080 | bytes 29360128 | tf_op jit(solution)/shard_map/unmix_streams/pallas_call | solution.py:248
  1699.5 22.3 %collective-permute-done.73 = f32[1,512,72]{1,2,0:T(8,128)S(1)} collective-permute-done((f32[1,512,72]{1,2,0:T(8,128)S(1)}, f32[1,512,72]{1,2,0:T(8,128)S(1)}, u32[]{:S(2)}, u32[]{:S(2)}) %collective-permute-start.73) | collective-permute-done | bytes 147488 | tf_op jit(solution)/shard_map/ppermute | solution.py:60
  (656 shorter events, 849.6 us)
Async XLA Ops:
  77.3 313.5 %all-to-all-start = ((bf16[4,256,4096]{2,1,0:T(8,128)(2,1)}), bf16[4,256,4096]{2,1,0:T(8,128)(2,1)}, u32[]{:S(2)}, u32[]{:S(2)}) async-start(bf16[4,256,4096]{2,1,0:T(8,128)(2,1)} %bitcast.429), calls=%async_computation | async-start | bytes 16777216 | tf_op jit(solution)/shard_map/all_to_all | solution.py:888
  83.0 147.8 %all-gather.6.cloned.1.call-start = ((), (), s32[]{:S(2)}) async-start(), calls=%async_computation.12 | async-start | bytes 5242880 | tf_op jit(solution)/shard_map/all_gather | solution.py:821
  87.8 154.7 %collective-permute-start.16 = (bf16[512,1024]{1,0:T(8,128)(2,1)S(1)}, bf16[512,1024]{1,0:T(8,128)(2,1)}, u32[]{:S(2)}, u32[]{:S(2)}) collective-permute-start(bf16[512,1024]{1,0:T(8,128)(2,1)S(1)} %copy-done.41), channel_id=1, source_target_pairs={{0,1},{1,0},{2,3},{3,2},{4,5},{5,4},{6,7},{7,6},{8,9},{9,8},{10,11... | collective-permute-start | bytes 3145736 | tf_op jit(solution)/shard_map/ppermute | solution.py:60
  333.2 165.0 %collective-permute-start.43 = (bf16[2,128,1024]{1,2,0:T(8,128)(2,1)}, bf16[2,128,1024]{1,2,0:T(8,128)(2,1)}, u32[]{:S(2)}, u32[]{:S(2)}) collective-permute-start(bf16[2,128,1024]{1,2,0:T(8,128)(2,1)} %get-tuple-element.189), channel_id=1, source_target_pairs={{0,24},{8,16},{16,8},{24,0},{1,25},{9,17},{17,9},{25,1},{2,26},{10... | collective-permute-start | bytes 1572872 | tf_op jit(solution)/shard_map/ppermute | solution.py:60
  353.0 145.1 %collective-permute-start.42 = (bf16[2,128,1024]{1,2,0:T(8,128)(2,1)}, bf16[2,128,1024]{1,2,0:T(8,128)(2,1)}, u32[]{:S(2)}, u32[]{:S(2)}) collective-permute-start(bf16[2,128,1024]{1,2,0:T(8,128)(2,1)} %get-tuple-element.190), channel_id=1, source_target_pairs={{0,16},{8,24},{16,0},{24,8},{1,17},{9,25},{17,1},{25,9},{2,18},{10... | collective-permute-start | bytes 1572872 | tf_op jit(solution)/shard_map/ppermute | solution.py:60
  375.5 122.7 %collective-permute-start.41 = (bf16[2,128,1024]{1,2,0:T(8,128)(2,1)S(1)}, bf16[2,128,1024]{1,2,0:T(8,128)(2,1)}, u32[]{:S(2)}, u32[]{:S(2)}) collective-permute-start(bf16[2,128,1024]{1,2,0:T(8,128)(2,1)S(1)} %get-tuple-element.191), channel_id=1, source_target_pairs={{0,8},{8,0},{16,24},{24,16},{1,9},{9,1},{17,25},{25,17},{2,10},{10... | collective-permute-start | bytes 1572872 | tf_op jit(solution)/shard_map/ppermute | solution.py:60
  435.8 155.6 %all-to-all-start.1 = ((bf16[4,256,1024]{2,1,0:T(8,128)(2,1)}), bf16[4,256,1024]{2,1,0:T(8,128)(2,1)}, u32[]{:S(2)}, u32[]{:S(2)}) async-start(bf16[4,256,1024]{2,1,0:T(8,128)(2,1)} %project_heads.2), calls=%async_computation.1 | async-start | bytes 4194304 | tf_op jit(solution)/shard_map/all_to_all | solution.py:899
  498.2 224.8 %all-gather.8.cloned.1.call-start = ((), (), s32[]{:S(2)}) async-start(), calls=%async_computation.13 | async-start | bytes 5242880 | tf_op jit(solution)/shard_map/all_gather | solution.py:862
  659.6 256.5 %all-to-all-start.3 = ((bf16[4,256,4096]{2,1,0:T(8,128)(2,1)}), bf16[4,256,4096]{2,1,0:T(8,128)(2,1)}, u32[]{:S(2)}, u32[]{:S(2)}) async-start(bf16[4,256,4096]{2,1,0:T(8,128)(2,1)} %bitcast.430), calls=%async_computation.3 | async-start | bytes 16777216 | tf_op jit(solution)/shard_map/all_to_all | solution.py:888
  665.4 151.0 %all-gather.10.cloned.1.call-start = ((), (), s32[]{:S(2)}) async-start(), calls=%async_computation.14 | async-start | bytes 5242880 | tf_op jit(solution)/shard_map/all_gather | solution.py:862
  666.1 980.0 %all-gather.14.cloned.1.call-start = ((), (), s32[]{:S(2)}) async-start(), calls=%async_computation.16 | async-start | bytes 10485760 | tf_op jit(solution)/shard_map/all_gather | solution.py:931
  718.2 103.0 %collective-permute-start.36 = (bf16[1024,1024]{1,0:T(8,128)(2,1)}, bf16[1024,1024]{1,0:T(8,128)(2,1)}, u32[]{:S(2)}, u32[]{:S(2)}) collective-permute-start(bf16[1024,1024]{1,0:T(8,128)(2,1)} %constant_dynamic-update-slice_fusion.own_ref), channel_id=1, source_target_pairs={{0,1},{1,0},{2,3},{3,2},{4,5},{5,4},{6,7},{7,6},{8,9},{9,8},{10,11... | collective-permute-start | bytes 6291464 | tf_op jit(solution)/shard_map/ppermute | solution.py:60
  857.8 83.0 %collective-permute-start.32 = (bf16[4,256,1024]{2,1,0:T(8,128)(2,1)}, bf16[4,256,1024]{2,1,0:T(8,128)(2,1)}, u32[]{:S(2)}, u32[]{:S(2)}) collective-permute-start(bf16[4,256,1024]{2,1,0:T(8,128)(2,1)} %back_project.5), channel_id=1, source_target_pairs={{0,1},{1,0},{2,3},{3,2},{4,5},{5,4},{6,7},{7,6},{8,9},{9,8},{10,11... | collective-permute-start | bytes 6291464 | tf_op jit(solution)/shard_map/ppermute | solution.py:60
  979.3 111.5 %all-to-all-start.4 = ((bf16[4,256,1024]{2,1,0:T(8,128)(2,1)}), bf16[4,256,1024]{2,1,0:T(8,128)(2,1)}, u32[]{:S(2)}, u32[]{:S(2)}) async-start(bf16[4,256,1024]{2,1,0:T(8,128)(2,1)} %project_heads.3), calls=%async_computation.4 | async-start | bytes 4194304 | tf_op jit(solution)/shard_map/all_to_all | solution.py:899
  1103.0 93.4 %all-to-all-start.5 = ((bf16[4,256,1024]{2,1,0:T(8,128)(2,1)}), bf16[4,256,1024]{2,1,0:T(8,128)(2,1)S(1)}, u32[]{:S(2)}, u32[]{:S(2)}) async-start(bf16[4,256,1024]{2,1,0:T(8,128)(2,1)} %bitcast.411), calls=%async_computation.5 | async-start | bytes 4194304 | tf_op jit(solution)/shard_map/all_to_all | solution.py:905
  1196.4 147.8 %all-to-all-start.10 = ((bf16[4,4,128,1024]{3,2,1,0:T(8,128)(2,1)}), bf16[4,4,128,1024]{3,2,1,0:T(8,128)(2,1)}, u32[]{:S(2)}, u32[]{:S(2)}) async-start(bf16[4,4,128,1024]{3,2,1,0:T(8,128)(2,1)} %bitcast.437), calls=%async_computation.10 | async-start | bytes 8388608 | tf_op jit(solution)/shard_map/all_to_all | solution.py:952
  1201.3 464.3 %all-gather.12.cloned.1.call-start = ((), (), s32[]{:S(2)}) async-start(), calls=%async_computation.15 | async-start | bytes 10485760 | tf_op jit(solution)/shard_map/all_gather | solution.py:931
  1252.0 108.2 %collective-permute-start.44 = (bf16[1024,1024]{1,0:T(8,128)(2,1)}, bf16[1024,1024]{1,0:T(8,128)(2,1)}, u32[]{:S(2)}, u32[]{:S(2)}) collective-permute-start(bf16[1024,1024]{1,0:T(8,128)(2,1)} %get-tuple-element.68), channel_id=1, source_target_pairs={{0,1},{1,0},{2,3},{3,2},{4,5},{5,4},{6,7},{7,6},{8,9},{9,8},{10,11... | collective-permute-start | bytes 6291464 | tf_op jit(solution)/shard_map/ppermute | solution.py:60
  1344.2 172.5 %all-to-all-start.11 = ((bf16[4,4,128,1024]{3,2,1,0:T(8,128)(2,1)}), bf16[4,4,128,1024]{3,2,1,0:T(8,128)(2,1)}, u32[]{:S(2)}, u32[]{:S(2)}) async-start(bf16[4,4,128,1024]{3,2,1,0:T(8,128)(2,1)} %bitcast.436), calls=%async_computation.11 | async-start | bytes 8388608 | tf_op jit(solution)/shard_map/all_to_all | solution.py:952
  1367.0 156.0 %collective-permute-start.46 = (bf16[256,1024]{1,0:T(8,128)(2,1)}, bf16[256,1024]{1,0:T(8,128)(2,1)}, u32[]{:S(2)}, u32[]{:S(2)}) collective-permute-start(bf16[256,1024]{1,0:T(8,128)(2,1)} %get-tuple-element.181), channel_id=1, source_target_pairs={{0,16},{8,24},{16,0},{24,8},{1,17},{9,25},{17,1},{25,9},{2,18},{10... | collective-permute-start | bytes 1572872 | tf_op jit(solution)/shard_map/ppermute | solution.py:60
  1380.0 146.1 %collective-permute-start.60 = (bf16[256,1024]{1,0:T(8,128)(2,1)}, bf16[256,1024]{1,0:T(8,128)(2,1)}, u32[]{:S(2)}, u32[]{:S(2)}) collective-permute-start(bf16[256,1024]{1,0:T(8,128)(2,1)} %get-tuple-element.185), channel_id=1, source_target_pairs={{0,8},{8,0},{16,24},{24,16},{1,9},{9,1},{17,25},{25,17},{2,10},{10... | collective-permute-start | bytes 1572872 | tf_op jit(solution)/shard_map/ppermute | solution.py:60
  1431.1 108.0 %collective-permute-start.95 = (bf16[512,1024]{1,0:T(8,128)(2,1)S(1)}, bf16[512,1024]{1,0:T(8,128)(2,1)}, u32[]{:S(2)}, u32[]{:S(2)}) collective-permute-start(bf16[512,1024]{1,0:T(8,128)(2,1)S(1)} %get-tuple-element.143), channel_id=1, source_target_pairs={{0,16},{8,24},{16,0},{24,8},{1,17},{9,25},{17,1},{25,9},{2,18},{10... | collective-permute-start | bytes 3145736 | tf_op jit(solution)/shard_map/ppermute | solution.py:60
  1432.3 97.8 %collective-permute-start.93 = (bf16[512,1024]{1,0:T(8,128)(2,1)S(1)}, bf16[512,1024]{1,0:T(8,128)(2,1)}, u32[]{:S(2)}, u32[]{:S(2)}) collective-permute-start(bf16[512,1024]{1,0:T(8,128)(2,1)S(1)} %get-tuple-element.146), channel_id=1, source_target_pairs={{0,8},{8,0},{16,24},{24,16},{1,9},{9,1},{17,25},{25,17},{2,10},{10... | collective-permute-start | bytes 3145736 | tf_op jit(solution)/shard_map/ppermute | solution.py:60
  1449.5 84.4 %collective-permute-start.90 = (bf16[512,1024]{1,0:T(8,128)(2,1)}, bf16[512,1024]{1,0:T(8,128)(2,1)}, u32[]{:S(2)}, u32[]{:S(2)}) collective-permute-start(bf16[512,1024]{1,0:T(8,128)(2,1)} %get-tuple-element.148), channel_id=1, source_target_pairs={{0,16},{8,24},{16,0},{24,8},{1,17},{9,25},{17,1},{25,9},{2,18},{10... | collective-permute-start | bytes 3145736 | tf_op jit(solution)/shard_map/ppermute | solution.py:60
  (190 other events, 3783.8 us)
Sparse Core Ops, SparseCore 0:
  86.0 144.7 all-gather.5
  508.5 125.2 all-gather.7
  668.4 147.9 all-gather.9
  956.8 246.3 all-gather.13
  1261.2 256.9 all-gather.11

commit v2 on v1

--- a/solution.py
+++ b/solution.py
@@ -14,6 +14,7 @@
 MB = 2
 MIX = 18
 STREAMS = 4
+COST = 1
 
 PRECISE = lax.Precision.HIGHEST
 NORM_EPSILON = 1e-05
@@ -75,6 +76,56 @@
         for m in [m for m in pieces if m & flag]:
             arrived = swap_mask(pieces.pop(m).astype(link), axis, flag)
             pieces[m ^ flag] = pieces[m ^ flag].astype(f32) + arrived.astype(f32)
+    return pieces[0]
+
+
+def core_orders():
+    bits = list(range(bit_count(lax.axis_size("dp"))))
+    return bits, bits[1:] + bits[:1]
+
+
+def place_mask(place):
+    masks = []
+    for order in core_orders():
+        masks.append(sum(1 << bit for at, bit in enumerate(order) if (place >> at) & 1))
+    return jnp.where(lax.axis_index("mp") % 2 == 0, masks[0], masks[1])
+
+
+def place_index(place):
+    return lax.axis_index("dp") ^ place_mask(place)
+
+
+def core_hop(values, at):
+    orders, cores = core_orders(), lax.axis_size("mp")
+    pairs = []
+    for i in range(lax.axis_size("dp")):
+        for core in range(cores):
+            partner = i ^ (1 << orders[core % 2][at])
+            pairs.append((i * cores + core, partner * cores + core))
+    return lax.ppermute(values, ("dp", "mp"), pairs)
+
+
+def group_gather(values):
+    pieces = values[None]
+    for at in range(bit_count(lax.axis_size("dp"))):
+        pieces = jnp.concatenate([pieces, core_hop(pieces, at)], axis=0)
+    buffer = None
+    for place in range(pieces.shape[0]):
+        buffer = place_block(
+            buffer, pieces[place][None], place_index(place), pieces.shape[0]
+        )
+    return buffer[0]
+
+
+def group_scatter(blocks):
+    count = blocks.shape[0]
+    pieces = [
+        lax.dynamic_index_in_dim(blocks, place_index(p), 0, keepdims=False) for p in range(count)
+    ]
+    for at in reversed(range(bit_count(count))):
+        half = 1 << at
+        arrived = core_hop(jnp.stack(pieces[half : 2 * half]).astype(bf16), at).astype(f32)
+        pieces = [pieces[p] + arrived[p] for p in range(half)]
     return pieces[0]
 
 
@@ -110,6 +161,77 @@
     return values[0]
 
 
+def line_size():
+    return lax.axis_size("depth"), lax.axis_index("depth")
+
+
+def fence(*values):
+    return lax.optimization_barrier(values)
+
+
+class LineGather:
+
+    def __init__(self, values):
+        self.up, self.down = [values], [values]
+
+    def step(self):
+        size, _ = line_size()
+        at = len(self.up)
+        if at < size:
+            up_pairs = [(i, i + 1) for i in range(at - 1, size - 1)]
+            down_pairs = [(i, i - 1) for i in range(1, size - at + 1)]
+            self.up.append(lax.ppermute(self.up[-1], "depth", up_pairs))
+            self.down.append(lax.ppermute(self.down[-1], "depth", down_pairs))
+
+    def hold(self, *others):
+        kept = fence((self.up[1:], self.down[1:]), *others)
+        (up, down), rest = kept[0], kept[1:]
+        self.up, self.down = self.up[:1] + list(up), self.down[:1] + list(down)
+        return rest
+
+    def placed(self):
+        size, here = line_size()
+        buffer = place_block(None, self.up[0], here, size)
+        for at in range(1, size):
+            buffer = place_block(
+                buffer,
+                self.up[at],
+                lax.rem(here - at + size, size),
+                size,
+                self.down[size - at],
+                here >= at,
+            )
+        return buffer
+
+
+class LineScatter:
+
+    def __init__(self, terms):
+        self.terms, self.at = terms, 0
+        self.up = self.down = None
+
+    def step(self):
+        size, here = line_size()
+        self.at += 1
+        if self.at >= size:
+            return
+        goes_up, goes_down = hop_sums(
+            self.terms,
+            jnp.minimum(size - self.at + here, size - 1),
+            jnp.maximum(here - size + self.at, 0),
+            self.up,
+            self.down,
+        )
+        up_pairs = [(i, i + 1) for i in range(min(self.at, size - 1))]
+        down_pairs = [(size - 1 - i, size - 2 - i) for i in range(min(self.at, size - 1))]
+        self.up = lax.ppermute(goes_up, "depth", up_pairs)
+        self.down = lax.ppermute(goes_down, "depth", down_pairs)
+
+    def hold(self, *others):
+        (self.up, self.down), *rest = fence((self.up, self.down), *others)
+        return rest
+
+
 def other_core(values):
     return swap_mask(values, "mp", 1)
 
@@ -134,11 +256,228 @@
             out_specs=pl.BlockSpec((rows, 2 * width), lambda i, m: (i, 0)),
         ),
         out_shape=jax.ShapeDtypeStruct((tall, 2 * width), own.dtype),
-        cost_estimate=pl.CostEstimate(
+        cost_estimate=spent(
             flops=0, bytes_accessed=8 * tall * width, transcendentals=0
         ),
         name="join_halves",
     )(model_at.astype(jnp.int32)[None], own, other)
+
+
+def spent(flops, bytes_accessed, transcendentals):
+    return pl.CostEstimate(
+        flops=flops // COST, bytes_accessed=bytes_accessed // COST, transcendentals=transcendentals // COST
+    )
+
+
+def chunk_of(tall, wide):
+    rows = tall
+    while rows * wide > 1 << 19 and rows % 32 == 0:
+        rows //= 2
+    return rows
+
+
+def place_kernel(at_ref, *refs):
+    if len(refs) < 4:
+        refs[-1][0, 0] = refs[0][0]
+        return
+
+    @pl.when(at_ref[1] == 1)
+    def _():
+        refs[-1][0, 0] = refs[0][0]
+
+    @pl.when(at_ref[1] == 0)
+    def _():
+        refs[-1][0, 0] = refs[1][0]
+
+
+def place_block(buffer, block, index, count, instead=None, first=None):
+    lead, tall, wide = block.shape
+    rows = chunk_of(tall, wide)
+    spec = pl.BlockSpec((1, rows, wide), lambda l, i, m: (l, i, 0))
+    blocks = [block] if instead is None else [block, instead]
+    where = [index, 1 if first is None else first]
+    where = jnp.stack([jnp.asarray(v).astype(jnp.int32) for v in where])
+    in_specs, operands, aliases = [spec] * len(blocks), list(blocks), {}
+    if buffer is not None or instead is not None:
+        in_specs.append(pl.BlockSpec(memory_space=pl.ANY))
+        operands.append(block if buffer is None else buffer)
+        aliases = {} if buffer is None else {len(operands): 0}
+    return pl.pallas_call(
+        place_kernel,
+        grid_spec=pltpu.PrefetchScalarGridSpec(
+            num_scalar_prefetch=1,
+            grid=(lead, tall // rows),
+            in_specs=in_specs,
+            out_specs=pl.BlockSpec((1, 1, rows, wide), lambda l, i, m: (l, m[0], i, 0)),
+        ),
+        out_shape=jax.ShapeDtypeStruct((lead, count, tall, wide), block.dtype),
+        input_output_aliases=aliases,
+        cost_estimate=spent(
+            flops=0, bytes_accessed=4 * lead * tall * wide, transcendentals=0
+        ),
+        name="place_block",
+    )(where, *operands)
+
+
+def hop_kernel(at_ref, *refs):
+    ins, outs = refs[:-2], refs[-2:]
+    for way in range(2):
+        term = ins[way][0, 0].astype(f32)
+        if len(ins) > 2:
+            term = term + ins[2 + way][0].astype(f32)
+        outs[way][0] = term.astype(bf16)
+
+
+def hop_sums(terms, up_at, down_at, up, down):
+    lead, _, tall, wide = terms.shape
+    rows = chunk_of(tall, wide)
+    block = pl.BlockSpec((1, rows, wide), lambda l, i, m: (l, i, 0))
+    in_specs = [
+        pl.BlockSpec((1, 1, rows, wide), lambda l, i, m: (l, m[0], i, 0)),
+        pl.BlockSpec((1, 1, rows, wide), lambda l, i, m: (l, m[1], i, 0)),
+    ]
+    operands = [terms, terms]
+    if up is not None:
+        in_specs += [block, block]
+        operands += [up, down]
+    return pl.pallas_call(
+        hop_kernel,
+        grid_spec=pltpu.PrefetchScalarGridSpec(
+            num_scalar_prefetch=1,
+            grid=(lead, tall // rows),
+            in_specs=in_specs,
+            out_specs=[block, block],
+        ),
+        out_shape=[jax.ShapeDtypeStruct((lead, tall, wide), bf16)] * 2,
+        cost_estimate=spent(
+            flops=2 * lead * tall * wide, bytes_accessed=12 * lead * tall * wide, transcendentals=0
+        ),
+        name="hop_sums",
+    )(jnp.stack([up_at, down_at]).astype(jnp.int32), *operands)
+
+
+def end_kernel(at_ref, term_ref, up_ref, down_ref, out_ref):
+    total = term_ref[0, 0].astype(f32) + up_ref[0].astype(f32) + down_ref[0].astype(f32)
+    out_ref[0] = total.astype(out_ref.dtype)
+
+
+def end_sums(sums, dtype):
+    lead, _, tall, wide = sums.terms.shape
+    rows = chunk_of(tall, wide)
+    block = pl.BlockSpec((1, rows, wide), lambda l, i, m: (l, i, 0))
+    return pl.pallas_call(
+        end_kernel,
+        grid_spec=pltpu.PrefetchScalarGridSpec(
+            num_scalar_prefetch=1,
+            grid=(lead, tall // rows),
+            in_specs=[
+                pl.BlockSpec((1, 1, rows, wide), lambda l, i, m: (l, m[0], i, 0)),
+                block,
+                block,
+            ],
+            out_specs=block,
+        ),
+        out_shape=jax.ShapeDtypeStruct((lead, tall, wide), dtype),
+        cost_estimate=spent(
+            flops=2 * lead * tall * wide, bytes_accessed=10 * lead * tall * wide, transcendentals=0
+        ),
+        name="end_sums",
+    )(lax.axis_index("depth").astype(jnp.int32)[None], sums.terms, sums.up, sums.down)
+
+
+def attention_grad_kernel(
+    at_ref, x0_ref, x1_ref, cot_ref, g0_ref, g1_ref, out_ref
+):
+    tall = x0_ref.shape[1]
+
+    def store(total):
+        out_ref[...] = total.reshape(out_ref.shape).astype(out_ref.dtype)
+
+    @pl.when(pl.program_id(0) < 3)
+    def _():
+        store(dot_tn(x0_ref[0], g0_ref[0]) + dot_tn(x1_ref[0], g1_ref[0]))
+
+    @pl.when(pl.program_id(0) == 3)
+    def _():
+        store(
+            dot_tn(cot_ref[0:tall, :], g0_ref[0]) + dot_tn(cot_ref[tall : 2 * tall, :], g1_ref[0])
+        )
+
+
+def attention_grads(normed, cot, flat, place, depth_count, dp_count, dtype):
+    _, tall, model = normed[0].shape
+    heads_width = flat[0].shape[2]
+    block = model // dp_count
+    own_rows = block // depth_count
+    normed_spec = pl.BlockSpec((1, tall, block), lambda k, m: (jnp.minimum(k, 2), 0, m[0]))
+    flat_spec = pl.BlockSpec((1, tall, heads_width), lambda k, m: (lax.rem(k + 1, 4), 0, 0))
+    return pl.pallas_call(
+        attention_grad_kernel,
+        grid_spec=pltpu.PrefetchScalarGridSpec(
+            num_scalar_prefetch=1,
+            grid=(4,),
+            in_specs=[
+                normed_spec,
+                normed_spec,
+                pl.BlockSpec((2 * tall, block), lambda k, m: (0, m[0])),
+                flat_spec,
+                flat_spec,
+            ],
+            out_specs=pl.BlockSpec(
+                (depth_count, 1, own_rows, heads_width), lambda k, m: (0, k, 0, 0)
+            ),
+        ),
+        out_shape=jax.ShapeDtypeStruct((depth_count, 4, own_rows, heads_width), dtype),
+        compiler_params=pltpu.CompilerParams(vmem_limit_bytes=40 << 20),
+        cost_estimate=spent(
+            flops=16 * tall * block * heads_width,
+            bytes_accessed=16 * block * heads_width,
+            transcendentals=0,
+        ),
+        name="attention_grads",
+    )(place, *normed, cot, *flat)
+
+
+def hidden_grad_kernel(x0_ref, x1_ref, c0_ref, c1_ref, u0_ref, u1_ref, h0_ref, h1_ref, out_ref):
+    def store(total):
+        out_ref[...] = total.reshape(out_ref.shape)
+
+    @pl.when(pl.program_id(0) == 0)
+    def _():
+        store(dot_tn(x0_ref[...], u0_ref[...]) + dot_tn(x1_ref[...], u1_ref[...]))
+
+    @pl.when(pl.program_id(0) == 1)
+    def _():
+        store(dot_tn(c0_ref[0], h0_ref[...]) + dot_tn(c1_ref[0], h1_ref[...]))
+
+
+def hidden_grads(x, cot, up_grads, hidden, dp_count, depth_count):
+    tall, model = x[0].shape
+    part = hidden[0].shape[1]
+    block = model // dp_count
+    cols = pl.BlockSpec((tall, block), lambda k, n: (0, n * (1 - k)))
+    whole = pl.BlockSpec((tall, part), lambda k, n: (0, 0))
+    return pl.pallas_call(
+        hidden_grad_kernel,
+        grid=(2, dp_count),
+        in_specs=[cols, cols]
+        + [
+            pl.BlockSpec((1, tall, block), lambda k, n: (0, 0, n * k)),
+            pl.BlockSpec((1, tall, block), lambda k, n: (1, 0, n * k)),
+        ]
+        + [whole] * 4,
+        out_specs=pl.BlockSpec(
+            (1, depth_count, block // depth_count, part), lambda k, n: (k * dp_count + n, 0, 0, 0)
+        ),
+        out_shape=jax.ShapeDtypeStruct(
+            (2 * dp_count, depth_count, block // depth_count, part), f32
+        ),
+        compiler_params=pltpu.CompilerParams(vmem_limit_bytes=48 << 20),
+        cost_estimate=spent(
+            flops=8 * tall * model * part, bytes_accessed=8 * model * part, transcendentals=0
+        ),
+        name="hidden_grads",
+    )(*x, cot, cot, *up_grads, *hidden)
 
 
 def mix_kernel(slots, mix_ref, hist_ref, out_ref):
@@ -179,7 +518,7 @@
         ],
         out_specs=pl.BlockSpec((rows, STREAMS * width), lambda i: (i, 0)),
         out_shape=jax.ShapeDtypeStruct((depth_count * rows_mb, STREAMS * width), bf16),
-        cost_estimate=pl.CostEstimate(
+        cost_estimate=spent(
             flops=2 * slots * STREAMS * depth_count * rows_mb * width,
             bytes_accessed=2 * (slots + STREAMS) * depth_count * rows_mb * width,
             transcendentals=0,
@@ -258,7 +597,7 @@
             jax.ShapeDtypeStruct((depth_count * rows_mb, 128), f32),
         ],
         input_output_aliases=aliases,
-        cost_estimate=pl.CostEstimate(
+        cost_estimate=spent(
             flops=4 * slots * STREAMS * depth_count * rows_mb * width,
             bytes_accessed=2 * (2 * slots + STREAMS) * depth_count * rows_mb * width,
             transcendentals=0,
@@ -273,47 +612,100 @@
     return pl.ds(own_at, width), pl.ds(other_at, width)
 
 
-def total_kernel(part_ref, cur_ref, last_ref, low_ref, resid_ref):
+def ff_split_kernel(at_ref, up_ref, down_ref, out_ref):
+    out_ref[0, 0] = up_ref[...]
+    out_ref[0, 1] = down_ref[...].T
+
+
+def ff_split(up_weight, down_weight, partners):
+    own_rows, ff_width = up_weight.shape
+    count = partners.shape[0]
+    part = ff_width // count
+    return pl.pallas_call(
+        ff_split_kernel,
+        grid_spec=pltpu.PrefetchScalarGridSpec(
+            num_scalar_prefetch=1,
+            grid=(count,),
+            in_specs=[
+                pl.BlockSpec((own_rows, part), lambda i, m: (0, m[i])),
+                pl.BlockSpec((part, own_rows), lambda i, m: (m[i], 0)),
+            ],
+            out_specs=pl.BlockSpec((1, 2, own_rows, part), lambda i, m: (i, 0, 0, 0)),
+        ),
+        out_shape=jax.ShapeDtypeStruct((count, 2, own_rows, part), bf16),
+        cost_estimate=spent(flops=0, bytes_accessed=8 * own_rows * ff_width, transcendentals=0),
+        name="ff_split",
+    )(partners, up_weight, down_weight)
+
+
+def ff_join_kernel(at_ref, piece_ref, up_ref, down_ref):
+    up_ref[...] = piece_ref[0, 0].astype(f32)
+    down_ref[...] = piece_ref[0, 1].astype(f32).T
+
+
+def ff_join(pieces, partners):
+    count, _, own_rows, part = pieces.shape
+    return pl.pallas_call(
+        ff_join_kernel,
+        grid_spec=pltpu.PrefetchScalarGridSpec(
+            num_scalar_prefetch=1,
+            grid=(count,),
+            in_specs=[pl.BlockSpec((1, 2, own_rows, part), lambda i, m: (i, 0, 0, 0))],
+            out_specs=[
+                pl.BlockSpec((own_rows, part), lambda i, m: (0, m[i])),
+                pl.BlockSpec((part, own_rows), lambda i, m: (m[i], 0)),
+            ],
+        ),
+        out_shape=[
+            jax.ShapeDtypeStruct((own_rows, count * part), f32),
+            jax.ShapeDtypeStruct((count * part, own_rows), f32),
+        ],
+        cost_estimate=spent(
+            flops=0, bytes_accessed=12 * own_rows * count * part, transcendentals=0
+        ),
+        name="ff_join",
+    )(partners, pieces)
+
+
+def total_kernel(depth_ref, part_ref, up_ref, down_ref, cur_ref, last_ref, low_ref, resid_ref):
     width = resid_ref.shape[1]
     current = cur_ref[...].astype(f32)
     for s in range(STREAMS):
         lanes = slice(s * width, (s + 1) * width)
-        total = part_ref[0, :, lanes].astype(f32)
-        for at in range(1, part_ref.shape[0]):
-            total = total + part_ref[at, :, lanes].astype(f32)
+        total = part_ref[0, 0, :, lanes].astype(f32)
+        total = total + up_ref[0, :, lanes].astype(f32) + down_ref[0, :, lanes].astype(f32)
         total = total + last_ref[:, s : s + 1] * current
         if s == STREAMS - 1:
             resid_ref[...] = total
         low_ref[:, lanes] = total.astype(bf16)
 
 
-def total_streams(parts, current_half, last):
-    count, tall, wide = parts.shape
+def total_streams(sums, current_half, last, depth_at):
+    _, _, tall, wide = sums.terms.shape
     width = wide // STREAMS
     rows = min(64, tall)
+    row = lambda i, d: (i, 0)
     return pl.pallas_call(
         total_kernel,
-        grid=(tall // rows,),
-        in_specs=[
-            pl.BlockSpec((count, rows, wide), lambda i: (0, i, 0)),
-            pl.BlockSpec((rows, width), lambda i: (i, 0)),
-            pl.BlockSpec((rows, 128), lambda i: (i, 0)),
-        ],
-        out_specs=[
-            pl.BlockSpec((rows, wide), lambda i: (i, 0)),
-            pl.BlockSpec((rows, width), lambda i: (i, 0)),
-        ],
+        grid_spec=pltpu.PrefetchScalarGridSpec(
+            num_scalar_prefetch=1,
+            grid=(tall // rows,),
+            in_specs=[
+                pl.BlockSpec((1, 1, rows, wide), lambda i, d: (0, d[0], i, 0)),
+                pl.BlockSpec((1, rows, wide), lambda i, d: (0, i, 0)),
+                pl.BlockSpec((1, rows, wide), lambda i, d: (0, i, 0)),
+                pl.BlockSpec((rows, width), row),
+                pl.BlockSpec((rows, 128), row),
+            ],
+            out_specs=[pl.BlockSpec((rows, wide), row), pl.BlockSpec((rows, width), row)],
+        ),
         out_shape=[
             jax.ShapeDtypeStruct((tall, wide), bf16),
             jax.ShapeDtypeStruct((tall, width), f32),
         ],
-        cost_estimate=pl.CostEstimate(
-            flops=(count + 2) * tall * wide,
-            bytes_accessed=2 * (count + 2) * tall * wide,
-            transcendentals=0,
-        ),
+        cost_estimate=spent(flops=5 * tall * wide, bytes_accessed=9 * tall * wide, transcendentals=0),
         name="total_streams",
-    )(parts, current_half, last)
+    )(depth_at, sums.terms, sums.up, sums.down, current_half, last)
 
 
 def norm_kernel(model_ref, own_ref, other_ref, gain_ref, normed_ref, ff_ref, stat_ref):
@@ -373,7 +765,7 @@
             jax.ShapeDtypeStruct((tall, width), bf16),
             jax.ShapeDtypeStruct((tall, 128), f32),
         ],
-        cost_estimate=pl.CostEstimate(
+        cost_estimate=spent(
             flops=20 * tall * wide, bytes_accessed=8 * tall * wide, transcendentals=0
         ),
         name="norm_streams",
@@ -389,11 +781,11 @@
 def project_kernel(
     x_ref, cot_ref, wq_ref, wk_ref, wv_ref, wo_ref, cos_ref, up_ref, down_ref, out_ref
 ):
-    span = wq_ref.shape[1]
+    span = wq_ref.shape[-1]
     tables = cos_ref[...], up_ref[...], down_ref[...]
     for kind, w_ref in enumerate((wq_ref, wk_ref, wv_ref, wo_ref)):
         rows = cot_ref[...] if kind == 3 else x_ref[kind]
-        product = dot_nn(rows, w_ref[...])
+        product = dot_nn(rows, w_ref[...].reshape(-1, span))
         for begin in range(0, span, HDIM):
             head = product[:, begin : begin + HDIM]
             if kind < 2:
@@ -403,8 +795,14 @@
 
 def project_heads(normed, cot, weights, tables, depth_count):
     _, rows, model = normed.shape
-    span = weights[0].shape[1] // depth_count
+    groups, _, _, own_rows, heads_width = weights.shape
+    span = heads_width // depth_count
     whole = lambda j: (0, 0)
+
+    def matrix(kind):
+        shape = (groups, depth_count, 1, own_rows, span)
+        return pl.BlockSpec(shape, lambda j: (0, 0, kind, 0, j))
+
     return pl.pallas_call(
         project_kernel,
         grid=(depth_count,),
@@ -412,18 +810,18 @@
             pl.BlockSpec((3, rows, model), lambda j: (0, 0, 0)),
             pl.BlockSpec((rows, model), whole),
         ]
-        + [pl.BlockSpec((model, span), lambda j: (0, j))] * 4
+        + [matrix(kind) for kind in range(4)]
         + [pl.BlockSpec((rows, HDIM), whole)] * 3,
         out_specs=pl.BlockSpec((1, rows, 4 * span), lambda j: (j, 0, 0)),
         out_shape=jax.ShapeDtypeStruct((depth_count, rows, 4 * span), bf16),
         compiler_params=pltpu.CompilerParams(vmem_limit_bytes=40 << 20),
-        cost_estimate=pl.CostEstimate(
+        cost_estimate=spent(
             flops=8 * rows * model * span * depth_count,
             bytes_accessed=8 * model * span * depth_count + 8 * rows * model,
             transcendentals=0,
         ),
         name="project_heads",
-    )(normed, cot, *weights, *tables)
+    )(normed, cot, *[weights] * 4, *tables)
 
 
 def attend_kernel(
@@ -490,7 +888,7 @@
         out_shape=jax.ShapeDtypeStruct((length, 4 * heads_each * HDIM), bf16),
         scratch_shapes=[pltpu.VMEM((length, HDIM), f32)] * 2,
         compiler_params=pltpu.CompilerParams(vmem_limit_bytes=48 << 20),
-        cost_estimate=pl.CostEstimate(
+        cost_estimate=spent(
             flops=9 * heads_each * length * length * HDIM,
             bytes_accessed=16 * length * heads_each * HDIM + 12 * length * HDIM,
             transcendentals=heads_each * length * length,
@@ -509,27 +907,39 @@
     model_ref, x_ref, cot_ref, up_ref, down_ref,
     hidden_ref, grad_ref, out_own_ref, out_other_ref, back_own_ref, back_other_ref,
 ):
-    own_span, other_span = own_spans(model_ref, out_own_ref.shape[1])
-    up_pre = dot_nn(x_ref[...], up_ref[...])
+    part = up_ref.shape[-1]
+    half = up_ref.shape[1] // 2
+
+    def rows_of(ref, which):
+        return ref[0, pl.ds(which * half, half)].reshape(-1, part)
+
+    own, other = model_ref[0], 1 - model_ref[0]
+    up_pre = dot_nn(x_ref[...], up_ref[...].reshape(-1, part))
     hidden, slope = gelu_parts(up_pre)
     hidden = hidden.astype(bf16)
-    grad_up = (dot_nn(cot_ref[...], down_ref[...]) * slope).astype(bf16)
+    grad_up = (dot_nn(cot_ref[0], down_ref[...].reshape(-1, part)) * slope).astype(bf16)
     hidden_ref[...] = hidden
     grad_ref[...] = grad_up
-    back_other_ref[...] = dot_nt(grad_up, up_ref[other_span, :]).astype(bf16)
-    back_own_ref[...] = dot_nt(grad_up, up_ref[own_span, :])
-    out_other_ref[...] = dot_nt(hidden, down_ref[other_span, :]).astype(bf16)
-    out_own_ref[...] = dot_nt(hidden, down_ref[own_span, :])
-
-
-def feed_forward(x, cot, up_w, down_wt, which):
+    back_other_ref[...] = dot_nt(grad_up, rows_of(up_ref, other)).astype(bf16)
+    back_own_ref[...] = dot_nt(grad_up, rows_of(up_ref, own))
+    out_other_ref[...] = dot_nt(hidden, rows_of(down_ref, other)).astype(bf16)
+    out_own_ref[...] = dot_nt(hidden, rows_of(down_ref, own))
+
+
+def feed_forward(x, cot, micro_at, weights, which):
     tall, model = x.shape
-    part = up_w.shape[1]
+    part = weights.shape[-1]
     width = model // 2
     rows = min(256, tall)
     row = lambda i, m: (i, 0)
-    whole = lambda i, m: (0, 0)
-    resident = pl.BlockSpec((model, part), whole, pipeline_mode=pl.Buffered(1))
+
+    def resident(kind):
+        return pl.BlockSpec(
+            (1,) + weights.shape[1:],
+            lambda i, m: (kind, 0, 0, 0, 0),
+            pipeline_mode=pl.Buffered(1),
+        )
+
     return pl.pallas_call(
         ff_kernel,
         grid_spec=pltpu.PrefetchScalarGridSpec(
@@ -537,9 +947,9 @@
             grid=(tall // rows,),
             in_specs=[
                 pl.BlockSpec((rows, model), row),
-                pl.BlockSpec((rows, model), row),
-                resident,
-                resident,
+                pl.BlockSpec((1, rows, model), lambda i, m: (micro_at, i, 0)),
+                resident(0),
+                resident(1),
             ],
             out_specs=[pl.BlockSpec((rows, part), row)] * 2
             + [pl.BlockSpec((rows, width), row)] * 4,
@@ -552,13 +962,13 @@
             jax.ShapeDtypeStruct((tall, width), bf16),
         ],
         compiler_params=pltpu.CompilerParams(vmem_limit_bytes=48 << 20),
-        cost_estimate=pl.CostEstimate(
+        cost_estimate=spent(
             flops=8 * tall * model * part,
             bytes_accessed=4 * model * part + 16 * tall * model,
             transcendentals=2 * tall * part,
         ),
         name="feed_forward",
-    )(which, x, cot, up_w, down_wt)
+    )(which, x, cot, weights, weights)
 
 
 def back_kernel(half_ref, ans_ref, wo_ref, wq_ref, wk_ref, wv_ref, out_ref, *flat):
@@ -568,7 +978,8 @@
         total = None
         for j in range(count):
             term = dot_nt(
-                ans_ref[j, :, kind * span : (kind + 1) * span], w_ref[:, j * span : (j + 1) * span]
+                ans_ref[j, :, kind * span : (kind + 1) * span],
+                w_ref[:, :, :, :, j * span : (j + 1) * span].reshape(-1, span),
             )
             total = term if total is None else total + term
         out_ref[kind] = total.astype(out_ref.dtype)
@@ -585,10 +996,15 @@
 
 def back_project(answer, weights, half, dtype, flat):
     count, rows, wide = answer.shape
-    model, heads_width = weights[0].shape
-    width = model // 2
-    steps = 2
-    part = width // steps
+    groups, _, _, own_rows, heads_width = weights.shape
+    part = count * own_rows
+    steps = groups // 2
+    width = part * steps
+
+    def matrix(kind):
+        shape = (1, count, 1, own_rows, heads_width)
+        return pl.BlockSpec(shape, lambda i, m: (m[0] * steps + i, 0, kind, 0, 0))
+
     out_specs = [pl.BlockSpec((4, rows, part), lambda i, m: (0, 0, i))]
     out_shape = [jax.ShapeDtypeStruct((4, rows, width), dtype)]
     if flat:
@@ -600,18 +1016,18 @@
             num_scalar_prefetch=1,
             grid=(steps,),
             in_specs=[pl.BlockSpec((count, rows, wide), lambda i, m: (0, 0, 0))]
-            + [pl.BlockSpec((part, heads_width), lambda i, m: (m[0] * steps + i, 0))] * 4,
+            + [matrix(kind) for kind in (3, 0, 1, 2)],
             out_specs=out_specs,
         ),
         out_shape=out_shape,
         compiler_params=pltpu.CompilerParams(vmem_limit_bytes=40 << 20),
-        cost_estimate=pl.CostEstimate(
+        cost_estimate=spent(
             flops=8 * rows * heads_width * width,
             bytes_accessed=8 * heads_width * width + 20 * rows * width,
             transcendentals=0,
         ),
         name="back_project",
-    )(half, answer, *weights)
+    )(half, answer, *[weights] * 4)
 
 
 def slope_kernel(
@@ -679,7 +1095,7 @@
             jax.ShapeDtypeStruct((tall, 128), f32),
             jax.ShapeDtypeStruct((STREAMS, width), f32),
         ],
-        cost_estimate=pl.CostEstimate(
+        cost_estimate=spent(
             flops=12 * tall * wide, bytes_accessed=12 * tall * wide, transcendentals=0
         ),
         name="norm_slopes",
@@ -745,7 +1161,7 @@
             jax.ShapeDtypeStruct((tall, width), f32),
             jax.ShapeDtypeStruct((tall, 128), f32),
         ],
-        cost_estimate=pl.CostEstimate(
+        cost_estimate=spent(
             flops=12 * tall * wide, bytes_accessed=10 * tall * wide, transcendentals=0
         ),
         name="stream_grads",
@@ -789,8 +1205,6 @@
     dp_at = lax.axis_index("dp")
     model_at = lax.axis_index("mp")
     dp_bits = list(range(bit_count(dp_count)))
-    order_one, order_two = dp_bits, dp_bits[1:] + dp_bits[:1]
-    back_one, back_two = order_one[::-1], order_two[::-1]
     slots, tokens_held, width = history.shape
     model = current.shape[1]
     rows_mb = current.shape[0] // MB
@@ -819,14 +1233,6 @@
 
     stacked = jnp.concatenate([query_weight, key_weight, value_weight, out_weight.T], axis=0)
     over_depth = lax.all_gather(stacked, "depth", axis=0, tiled=True)
-    over_depth = over_depth.reshape(depth_count, 4, own_rows, heads_width)
-    gathered = []
-    for at in range(4):
-        piece = over_depth[:, at].reshape(depth_count * own_rows, heads_width)
-        pieces = gather_masked(piece, "dp", order_one if at % 2 == 0 else order_two)
-        gathered.append(reorder_masked(jnp.stack(pieces), "dp").reshape(model, heads_width))
-    query_w, key_w, value_w, out_wt = gathered
-
     current_f = current.astype(f32)
     current_half = half_of(current, 1, model_at)
     mean_square = jnp.mean(current_f * current_f, axis=-1, keepdims=True)
@@ -848,151 +1254,253 @@
     mix_all = gather_small(mixing, ("depth",)).reshape(depth_count * MB * rows_mb, STREAMS * MIX)
     slot_mix = dot_nn(mix_all, pick.astype(bf16))
 
-    ff_local = jnp.stack([up_weight, down_weight.T])
-    ff_local, slot_mix = lax.optimization_barrier((ff_local, slot_mix))
-    ff_pieces = [
-        lax.dynamic_slice_in_dim(ff_local, (dp_at ^ m) * ff_part, ff_part, 2)
-        for m in range(dp_count)
-    ]
-    ff_pieces = [ff_pieces[0]] + [swap_mask(ff_pieces[m], "dp", m) for m in range(1, dp_count)]
-    ff_rows = reorder_masked(jnp.stack(ff_pieces), "dp")
-
-    def ff_gather(at):
-        flat = ff_rows[:, at].reshape(dp_count * own_rows, ff_part)
-        full = lax.all_gather(flat, "depth", axis=0, tiled=True)
-        full = full.reshape(depth_count, dp_count, own_rows, ff_part)
-        return jnp.swapaxes(full, 0, 1).reshape(model, ff_part)
-
-    up_w, down_wt = ff_gather(0), ff_gather(1)
-
-    cotangent, slot_mix = lax.optimization_barrier((cotangent, slot_mix))
-    cot_full = join_halves(cotangent, other_core(cotangent), model_at)
-    cot_group = []
-    for micro_at in range(MB):
-        rows = cotangent[micro_at * rows_mb : (micro_at + 1) * rows_mb]
-        order = order_one if micro_at % 2 == 0 else order_two
-        mine = jnp.concatenate(gather_masked(rows, "dp", order), axis=0)
-        cot_group.append(join_halves(mine, other_core(mine), model_at))
+    def over_depth_swap(values):
+        return lax.all_to_all(values, "depth", 0, 0, tiled=True)
+
+    def mix_part(micro_at, slot_mix):
+        partial = mix_streams(slot_mix, history, micro_at, depth_count, rows_mb)
+        return partial.reshape(1, depth_count, rows_mb, STREAMS * width)
+
+    partners = jnp.stack([dp_at ^ m for m in range(dp_count)]).astype(jnp.int32)
+    ff_local = ff_split(up_weight, down_weight, partners)
+    ff_local, slot_mix = fence(ff_local, slot_mix)
+    ff_rows = place_block(None, ff_local[0], partners[0], dp_count)
+    for m in range(1, dp_count):
+        arrived = swap_mask(ff_local[m], "dp", m)
+        ff_rows = place_block(ff_rows, arrived, partners[m], dp_count)
+    ff_rows = ff_rows.reshape(2 * dp_count, own_rows, ff_part)
+
+    partial = mix_part(0, slot_mix)
+    over_depth, partial, slot_mix, ff_rows, cotangent, positions = fence(
+        over_depth, partial, slot_mix, ff_rows, cotangent, positions
+    )
+
+    weights_line = LineGather(ff_rows)
+    weights_line.step()
+    flat_rows = depth_count * 4 * own_rows
+    pieces = [over_depth.reshape(flat_rows, heads_width)]
+    pieces.append(core_hop(pieces[0], 0))
+    weights = place_block(None, pieces[0][None], place_index(0), dp_count)
+    partial_next = mix_part(1, slot_mix)
+    pieces, partial, partial_next, weights, cotangent = weights_line.hold(
+        pieces, partial, partial_next, weights, cotangent
+    )
+    hops_left = [(p, at) for at in range(1, len(dp_bits)) for p in range(1 << at)]
+    placed = 1
+    cot_other = cot_mine = None
+    sums, sums_next = LineScatter(partial), LineScatter(partial_next)
+    for hop in range(1, depth_count):
+        sums.step()
+        weights_line.step()
+        last_hop = hop == depth_count - 1
+        for place in range(placed, len(pieces)):
+            weights = place_block(weights, pieces[place][None], place_index(place), dp_count)
+        placed = len(pieces)
+        while hops_left:
+            place, at = hops_left.pop(0)
+            pieces.append(core_hop(pieces[place], at))
+            if len(hops_left) <= depth_count - 2 - hop:
+                break
+        if last_hop:
+            cot_other = other_core(cotangent)
+            cot_mine = group_gather(cotangent)
+            sums_next.step()
+        (state,) = weights_line.hold((sums.up, sums.down, pieces, weights, cotangent))
+        sums.up, sums.down, pieces, weights, cotangent = state
+    while sums_next.at < depth_count - 3:
+        sums_next.hold()
+        sums_next.step()
+    for place in range(placed, len(pieces)):
+        weights = place_block(weights, pieces[place][None], place_index(place), dp_count)
+    weights = weights.reshape(dp_count, depth_count, 4, own_rows, heads_width)
+    ff_weights = weights_line.placed().reshape(2, dp_count, depth_count, own_rows, ff_part)
+
+    cot_full = join_halves(cotangent, cot_other, model_at)
+    cot_mine = jnp.swapaxes(cot_mine.reshape(dp_count, MB, rows_mb, width), 0, 1)
+    cot_mine = cot_mine.reshape(MB * dp_count * rows_mb, width)
+    cot_group = join_halves(cot_mine, other_core(cot_mine), model_at)
+    cot_group = cot_group.reshape(MB, dp_count * rows_mb, model)
 
     places_all = gather_small(positions, ("depth",))
     document_view = doc_ids.reshape(depth_count, MB, rows_mb)
     own_tables = turning_tables(positions)
     which = model_at.astype(jnp.int32)[None]
+    depth_at = lax.axis_index("depth").astype(jnp.int32)[None]
     gains = gain_float
 
-    saved = []
-    for micro_at in range(MB):
+    def enter(micro_at, sums):
         span = slice(micro_at * rows_mb, (micro_at + 1) * rows_mb)
-        partial = mix_streams(slot_mix, history, micro_at, depth_count, rows_mb)
-        parts = partial.reshape(depth_count, rows_mb, STREAMS * width)
-        parts = lax.all_to_all(parts, "depth", 0, 0, tiled=True)
-        low, resid = total_streams(parts, current_half[span], last[span])
+        low, resid = total_streams(sums, current_half[span], last[span], depth_at)
         normed, ff_normed, stats = norm_streams(low, other_core(low), gains, which)
-
         packed = project_heads(
             normed,
             cot_full[span],
-            [query_w, key_w, value_w, out_wt],
+            weights,
             [t[span] for t in own_tables],
             depth_count,
         )
-        by_head = lax.all_to_all(packed, "depth", 0, 0, tiled=True)
-        by_head = by_head.reshape(length, 4 * heads_each * HDIM)
+        return dict(
+            low=low, resid=resid, normed=normed, ff_normed=ff_normed, stats=stats, packed=packed
+        )
+
+    def attention(micro_at, by_head):
+        span = slice(micro_at * rows_mb, (micro_at + 1) * rows_mb)
         documents = document_view[:, micro_at].reshape(length)
         seq_places = places_all[:, span].reshape(length)
+        by_head = by_head.reshape(length, 4 * heads_each * HDIM)
         answer = attend(by_head, documents, turning_tables(seq_places), heads_each)
-        answer = answer.reshape(depth_count, rows_mb, 4 * heads_each * HDIM)
-        answer = lax.all_to_all(answer, "depth", 0, 0, tiled=True)
-
-        order = order_one if micro_at % 2 == 0 else order_two
-        back = back_one if micro_at % 2 == 0 else back_two
-        mine = jnp.concatenate(gather_masked(ff_normed, "dp", order), axis=0)
-        group_normed = join_halves(mine, other_core(mine), model_at)
+        return answer.reshape(depth_count, rows_mb, 4 * heads_each * HDIM)
+
+    def group_rows(ff_normed):
+        mine = group_gather(ff_normed).reshape(dp_count * rows_mb, width)
+        return join_halves(mine, other_core(mine), model_at)
+
+    def hidden_units(micro_at, group_normed):
         hidden, grad_up, out_own, out_other, back_own, back_other = feed_forward(
-            group_normed, cot_group[micro_at], up_w, down_wt, which
+            group_normed, cot_group, micro_at, ff_weights, which
         )
-
-        def reduce_group(own, other, back=back):
-            total = own + other_core(other).astype(f32)
-            return scatter_masked(jnp.split(total, dp_count, axis=0), "dp", back)
-
-        grad_norm_ff = reduce_group(back_own, back_other)
-        ff_out = reduce_group(out_own, out_other)
-
-        weights = [out_wt, query_w, key_w, value_w]
+        return (
+            dict(group_normed=group_normed, hidden=hidden, grad_up=grad_up),
+            ((back_own, other_core(back_other)), (out_own, other_core(out_other))),
+        )
+
+    def reduce_group(own, other):
+        total = own + other.astype(f32)
+        return group_scatter(total.reshape(dp_count, rows_mb, width))
+
+    def back(kept, answer, ff_parts):
         (theirs,) = back_project(answer, weights, 1 - which, bf16, False)
         got = other_core(theirs)
-        own, flat = back_project(answer, weights, which, f32, True)
-        layer_rows = (resid + own[0] + got[0].astype(f32) + ff_out).astype(bf16)
+        own, kept["flat"] = back_project(answer, weights, which, f32, True)
+        grad_norm_ff = reduce_group(*ff_parts[0])
+        ff_out = reduce_group(*ff_parts[1])
+        kept["layer_rows"] = (kept["resid"] + own[0] + got[0].astype(f32) + ff_out).astype(bf16)
+        return own, got, grad_norm_ff
+
+    def leave(micro_at, kept, own, got, grad_norm_ff):
+        span = slice(micro_at * rows_mb, (micro_at + 1) * rows_mb)
+        low, stats = kept["low"], kept["stats"]
         scaled, sums, gain_part = norm_slopes(own, got, grad_norm_ff, low, stats, gains, which)
         grad_low, current_mix, last_dot = stream_grads(
             scaled, sums, other_core(sums), low, stats, cotangent[span], current_half[span], last[span]
         )
-        grad_all = lax.all_gather(grad_low, "depth", axis=0, tiled=True)
-        saved.append(
-            dict(
-                normed=normed,
-                group_normed=group_normed,
-                hidden=hidden,
-                grad_up=grad_up,
-                flat=flat,
-                grad_all=grad_all,
-                grad_low=grad_low,
-                layer_rows=layer_rows,
-                gain=gain_part,
-                current_mix=current_mix,
-                last_dot=last_dot,
+        kept.update(gain=gain_part, current_mix=current_mix, last_dot=last_dot)
+        return grad_low
+
+    sums_next.step()
+    first = enter(0, sums)
+    packed, ff_normed = sums_next.hold(first["packed"], first["ff_normed"])
+    sums_next.step()
+    by_head = over_depth_swap(packed)
+    group_normed = group_rows(ff_normed)
+    by_head, group_normed = sums_next.hold(by_head, group_normed)
+    answer = attention(0, by_head)
+    answer, group_normed = sums_next.hold(answer, group_normed)
+
+    answer = over_depth_swap(answer)
+    second = enter(1, sums_next)
+    kept, ff_parts = hidden_units(0, group_normed)
+    first.update(kept)
+    answer, packed, ff_normed, ff_parts = fence(
+        answer, second["packed"], second["ff_normed"], ff_parts
+    )
+    by_head = over_depth_swap(packed)
+    group_normed = group_rows(ff_normed)
+    ways = back(first, answer, ff_parts)
+    by_head, group_normed, ways = fence(by_head, group_normed, ways)
+    answer = attention(1, by_head)
+    answer, group_normed, ways = fence(answer, group_normed, ways)
+
+    answer = over_depth_swap(answer)
+    grad_low = leave(0, first, *ways)
+    kept, ff_parts = hidden_units(1, group_normed)
+    second.update(kept)
+    answer, grad_low, ff_parts = fence(answer, grad_low, ff_parts)
+    saved = [first, second]
+
+    def each(name):
+        return [s[name] for s in saved]
+
+    def rows_of(name):
+        return jnp.concatenate(each(name), axis=0)
+
+    grad_line = LineGather(grad_low[None])
+    for hop in range(1, depth_count):
+        grad_line.step()
+        if hop == 1:
+            ways = back(second, answer, ff_parts)
+            (ways,) = grad_line.hold(ways)
+        elif hop == 2:
+            grad_low = leave(1, second, *ways)
+            ff_products = hidden_grads(
+                each("group_normed"), cot_group, each("grad_up"), each("hidden"), dp_count, depth_count
             )
-        )
-
-    def rows_of(name, at=None):
-        return jnp.concatenate([s[name] if at is None else s[name][at] for s in saved], axis=0)
-
-    def over_depth_sum(values):
-        arrived = lax.all_to_all(values, "depth", 0, 0, tiled=True).astype(f32)
-        return jnp.sum(arrived, axis=0)
-
-    left = [rows_of("normed", 0), rows_of("normed", 1), rows_of("normed", 2), cot_full]
-    right = [rows_of("flat", 1), rows_of("flat", 2), rows_of("flat", 3), rows_of("flat", 0)]
-    scattered = []
-    for at in range(4):
-        by_dp = dot_tn(left[at], right[at]).reshape(dp_count, model // dp_count, heads_width)
-        pieces = [
-            lax.dynamic_index_in_dim(by_dp, dp_at ^ m, 0, keepdims=False) for m in range(dp_count)
-        ]
-        total = scatter_masked(pieces, "dp", back_one if at % 2 == 0 else back_two)
-        total = total.astype(bf16).reshape(depth_count, own_rows, heads_width)
-        scattered.append(over_depth_sum(total))
-
-    def ff_scatter(left, right):
-        grads = dot_tn(left, right).astype(bf16)
-        grads = grads.reshape(dp_count, depth_count, own_rows, ff_part)
-        return over_depth_sum(jnp.swapaxes(grads, 0, 1))
-
-    cot_group_all = jnp.concatenate(cot_group, axis=0)
-    ff_grads = [
-        ff_scatter(rows_of("group_normed"), rows_of("grad_up")),
-        ff_scatter(cot_group_all, rows_of("hidden")),
+            grad_low, ff_products = grad_line.hold(grad_low, ff_products)
+        elif hop == 3:
+            place_list = jnp.stack([place_index(p) for p in range(dp_count)]).astype(jnp.int32)
+            pieces = [
+                attention_grads(
+                    each("normed"),
+                    cot_full,
+                    each("flat"),
+                    place_list[p : p + 1],
+                    depth_count,
+                    dp_count,
+                    bf16 if p >= dp_count // 2 else f32,
+                )
+                for p in range(dp_count)
+            ]
+            grad_low, ff_products, pieces = grad_line.hold(grad_low, ff_products, pieces)
+        else:
+            grad_low, ff_products, pieces = grad_line.hold(grad_low, ff_products, pieces)
+
+    last_line = LineGather(grad_low[None])
+    last_line.step()
+    ff_sums = LineScatter(ff_products)
+    hops_left = [
+        (p, at) for at in reversed(range(len(dp_bits))) for p in range(1 << at, 2 << at)
     ]
-    ff_grads = jnp.stack(ff_grads).astype(bf16)
-    ff_pieces = [
-        lax.dynamic_index_in_dim(ff_grads, dp_at ^ m, 1, keepdims=False) for m in range(dp_count)
-    ]
-    ff_pieces = [ff_pieces[0]] + [swap_mask(ff_pieces[m], "dp", m) for m in range(1, dp_count)]
-    ff_cols = reorder_masked(jnp.stack(ff_pieces), "dp").astype(f32)
-    up_grad = jnp.swapaxes(ff_cols[:, 0], 0, 1).reshape(own_rows, ff_width)
-    down_grad = jnp.swapaxes(ff_cols[:, 1], 1, 2).reshape(ff_width, own_rows)
-
-    history_grad = None
-    slot_parts = []
-    for micro_at in range(MB):
-        history_grad, slot_part = unmix_streams(
-            slot_mix, history, saved[micro_at]["grad_all"], micro_at, depth_count, rows_mb, history_grad
-        )
-        slot_parts.append(slot_part.reshape(depth_count, 1, rows_mb, 128))
+
+    def sums_hop():
+        place, at = hops_left.pop(0)
+        arrived = core_hop(pieces[place].astype(bf16), at).astype(f32)
+        pieces[place - (1 << at)] = pieces[place - (1 << at)] + arrived
+
+    sums_hop()
+    (pieces,) = last_line.hold(pieces)
+    grad_first = grad_line.placed().reshape(length, -1)
+    history_grad, slot_part = unmix_streams(
+        slot_mix, history, grad_first, 0, depth_count, rows_mb, None
+    )
+    slot_parts = [slot_part.reshape(depth_count, 1, rows_mb, 128)]
+    for hop in range(1, depth_count):
+        last_line.step()
+        ff_sums.step()
+        if hops_left:
+            sums_hop()
+        if hop < depth_count - 1:
+            (state,) = last_line.hold((ff_sums.up, ff_sums.down, pieces))
+            ff_sums.up, ff_sums.down, pieces = state
+    while hops_left:
+        sums_hop()
+    last_grads = last_line.placed().reshape(length, -1)
+    totals = pieces[0].astype(bf16)
+    history_grad, slot_part = unmix_streams(
+        slot_mix, history, last_grads, 1, depth_count, rows_mb, history_grad
+    )
+    slot_parts.append(slot_part.reshape(depth_count, 1, rows_mb, 128))
+    arrived = over_depth_swap(totals)
+
     slot_grads = jnp.concatenate(slot_parts, axis=1).reshape(-1, 128)[:, : STREAMS * slots]
     mix_grads = dot_exact(slot_grads, pick.T).reshape(depth_count, MB * rows_mb, STREAMS * MIX)
     grad_mixing = scatter_small(mix_grads, ("depth",))
+    (grad_mixing,) = ff_sums.hold(grad_mixing)
+    ff_grads = end_sums(ff_sums, bf16).reshape(2, dp_count, own_rows, ff_part)
+    ff_pieces = [
+        lax.dynamic_index_in_dim(ff_grads, partners[m], 1, keepdims=False) for m in range(dp_count)
+    ]
+    ff_pieces = [ff_pieces[0]] + [swap_mask(ff_pieces[m], "dp", m) for m in range(1, dp_count)]
+    up_grad, down_grad = ff_join(jnp.stack(ff_pieces), partners)
     last_dots = rows_of("last_dot")
     grad_mixing = grad_mixing + dot_exact(last_dots, pick_last.astype(f32).T)
     grad_mixing = grad_mixing + other_core(grad_mixing)
@@ -1003,6 +1511,8 @@
     grad_first = dot_exact(gen_normed.astype(f32).T, grad_pre)
     grad_gen_normed = dot_exact(grad_pre, gen_first.astype(f32).T)
     gain_gen = jnp.sum(grad_gen_normed * unit, axis=0)
+    gain_gen, arrived = fence(gain_gen, arrived)
+    scattered = jnp.sum(arrived.astype(f32), axis=0)
     grad_unit = grad_gen_normed * gain_float[4]
     shared = jnp.mean(grad_unit * unit, axis=-1, keepdims=True)
     current_gen = half_of(inverse_rms * (grad_unit - unit * shared), 1, model_at)

time: 1790 us -> 1460 us (0.82)
  waiting for transfers between devices: 968 us -> 569 us
  Pallas kernels: 249 us -> 486 us
  starting transfers between devices: 247 us -> 184 us
  other arithmetic: 139 us -> 93.5 us
  local copies, waits for them, and re-layouts: 118 us -> 77.6 us
  matrix products: 47.1 us -> 13.1 us
    ppermute x0 -> x56, waiting for transfers between devices: none -> 333 us  [the longest x20 169 us: core_hop(): return lax.ppermute(values, ('dp', 'mp'), pairs)]
    all_to_all x12 -> x5, waiting for transfers between devices: 311 us -> 8.43 us  [over_depth_swap(): return lax.all_to_all(values, 'depth', 0, 0, tiled=True)]
    pallas_call x2 -> x51, Pallas kernels: 12.1 us -> 249 us  [the longest x32 120 us: place_block(): pl.pallas_call(place_kernel, grid_spec=pltpu.PrefetchScalarGridSpec(num_s...]
    ppermute x104 -> x55, waiting for transfers between devices: 424 us -> 228 us  [swap_mask(): return lax.ppermute(values, axis, [(i, i ^ mask) for i in range(size)])]
    all_gather x1, waiting for transfers between devices: 143 us -> 0.01 us  [local(): over_depth = lax.all_gather(stacked, 'depth', axis=0, tiled=True)]
    ppermute x0 -> x56, starting transfers between devices: none -> 113 us  [the longest x9 45.2 us: step(): self.up = lax.ppermute(goes_up, 'depth', up_pairs)]
    all_to_all x12 -> x5, starting transfers between devices: 134 us -> 23.3 us  [over_depth_swap(): return lax.all_to_all(values, 'depth', 0, 0, tiled=True)]
    all_gather x4 -> x0, waiting for transfers between devices: 88.7 us -> none  [the longest x2 88.7 us: ff_gather(): full = lax.all_gather(flat, 'depth', axis=0, tiled=True)]
  transfers between devices with their start and end apart: 121 -> 117, of which waited for: 60 -> 44; matrix products, arithmetic and copies ran while one was open for 14% -> 9% of each run, Pallas kernels for 13% -> 32%
where the time goes in v2:
time: 1460 us; the launch traced here: 1440 us
  waiting for transfers between devices  569 us (39%)
  Pallas kernels  486 us (33%)
  starting transfers between devices  184 us (13%)
  other arithmetic  93.5 us (6%)
  local copies, waits for them, and re-layouts  77.6 us (5%)
  between operations  16.4 us (1%)
    ppermute x55, waiting for transfers between devices, swap_mask(): return lax.ppermute(values, axis, [(i, i ^ mask) for i in range(size)])  228 us
    ppermute x20, waiting for transfers between devices, core_hop(): return lax.ppermute(values, ('dp', 'mp'), pairs)  169 us
    pallas_call x32, Pallas kernels, place_block(): pl.pallas_call(place_kernel, grid_spec=pltpu.PrefetchScalarGridSpec(num_s...  120 us
    ppermute x9, waiting for transfers between devices, step(): self.down.append(lax.ppermute(self.down[-1], 'depth', down_pairs))  79.8 us
    pallas_call x9, Pallas kernels, hop_sums(): pl.pallas_call(hop_kernel, grid_spec=pltpu.PrefetchScalarGridSpec(num_sca...  58.3 us
    ppermute x55, starting transfers between devices, swap_mask(): return lax.ppermute(values, axis, [(i, i ^ mask) for i in range(size)])  47.6 us
    pallas_call x2, Pallas kernels, feed_forward(): pl.pallas_call(ff_kernel, grid_spec=pltpu.PrefetchScalarGridSpec(num_scal...  47 us
    ppermute x9, starting transfers between devices, step(): self.up = lax.ppermute(goes_up, 'depth', up_pairs)  45.2 us
  transfers between devices with their start and end apart: 117, of which 44 were waited for; matrix products, arithmetic and copies ran while one was open for 9% of the time, Pallas kernels for 32%

profile of v2, /device:TPU:0, one launch (start us, length us, event | category | flops | bytes accessed | tf_op | source)
XLA Modules:
  0.0 1440.0 jit_solution(12123529917936046930)
XLA Ops:
  85.1 14.3 mix_streams.2
  119.6 14.3 mix_streams.3
  133.9 15.9 %collective-permute-done.18.refs_0_ = bf16[8,128,1024]{2,1,0:T(8,128)(2,1)} collective-permute-done((bf16[8,128,1024]{2,1,0:T(8,128)(2,1)}, bf16[8,128,1024]{2,1,0:T(8,128)(2,1)}, u32[]{:S(2)}, u32[]{:S(2)}) %collective-permute-start.18) | collective-permute-done | bytes 2097184 | tf_op jit(solution)/shard_map/ppermute | solution.py:183
  183.8 19.6 %collective-permute-done.22.refs_1_ = bf16[8,128,1024]{2,1,0:T(8,128)(2,1)} collective-permute-done((bf16[8,128,1024]{2,1,0:T(8,128)(2,1)}, bf16[8,128,1024]{2,1,0:T(8,128)(2,1)}, u32[]{:S(2)}, u32[]{:S(2)}) %collective-permute-start.22) | collective-permute-done | bytes 2097184 | tf_op jit(solution)/shard_map/ppermute | solution.py:184
  235.4 19.5 %collective-permute-done.27.refs_1_ = bf16[8,128,1024]{2,1,0:T(8,128)(2,1)} collective-permute-done((bf16[8,128,1024]{2,1,0:T(8,128)(2,1)}, bf16[8,128,1024]{2,1,0:T(8,128)(2,1)}, u32[]{:S(2)}, u32[]{:S(2)}) %collective-permute-start.27) | collective-permute-done | bytes 2097184 | tf_op jit(solution)/shard_map/ppermute | solution.py:184
  293.3 18.2 %collective-permute-done.48.refs_0_ = bf16[1,512,1024]{2,1,0:T(8,128)(2,1)} collective-permute-done((bf16[1,512,1024]{2,1,0:T(8,128)(2,1)S(1)}, bf16[1,512,1024]{2,1,0:T(8,128)(2,1)}, u32[]{:S(2)}, u32[]{:S(2)}) %collective-permute-start.48) | collective-permute-done | bytes 1048608 | tf_op jit(solution)/shard_map/ppermute | solution.py:105
  329.5 26.3 %collective-permute-done.33.refs_2_ = bf16[1,256,4096]{2,1,0:T(8,128)(2,1)} collective-permute-done((bf16[1,256,4096]{2,1,0:T(8,128)(2,1)}, bf16[1,256,4096]{2,1,0:T(8,128)(2,1)}, u32[]{:S(2)}, u32[]{:S(2)}) %collective-permute-start.33) | collective-permute-done | bytes 2097184 | tf_op jit(solution)/shard_map/ppermute | solution.py:227
  456.9 55.3 %collective-permute-done.44 = s32[1,512]{1,0:T(1,128)S(1)} collective-permute-done((s32[1,512]{1,0:T(1,128)S(1)}, s32[1,512]{1,0:T(1,128)S(1)}, u32[]{:S(2)}, u32[]{:S(2)}) %collective-permute-start.44) | collective-permute-done | bytes 2080 | tf_op jit(solution)/shard_map/ppermute | solution.py:61
  570.2 10.7 attend.2
  592.1 23.5 %feed_forward.2 = (bf16[1024,1024]{1,0:T(8,128)(2,1)S(1)}, bf16[1024,1024]{1,0:T(8,128)(2,1)S(1)}, f32[1024,1024]{1,0:T(8,128)}, bf16[1024,1024]{1,0:T(8,128)(2,...) custom-call(s32[1]{0:T(128)} %bitcast.56.model_ref.half_ref, bf16[1024,2048]{1,0:T(8,128)(2,1)} %join_halves.5.x_ref.x0_ref, ...), custom_call_target="tpu_custom_call" | custom-call | flops 17179869184 | bytes 41943040 | tf_op jit(solution)/shard_map/feed_forward/pallas_call | solution.py:943
  704.8 10.7 attend.3
  720.9 23.5 %feed_forward.3 = (bf16[1024,1024]{1,0:T(8,128)(2,1)S(1)}, bf16[1024,1024]{1,0:T(8,128)(2,1)S(1)}, f32[1024,1024]{1,0:T(8,128)}, bf16[1024,1024]{1,0:T(8,128)(2,...) custom-call(s32[1]{0:T(128)} %bitcast.56.model_ref.half_ref, bf16[1024,2048]{1,0:T(8,128)(2,1)} %join_halves.7.x_ref.x1_ref, ...), custom_call_target="tpu_custom_call" | custom-call | flops 17179869184 | bytes 41943040 | tf_op jit(solution)/shard_map/feed_forward/pallas_call | solution.py:943
  798.7 27.4 %collective-permute-done.67.refs_0_ = bf16[1,256,4096]{2,1,0:T(8,128)(2,1)} collective-permute-done((bf16[1,256,4096]{2,1,0:T(8,128)(2,1)S(1)}, bf16[1,256,4096]{2,1,0:T(8,128)(2,1)}, u32[]{:S(2)}, u32[]{:S(2)}) %collective-permute-start.67) | collective-permute-done | bytes 2097184 | tf_op jit(solution)/shard_map/ppermute | solution.py:183
  843.8 24.5 %hidden_grads.1.refs_0_.refs_1_.term_ref = f32[8,4,128,1024]{3,2,1,0:T(8,128)} custom-call(bf16[1024,2048]{1,0:T(8,128)(2,1)} %join_halves.5.x_ref.x0_ref, bf16[1024,2048]{1,0:T(8,128)(2,1)} %join_halves.7.x_ref.x1_ref, bf16[2,1024,2048]{2,1,0:T(8,128)(2,1)} %bitcast.392, bf16[2,1024,2048]{2,1,0:T(8,128)(2,1)} %bitcast.393, ...), custom_call_target="tpu_custom_call" | custom-call | flops 17179869184 | bytes 16777216 | tf_op jit(solution)/shard_map/hidden_grads/pallas_call | solution.py:460
  912.9 19.7 %collective-permute-done.75.refs_1_ = bf16[1,256,4096]{2,1,0:T(8,128)(2,1)} collective-permute-done((bf16[1,256,4096]{2,1,0:T(8,128)(2,1)}, bf16[1,256,4096]{2,1,0:T(8,128)(2,1)}, u32[]{:S(2)}, u32[]{:S(2)}) %collective-permute-start.75) | collective-permute-done | bytes 2097184 | tf_op jit(solution)/shard_map/ppermute | solution.py:184
  937.3 44.1 %collective-permute-done.78 = bf16[4,4,128,1024]{3,2,1,0:T(8,128)(2,1)S(1)} collective-permute-done((bf16[4,4,128,1024]{3,2,1,0:T(8,128)(2,1)}, bf16[4,4,128,1024]{3,2,1,0:T(8,128)(2,1)S(1)}, u32[]{:S(2)}, u32[]{:S(2)}) %collective-permute-start.78) | collective-permute-done | bytes 4194336 | tf_op jit(solution)/shard_map/ppermute | solution.py:105
  1000.7 34.1 %collective-permute-done.83 = bf16[4,4,128,1024]{3,2,1,0:T(8,128)(2,1)} collective-permute-done((bf16[4,4,128,1024]{3,2,1,0:T(8,128)(2,1)}, bf16[4,4,128,1024]{3,2,1,0:T(8,128)(2,1)}, u32[]{:S(2)}, u32[]{:S(2)}) %collective-permute-start.83) | collective-permute-done | bytes 4194336 | tf_op jit(solution)/shard_map/ppermute | solution.py:105
  1058.5 17.0 %collective-permute-done.54 = bf16[2,256,1024]{2,1,0:T(8,128)(2,1)S(1)} collective-permute-done((bf16[2,256,1024]{2,1,0:T(8,128)(2,1)S(1)}, bf16[2,256,1024]{2,1,0:T(8,128)(2,1)S(1)}, u32[]{:S(2)}, u32[]{:S(2)}) %collective-permute-start.54) | collective-permute-done | bytes 1048608 | tf_op jit(solution)/shard_map/ppermute | solution.py:105
  1089.7 30.1 %collective-permute-done.55 = bf16[1,256,1024]{2,1,0:T(8,128)(2,1)} collective-permute-done((bf16[1,256,1024]{2,1,0:T(8,128)(2,1)}, bf16[1,256,1024]{2,1,0:T(8,128)(2,1)}, u32[]{:S(2)}, u32[]{:S(2)}) %collective-permute-start.55) | collective-permute-done | bytes 524320 | tf_op jit(solution)/shard_map/ppermute | solution.py:105
  1150.1 19.5 %unmix_streams.2 = (bf16[5,2048,1024]{2,1,0:T(8,128)(2,1)}, f32[1024,128]{1,0:T(8,128)}) custom-call(f32[2048,20]{1,0:T(8,128)} %copy.118.mix_ref, bf16[5,2048,1024]{2,1,0:T(8,128)(2,1)} %hist_ref.7, bf16[1024,4096]{1,0:T(8,128)(2,1)} %bitcast.360), custom_call_target="tpu_custom_call" | custom-call | flops 83886080 | bytes 29360128 | tf_op jit(solution)/shard_map/unmix_streams/pallas_call | solution.py:587
  1208.8 19.6 %unmix_streams.3 = (bf16[5,2048,1024]{2,1,0:T(8,128)(2,1)}, f32[1024,128]{1,0:T(8,128)}) custom-call(f32[2048,20]{1,0:T(8,128)} %copy.118.mix_ref, bf16[5,2048,1024]{2,1,0:T(8,128)(2,1)} %hist_ref.7, bf16[1024,4096]{1,0:T(8,128)(2,1)} %bitcast.359, bf16[5,2048,1024]{2,1,0:T(8,128)(2,1)} %get-tuple-element.378.rest_0_), custom_call_target="tpu_custom_call", output_to_operand_aliasing={{0}: (3, {})} | custom-call | flops 83886080 | bytes 29360128 | tf_op jit(solution)/shard_map/unmix_streams/pallas_call | solution.py:587
  1240.2 99.7 %collective-permute-done.92 = f32[1,512,72]{1,2,0:T(8,128)S(1)} collective-permute-done((f32[1,512,72]{1,2,0:T(8,128)S(1)}, f32[1,512,72]{1,2,0:T(8,128)S(1)}, u32[]{:S(2)}, u32[]{:S(2)}) %collective-permute-start.92) | collective-permute-done | bytes 147488 | tf_op jit(solution)/shard_map/ppermute | solution.py:61
  1368.5 14.0 collective-permute-done.103
  1402.4 10.3 collective-permute-done.108
  (643 shorter events, 811.8 us)
Async XLA Ops:
  7.2 100.3 %all-gather.2.cloned.1.call-start = ((), (), s32[]{:S(2)}) async-start(), calls=%async_computation.5 | async-start | bytes 5242880 | tf_op jit(solution)/shard_map/all_gather | solution.py:1235
  282.6 73.2 %collective-permute-start.33 = (bf16[1,256,4096]{2,1,0:T(8,128)(2,1)}, bf16[1,256,4096]{2,1,0:T(8,128)(2,1)}, u32[]{:S(2)}, u32[]{:S(2)}) collective-permute-start(bf16[1,256,4096]{2,1,0:T(8,128)(2,1)} %get-tuple-element.251), channel_id=1, source_target_pairs={{0,2},{1,3},{8,10},{9,11},{16,18},{17,19},{24,26},{25,27}} | collective-permute-start | bytes 6291464 | tf_op jit(solution)/shard_map/ppermute | solution.py:227
  288.5 67.3 %collective-permute-start.34 = (bf16[1,256,4096]{2,1,0:T(8,128)(2,1)}, bf16[1,256,4096]{2,1,0:T(8,128)(2,1)}, u32[]{:S(2)}, u32[]{:S(2)}) collective-permute-start(bf16[1,256,4096]{2,1,0:T(8,128)(2,1)} %get-tuple-element.252), channel_id=1, source_target_pairs={{6,4},{7,5},{14,12},{15,13},{22,20},{23,21},{30,28},{31,29}} | collective-permute-start | bytes 6291464 | tf_op jit(solution)/shard_map/ppermute | solution.py:228
  314.2 67.6 %collective-permute-start.49 = (bf16[2,512,1024]{2,1,0:T(8,128)(2,1)}, bf16[2,512,1024]{2,1,0:T(8,128)(2,1)}, u32[]{:S(2)}, u32[]{:S(2)}) collective-permute-start(bf16[2,512,1024]{2,1,0:T(8,128)(2,1)} %pad_maximum_fusion), channel_id=1, source_target_pairs={{0,16},{1,9},{8,24},{9,1},{16,0},{17,25},{24,8},{25,17},{2,18},{3,... | collective-permute-start | bytes 6291464 | tf_op jit(solution)/shard_map/ppermute | solution.py:105
  327.1 68.2 %collective-permute-start.37 = (bf16[256,4096]{1,0:T(8,128)(2,1)}, bf16[256,4096]{1,0:T(8,128)(2,1)}, u32[]{:S(2)}, u32[]{:S(2)}) collective-permute-start(bf16[256,4096]{1,0:T(8,128)(2,1)} %get-tuple-element.255.own_ref.low_ref), channel_id=1, source_target_pairs={{0,1},{1,0},{2,3},{3,2},{4,5},{5,4},{6,7},{7,6},{8,9},{9,8},{10,11... | collective-permute-start | bytes 6291464 | tf_op jit(solution)/shard_map/ppermute | solution.py:61
  395.4 161.3 %collective-permute-start.50 = (bf16[2048,1024]{1,0:T(8,128)(2,1)}, bf16[2048,1024]{1,0:T(8,128)(2,1)}, u32[]{:S(2)}, u32[]{:S(2)}) collective-permute-start(bf16[2048,1024]{1,0:T(8,128)(2,1)} %bitcast.73.own_ref), channel_id=1, source_target_pairs={{0,1},{1,0},{2,3},{3,2},{4,5},{5,4},{6,7},{7,6},{8,9},{9,8},{10,11... | collective-permute-start | bytes 12582920 | tf_op jit(solution)/shard_map/ppermute | solution.py:61
  425.0 145.2 %all-to-all-start = ((bf16[4,256,1024]{2,1,0:T(8,128)(2,1)}), bf16[4,256,1024]{2,1,0:T(8,128)(2,1)}, u32[]{:S(2)}, u32[]{:S(2)}) async-start(bf16[4,256,1024]{2,1,0:T(8,128)(2,1)} %project_heads.2), calls=%async_computation | async-start | bytes 4194304 | tf_op jit(solution)/shard_map/all_to_all | solution.py:1258
  446.6 118.9 %collective-permute-start.43 = (bf16[1024,1024]{1,0:T(8,128)(2,1)}, bf16[1024,1024]{1,0:T(8,128)(2,1)}, u32[]{:S(2)}, u32[]{:S(2)}) collective-permute-start(bf16[1024,1024]{1,0:T(8,128)(2,1)} %bitcast.371), channel_id=1, source_target_pairs={{0,1},{1,0},{2,3},{3,2},{4,5},{5,4},{6,7},{7,6},{8,9},{9,8},{10,11... | collective-permute-start | bytes 6291464 | tf_op jit(solution)/shard_map/ppermute | solution.py:61
  446.6 123.6 %collective-permute-start.39 = (bf16[1,256,4096]{2,1,0:T(8,128)(2,1)}, bf16[1,256,4096]{2,1,0:T(8,128)(2,1)}, u32[]{:S(2)}, u32[]{:S(2)}) collective-permute-start(bf16[1,256,4096]{2,1,0:T(8,128)(2,1)} %get-tuple-element.263), channel_id=1, source_target_pairs={{0,2},{2,4},{4,6},{1,3},{3,5},{5,7},{8,10},{10,12},{12,14},{9,11},... | collective-permute-start | bytes 6291464 | tf_op jit(solution)/shard_map/ppermute | solution.py:227
  451.8 118.3 %collective-permute-start.40 = (bf16[1,256,4096]{2,1,0:T(8,128)(2,1)}, bf16[1,256,4096]{2,1,0:T(8,128)(2,1)}, u32[]{:S(2)}, u32[]{:S(2)}) collective-permute-start(bf16[1,256,4096]{2,1,0:T(8,128)(2,1)} %get-tuple-element.264), channel_id=1, source_target_pairs={{6,4},{4,2},{2,0},{7,5},{5,3},{3,1},{14,12},{12,10},{10,8},{15,13}... | collective-permute-start | bytes 6291464 | tf_op jit(solution)/shard_map/ppermute | solution.py:228
  453.6 58.7 %collective-permute-start.44 = (s32[1,512]{1,0:T(1,128)S(1)}, s32[1,512]{1,0:T(1,128)S(1)}, u32[]{:S(2)}, u32[]{:S(2)}) collective-permute-start(s32[1,512]{1,0:T(1,128)S(1)} %bitcast.454), channel_id=1, source_target_pairs={{0,2},{2,0},{4,6},{6,4},{1,3},{3,1},{5,7},{7,5},{8,10},{10,8},{12,... | collective-permute-start | bytes 6152 | tf_op jit(solution)/shard_map/ppermute | solution.py:61
  1045.4 124.2 %collective-permute-start.88 = (bf16[4,4,128,1024]{3,2,1,0:T(8,128)(2,1)}, bf16[4,4,128,1024]{3,2,1,0:T(8,128)(2,1)}, u32[]{:S(2)}, u32[]{:S(2)}) collective-permute-start(bf16[4,4,128,1024]{3,2,1,0:T(8,128)(2,1)} %convert_add_fusion.1), channel_id=1, source_target_pairs={{0,8},{1,17},{8,0},{9,25},{16,24},{17,1},{24,16},{25,9},{2,10},{3,... | collective-permute-start | bytes 12582920 | tf_op jit(solution)/shard_map/ppermute | solution.py:105
  1057.9 65.3 %collective-permute-start.65 = (bf16[2,256,1024]{2,1,0:T(8,128)(2,1)}, bf16[2,256,1024]{2,1,0:T(8,128)(2,1)S(1)}, u32[]{:S(2)}, u32[]{:S(2)}) collective-permute-start(bf16[2,256,1024]{2,1,0:T(8,128)(2,1)} %pad_maximum_fusion.7), channel_id=1, source_target_pairs={{0,16},{1,9},{8,24},{9,1},{16,0},{17,25},{24,8},{25,17},{2,18},{3,... | collective-permute-start | bytes 3145736 | tf_op jit(solution)/shard_map/ppermute | solution.py:105
  1077.4 101.5 %collective-permute-start.84 = (bf16[1,256,4096]{2,1,0:T(8,128)(2,1)}, bf16[1,256,4096]{2,1,0:T(8,128)(2,1)}, u32[]{:S(2)}, u32[]{:S(2)}) collective-permute-start(bf16[1,256,4096]{2,1,0:T(8,128)(2,1)} %collective-permute-done.79.refs_0_), channel_id=1, source_target_pairs={{4,6},{5,7},{12,14},{13,15},{20,22},{21,23},{28,30},{29,31}} | collective-permute-start | bytes 6291464 | tf_op jit(solution)/shard_map/ppermute | solution.py:183
  1079.4 99.6 %collective-permute-start.85 = (bf16[1,256,4096]{2,1,0:T(8,128)(2,1)}, bf16[1,256,4096]{2,1,0:T(8,128)(2,1)}, u32[]{:S(2)}, u32[]{:S(2)}) collective-permute-start(bf16[1,256,4096]{2,1,0:T(8,128)(2,1)} %collective-permute-done.80.refs_1_), channel_id=1, source_target_pairs={{2,0},{3,1},{10,8},{11,9},{18,16},{19,17},{26,24},{27,25}} | collective-permute-start | bytes 6291464 | tf_op jit(solution)/shard_map/ppermute | solution.py:184
  1119.8 59.2 %collective-permute-start.86 = (bf16[8,128,1024]{2,1,0:T(8,128)(2,1)}, bf16[8,128,1024]{2,1,0:T(8,128)(2,1)}, u32[]{:S(2)}, u32[]{:S(2)}) collective-permute-start(bf16[8,128,1024]{2,1,0:T(8,128)(2,1)} %get-tuple-element.362), channel_id=1, source_target_pairs={{0,2},{2,4},{1,3},{3,5},{8,10},{10,12},{9,11},{11,13},{16,18},{18,... | collective-permute-start | bytes 6291464 | tf_op jit(solution)/shard_map/ppermute | solution.py:227
  1123.2 55.8 %collective-permute-start.87 = (bf16[8,128,1024]{2,1,0:T(8,128)(2,1)}, bf16[8,128,1024]{2,1,0:T(8,128)(2,1)}, u32[]{:S(2)}, u32[]{:S(2)}) collective-permute-start(bf16[8,128,1024]{2,1,0:T(8,128)(2,1)} %get-tuple-element.363), channel_id=1, source_target_pairs={{6,4},{4,2},{7,5},{5,3},{14,12},{12,10},{15,13},{13,11},{22,20},{2... | collective-permute-start | bytes 6291464 | tf_op jit(solution)/shard_map/ppermute | solution.py:228
  1169.7 66.6 %collective-permute-start.66 = (bf16[1,256,1024]{2,1,0:T(8,128)(2,1)}, bf16[1,256,1024]{2,1,0:T(8,128)(2,1)}, u32[]{:S(2)}, u32[]{:S(2)}) collective-permute-start(bf16[1,256,1024]{2,1,0:T(8,128)(2,1)} %fusion.9), channel_id=1, source_target_pairs={{0,8},{1,17},{8,0},{9,25},{16,24},{17,1},{24,16},{25,9},{2,10},{3,... | collective-permute-start | bytes 1572872 | tf_op jit(solution)/shard_map/ppermute | solution.py:105
  1178.9 166.7 %collective-permute-start.95 = (f32[4,1024]{1,0:T(4,128)S(1)}, f32[4,1024]{1,0:T(4,128)S(1)}, u32[]{:S(2)}, u32[]{:S(2)}) collective-permute-start(f32[4,1024]{1,0:T(4,128)S(1)} %add.391), channel_id=1, source_target_pairs={{0,1},{1,0},{2,3},{3,2},{4,5},{5,4},{6,7},{7,6},{8,9},{9,8},{10,11... | collective-permute-start | bytes 49160 | tf_op jit(solution)/shard_map/ppermute | solution.py:61
  1188.0 157.5 %collective-permute-start.89 = (bf16[8,128,1024]{2,1,0:T(8,128)(2,1)}, bf16[8,128,1024]{2,1,0:T(8,128)(2,1)}, u32[]{:S(2)}, u32[]{:S(2)}) collective-permute-start(bf16[8,128,1024]{2,1,0:T(8,128)(2,1)} %get-tuple-element.384), channel_id=1, source_target_pairs={{0,2},{2,4},{4,6},{1,3},{3,5},{5,7},{8,10},{10,12},{12,14},{9,11},... | collective-permute-start | bytes 6291464 | tf_op jit(solution)/shard_map/ppermute | solution.py:227
  1190.7 154.8 %collective-permute-start.90 = (bf16[8,128,1024]{2,1,0:T(8,128)(2,1)}, bf16[8,128,1024]{2,1,0:T(8,128)(2,1)}, u32[]{:S(2)}, u32[]{:S(2)}) collective-permute-start(bf16[8,128,1024]{2,1,0:T(8,128)(2,1)} %get-tuple-element.385), channel_id=1, source_target_pairs={{6,4},{4,2},{2,0},{7,5},{5,3},{3,1},{14,12},{12,10},{10,8},{15,13}... | collective-permute-start | bytes 6291464 | tf_op jit(solution)/shard_map/ppermute | solution.py:228
  1192.0 199.1 %all-to-all-start.4 = ((bf16[4,4,128,1024]{3,2,1,0:T(8,128)(2,1)}), bf16[4,4,128,1024]{3,2,1,0:T(8,128)(2,1)}, u32[]{:S(2)}, u32[]{:S(2)}) async-start(bf16[4,4,128,1024]{3,2,1,0:T(8,128)(2,1)} %convert_add_fusion), calls=%async_computation.4 | async-start | bytes 8388608 | tf_op jit(solution)/shard_map/all_to_all | solution.py:1258
  1233.2 106.6 %collective-permute-start.92 = (f32[1,512,72]{1,2,0:T(8,128)S(1)}, f32[1,512,72]{1,2,0:T(8,128)S(1)}, u32[]{:S(2)}, u32[]{:S(2)}) collective-permute-start(f32[1,512,72]{1,2,0:T(8,128)S(1)} %get-tuple-element.465), channel_id=1, source_target_pairs={{0,4},{2,6},{4,0},{6,2},{1,5},{3,7},{5,1},{7,3},{8,12},{10,14},{12... | collective-permute-start | bytes 442376 | tf_op jit(solution)/shard_map/ppermute | solution.py:61
  1239.8 102.6 %collective-permute-start.91 = (f32[1,512,72]{1,2,0:T(8,128)S(1)}, f32[1,512,72]{1,2,0:T(8,128)S(1)}, u32[]{:S(2)}, u32[]{:S(2)}) collective-permute-start(f32[1,512,72]{1,2,0:T(8,128)S(1)} %get-tuple-element.464), channel_id=1, source_target_pairs={{0,4},{2,6},{4,0},{6,2},{1,5},{3,7},{5,1},{7,3},{8,12},{10,14},{12... | collective-permute-start | bytes 442376 | tf_op jit(solution)/shard_map/ppermute | solution.py:61
  (176 other events, 3510.3 us)
Sparse Core Ops, SparseCore 0:
  10.8 90.9 all-gather.1

commit v3 on v2

--- a/solution.py
+++ b/solution.py
@@ -105,10 +105,18 @@
     return lax.ppermute(values, ("dp", "mp"), pairs)
 
 
+def group_hop(pieces, at):
+    return jnp.concatenate([pieces, core_hop(pieces, at)], axis=0)
+
+
 def group_gather(values):
     pieces = values[None]
     for at in range(bit_count(lax.axis_size("dp"))):
-        pieces = jnp.concatenate([pieces, core_hop(pieces, at)], axis=0)
+        pieces = group_hop(pieces, at)
+    return group_rows_placed(pieces)
+
+
+def group_rows_placed(pieces):
     buffer = None
     for place in range(pieces.shape[0]):
         buffer = place_block(
@@ -1253,6 +1261,7 @@
     pick = (column[:, None] == from_col[None, :]).astype(f32)
     mix_all = gather_small(mixing, ("depth",)).reshape(depth_count * MB * rows_mb, STREAMS * MIX)
     slot_mix = dot_nn(mix_all, pick.astype(bf16))
+    places_all = gather_small(positions, ("depth",))
 
     def over_depth_swap(values):
         return lax.all_to_all(values, "depth", 0, 0, tiled=True)
@@ -1263,7 +1272,8 @@
 
     partners = jnp.stack([dp_at ^ m for m in range(dp_count)]).astype(jnp.int32)
     ff_local = ff_split(up_weight, down_weight, partners)
-    ff_local, slot_mix = fence(ff_local, slot_mix)
+    ff_local, cotangent, slot_mix = fence(ff_local, cotangent, slot_mix)
+    cot_pieces = group_hop(cotangent[None], 0)
     ff_rows = place_block(None, ff_local[0], partners[0], dp_count)
     for m in range(1, dp_count):
         arrived = swap_mask(ff_local[m], "dp", m)
@@ -1271,8 +1281,8 @@
     ff_rows = ff_rows.reshape(2 * dp_count, own_rows, ff_part)
 
     partial = mix_part(0, slot_mix)
-    over_depth, partial, slot_mix, ff_rows, cotangent, positions = fence(
-        over_depth, partial, slot_mix, ff_rows, cotangent, positions
+    over_depth, partial, slot_mix, ff_rows, cot_pieces, places_all = fence(
+        over_depth, partial, slot_mix, ff_rows, cot_pieces, places_all
     )
 
     weights_line = LineGather(ff_rows)
@@ -1282,12 +1292,13 @@
     pieces.append(core_hop(pieces[0], 0))
     weights = place_block(None, pieces[0][None], place_index(0), dp_count)
     partial_next = mix_part(1, slot_mix)
-    pieces, partial, partial_next, weights, cotangent = weights_line.hold(
-        pieces, partial, partial_next, weights, cotangent
+    cot_other = other_core(cotangent)
+    pieces, partial, partial_next, weights, cot_pieces, cot_other = weights_line.hold(
+        pieces, partial, partial_next, weights, cot_pieces, cot_other
     )
     hops_left = [(p, at) for at in range(1, len(dp_bits)) for p in range(1 << at)]
     placed = 1
-    cot_other = cot_mine = None
+    cots = None
     sums, sums_next = LineScatter(partial), LineScatter(partial_next)
     for hop in range(1, depth_count):
         sums.step()
@@ -1302,26 +1313,25 @@
             if len(hops_left) <= depth_count - 2 - hop:
                 break
         if last_hop:
-            cot_other = other_core(cotangent)
-            cot_mine = group_gather(cotangent)
+            cot_full = join_halves(cotangent, cot_other, model_at)
+            for at in range(1, len(dp_bits)):
+                cot_pieces = group_hop(cot_pieces, at)
+            ff_weights = weights_line.placed()
             sums_next.step()
-        (state,) = weights_line.hold((sums.up, sums.down, pieces, weights, cotangent))
-        sums.up, sums.down, pieces, weights, cotangent = state
+            cots = cot_full, ff_weights
+        (state,) = weights_line.hold(
+            (sums.up, sums.down, pieces, weights, cot_pieces, cot_other, cots)
+        )
+        sums.up, sums.down, pieces, weights, cot_pieces, cot_other, cots = state
     while sums_next.at < depth_count - 3:
         sums_next.hold()
         sums_next.step()
+    cot_full, ff_weights = cots
     for place in range(placed, len(pieces)):
         weights = place_block(weights, pieces[place][None], place_index(place), dp_count)
     weights = weights.reshape(dp_count, depth_count, 4, own_rows, heads_width)
-    ff_weights = weights_line.placed().reshape(2, dp_count, depth_count, own_rows, ff_part)
-
-    cot_full = join_halves(cotangent, cot_other, model_at)
-    cot_mine = jnp.swapaxes(cot_mine.reshape(dp_count, MB, rows_mb, width), 0, 1)
-    cot_mine = cot_mine.reshape(MB * dp_count * rows_mb, width)
-    cot_group = join_halves(cot_mine, other_core(cot_mine), model_at)
-    cot_group = cot_group.reshape(MB, dp_count * rows_mb, model)
-
-    places_all = gather_small(positions, ("depth",))
+    ff_weights = ff_weights.reshape(2, dp_count, depth_count, own_rows, ff_part)
+
     document_view = doc_ids.reshape(depth_count, MB, rows_mb)
     own_tables = turning_tables(positions)
     which = model_at.astype(jnp.int32)[None]
@@ -1374,26 +1384,32 @@
         own, kept["flat"] = back_project(answer, weights, which, f32, True)
         grad_norm_ff = reduce_group(*ff_parts[0])
         ff_out = reduce_group(*ff_parts[1])
-        kept["layer_rows"] = (kept["resid"] + own[0] + got[0].astype(f32) + ff_out).astype(bf16)
-        return own, got, grad_norm_ff
-
-    def leave(micro_at, kept, own, got, grad_norm_ff):
+        rows = (kept["resid"] + own[0] + got[0].astype(f32) + ff_out).astype(bf16)
+        return own, got, grad_norm_ff, rows
+
+    def leave(micro_at, kept, own, got, grad_norm_ff, rows):
         span = slice(micro_at * rows_mb, (micro_at + 1) * rows_mb)
         low, stats = kept["low"], kept["stats"]
         scaled, sums, gain_part = norm_slopes(own, got, grad_norm_ff, low, stats, gains, which)
         grad_low, current_mix, last_dot = stream_grads(
             scaled, sums, other_core(sums), low, stats, cotangent[span], current_half[span], last[span]
         )
-        kept.update(gain=gain_part, current_mix=current_mix, last_dot=last_dot)
+        kept.update(layer_rows=rows, gain=gain_part, current_mix=current_mix, last_dot=last_dot)
         return grad_low
 
     sums_next.step()
     first = enter(0, sums)
-    packed, ff_normed = sums_next.hold(first["packed"], first["ff_normed"])
+    packed, ff_normed, cot_pieces = sums_next.hold(
+        first["packed"], first["ff_normed"], cot_pieces
+    )
     sums_next.step()
+    cot_mine = group_rows_placed(cot_pieces).reshape(dp_count, MB, rows_mb, width)
+    cot_mine = jnp.swapaxes(cot_mine, 0, 1).reshape(MB * dp_count * rows_mb, width)
+    cot_group = join_halves(cot_mine, other_core(cot_mine), model_at)
+    cot_group = cot_group.reshape(MB, dp_count * rows_mb, model)
     by_head = over_depth_swap(packed)
     group_normed = group_rows(ff_normed)
-    by_head, group_normed = sums_next.hold(by_head, group_normed)
+    by_head, group_normed, cot_group = sums_next.hold(by_head, group_normed, cot_group)
     answer = attention(0, by_head)
     answer, group_normed = sums_next.hold(answer, group_normed)
 
@@ -1425,76 +1441,85 @@
         return jnp.concatenate(each(name), axis=0)
 
     grad_line = LineGather(grad_low[None])
-    for hop in range(1, depth_count):
-        grad_line.step()
-        if hop == 1:
-            ways = back(second, answer, ff_parts)
-            (ways,) = grad_line.hold(ways)
-        elif hop == 2:
-            grad_low = leave(1, second, *ways)
-            ff_products = hidden_grads(
-                each("group_normed"), cot_group, each("grad_up"), each("hidden"), dp_count, depth_count
-            )
-            grad_low, ff_products = grad_line.hold(grad_low, ff_products)
-        elif hop == 3:
-            place_list = jnp.stack([place_index(p) for p in range(dp_count)]).astype(jnp.int32)
-            pieces = [
-                attention_grads(
-                    each("normed"),
-                    cot_full,
-                    each("flat"),
-                    place_list[p : p + 1],
-                    depth_count,
-                    dp_count,
-                    bf16 if p >= dp_count // 2 else f32,
-                )
-                for p in range(dp_count)
-            ]
-            grad_low, ff_products, pieces = grad_line.hold(grad_low, ff_products, pieces)
-        else:
-            grad_low, ff_products, pieces = grad_line.hold(grad_low, ff_products, pieces)
-
-    last_line = LineGather(grad_low[None])
-    last_line.step()
-    ff_sums = LineScatter(ff_products)
+    place_list = jnp.stack([place_index(p) for p in range(dp_count)]).astype(jnp.int32)
+
+    def place_grads(place, dtype):
+        return attention_grads(
+            each("normed"),
+            cot_full,
+            each("flat"),
+            place_list[place : place + 1],
+            depth_count,
+            dp_count,
+            dtype,
+        )
+
+    half = dp_count // 2
     hops_left = [
         (p, at) for at in reversed(range(len(dp_bits))) for p in range(1 << at, 2 << at)
     ]
+    pieces = {}
 
     def sums_hop():
         place, at = hops_left.pop(0)
-        arrived = core_hop(pieces[place].astype(bf16), at).astype(f32)
-        pieces[place - (1 << at)] = pieces[place - (1 << at)] + arrived
-
-    sums_hop()
-    (pieces,) = last_line.hold(pieces)
+        arrived = core_hop(pieces.pop(place).astype(bf16), at)
+        target = place - (1 << at)
+        pieces[target] = pieces[target].astype(f32) + arrived.astype(f32)
+
+    grad_line.step()
+    ways = back(second, answer, ff_parts)
+    ff_products = hidden_grads(
+        each("group_normed"), cot_group, each("grad_up"), each("hidden"), dp_count, depth_count
+    )
+    ways, ff_products = grad_line.hold(ways, ff_products)
+    pieces = {p: place_grads(p, bf16) for p in range(half, dp_count)}
+    ff_sums = LineScatter(ff_products)
+    for hop in range(2, depth_count):
+        grad_line.step()
+        ff_sums.step()
+        if hop == 2:
+            arrived = core_hop(pieces.pop(half), hops_left.pop(0)[1])
+            grad_low = leave(1, second, *ways)
+            (state,) = grad_line.hold((grad_low, ff_sums.up, ff_sums.down, arrived, pieces))
+            grad_low, ff_sums.up, ff_sums.down, arrived, pieces = state
+        else:
+            if hop == 3:
+                pieces.update({p: place_grads(p, f32) for p in range(half)})
+                pieces[0] = pieces[0] + arrived.astype(f32)
+            sums_hop()
+            (state,) = grad_line.hold((grad_low, ff_sums.up, ff_sums.down, pieces))
+            grad_low, ff_sums.up, ff_sums.down, pieces = state
+
+    last_line = LineGather(grad_low[None])
+    last_line.step()
+    while hops_left:
+        sums_hop()
     grad_first = grad_line.placed().reshape(length, -1)
     history_grad, slot_part = unmix_streams(
         slot_mix, history, grad_first, 0, depth_count, rows_mb, None
     )
     slot_parts = [slot_part.reshape(depth_count, 1, rows_mb, 128)]
-    for hop in range(1, depth_count):
+    pieces, history_grad = last_line.hold(pieces, history_grad)
+    out_sums = LineScatter(pieces[0].reshape(1, depth_count, 4 * own_rows, heads_width))
+    for hop in range(2, depth_count):
         last_line.step()
-        ff_sums.step()
-        if hops_left:
-            sums_hop()
-        if hop < depth_count - 1:
-            (state,) = last_line.hold((ff_sums.up, ff_sums.down, pieces))
-            ff_sums.up, ff_sums.down, pieces = state
-    while hops_left:
-        sums_hop()
+        out_sums.step()
+        (state,) = last_line.hold((out_sums.up, out_sums.down))
+        out_sums.up, out_sums.down = state
+    ff_sums.step()
+    out_sums.step()
     last_grads = last_line.placed().reshape(length, -1)
-    totals = pieces[0].astype(bf16)
     history_grad, slot_part = unmix_streams(
         slot_mix, history, last_grads, 1, depth_count, rows_mb, history_grad
     )
     slot_parts.append(slot_part.reshape(depth_count, 1, rows_mb, 128))
-    arrived = over_depth_swap(totals)
 
     slot_grads = jnp.concatenate(slot_parts, axis=1).reshape(-1, 128)[:, : STREAMS * slots]
     mix_grads = dot_exact(slot_grads, pick.T).reshape(depth_count, MB * rows_mb, STREAMS * MIX)
+    (state,) = ff_sums.hold((mix_grads, out_sums.up, out_sums.down))
+    mix_grads, out_sums.up, out_sums.down = state
     grad_mixing = scatter_small(mix_grads, ("depth",))
-    (grad_mixing,) = ff_sums.hold(grad_mixing)
+    scattered = end_sums(out_sums, f32).reshape(4, own_rows, heads_width)
     ff_grads = end_sums(ff_sums, bf16).reshape(2, dp_count, own_rows, ff_part)
     ff_pieces = [
         lax.dynamic_index_in_dim(ff_grads, partners[m], 1, keepdims=False) for m in range(dp_count)
@@ -1511,8 +1536,6 @@
     grad_first = dot_exact(gen_normed.astype(f32).T, grad_pre)
     grad_gen_normed = dot_exact(grad_pre, gen_first.astype(f32).T)
     gain_gen = jnp.sum(grad_gen_normed * unit, axis=0)
-    gain_gen, arrived = fence(gain_gen, arrived)
-    scattered = jnp.sum(arrived.astype(f32), axis=0)
     grad_unit = grad_gen_normed * gain_float[4]
     shared = jnp.mean(grad_unit * unit, axis=-1, keepdims=True)
     current_gen = half_of(inverse_rms * (grad_unit - unit * shared), 1, model_at)

time: 1460 us -> 1310 us (0.90)
  waiting for transfers between devices: 569 us -> 337 us
  starting transfers between devices: 184 us -> 235 us
  Pallas kernels: 486 us -> 506 us
    ppermute x55, waiting for transfers between devices: 228 us -> 56.2 us  [swap_mask(): return lax.ppermute(values, axis, [(i, i ^ mask) for i in range(size)])]
    ppermute x20, waiting for transfers between devices: 169 us -> 30.1 us  [core_hop(): return lax.ppermute(values, ('dp', 'mp'), pairs)]
    ppermute x9 -> x12, waiting for transfers between devices: 40.1 us -> 121 us  [step(): self.up = lax.ppermute(goes_up, 'depth', up_pairs)]
    ppermute x9 -> x12, starting transfers between devices: 45.2 us -> 77 us  [step(): self.up = lax.ppermute(goes_up, 'depth', up_pairs)]
    ppermute x9, waiting for transfers between devices: 43.4 us -> 14.9 us  [step(): self.up.append(lax.ppermute(self.up[-1], 'depth', up_pairs))]
    ppermute x9 -> x12, waiting for transfers between devices: 0.02 us -> 23.6 us  [step(): self.down = lax.ppermute(goes_down, 'depth', down_pairs)]
    pallas_call x9 -> x12, Pallas kernels: 58.3 us -> 72.7 us  [hop_sums(): pl.pallas_call(hop_kernel, grid_spec=pltpu.PrefetchScalarGridSpec(num_sca...]
    unnamed x170 -> x218, local copies, waits for them, and re-layouts: 41.8 us -> 45.7 us
  transfers between devices with their start and end apart: 117 -> 122, of which waited for: 44 -> 47; matrix products, arithmetic and copies ran while one was open for 9% -> 11% of each run, Pallas kernels for 32% -> 36%
where the time goes in v3:
time: 1310 us; the launch traced here: 1300 us
  Pallas kernels  506 us (39%)
  waiting for transfers between devices  337 us (26%)
  starting transfers between devices  235 us (18%)
  other arithmetic  106 us (8%)
  local copies, waits for them, and re-layouts  85.4 us (7%)
  between operations  16.3 us (1%)
    ppermute x12, waiting for transfers between devices, step(): self.up = lax.ppermute(goes_up, 'depth', up_pairs)  121 us
    pallas_call x32, Pallas kernels, place_block(): pl.pallas_call(place_kernel, grid_spec=pltpu.PrefetchScalarGridSpec(num_s...  120 us
    ppermute x9, waiting for transfers between devices, step(): self.down.append(lax.ppermute(self.down[-1], 'depth', down_pairs))  87.7 us
    ppermute x12, starting transfers between devices, step(): self.up = lax.ppermute(goes_up, 'depth', up_pairs)  77 us
    pallas_call x12, Pallas kernels, hop_sums(): pl.pallas_call(hop_kernel, grid_spec=pltpu.PrefetchScalarGridSpec(num_sca...  72.7 us
    ppermute x55, waiting for transfers between devices, swap_mask(): return lax.ppermute(values, axis, [(i, i ^ mask) for i in range(size)])  56.2 us
    pallas_call x2, Pallas kernels, feed_forward(): pl.pallas_call(ff_kernel, grid_spec=pltpu.PrefetchScalarGridSpec(num_scal...  47.1 us
    ppermute x55, starting transfers between devices, swap_mask(): return lax.ppermute(values, axis, [(i, i ^ mask) for i in range(size)])  47.1 us
  transfers between devices with their start and end apart: 122, of which 47 were waited for; matrix products, arithmetic and copies ran while one was open for 11% of the time, Pallas kernels for 36%

profile of v3, /device:TPU:0, one launch (start us, length us, event | category | flops | bytes accessed | tf_op | source)
XLA Modules:
  0.0 1297.8 jit_solution(16083150267961073818)
XLA Ops:
  96.0 14.3 %mix_streams.2 = bf16[1024,4096]{1,0:T(8,128)(2,1)} custom-call(f32[2048,20]{1,0:T(8,128)} %copy.117.mix_ref, bf16[5,2048,1024]{2,1,0:T(8,128)(2,1)} %hist_ref.7), custom_call_target="tpu_custom_call" | custom-call | flops 41943040 | bytes 18874368 | tf_op jit(solution)/shard_map/mix_streams/pallas_call | solution.py:520
  144.5 14.3 %mix_streams.3 = bf16[1024,4096]{1,0:T(8,128)(2,1)} custom-call(f32[2048,20]{1,0:T(8,128)} %copy.118.mix_ref, bf16[5,2048,1024]{2,1,0:T(8,128)(2,1)} %hist_ref.7), custom_call_target="tpu_custom_call" | custom-call | flops 41943040 | bytes 18874368 | tf_op jit(solution)/shard_map/mix_streams/pallas_call | solution.py:520
  158.8 14.8 %collective-permute-done.22.refs_0_ = bf16[8,128,1024]{2,1,0:T(8,128)(2,1)} collective-permute-done((bf16[8,128,1024]{2,1,0:T(8,128)(2,1)S(1)}, bf16[8,128,1024]{2,1,0:T(8,128)(2,1)}, u32[]{:S(2)}, u32[]{:S(2)}) %collective-permute-start.22) | collective-permute-done | bytes 2097184 | tf_op jit(solution)/shard_map/ppermute | solution.py:191
  208.1 18.4 %collective-permute-done.31.refs_1_ = bf16[8,128,1024]{2,1,0:T(8,128)(2,1)} collective-permute-done((bf16[8,128,1024]{2,1,0:T(8,128)(2,1)}, bf16[8,128,1024]{2,1,0:T(8,128)(2,1)}, u32[]{:S(2)}, u32[]{:S(2)}) %collective-permute-start.31) | collective-permute-done | bytes 2097184 | tf_op jit(solution)/shard_map/ppermute | solution.py:192
  261.1 18.6 %collective-permute-done.36.refs_1_ = bf16[8,128,1024]{2,1,0:T(8,128)(2,1)} collective-permute-done((bf16[8,128,1024]{2,1,0:T(8,128)(2,1)}, bf16[8,128,1024]{2,1,0:T(8,128)(2,1)}, u32[]{:S(2)}, u32[]{:S(2)}) %collective-permute-start.36) | collective-permute-done | bytes 2097184 | tf_op jit(solution)/shard_map/ppermute | solution.py:192
  364.6 17.1 %collective-permute-done.26.refs_2_ = bf16[1,256,4096]{2,1,0:T(8,128)(2,1)} collective-permute-done((bf16[1,256,4096]{2,1,0:T(8,128)(2,1)}, bf16[1,256,4096]{2,1,0:T(8,128)(2,1)}, u32[]{:S(2)}, u32[]{:S(2)}) %collective-permute-start.26) | collective-permute-done | bytes 2097184 | tf_op jit(solution)/shard_map/ppermute | solution.py:235
  415.1 10.6 collective-permute-done.28.refs_2_
  512.1 29.6 %collective-permute-done.44.up_ref = bf16[1,256,4096]{2,1,0:T(8,128)(2,1)} collective-permute-done((bf16[1,256,4096]{2,1,0:T(8,128)(2,1)}, bf16[1,256,4096]{2,1,0:T(8,128)(2,1)}, u32[]{:S(2)}, u32[]{:S(2)}) %collective-permute-start.44) | collective-permute-done | bytes 2097184 | tf_op jit(solution)/shard_map/ppermute | solution.py:235
  550.3 10.8 attend.2
  577.4 23.6 %feed_forward.2 = (bf16[1024,1024]{1,0:T(8,128)(2,1)S(1)}, bf16[1024,1024]{1,0:T(8,128)(2,1)S(1)}, f32[1024,1024]{1,0:T(8,128)}, bf16[1024,1024]{1,0:T(8,128)(2,...) custom-call(s32[1]{0:T(128)} %bitcast.57.model_ref.half_ref, bf16[1024,2048]{1,0:T(8,128)(2,1)} %join_halves.5.x_ref.x0_ref, ...), custom_call_target="tpu_custom_call" | custom-call | flops 17179869184 | bytes 41943040 | tf_op jit(solution)/shard_map/feed_forward/pallas_call | solution.py:951
  703.1 10.8 attend.3
  720.8 23.5 %feed_forward.3 = (bf16[1024,1024]{1,0:T(8,128)(2,1)S(1)}, bf16[1024,1024]{1,0:T(8,128)(2,1)S(1)}, f32[1024,1024]{1,0:T(8,128)}, bf16[1024,1024]{1,0:T(8,128)(2,...) custom-call(s32[1]{0:T(128)} %bitcast.57.model_ref.half_ref, bf16[1024,2048]{1,0:T(8,128)(2,1)} %join_halves.7.x_ref.x1_ref, ...), custom_call_target="tpu_custom_call" | custom-call | flops 17179869184 | bytes 41943040 | tf_op jit(solution)/shard_map/feed_forward/pallas_call | solution.py:951
  809.4 24.7 %hidden_grads.1.refs_0_.refs_1_.term_ref = f32[8,4,128,1024]{3,2,1,0:T(8,128)} custom-call(bf16[1024,2048]{1,0:T(8,128)(2,1)} %join_halves.5.x_ref.x0_ref, bf16[1024,2048]{1,0:T(8,128)(2,1)} %join_halves.7.x_ref.x1_ref, bf16[2,1024,2048]{2,1,0:T(8,128)(2,1)} %bitcast.403, bf16[2,1024,2048]{2,1,0:T(8,128)(2,1)} %bitcast.404, ...), custom_call_target="tpu_custom_call" | custom-call | flops 17179869184 | bytes 16777216 | tf_op jit(solution)/shard_map/hidden_grads/pallas_call | solution.py:468
  885.6 15.0 %collective-permute-done.72.refs_1_ = bf16[1,256,4096]{2,1,0:T(8,128)(2,1)} collective-permute-done((bf16[1,256,4096]{2,1,0:T(8,128)(2,1)}, bf16[1,256,4096]{2,1,0:T(8,128)(2,1)}, u32[]{:S(2)}, u32[]{:S(2)}) %collective-permute-start.72) | collective-permute-done | bytes 2097184 | tf_op jit(solution)/shard_map/ppermute | solution.py:192
  949.3 10.3 convert_add_fusion.2
  975.8 11.1 collective-permute-start.82
  1003.2 19.5 %unmix_streams.2 = (bf16[5,2048,1024]{2,1,0:T(8,128)(2,1)}, f32[1024,128]{1,0:T(8,128)}) custom-call(f32[2048,20]{1,0:T(8,128)} %copy.118.mix_ref, bf16[5,2048,1024]{2,1,0:T(8,128)(2,1)} %hist_ref.7, bf16[1024,4096]{1,0:T(8,128)(2,1)} %bitcast.374), custom_call_target="tpu_custom_call" | custom-call | flops 83886080 | bytes 29360128 | tf_op jit(solution)/shard_map/unmix_streams/pallas_call | solution.py:595
  1041.0 12.3 collective-permute-start.87
  1054.0 18.5 %collective-permute-done.87.refs_2_ = bf16[1,512,1024]{2,1,0:T(8,128)(2,1)S(1)} collective-permute-done((bf16[1,512,1024]{2,1,0:T(8,128)(2,1)}, bf16[1,512,1024]{2,1,0:T(8,128)(2,1)S(1)}, u32[]{:S(2)}, u32[]{:S(2)}) %collective-permute-start.87) | collective-permute-done | bytes 1048608 | tf_op jit(solution)/shard_map/ppermute | solution.py:235
  1072.6 16.8 %collective-permute-done.86.refs_1_ = bf16[1,256,4096]{2,1,0:T(8,128)(2,1)} collective-permute-done((bf16[1,256,4096]{2,1,0:T(8,128)(2,1)S(1)}, bf16[1,256,4096]{2,1,0:T(8,128)(2,1)}, u32[]{:S(2)}, u32[]{:S(2)}) %collective-permute-start.86) | collective-permute-done | bytes 2097184 | tf_op jit(solution)/shard_map/ppermute | solution.py:192
  1115.8 11.5 collective-permute-done.91.refs_2_
  1128.6 13.5 %collective-permute-done.90.refs_1_ = bf16[1,256,4096]{2,1,0:T(8,128)(2,1)} collective-permute-done((bf16[1,256,4096]{2,1,0:T(8,128)(2,1)}, bf16[1,256,4096]{2,1,0:T(8,128)(2,1)}, u32[]{:S(2)}, u32[]{:S(2)}) %collective-permute-start.90) | collective-permute-done | bytes 2097184 | tf_op jit(solution)/shard_map/ppermute | solution.py:192
  1166.0 19.6 %unmix_streams.3 = (bf16[5,2048,1024]{2,1,0:T(8,128)(2,1)}, f32[1024,128]{1,0:T(8,128)}) custom-call(f32[2048,20]{1,0:T(8,128)} %copy.118.mix_ref, bf16[5,2048,1024]{2,1,0:T(8,128)(2,1)} %hist_ref.7, bf16[1024,4096]{1,0:T(8,128)(2,1)} %bitcast.373, bf16[5,2048,1024]{2,1,0:T(8,128)(2,1)} %get-tuple-element.395.rest_0_), custom_call_target="tpu_custom_call", output_to_operand_aliasing={{0}: (3, {})} | custom-call | flops 83886080 | bytes 29360128 | tf_op jit(solution)/shard_map/unmix_streams/pallas_call | solution.py:595
  1189.2 15.1 %collective-permute-done.96.down_ref = bf16[1,512,1024]{2,1,0:T(8,128)(2,1)} collective-permute-done((bf16[1,512,1024]{2,1,0:T(8,128)(2,1)}, bf16[1,512,1024]{2,1,0:T(8,128)(2,1)}, u32[]{:S(2)}, u32[]{:S(2)}) %collective-permute-start.96) | collective-permute-done | bytes 1048608 | tf_op jit(solution)/shard_map/ppermute | solution.py:236
  (702 shorter events, 887.1 us)
Async XLA Ops:
  7.2 125.1 %all-gather.2.cloned.1.call-start = ((), (), s32[]{:S(2)}) async-start(), calls=%async_computation.4 | async-start | bytes 5242880 | tf_op jit(solution)/shard_map/all_gather | solution.py:1243
  18.4 66.7 %collective-permute-start.19 = (s32[1,512]{1,0:T(1,128)S(1)}, s32[1,512]{1,0:T(1,128)S(1)}, u32[]{:S(2)}, u32[]{:S(2)}) collective-permute-start(s32[1,512]{1,0:T(1,128)S(1)} %bitcast.460), channel_id=1, source_target_pairs={{0,2},{2,0},{4,6},{6,4},{1,3},{3,1},{5,7},{7,5},{8,10},{10,8},{12,... | collective-permute-start | bytes 6152 | tf_op jit(solution)/shard_map/ppermute | solution.py:61
  30.9 57.5 %collective-permute-start.20 = (s32[1,512]{1,0:T(1,128)S(1)}, s32[1,512]{1,0:T(1,128)S(1)}, u32[]{:S(2)}, u32[]{:S(2)}) collective-permute-start(s32[1,512]{1,0:T(1,128)S(1)} %bitcast.461), channel_id=1, source_target_pairs={{0,4},{2,6},{4,0},{6,2},{1,5},{3,7},{5,1},{7,3},{8,12},{10,14},{12... | collective-permute-start | bytes 6152 | tf_op jit(solution)/shard_map/ppermute | solution.py:61
  234.2 53.7 %collective-permute-start.39 = (bf16[2048,1024]{1,0:T(8,128)(2,1)}, bf16[2048,1024]{1,0:T(8,128)(2,1)}, u32[]{:S(2)}, u32[]{:S(2)}) collective-permute-start(bf16[2048,1024]{1,0:T(8,128)(2,1)} %collective-permute-done.24), channel_id=1, source_target_pairs={{0,16},{1,9},{8,24},{9,1},{16,0},{17,25},{24,8},{25,17},{2,18},{3,... | collective-permute-start | bytes 12582920 | tf_op jit(solution)/shard_map/ppermute | solution.py:105
  288.0 66.5 %collective-permute-start.42 = (bf16[2,512,1024]{2,1,0:T(8,128)(2,1)}, bf16[2,512,1024]{2,1,0:T(8,128)(2,1)}, u32[]{:S(2)}, u32[]{:S(2)}) collective-permute-start(bf16[2,512,1024]{2,1,0:T(8,128)(2,1)} %pad_maximum_fusion.1), channel_id=1, source_target_pairs={{0,16},{1,9},{8,24},{9,1},{16,0},{17,25},{24,8},{25,17},{2,18},{3,... | collective-permute-start | bytes 6291464 | tf_op jit(solution)/shard_map/ppermute | solution.py:105
  294.9 64.1 %collective-permute-start.40 = (bf16[1,256,4096]{2,1,0:T(8,128)(2,1)}, bf16[1,256,4096]{2,1,0:T(8,128)(2,1)}, u32[]{:S(2)}, u32[]{:S(2)}) collective-permute-start(bf16[1,256,4096]{2,1,0:T(8,128)(2,1)} %get-tuple-element.260), channel_id=1, source_target_pairs={{0,2},{2,4},{4,6},{1,3},{3,5},{5,7},{8,10},{10,12},{12,14},{9,11},... | collective-permute-start | bytes 6291464 | tf_op jit(solution)/shard_map/ppermute | solution.py:235
  302.5 56.4 %collective-permute-start.41 = (bf16[1,256,4096]{2,1,0:T(8,128)(2,1)}, bf16[1,256,4096]{2,1,0:T(8,128)(2,1)}, u32[]{:S(2)}, u32[]{:S(2)}) collective-permute-start(bf16[1,256,4096]{2,1,0:T(8,128)(2,1)} %get-tuple-element.261), channel_id=1, source_target_pairs={{6,4},{4,2},{2,0},{7,5},{5,3},{3,1},{14,12},{12,10},{10,8},{15,13}... | collective-permute-start | bytes 6291464 | tf_op jit(solution)/shard_map/ppermute | solution.py:236
  308.3 73.4 %collective-permute-start.26 = (bf16[1,256,4096]{2,1,0:T(8,128)(2,1)}, bf16[1,256,4096]{2,1,0:T(8,128)(2,1)}, u32[]{:S(2)}, u32[]{:S(2)}) collective-permute-start(bf16[1,256,4096]{2,1,0:T(8,128)(2,1)} %get-tuple-element.225), channel_id=1, source_target_pairs={{0,2},{1,3},{8,10},{9,11},{16,18},{17,19},{24,26},{25,27}} | collective-permute-start | bytes 6291464 | tf_op jit(solution)/shard_map/ppermute | solution.py:235
  314.2 67.6 %collective-permute-start.27 = (bf16[1,256,4096]{2,1,0:T(8,128)(2,1)}, bf16[1,256,4096]{2,1,0:T(8,128)(2,1)}, u32[]{:S(2)}, u32[]{:S(2)}) collective-permute-start(bf16[1,256,4096]{2,1,0:T(8,128)(2,1)} %get-tuple-element.226), channel_id=1, source_target_pairs={{6,4},{7,5},{14,12},{15,13},{22,20},{23,21},{30,28},{31,29}} | collective-permute-start | bytes 6291464 | tf_op jit(solution)/shard_map/ppermute | solution.py:236
  444.2 59.0 %collective-permute-start.49 = (bf16[2048,1024]{1,0:T(8,128)(2,1)}, bf16[2048,1024]{1,0:T(8,128)(2,1)}, u32[]{:S(2)}, u32[]{:S(2)}) collective-permute-start(bf16[2048,1024]{1,0:T(8,128)(2,1)} %bitcast.75.own_ref), channel_id=1, source_target_pairs={{0,1},{1,0},{2,3},{3,2},{4,5},{5,4},{6,7},{7,6},{8,9},{9,8},{10,11... | collective-permute-start | bytes 12582920 | tf_op jit(solution)/shard_map/ppermute | solution.py:61
  456.3 94.0 %all-to-all-start = ((bf16[4,256,1024]{2,1,0:T(8,128)(2,1)}), bf16[4,256,1024]{2,1,0:T(8,128)(2,1)}, u32[]{:S(2)}, u32[]{:S(2)}) async-start(bf16[4,256,1024]{2,1,0:T(8,128)(2,1)} %project_heads.2), calls=%async_computation | async-start | bytes 4194304 | tf_op jit(solution)/shard_map/all_to_all | solution.py:1267
  481.6 60.1 %collective-permute-start.44 = (bf16[1,256,4096]{2,1,0:T(8,128)(2,1)}, bf16[1,256,4096]{2,1,0:T(8,128)(2,1)}, u32[]{:S(2)}, u32[]{:S(2)}) collective-permute-start(bf16[1,256,4096]{2,1,0:T(8,128)(2,1)} %get-tuple-element.276), channel_id=1, source_target_pairs={{0,2},{2,4},{4,6},{1,3},{3,5},{5,7},{8,10},{10,12},{12,14},{9,11},... | collective-permute-start | bytes 6291464 | tf_op jit(solution)/shard_map/ppermute | solution.py:235
  490.3 60.0 %collective-permute-start.45 = (bf16[1,256,4096]{2,1,0:T(8,128)(2,1)}, bf16[1,256,4096]{2,1,0:T(8,128)(2,1)}, u32[]{:S(2)}, u32[]{:S(2)}) collective-permute-start(bf16[1,256,4096]{2,1,0:T(8,128)(2,1)} %get-tuple-element.277), channel_id=1, source_target_pairs={{6,4},{4,2},{2,0},{7,5},{5,3},{3,1},{14,12},{12,10},{10,8},{15,13}... | collective-permute-start | bytes 6291464 | tf_op jit(solution)/shard_map/ppermute | solution.py:236
  562.5 59.6 %all-to-all-start.1 = ((bf16[4,256,1024]{2,1,0:T(8,128)(2,1)}), bf16[4,256,1024]{2,1,0:T(8,128)(2,1)S(1)}, u32[]{:S(2)}, u32[]{:S(2)}) async-start(bf16[4,256,1024]{2,1,0:T(8,128)(2,1)} %bitcast.323), calls=%async_computation.1 | async-start | bytes 4194304 | tf_op jit(solution)/shard_map/all_to_all | solution.py:1267
  625.0 78.1 %all-to-all-start.2 = ((bf16[4,256,1024]{2,1,0:T(8,128)(2,1)}), bf16[4,256,1024]{2,1,0:T(8,128)(2,1)}, u32[]{:S(2)}, u32[]{:S(2)}) async-start(bf16[4,256,1024]{2,1,0:T(8,128)(2,1)} %copy-done.19), calls=%async_computation.2 | async-start | bytes 4194304 | tf_op jit(solution)/shard_map/all_to_all | solution.py:1267
  636.4 58.2 %collective-permute-start.56 = (bf16[4,256,1024]{2,1,0:T(8,128)(2,1)}, bf16[4,256,1024]{2,1,0:T(8,128)(2,1)}, u32[]{:S(2)}, u32[]{:S(2)}) collective-permute-start(bf16[4,256,1024]{2,1,0:T(8,128)(2,1)} %back_project.5), channel_id=1, source_target_pairs={{0,1},{1,0},{2,3},{3,2},{4,5},{5,4},{6,7},{7,6},{8,9},{9,8},{10,11... | collective-permute-start | bytes 6291464 | tf_op jit(solution)/shard_map/ppermute | solution.py:61
  780.1 59.6 %collective-permute-start.64 = (bf16[1,256,4096]{2,1,0:T(8,128)(2,1)}, bf16[1,256,4096]{2,1,0:T(8,128)(2,1)}, u32[]{:S(2)}, u32[]{:S(2)}) collective-permute-start(bf16[1,256,4096]{2,1,0:T(8,128)(2,1)} %bitcast.95.refs_0_), channel_id=1, source_target_pairs={{0,2},{2,4},{4,6},{1,3},{3,5},{5,7},{8,10},{10,12},{12,14},{9,11},... | collective-permute-start | bytes 6291464 | tf_op jit(solution)/shard_map/ppermute | solution.py:191
  782.8 57.0 %collective-permute-start.65 = (bf16[1,256,4096]{2,1,0:T(8,128)(2,1)}, bf16[1,256,4096]{2,1,0:T(8,128)(2,1)}, u32[]{:S(2)}, u32[]{:S(2)}) collective-permute-start(bf16[1,256,4096]{2,1,0:T(8,128)(2,1)} %bitcast.95.refs_0_), channel_id=1, source_target_pairs={{2,0},{4,2},{6,4},{3,1},{5,3},{7,5},{10,8},{12,10},{14,12},{11,9},... | collective-permute-start | bytes 6291464 | tf_op jit(solution)/shard_map/ppermute | solution.py:192
  804.1 81.5 %collective-permute-start.76 = (bf16[4,4,128,1024]{3,2,1,0:T(8,128)(2,1)}, bf16[4,4,128,1024]{3,2,1,0:T(8,128)(2,1)}, u32[]{:S(2)}, u32[]{:S(2)}) collective-permute-start(bf16[4,4,128,1024]{3,2,1,0:T(8,128)(2,1)} %attention_grads.4), channel_id=1, source_target_pairs={{0,16},{1,9},{8,24},{9,1},{16,0},{17,25},{24,8},{25,17},{2,18},{3,... | collective-permute-start | bytes 12582920 | tf_op jit(solution)/shard_map/ppermute | solution.py:105
  975.8 57.6 %collective-permute-start.82 = (bf16[1,256,4096]{2,1,0:T(8,128)(2,1)}, bf16[1,256,4096]{2,1,0:T(8,128)(2,1)}, u32[]{:S(2)}, u32[]{:S(2)}) collective-permute-start(bf16[1,256,4096]{2,1,0:T(8,128)(2,1)} %bitcast.102.refs_0_), channel_id=1, source_target_pairs={{0,2},{2,4},{4,6},{1,3},{3,5},{5,7},{8,10},{10,12},{12,14},{9,11},... | collective-permute-start | bytes 6291464 | tf_op jit(solution)/shard_map/ppermute | solution.py:191
  1035.4 53.9 %collective-permute-start.86 = (bf16[1,256,4096]{2,1,0:T(8,128)(2,1)S(1)}, bf16[1,256,4096]{2,1,0:T(8,128)(2,1)}, u32[]{:S(2)}, u32[]{:S(2)}) collective-permute-start(bf16[1,256,4096]{2,1,0:T(8,128)(2,1)S(1)} %collective-permute-done.83.refs_1_), channel_id=1, source_target_pairs={{2,0},{4,2},{3,1},{5,3},{10,8},{12,10},{11,9},{13,11},{18,16},{20,... | collective-permute-start | bytes 6291464 | tf_op jit(solution)/shard_map/ppermute | solution.py:192
  1114.1 73.8 %collective-permute-start.93 = (bf16[8,128,1024]{2,1,0:T(8,128)(2,1)}, bf16[8,128,1024]{2,1,0:T(8,128)(2,1)S(1)}, u32[]{:S(2)}, u32[]{:S(2)}) collective-permute-start(bf16[8,128,1024]{2,1,0:T(8,128)(2,1)} %get-tuple-element.401), channel_id=1, source_target_pairs={{0,2},{2,4},{4,6},{1,3},{3,5},{5,7},{8,10},{10,12},{12,14},{9,11},... | collective-permute-start | bytes 6291464 | tf_op jit(solution)/shard_map/ppermute | solution.py:235
  1127.3 60.6 %collective-permute-start.94 = (bf16[8,128,1024]{2,1,0:T(8,128)(2,1)}, bf16[8,128,1024]{2,1,0:T(8,128)(2,1)}, u32[]{:S(2)}, u32[]{:S(2)}) collective-permute-start(bf16[8,128,1024]{2,1,0:T(8,128)(2,1)} %get-tuple-element.402), channel_id=1, source_target_pairs={{6,4},{4,2},{2,0},{7,5},{5,3},{3,1},{14,12},{12,10},{10,8},{15,13}... | collective-permute-start | bytes 6291464 | tf_op jit(solution)/shard_map/ppermute | solution.py:236
  1149.5 54.8 %collective-permute-start.96 = (bf16[1,512,1024]{2,1,0:T(8,128)(2,1)}, bf16[1,512,1024]{2,1,0:T(8,128)(2,1)}, u32[]{:S(2)}, u32[]{:S(2)}) collective-permute-start(bf16[1,512,1024]{2,1,0:T(8,128)(2,1)} %get-tuple-element.408), channel_id=1, source_target_pairs={{6,4},{4,2},{2,0},{7,5},{5,3},{3,1},{14,12},{12,10},{10,8},{15,13}... | collective-permute-start | bytes 3145736 | tf_op jit(solution)/shard_map/ppermute | solution.py:236
  (205 other events, 3165.5 us)
Sparse Core Ops, SparseCore 0:
  18.5 90.0 all-gather.1

commit v4 on v3

--- a/solution.py
+++ b/solution.py
@@ -14,7 +14,7 @@
 MB = 2
 MIX = 18
 STREAMS = 4
-COST = 1
+COST = 20
 
 PRECISE = lax.Precision.HIGHEST
 NORM_EPSILON = 1e-05
@@ -109,32 +109,12 @@
     return jnp.concatenate([pieces, core_hop(pieces, at)], axis=0)
 
 
-def group_gather(values):
-    pieces = values[None]
-    for at in range(bit_count(lax.axis_size("dp"))):
-        pieces = group_hop(pieces, at)
-    return group_rows_placed(pieces)
-
-
-def group_rows_placed(pieces):
-    buffer = None
-    for place in range(pieces.shape[0]):
-        buffer = place_block(
-            buffer, pieces[place][None], place_index(place), pieces.shape[0]
-        )
-    return buffer[0]
-
-
-def group_scatter(blocks):
-    count = blocks.shape[0]
-    pieces = [
-        lax.dynamic_index_in_dim(blocks, place_index(p), 0, keepdims=False) for p in range(count)
-    ]
-    for at in reversed(range(bit_count(count))):
-        half = 1 << at
-        arrived = core_hop(jnp.stack(pieces[half : 2 * half]).astype(bf16), at).astype(f32)
-        pieces = [pieces[p] + arrived[p] for p in range(half)]
-    return pieces[0]
+def place_of(core):
+    partner = jnp.arange(lax.axis_size("dp")) ^ lax.axis_index("dp")
+    places = []
+    for order in core_orders():
+        places.append(sum(((partner >> bit) & 1) << at for at, bit in enumerate(order)))
+    return jnp.where(core % 2 == 0, places[0], places[1])
 
 
 def reorder_masked(stacked, axis):
@@ -199,17 +179,9 @@
 
     def placed(self):
         size, here = line_size()
-        buffer = place_block(None, self.up[0], here, size)
-        for at in range(1, size):
-            buffer = place_block(
-                buffer,
-                self.up[at],
-                lax.rem(here - at + size, size),
-                size,
-                self.down[size - at],
-                here >= at,
-            )
-        return buffer
+        steps = jnp.arange(size)
+        index = lax.rem(here - steps + size, size)
+        return place_line(index, here >= steps, self.up, self.down[1:][::-1])
 
 
 class LineScatter:
@@ -218,11 +190,11 @@
         self.terms, self.at = terms, 0
         self.up = self.down = None
 
-    def step(self):
+    def step(self, *later):
         size, here = line_size()
         self.at += 1
         if self.at >= size:
-            return
+            return later
         goes_up, goes_down = hop_sums(
             self.terms,
             jnp.minimum(size - self.at + here, size - 1),
@@ -230,10 +202,12 @@
             self.up,
             self.down,
         )
+        (goes_up, goes_down), *later = fence((goes_up, goes_down), *later)
         up_pairs = [(i, i + 1) for i in range(min(self.at, size - 1))]
         down_pairs = [(size - 1 - i, size - 2 - i) for i in range(min(self.at, size - 1))]
         self.up = lax.ppermute(goes_up, "depth", up_pairs)
         self.down = lax.ppermute(goes_down, "depth", down_pairs)
+        return later
 
     def hold(self, *others):
         (self.up, self.down), *rest = fence((self.up, self.down), *others)
@@ -325,6 +299,115 @@
         ),
         name="place_block",
     )(where, *operands)
+
+
+def place_line_kernel(size, at_ref, *refs):
+    out_ref = refs[-1]
+    for step in range(size):
+        if step == 0 or len(refs) == size + 1:
+            out_ref[0, at_ref[step]] = refs[step][0]
+            continue
+
+        @pl.when(at_ref[size + step] == 1)
+        def _(step=step):
+            out_ref[0, at_ref[step]] = refs[step][0]
+
+        @pl.when(at_ref[size + step] == 0)
+        def _(step=step):
+            out_ref[0, at_ref[step]] = refs[size + step - 1][0]
+
+
+def place_line(index, first, blocks, instead):
+    size = len(blocks)
+    lead, tall, wide = blocks[0].shape
+    rows = tall
+    while rows * wide > 1 << 18 and rows % 32 == 0:
+        rows //= 2
+    spec = pl.BlockSpec((1, rows, wide), lambda l, i, m: (l, i, 0))
+    where = jnp.concatenate([index, first]).astype(jnp.int32)
+    operands = list(blocks) + list(instead)
+    return pl.pallas_call(
+        functools.partial(place_line_kernel, size),
+        grid_spec=pltpu.PrefetchScalarGridSpec(
+            num_scalar_prefetch=1,
+            grid=(lead, tall // rows),
+            in_specs=[spec] * len(operands),
+            out_specs=pl.BlockSpec((1, size, rows, wide), lambda l, i, m: (l, 0, i, 0)),
+        ),
+        out_shape=jax.ShapeDtypeStruct((lead, size, tall, wide), blocks[0].dtype),
+        compiler_params=pltpu.CompilerParams(vmem_limit_bytes=40 << 20),
+        cost_estimate=spent(
+            flops=0, bytes_accessed=6 * size * lead * tall * wide, transcendentals=0
+        ),
+        name="place_line",
+    )(where, *operands)
+
+
+def place_many(index, blocks):
+    ones = jnp.ones(len(blocks), jnp.int32)
+    return place_line(index, ones, blocks, [])
+
+
+def group_join_kernel(at_ref, own_ref, other_ref, out_ref):
+    width = own_ref.shape[2]
+    own_span, other_span = own_spans(at_ref, width)
+    out_ref[:, own_span] = own_ref[0]
+    out_ref[:, other_span] = other_ref[0]
+
+
+def group_join(own, other, model_at):
+    count, tall, width = own.shape
+    rows = chunk_of(tall, width)
+    per = tall // rows
+    where = jnp.concatenate([model_at[None], place_of(model_at), place_of(1 - model_at)])
+    return pl.pallas_call(
+        group_join_kernel,
+        grid_spec=pltpu.PrefetchScalarGridSpec(
+            num_scalar_prefetch=1,
+            grid=(count, per),
+            in_specs=[
+                pl.BlockSpec((1, rows, width), lambda n, i, m: (m[1 + n], i, 0)),
+                pl.BlockSpec((1, rows, width), lambda n, i, m: (m[1 + count + n], i, 0)),
+            ],
+            out_specs=pl.BlockSpec((rows, 2 * width), lambda n, i, m: (n * per + i, 0)),
+        ),
+        out_shape=jax.ShapeDtypeStruct((count * tall, 2 * width), own.dtype),
+        cost_estimate=spent(
+            flops=0, bytes_accessed=8 * count * tall * width, transcendentals=0
+        ),
+        name="group_join",
+    )(where.astype(jnp.int32), own, other)
+
+
+def group_split_kernel(at_ref, near_own, near_other, far_own, far_other, near_ref, far_ref):
+    near_ref[0, 0] = near_own[0] + near_other[0].astype(f32)
+    far_ref[0, 0] = (far_own[0] + far_other[0].astype(f32)).astype(bf16)
+
+
+def group_split(own, other, places):
+    _, tall, width = own.shape
+    count = places.shape[0]
+    half, rows = count // 2, tall // count
+    near = pl.BlockSpec((1, rows, width), lambda p, k, m: (k, m[p], 0))
+    far = pl.BlockSpec((1, rows, width), lambda p, k, m: (k, m[half + p], 0))
+    out = pl.BlockSpec((1, 1, rows, width), lambda p, k, m: (p, k, 0, 0))
+    return pl.pallas_call(
+        group_split_kernel,
+        grid_spec=pltpu.PrefetchScalarGridSpec(
+            num_scalar_prefetch=1,
+            grid=(half, 2),
+            in_specs=[near, near, far, far],
+            out_specs=[out, out],
+        ),
+        out_shape=[
+            jax.ShapeDtypeStruct((half, 2, rows, width), f32),
+            jax.ShapeDtypeStruct((half, 2, rows, width), bf16),
+        ],
+        cost_estimate=spent(
+            flops=2 * tall * width, bytes_accessed=20 * tall * width, transcendentals=0
+        ),
+        name="group_split",
+    )(places, own, other, own, other)
 
 
 def hop_kernel(at_ref, *refs):
@@ -456,7 +539,9 @@
 
     @pl.when(pl.program_id(0) == 1)
     def _():
-        store(dot_tn(c0_ref[0], h0_ref[...]) + dot_tn(c1_ref[0], h1_ref[...]))
+        tall, wide = h0_ref.shape[0], c0_ref.shape[3]
+        c0, c1 = c0_ref[:, 0].reshape(tall, wide), c1_ref[:, 0].reshape(tall, wide)
+        store(dot_tn(c0, h0_ref[...]) + dot_tn(c1, h1_ref[...]))
 
 
 def hidden_grads(x, cot, up_grads, hidden, dp_count, depth_count):
@@ -470,8 +555,8 @@
         grid=(2, dp_count),
         in_specs=[cols, cols]
         + [
-            pl.BlockSpec((1, tall, block), lambda k, n: (0, 0, n * k)),
-            pl.BlockSpec((1, tall, block), lambda k, n: (1, 0, n * k)),
+            pl.BlockSpec((dp_count, 1, cot.shape[2], block), lambda k, n: (0, 0, 0, n * k)),
+            pl.BlockSpec((dp_count, 1, cot.shape[2], block), lambda k, n: (0, 1, 0, n * k)),
         ]
         + [whole] * 4,
         out_specs=pl.BlockSpec(
@@ -913,7 +998,7 @@
 
 def ff_kernel(
     model_ref, x_ref, cot_ref, up_ref, down_ref,
-    hidden_ref, grad_ref, out_own_ref, out_other_ref, back_own_ref, back_other_ref,
+    hidden_ref, grad_ref, own_ref, other_ref,
 ):
     part = up_ref.shape[-1]
     half = up_ref.shape[1] // 2
@@ -925,20 +1010,20 @@
     up_pre = dot_nn(x_ref[...], up_ref[...].reshape(-1, part))
     hidden, slope = gelu_parts(up_pre)
     hidden = hidden.astype(bf16)
-    grad_up = (dot_nn(cot_ref[0], down_ref[...].reshape(-1, part)) * slope).astype(bf16)
+    grad_up = (dot_nn(cot_ref[0, 0], down_ref[...].reshape(-1, part)) * slope).astype(bf16)
     hidden_ref[...] = hidden
     grad_ref[...] = grad_up
-    back_other_ref[...] = dot_nt(grad_up, rows_of(up_ref, other)).astype(bf16)
-    back_own_ref[...] = dot_nt(grad_up, rows_of(up_ref, own))
-    out_other_ref[...] = dot_nt(hidden, rows_of(down_ref, other)).astype(bf16)
-    out_own_ref[...] = dot_nt(hidden, rows_of(down_ref, own))
+    other_ref[0] = dot_nt(grad_up, rows_of(up_ref, other)).astype(bf16)
+    own_ref[0] = dot_nt(grad_up, rows_of(up_ref, own))
+    other_ref[1] = dot_nt(hidden, rows_of(down_ref, other)).astype(bf16)
+    own_ref[1] = dot_nt(hidden, rows_of(down_ref, own))
 
 
 def feed_forward(x, cot, micro_at, weights, which):
     tall, model = x.shape
     part = weights.shape[-1]
     width = model // 2
-    rows = min(256, tall)
+    rows = cot.shape[2]
     row = lambda i, m: (i, 0)
 
     def resident(kind):
@@ -955,19 +1040,17 @@
             grid=(tall // rows,),
             in_specs=[
                 pl.BlockSpec((rows, model), row),
-                pl.BlockSpec((1, rows, model), lambda i, m: (micro_at, i, 0)),
+                pl.BlockSpec((1, 1, rows, model), lambda i, m: (i, micro_at, 0, 0)),
                 resident(0),
                 resident(1),
             ],
             out_specs=[pl.BlockSpec((rows, part), row)] * 2
-            + [pl.BlockSpec((rows, width), row)] * 4,
+            + [pl.BlockSpec((2, rows, width), lambda i, m: (0, i, 0))] * 2,
         ),
         out_shape=[jax.ShapeDtypeStruct((tall, part), bf16)] * 2
         + [
-            jax.ShapeDtypeStruct((tall, width), f32),
-            jax.ShapeDtypeStruct((tall, width), bf16),
-            jax.ShapeDtypeStruct((tall, width), f32),
-            jax.ShapeDtypeStruct((tall, width), bf16),
+            jax.ShapeDtypeStruct((2, tall, width), f32),
+            jax.ShapeDtypeStruct((2, tall, width), bf16),
         ],
         compiler_params=pltpu.CompilerParams(vmem_limit_bytes=48 << 20),
         cost_estimate=spent(
@@ -1041,7 +1124,7 @@
 def slope_kernel(
     model_ref, own_ref, got_ref, ff_ref, low_ref, stat_ref, gain_ref, scaled_ref, sum_ref, gain_out_ref
 ):
-    rows, width = ff_ref.shape
+    _, rows, width = ff_ref.shape
     own_span, _ = own_spans(model_ref, width)
     lane = lax.broadcasted_iota(jnp.int32, (rows, 128), 1)
     packed = jnp.zeros((rows, 128), f32)
@@ -1051,7 +1134,7 @@
         if s < 3:
             grad = own_ref[s + 1] + got_ref[s + 1].astype(f32)
         else:
-            grad = ff_ref[...]
+            grad = ff_ref[0]
         average, inverse = stat_ref[:, 2 * s : 2 * s + 1], stat_ref[:, 2 * s + 1 : 2 * s + 2]
         hat = (low_ref[:, lanes].astype(f32) - average) * inverse
         totals.append(jnp.sum(grad * hat, axis=0, keepdims=True))
@@ -1087,7 +1170,7 @@
             in_specs=[
                 cube,
                 cube,
-                pl.BlockSpec((rows, width), row),
+                pl.BlockSpec((1, rows, width), lambda i, m: (0, i, 0)),
                 pl.BlockSpec((rows, wide), row),
                 pl.BlockSpec((rows, 128), row),
                 pl.BlockSpec(gains.shape, lambda i, m: (0, 0)),
@@ -1227,11 +1310,17 @@
     def half_of(values, axis, which):
         return lax.dynamic_slice_in_dim(values, which * width, width, axis)
 
+    partners = jnp.stack([dp_at ^ m for m in range(dp_count)]).astype(jnp.int32)
+    ff_local = ff_split(up_weight, down_weight, partners)
+    ff_rows = [ff_local[0]] + [swap_mask(ff_local[m], "dp", m) for m in range(1, dp_count)]
+    ff_rows = place_many(partners, ff_rows).reshape(2 * dp_count, own_rows, ff_part)
+
     small_cols = jnp.concatenate(
         [generator_in, norm_gains.T, jnp.zeros((own_rows, 128 - GEN - 5), bf16)], axis=1
     )
     small_all = gather_small(small_cols, both).reshape(model, 128)
     gen_first = small_all[:, :GEN]
+    gen_first, ff_rows = fence(gen_first, ff_rows)
     gain_float = small_all[:, GEN : GEN + 5].astype(f32).T
     second_rows = generator_out.shape[0]
     second_pad = -second_rows % 128
@@ -1270,33 +1359,16 @@
         partial = mix_streams(slot_mix, history, micro_at, depth_count, rows_mb)
         return partial.reshape(1, depth_count, rows_mb, STREAMS * width)
 
-    partners = jnp.stack([dp_at ^ m for m in range(dp_count)]).astype(jnp.int32)
-    ff_local = ff_split(up_weight, down_weight, partners)
-    ff_local, cotangent, slot_mix = fence(ff_local, cotangent, slot_mix)
-    cot_pieces = group_hop(cotangent[None], 0)
-    ff_rows = place_block(None, ff_local[0], partners[0], dp_count)
-    for m in range(1, dp_count):
-        arrived = swap_mask(ff_local[m], "dp", m)
-        ff_rows = place_block(ff_rows, arrived, partners[m], dp_count)
-    ff_rows = ff_rows.reshape(2 * dp_count, own_rows, ff_part)
-
+    slot_mix, ff_rows, cotangent, places_all = fence(slot_mix, ff_rows, cotangent, places_all)
     partial = mix_part(0, slot_mix)
-    over_depth, partial, slot_mix, ff_rows, cot_pieces, places_all = fence(
-        over_depth, partial, slot_mix, ff_rows, cot_pieces, places_all
-    )
+    partial_next = mix_part(1, slot_mix)
 
     weights_line = LineGather(ff_rows)
     weights_line.step()
-    flat_rows = depth_count * 4 * own_rows
-    pieces = [over_depth.reshape(flat_rows, heads_width)]
-    pieces.append(core_hop(pieces[0], 0))
+    over_depth, partial, partial_next = weights_line.hold(over_depth, partial, partial_next)
+    pieces = [over_depth]
     weights = place_block(None, pieces[0][None], place_index(0), dp_count)
-    partial_next = mix_part(1, slot_mix)
-    cot_other = other_core(cotangent)
-    pieces, partial, partial_next, weights, cot_pieces, cot_other = weights_line.hold(
-        pieces, partial, partial_next, weights, cot_pieces, cot_other
-    )
-    hops_left = [(p, at) for at in range(1, len(dp_bits)) for p in range(1 << at)]
+    hops_left = [(p, at) for at in range(len(dp_bits)) for p in range(1 << at)]
     placed = 1
     cots = None
     sums, sums_next = LineScatter(partial), LineScatter(partial_next)
@@ -1310,23 +1382,15 @@
         while hops_left:
             place, at = hops_left.pop(0)
             pieces.append(core_hop(pieces[place], at))
-            if len(hops_left) <= depth_count - 2 - hop:
+            if len(hops_left) <= depth_count - 1 - hop:
                 break
         if last_hop:
-            cot_full = join_halves(cotangent, cot_other, model_at)
-            for at in range(1, len(dp_bits)):
-                cot_pieces = group_hop(cot_pieces, at)
+            cot_full = join_halves(cotangent, other_core(cotangent), model_at)
             ff_weights = weights_line.placed()
-            sums_next.step()
-            cots = cot_full, ff_weights
-        (state,) = weights_line.hold(
-            (sums.up, sums.down, pieces, weights, cot_pieces, cot_other, cots)
-        )
-        sums.up, sums.down, pieces, weights, cot_pieces, cot_other, cots = state
-    while sums_next.at < depth_count - 3:
-        sums_next.hold()
-        sums_next.step()
-    cot_full, ff_weights = cots
+            cots = cot_full, cotangent, ff_weights
+        (state,) = weights_line.hold((sums.up, sums.down, pieces, weights, cots))
+        sums.up, sums.down, pieces, weights, cots = state
+    cot_full, cotangent, ff_weights = cots
     for place in range(placed, len(pieces)):
         weights = place_block(weights, pieces[place][None], place_index(place), dp_count)
     weights = weights.reshape(dp_count, depth_count, 4, own_rows, heads_width)
@@ -1361,77 +1425,77 @@
         answer = attend(by_head, documents, turning_tables(seq_places), heads_each)
         return answer.reshape(depth_count, rows_mb, 4 * heads_each * HDIM)
 
+    place_list = jnp.stack([place_index(p) for p in range(dp_count)]).astype(jnp.int32)
+
     def group_rows(ff_normed):
-        mine = group_gather(ff_normed).reshape(dp_count * rows_mb, width)
+        return lax.all_gather(ff_normed, "dp", axis=0, tiled=True)
+
+    def group_joined(mine):
         return join_halves(mine, other_core(mine), model_at)
 
     def hidden_units(micro_at, group_normed):
-        hidden, grad_up, out_own, out_other, back_own, back_other = feed_forward(
+        hidden, grad_up, own, other = feed_forward(
             group_normed, cot_group, micro_at, ff_weights, which
         )
-        return (
-            dict(group_normed=group_normed, hidden=hidden, grad_up=grad_up),
-            ((back_own, other_core(back_other)), (out_own, other_core(out_other))),
-        )
-
-    def reduce_group(own, other):
-        total = own + other.astype(f32)
-        return group_scatter(total.reshape(dp_count, rows_mb, width))
-
-    def back(kept, answer, ff_parts):
+        return dict(group_normed=group_normed, hidden=hidden, grad_up=grad_up), (own, other)
+
+    def group_back_rest(near):
+        for at in reversed(range(len(dp_bits) - 1)):
+            half = 1 << at
+            near = near[:half] + core_hop(near[half:].astype(bf16), at).astype(f32)
+        return near[0]
+
+    def group_back(own, other):
+        near, far = group_split(own, other, place_list)
+        return group_back_rest(near + core_hop(far, len(dp_bits) - 1).astype(f32))
+
+    def back(kept, answer):
         (theirs,) = back_project(answer, weights, 1 - which, bf16, False)
         got = other_core(theirs)
-        own, kept["flat"] = back_project(answer, weights, which, f32, True)
-        grad_norm_ff = reduce_group(*ff_parts[0])
-        ff_out = reduce_group(*ff_parts[1])
-        rows = (kept["resid"] + own[0] + got[0].astype(f32) + ff_out).astype(bf16)
-        return own, got, grad_norm_ff, rows
-
-    def leave(micro_at, kept, own, got, grad_norm_ff, rows):
+        own, flat = back_project(answer, weights, which, f32, True)
+        return own, got, flat
+
+    def leave(micro_at, kept, own, got, ff_sum):
         span = slice(micro_at * rows_mb, (micro_at + 1) * rows_mb)
+        rows = (kept["resid"] + own[0] + got[0].astype(f32) + ff_sum[1]).astype(bf16)
         low, stats = kept["low"], kept["stats"]
-        scaled, sums, gain_part = norm_slopes(own, got, grad_norm_ff, low, stats, gains, which)
+        scaled, sums, gain_part = norm_slopes(own, got, ff_sum, low, stats, gains, which)
         grad_low, current_mix, last_dot = stream_grads(
             scaled, sums, other_core(sums), low, stats, cotangent[span], current_half[span], last[span]
         )
         kept.update(layer_rows=rows, gain=gain_part, current_mix=current_mix, last_dot=last_dot)
         return grad_low
 
-    sums_next.step()
+    ((sums.up, sums.down),) = sums_next.step((sums.up, sums.down))
     first = enter(0, sums)
-    packed, ff_normed, cot_pieces = sums_next.hold(
-        first["packed"], first["ff_normed"], cot_pieces
-    )
-    sums_next.step()
-    cot_mine = group_rows_placed(cot_pieces).reshape(dp_count, MB, rows_mb, width)
-    cot_mine = jnp.swapaxes(cot_mine, 0, 1).reshape(MB * dp_count * rows_mb, width)
+    cot_mine = lax.all_gather(cotangent, "dp", axis=0, tiled=True)
+    packed, ff_normed, cot_mine = sums_next.hold(first["packed"], first["ff_normed"], cot_mine)
+    while sums_next.at < depth_count - 3:
+        sums_next.step()
+        sums_next.hold()
+    packed, ff_normed = sums_next.step(packed, ff_normed)
+    by_head = over_depth_swap(packed)
     cot_group = join_halves(cot_mine, other_core(cot_mine), model_at)
-    cot_group = cot_group.reshape(MB, dp_count * rows_mb, model)
-    by_head = over_depth_swap(packed)
-    group_normed = group_rows(ff_normed)
-    by_head, group_normed, cot_group = sums_next.hold(by_head, group_normed, cot_group)
+    cot_group = cot_group.reshape(dp_count, MB, rows_mb, model)
+    by_head, mine, cot_group = sums_next.hold(by_head, group_rows(ff_normed), cot_group)
+    by_head, mine = sums_next.step(by_head, mine)
+    kept, ff_parts = hidden_units(0, group_joined(mine))
+    first.update(kept)
     answer = attention(0, by_head)
-    answer, group_normed = sums_next.hold(answer, group_normed)
+    answer, ff_parts = sums_next.hold(answer, ff_parts)
 
     answer = over_depth_swap(answer)
     second = enter(1, sums_next)
-    kept, ff_parts = hidden_units(0, group_normed)
-    first.update(kept)
-    answer, packed, ff_normed, ff_parts = fence(
-        answer, second["packed"], second["ff_normed"], ff_parts
+    ff_sum = group_back(ff_parts[0], other_core(ff_parts[1]))
+    answer, packed, ff_normed, ff_sum = fence(
+        answer, second["packed"], second["ff_normed"], ff_sum
     )
     by_head = over_depth_swap(packed)
-    group_normed = group_rows(ff_normed)
-    ways = back(first, answer, ff_parts)
-    by_head, group_normed, ways = fence(by_head, group_normed, ways)
-    answer = attention(1, by_head)
-    answer, group_normed, ways = fence(answer, group_normed, ways)
-
-    answer = over_depth_swap(answer)
-    grad_low = leave(0, first, *ways)
-    kept, ff_parts = hidden_units(1, group_normed)
-    second.update(kept)
-    answer, grad_low, ff_parts = fence(answer, grad_low, ff_parts)
+    own, got, first["flat"] = back(first, answer)
+    grad_low = leave(0, first, own, got, ff_sum)
+    by_head, grad_low, group_normed = fence(
+        by_head, grad_low, group_joined(group_rows(ff_normed))
+    )
     saved = [first, second]
 
     def each(name):
@@ -1439,9 +1503,6 @@
 
     def rows_of(name):
         return jnp.concatenate(each(name), axis=0)
-
-    grad_line = LineGather(grad_low[None])
-    place_list = jnp.stack([place_index(p) for p in range(dp_count)]).astype(jnp.int32)
 
     def place_grads(place, dtype):
         return attention_grads(
@@ -1466,29 +1527,46 @@
         target = place - (1 << at)
         pieces[target] = pieces[target].astype(f32) + arrived.astype(f32)
 
+    grad_line = LineGather(grad_low[None])
     grad_line.step()
-    ways = back(second, answer, ff_parts)
+    answer = attention(1, by_head)
+    kept, ff_parts = hidden_units(1, group_normed)
+    second.update(kept)
+    answer, ff_parts = grad_line.hold(answer, ff_parts)
+    answer = over_depth_swap(answer)
+    near, far = group_split(ff_parts[0], other_core(ff_parts[1]), place_list)
     ff_products = hidden_grads(
         each("group_normed"), cot_group, each("grad_up"), each("hidden"), dp_count, depth_count
     )
-    ways, ff_products = grad_line.hold(ways, ff_products)
-    pieces = {p: place_grads(p, bf16) for p in range(half, dp_count)}
+    near = near + core_hop(far, len(dp_bits) - 1).astype(f32)
+    answer, near, ff_products = fence(answer, near, ff_products)
+
     ff_sums = LineScatter(ff_products)
-    for hop in range(2, depth_count):
+    grad_line.step()
+    (answer,) = ff_sums.step(answer)
+    own, got, flat = back(second, answer)
+    ff_sum = group_back_rest(near)
+    second["flat"] = flat
+    far_grads = [place_grads(p, bf16) for p in range(half, dp_count)]
+    arrived = core_hop(far_grads[0], hops_left.pop(0)[1])
+    (state,) = grad_line.hold(
+        (ff_sums.up, ff_sums.down, own, got, flat, ff_sum, far_grads, arrived)
+    )
+    ff_sums.up, ff_sums.down, own, got, second["flat"], ff_sum, far_grads, arrived = state
+    while len(grad_line.up) < depth_count - 1:
         grad_line.step()
         ff_sums.step()
-        if hop == 2:
-            arrived = core_hop(pieces.pop(half), hops_left.pop(0)[1])
-            grad_low = leave(1, second, *ways)
-            (state,) = grad_line.hold((grad_low, ff_sums.up, ff_sums.down, arrived, pieces))
-            grad_low, ff_sums.up, ff_sums.down, arrived, pieces = state
-        else:
-            if hop == 3:
-                pieces.update({p: place_grads(p, f32) for p in range(half)})
-                pieces[0] = pieces[0] + arrived.astype(f32)
-            sums_hop()
-            (state,) = grad_line.hold((grad_low, ff_sums.up, ff_sums.down, pieces))
-            grad_low, ff_sums.up, ff_sums.down, pieces = state
+        (state,) = grad_line.hold((ff_sums.up, ff_sums.down))
+        ff_sums.up, ff_sums.down = state
+    grad_line.step()
+    (ff_sum,) = ff_sums.step(ff_sum)
+    grad_low = leave(1, second, own, got, ff_sum)
+    pieces = {p: place_grads(p, f32) for p in range(half)}
+    pieces[0] = pieces[0] + arrived.astype(f32)
+    pieces.update({half + at: far_grads[at] for at in range(1, half)})
+    sums_hop()
+    (state,) = grad_line.hold((ff_sums.up, ff_sums.down, grad_low, pieces))
+    ff_sums.up, ff_sums.down, grad_low, pieces = state
 
     last_line = LineGather(grad_low[None])
     last_line.step()
@@ -1504,10 +1582,10 @@
     for hop in range(2, depth_count):
         last_line.step()
         out_sums.step()
-        (state,) = last_line.hold((out_sums.up, out_sums.down))
-        out_sums.up, out_sums.down = state
+        (state,) = last_line.hold((out_sums.up, out_sums.down, ff_sums.up, ff_sums.down))
+        out_sums.up, out_sums.down, ff_sums.up, ff_sums.down = state
+    out_sums.step()
     ff_sums.step()
-    out_sums.step()
     last_grads = last_line.placed().reshape(length, -1)
     history_grad, slot_part = unmix_streams(
         slot_mix, history, last_grads, 1, depth_count, rows_mb, history_grad
@@ -1516,10 +1594,9 @@
 
     slot_grads = jnp.concatenate(slot_parts, axis=1).reshape(-1, 128)[:, : STREAMS * slots]
     mix_grads = dot_exact(slot_grads, pick.T).reshape(depth_count, MB * rows_mb, STREAMS * MIX)
-    (state,) = ff_sums.hold((mix_grads, out_sums.up, out_sums.down))
-    mix_grads, out_sums.up, out_sums.down = state
+    (state,) = out_sums.hold((mix_grads, ff_sums.up, ff_sums.down))
+    mix_grads, ff_sums.up, ff_sums.down = state
     grad_mixing = scatter_small(mix_grads, ("depth",))
-    scattered = end_sums(out_sums, f32).reshape(4, own_rows, heads_width)
     ff_grads = end_sums(ff_sums, bf16).reshape(2, dp_count, own_rows, ff_part)
     ff_pieces = [
         lax.dynamic_index_in_dim(ff_grads, partners[m], 1, keepdims=False) for m in range(dp_count)
@@ -1536,6 +1613,7 @@
     grad_first = dot_exact(gen_normed.astype(f32).T, grad_pre)
     grad_gen_normed = dot_exact(grad_pre, gen_first.astype(f32).T)
     gain_gen = jnp.sum(grad_gen_normed * unit, axis=0)
+    scattered = end_sums(out_sums, f32).reshape(4, own_rows, heads_width)
     grad_unit = grad_gen_normed * gain_float[4]
     shared = jnp.mean(grad_unit * unit, axis=-1, keepdims=True)
     current_gen = half_of(inverse_rms * (grad_unit - unit * shared), 1, model_at)

time: 1310 us -> 1320 us (level)
  waiting for transfers between devices: 337 us -> 451 us
  Pallas kernels: 506 us -> 453 us
  other arithmetic: 106 us -> 68.3 us
    pallas_call x32 -> x4, Pallas kernels: 120 us -> 22 us  [place_block(): pl.pallas_call(place_kernel, grid_spec=pltpu.PrefetchScalarGridSpec(num_s...]
    ppermute x12, waiting for transfers between devices: 121 us -> 168 us  [step(): self.up = lax.ppermute(goes_up, 'depth', up_pairs)]
    pallas_call x0 -> x6, Pallas kernels: none -> 44.2 us  [the longest x4 28.4 us: place_line(): pl.pallas_call(functools.partial(place_line_kernel, size), grid_spec=pltp...]
    ppermute x9, waiting for transfers between devices: 87.7 us -> 121 us  [step(): self.down.append(lax.ppermute(self.down[-1], 'depth', down_pairs))]
    all_gather x0 -> x3, waiting for transfers between devices: none -> 23.1 us  [the longest x2 23.1 us: group_rows(): return lax.all_gather(ff_normed, 'dp', axis=0, tiled=True)]
    ppermute x55 -> x53, waiting for transfers between devices: 56.2 us -> 74.8 us  [swap_mask(): return lax.ppermute(values, axis, [(i, i ^ mask) for i in range(size)])]
    ppermute x20 -> x10, starting transfers between devices: 23.7 us -> 9.3 us  [core_hop(): return lax.ppermute(values, ('dp', 'mp'), pairs)]
    ppermute x20 -> x10, waiting for transfers between devices: 30.1 us -> 33.1 us  [core_hop(): return lax.ppermute(values, ('dp', 'mp'), pairs)]
  transfers between devices with their start and end apart: 122 -> 113, of which waited for: 47 -> 52; matrix products, arithmetic and copies ran while one was open for 11% -> 8% of each run, Pallas kernels for 36% -> 33%
where the time goes in v4:
time: 1320 us; the launch traced here: 1310 us
  Pallas kernels  453 us (34%)
  waiting for transfers between devices  451 us (34%)
  starting transfers between devices  232 us (18%)
  local copies, waits for them, and re-layouts  76.3 us (6%)
  other arithmetic  68.3 us (5%)
  between operations  15.8 us (1%)
    ppermute x12, waiting for transfers between devices, step(): self.up = lax.ppermute(goes_up, 'depth', up_pairs)  168 us
    ppermute x9, waiting for transfers between devices, step(): self.down.append(lax.ppermute(self.down[-1], 'depth', down_pairs))  121 us
    ppermute x12, starting transfers between devices, step(): self.up = lax.ppermute(goes_up, 'depth', up_pairs)  89.1 us
    ppermute x53, waiting for transfers between devices, swap_mask(): return lax.ppermute(values, axis, [(i, i ^ mask) for i in range(size)])  74.8 us
    pallas_call x12, Pallas kernels, hop_sums(): pl.pallas_call(hop_kernel, grid_spec=pltpu.PrefetchScalarGridSpec(num_sca...  73.3 us
    pallas_call x2, Pallas kernels, feed_forward(): pl.pallas_call(ff_kernel, grid_spec=pltpu.PrefetchScalarGridSpec(num_scal...  48.1 us
    unnamed x186, local copies, waits for them, and re-layouts  45.3 us
    ppermute x53, starting transfers between devices, swap_mask(): return lax.ppermute(values, axis, [(i, i ^ mask) for i in range(size)])  44.1 us
  transfers between devices with their start and end apart: 113, of which 52 were waited for; matrix products, arithmetic and copies ran while one was open for 8% of the time, Pallas kernels for 33%

profile of v4, /device:TPU:0, one launch (start us, length us, event | category | flops | bytes accessed | tf_op | source)
XLA Modules:
  0.0 1307.4 jit_solution(13184263068649329577)
XLA Ops:
  107.6 14.3 %mix_streams.2 = bf16[1024,4096]{1,0:T(8,128)(2,1)} custom-call(f32[2048,20]{1,0:T(8,128)} %copy.94.mix_ref, bf16[5,2048,1024]{2,1,0:T(8,128)(2,1)} %hist_ref.7), custom_call_target="tpu_custom_call" | custom-call | flops 2097152 | bytes 943718 | tf_op jit(solution)/shard_map/mix_streams/pallas_call | solution.py:605
  121.9 14.3 %mix_streams.3 = bf16[1024,4096]{1,0:T(8,128)(2,1)} custom-call(f32[2048,20]{1,0:T(8,128)} %copy.94.mix_ref, bf16[5,2048,1024]{2,1,0:T(8,128)(2,1)} %hist_ref.7), custom_call_target="tpu_custom_call" | custom-call | flops 2097152 | bytes 943718 | tf_op jit(solution)/shard_map/mix_streams/pallas_call | solution.py:605
  136.2 11.5 collective-permute-done.21.refs_1_
  177.6 28.3 %collective-permute-done.24.refs_5_ = bf16[8,128,1024]{2,1,0:T(8,128)(2,1)} collective-permute-done((bf16[8,128,1024]{2,1,0:T(8,128)(2,1)}, bf16[8,128,1024]{2,1,0:T(8,128)(2,1)}, u32[]{:S(2)}, u32[]{:S(2)}) %collective-permute-start.24) | collective-permute-done | bytes 2097184 | tf_op jit(solution)/shard_map/ppermute | solution.py:172
  236.8 26.4 %collective-permute-done.29.refs_4_ = bf16[8,128,1024]{2,1,0:T(8,128)(2,1)} collective-permute-done((bf16[8,128,1024]{2,1,0:T(8,128)(2,1)}, bf16[8,128,1024]{2,1,0:T(8,128)(2,1)}, u32[]{:S(2)}, u32[]{:S(2)}) %collective-permute-start.29) | collective-permute-done | bytes 2097184 | tf_op jit(solution)/shard_map/ppermute | solution.py:172
  277.4 12.4 collective-permute-start.33
  312.5 18.8 %collective-permute-done.33.up_ref = bf16[1,256,4096]{2,1,0:T(8,128)(2,1)} collective-permute-done((bf16[1,256,4096]{2,1,0:T(8,128)(2,1)}, bf16[1,256,4096]{2,1,0:T(8,128)(2,1)}, u32[]{:S(2)}, u32[]{:S(2)}) %collective-permute-start.33) | collective-permute-done | bytes 2097184 | tf_op jit(solution)/shard_map/ppermute | solution.py:208
  383.0 14.6 %collective-permute-done.37.refs_2_ = bf16[1,256,4096]{2,1,0:T(8,128)(2,1)} collective-permute-done((bf16[1,256,4096]{2,1,0:T(8,128)(2,1)}, bf16[1,256,4096]{2,1,0:T(8,128)(2,1)}, u32[]{:S(2)}, u32[]{:S(2)}) %collective-permute-start.37) | collective-permute-done | bytes 2097184 | tf_op jit(solution)/shard_map/ppermute | solution.py:208
  424.8 62.7 %collective-permute-done.40.refs_2_ = bf16[1,256,4096]{2,1,0:T(8,128)(2,1)} collective-permute-done((bf16[1,256,4096]{2,1,0:T(8,128)(2,1)}, bf16[1,256,4096]{2,1,0:T(8,128)(2,1)}, u32[]{:S(2)}, u32[]{:S(2)}) %collective-permute-start.40) | collective-permute-done | bytes 2097184 | tf_op jit(solution)/shard_map/ppermute | solution.py:208
  493.4 18.2 %collective-permute-start.43 = (bf16[1,256,4096]{2,1,0:T(8,128)(2,1)}, bf16[1,256,4096]{2,1,0:T(8,128)(2,1)}, u32[]{:S(2)}, u32[]{:S(2)}) collective-permute-start(bf16[1,256,4096]{2,1,0:T(8,128)(2,1)} %get-tuple-element.285), channel_id=1, source_target_pairs={{0,2},{2,4},{4,6},{1,3},{3,5},{5,7},{8,10},{10,12},{12,14},{9,11},... | collective-permute-start | bytes 6291464 | tf_op jit(solution)/shard_map/ppermute | solution.py:208
  537.2 24.0 %feed_forward.2 = (bf16[1024,1024]{1,0:T(8,128)(2,1)S(1)}, bf16[1024,1024]{1,0:T(8,128)(2,1)S(1)}, f32[2,1024,1024]{2,1,0:T(8,128)}, bf16[2,1024,1024]{2,1,0:T(8,128)(2,1)}) custom-call(s32[1]{0:T(128)} %bitcast.61.model_ref.half_ref, bf16[1024,2048]{1,0:T(8,128)(2,1)} %join_halves.6.x_ref.x0_ref, bf16[4,2,256,2048]{3,2,1,0:T(8,128)(2,1)} %bitcast.359, ...), custom_call_target="tpu_custom_call" | custom-call | flops 858993472 | bytes 2097152 | tf_op jit(solution)/shard_map/feed_forward/pallas_call | solution.py:1036
  590.2 15.5 %collective-permute-done.48 = bf16[2,2,256,1024]{3,2,1,0:T(8,128)(2,1)} collective-permute-done((bf16[2,2,256,1024]{3,2,1,0:T(8,128)(2,1)}, bf16[2,2,256,1024]{3,2,1,0:T(8,128)(2,1)}, u32[]{:S(2)}, u32[]{:S(2)}) %collective-permute-start.48) | collective-permute-done | bytes 2097184 | tf_op jit(solution)/shard_map/ppermute | solution.py:105
  645.9 23.1 %all-gather.11.cloned.1.call-done.own_ref = bf16[1024,1024]{1,0:T(8,128)(2,1)} async-done(((bf16[256,1024]{1,0:T(8,128)(2,1)}), bf16[1024,1024]{1,0:T(8,128)(2,1)}) %all-gather.11.cloned.1.call-update) | async-done | bytes 2097168 | tf_op jit(solution)/shard_map/all_gather | solution.py:1431
  720.4 24.1 %feed_forward.3 = (bf16[1024,1024]{1,0:T(8,128)(2,1)S(1)}, bf16[1024,1024]{1,0:T(8,128)(2,1)S(1)}, f32[2,1024,1024]{2,1,0:T(8,128)}, bf16[2,1024,1024]{2,1,0:T(8,128)(2,1)}) custom-call(s32[1]{0:T(128)} %bitcast.61.model_ref.half_ref, bf16[1024,2048]{1,0:T(8,128)(2,1)} %join_halves.7.x_ref.x1_ref, bf16[4,2,256,2048]{3,2,1,0:T(8,128)(2,1)} %bitcast.360, ...), custom_call_target="tpu_custom_call" | custom-call | flops 858993472 | bytes 2097152 | tf_op jit(solution)/shard_map/feed_forward/pallas_call | solution.py:1036
  773.4 24.3 %hidden_grads.1.refs_0_.refs_1_.term_ref = f32[8,4,128,1024]{3,2,1,0:T(8,128)} custom-call(bf16[1024,2048]{1,0:T(8,128)(2,1)} %join_halves.6.x_ref.x0_ref, bf16[1024,2048]{1,0:T(8,128)(2,1)} %join_halves.7.x_ref.x1_ref, bf16[4,2,256,2048]{3,2,1,0:T(8,128)(2,1)} %bitcast.361, bf16[4,2,256,2048]{3,2,1,0:T(8,128)(2,1)} %bitcast.362, ...), custom_call_target="tpu_custom_call" | custom-call | flops 858993472 | bytes 838860 | tf_op jit(solution)/shard_map/hidden_grads/pallas_call | solution.py:553
  861.6 17.3 %collective-permute-done.56.refs_5_ = bf16[1,256,4096]{2,1,0:T(8,128)(2,1)} collective-permute-done((bf16[1,256,4096]{2,1,0:T(8,128)(2,1)}, bf16[1,256,4096]{2,1,0:T(8,128)(2,1)}, u32[]{:S(2)}, u32[]{:S(2)}) %collective-permute-start.56) | collective-permute-done | bytes 2097184 | tf_op jit(solution)/shard_map/ppermute | solution.py:172
  960.6 20.5 %collective-permute-start.70 = (bf16[1,256,4096]{2,1,0:T(8,128)(2,1)S(1)}, bf16[1,256,4096]{2,1,0:T(8,128)(2,1)}, u32[]{:S(2)}, u32[]{:S(2)}) collective-permute-start(bf16[1,256,4096]{2,1,0:T(8,128)(2,1)S(1)} %bitcast.303), channel_id=1, source_target_pairs={{0,2},{2,4},{4,6},{1,3},{3,5},{5,7},{8,10},{10,12},{12,14},{9,11},... | collective-permute-start | bytes 6291464 | tf_op jit(solution)/shard_map/ppermute | solution.py:171
  990.9 19.5 %unmix_streams.2 = (bf16[5,2048,1024]{2,1,0:T(8,128)(2,1)}, f32[1024,128]{1,0:T(8,128)}) custom-call(f32[2048,20]{1,0:T(8,128)} %copy.94.mix_ref, bf16[5,2048,1024]{2,1,0:T(8,128)(2,1)} %hist_ref.7, bf16[1024,4096]{1,0:T(8,128)(2,1)} %bitcast.368), custom_call_target="tpu_custom_call" | custom-call | flops 4194304 | bytes 1468006 | tf_op jit(solution)/shard_map/unmix_streams/pallas_call | solution.py:680
  1048.7 19.5 %collective-permute-done.75.refs_2_ = bf16[1,512,1024]{2,1,0:T(8,128)(2,1)S(1)} collective-permute-done((bf16[1,512,1024]{2,1,0:T(8,128)(2,1)}, bf16[1,512,1024]{2,1,0:T(8,128)(2,1)S(1)}, u32[]{:S(2)}, u32[]{:S(2)}) %collective-permute-start.75) | collective-permute-done | bytes 1048608 | tf_op jit(solution)/shard_map/ppermute | solution.py:208
  1068.2 17.0 %collective-permute-done.74.refs_5_ = bf16[1,256,4096]{2,1,0:T(8,128)(2,1)} collective-permute-done((bf16[1,256,4096]{2,1,0:T(8,128)(2,1)}, bf16[1,256,4096]{2,1,0:T(8,128)(2,1)}, u32[]{:S(2)}, u32[]{:S(2)}) %collective-permute-start.74) | collective-permute-done | bytes 2097184 | tf_op jit(solution)/shard_map/ppermute | solution.py:172
  1101.1 18.6 %collective-permute-done.79.refs_2_ = bf16[1,512,1024]{2,1,0:T(8,128)(2,1)S(1)} collective-permute-done((bf16[1,512,1024]{2,1,0:T(8,128)(2,1)}, bf16[1,512,1024]{2,1,0:T(8,128)(2,1)S(1)}, u32[]{:S(2)}, u32[]{:S(2)}) %collective-permute-start.79) | collective-permute-done | bytes 1048608 | tf_op jit(solution)/shard_map/ppermute | solution.py:208
  1119.7 15.0 %collective-permute-done.78.refs_4_ = bf16[1,256,4096]{2,1,0:T(8,128)(2,1)} collective-permute-done((bf16[1,256,4096]{2,1,0:T(8,128)(2,1)}, bf16[1,256,4096]{2,1,0:T(8,128)(2,1)}, u32[]{:S(2)}, u32[]{:S(2)}) %collective-permute-start.78) | collective-permute-done | bytes 2097184 | tf_op jit(solution)/shard_map/ppermute | solution.py:172
  1170.9 19.6 %unmix_streams.3 = (bf16[5,2048,1024]{2,1,0:T(8,128)(2,1)}, f32[1024,128]{1,0:T(8,128)}) custom-call(f32[2048,20]{1,0:T(8,128)} %copy.94.mix_ref, bf16[5,2048,1024]{2,1,0:T(8,128)(2,1)} %hist_ref.7, bf16[1024,4096]{1,0:T(8,128)(2,1)} %bitcast.367, bf16[5,2048,1024]{2,1,0:T(8,128)(2,1)} %get-tuple-element.395.rest_0_), custom_call_target="tpu_custom_call", output_to_operand_aliasing={{0}: (3, {})} | custom-call | flops 4194304 | bytes 1468006 | tf_op jit(solution)/shard_map/unmix_streams/pallas_call | solution.py:680
  1192.8 17.1 %collective-permute-done.81.up_ref = bf16[1,512,1024]{2,1,0:T(8,128)(2,1)} collective-permute-done((bf16[1,512,1024]{2,1,0:T(8,128)(2,1)}, bf16[1,512,1024]{2,1,0:T(8,128)(2,1)}, u32[]{:S(2)}, u32[]{:S(2)}) %collective-permute-start.81) | collective-permute-done | bytes 1048608 | tf_op jit(solution)/shard_map/ppermute | solution.py:208
  (609 shorter events, 795.0 us)
Async XLA Ops:
  7.2 146.6 %all-gather.5.cloned.1.call-start = ((), (), s32[]{:S(2)}) async-start(), calls=%async_computation.4 | async-start | bytes 5242880 | tf_op jit(solution)/shard_map/all_gather | solution.py:1332
  20.1 377.5 %all-gather.7.cloned.1.call-start = ((), (), s32[]{:S(2)}) async-start(), calls=%async_computation.5 | async-start | bytes 5242880 | tf_op jit(solution)/shard_map/all_gather | solution.py:1471
  153.8 57.7 %collective-permute-start.27 = (bf16[2048,1024]{1,0:T(8,128)(2,1)}, bf16[2048,1024]{1,0:T(8,128)(2,1)}, u32[]{:S(2)}, u32[]{:S(2)}) collective-permute-start(bf16[2048,1024]{1,0:T(8,128)(2,1)} %all-gather.5.cloned.1.call-done), channel_id=1, source_target_pairs={{0,8},{1,17},{8,0},{9,25},{16,24},{17,1},{24,16},{25,9},{2,10},{3,... | collective-permute-start | bytes 12582920 | tf_op jit(solution)/shard_map/ppermute | solution.py:105
  211.5 60.0 %collective-permute-start.32 = (bf16[2048,1024]{1,0:T(8,128)(2,1)}, bf16[2048,1024]{1,0:T(8,128)(2,1)}, u32[]{:S(2)}, u32[]{:S(2)}) collective-permute-start(bf16[2048,1024]{1,0:T(8,128)(2,1)} %all-gather.5.cloned.1.call-done), channel_id=1, source_target_pairs={{0,16},{1,9},{8,24},{9,1},{16,0},{17,25},{24,8},{25,17},{2,18},{3,... | collective-permute-start | bytes 12582920 | tf_op jit(solution)/shard_map/ppermute | solution.py:105
  271.5 65.3 %collective-permute-start.35 = (bf16[2048,1024]{1,0:T(8,128)(2,1)}, bf16[2048,1024]{1,0:T(8,128)(2,1)}, u32[]{:S(2)}, u32[]{:S(2)}) collective-permute-start(bf16[2048,1024]{1,0:T(8,128)(2,1)} %collective-permute-done.27), channel_id=1, source_target_pairs={{0,16},{1,9},{8,24},{9,1},{16,0},{17,25},{24,8},{25,17},{2,18},{3,... | collective-permute-start | bytes 12582920 | tf_op jit(solution)/shard_map/ppermute | solution.py:105
  277.4 53.9 %collective-permute-start.33 = (bf16[1,256,4096]{2,1,0:T(8,128)(2,1)}, bf16[1,256,4096]{2,1,0:T(8,128)(2,1)}, u32[]{:S(2)}, u32[]{:S(2)}) collective-permute-start(bf16[1,256,4096]{2,1,0:T(8,128)(2,1)} %get-tuple-element.248), channel_id=1, source_target_pairs={{0,2},{2,4},{4,6},{1,3},{3,5},{5,7},{8,10},{10,12},{12,14},{9,11},... | collective-permute-start | bytes 6291464 | tf_op jit(solution)/shard_map/ppermute | solution.py:208
  403.4 84.1 %all-to-all-start = ((bf16[4,256,1024]{2,1,0:T(8,128)(2,1)}), bf16[4,256,1024]{2,1,0:T(8,128)(2,1)S(1)}, u32[]{:S(2)}, u32[]{:S(2)}) async-start(bf16[4,256,1024]{2,1,0:T(8,128)(2,1)} %project_heads.2), calls=%async_computation | async-start | bytes 4194304 | tf_op jit(solution)/shard_map/all_to_all | solution.py:1356
  407.9 79.7 %all-gather.9.cloned.1.call-start = ((), (), s32[]{:S(2)}) async-start(), calls=%async_computation.6 | async-start | bytes 2621440 | tf_op jit(solution)/shard_map/all_gather | solution.py:1431
  408.6 78.9 %collective-permute-start.40 = (bf16[1,256,4096]{2,1,0:T(8,128)(2,1)}, bf16[1,256,4096]{2,1,0:T(8,128)(2,1)}, u32[]{:S(2)}, u32[]{:S(2)}) collective-permute-start(bf16[1,256,4096]{2,1,0:T(8,128)(2,1)} %get-tuple-element.274), channel_id=1, source_target_pairs={{0,2},{2,4},{1,3},{3,5},{8,10},{10,12},{9,11},{11,13},{16,18},{18,... | collective-permute-start | bytes 6291464 | tf_op jit(solution)/shard_map/ppermute | solution.py:208
  413.9 73.7 %collective-permute-start.41 = (bf16[1,256,4096]{2,1,0:T(8,128)(2,1)}, bf16[1,256,4096]{2,1,0:T(8,128)(2,1)}, u32[]{:S(2)}, u32[]{:S(2)}) collective-permute-start(bf16[1,256,4096]{2,1,0:T(8,128)(2,1)} %get-tuple-element.275), channel_id=1, source_target_pairs={{6,4},{4,2},{7,5},{5,3},{14,12},{12,10},{15,13},{13,11},{22,20},{2... | collective-permute-start | bytes 6291464 | tf_op jit(solution)/shard_map/ppermute | solution.py:209
  493.4 70.5 %collective-permute-start.43 = (bf16[1,256,4096]{2,1,0:T(8,128)(2,1)}, bf16[1,256,4096]{2,1,0:T(8,128)(2,1)}, u32[]{:S(2)}, u32[]{:S(2)}) collective-permute-start(bf16[1,256,4096]{2,1,0:T(8,128)(2,1)} %get-tuple-element.285), channel_id=1, source_target_pairs={{0,2},{2,4},{4,6},{1,3},{3,5},{5,7},{8,10},{10,12},{12,14},{9,11},... | collective-permute-start | bytes 6291464 | tf_op jit(solution)/shard_map/ppermute | solution.py:208
  579.3 55.9 %all-to-all-start.1 = ((bf16[4,256,1024]{2,1,0:T(8,128)(2,1)}), bf16[4,256,1024]{2,1,0:T(8,128)(2,1)S(1)}, u32[]{:S(2)}, u32[]{:S(2)}) async-start(bf16[4,256,1024]{2,1,0:T(8,128)(2,1)} %bitcast.298), calls=%async_computation.1 | async-start | bytes 4194304 | tf_op jit(solution)/shard_map/all_to_all | solution.py:1356
  583.2 85.8 %all-gather.11.cloned.1.call-start = ((), (), s32[]{:S(2)}) async-start(), calls=%async_computation.7 | async-start | bytes 2621440 | tf_op jit(solution)/shard_map/all_gather | solution.py:1431
  635.2 63.8 %all-to-all-start.2 = ((bf16[4,256,1024]{2,1,0:T(8,128)(2,1)}), bf16[4,256,1024]{2,1,0:T(8,128)(2,1)}, u32[]{:S(2)}, u32[]{:S(2)}) async-start(bf16[4,256,1024]{2,1,0:T(8,128)(2,1)} %copy-done.16), calls=%async_computation.2 | async-start | bytes 4194304 | tf_op jit(solution)/shard_map/all_to_all | solution.py:1356
  753.3 52.7 %all-to-all-start.3 = ((bf16[4,256,1024]{2,1,0:T(8,128)(2,1)}), bf16[4,256,1024]{2,1,0:T(8,128)(2,1)S(1)}, u32[]{:S(2)}, u32[]{:S(2)}) async-start(bf16[4,256,1024]{2,1,0:T(8,128)(2,1)} %bitcast.299), calls=%async_computation.3 | async-start | bytes 4194304 | tf_op jit(solution)/shard_map/all_to_all | solution.py:1356
  827.8 60.0 %collective-permute-start.63 = (bf16[4,4,128,1024]{3,2,1,0:T(8,128)(2,1)}, bf16[4,4,128,1024]{3,2,1,0:T(8,128)(2,1)}, u32[]{:S(2)}, u32[]{:S(2)}) collective-permute-start(bf16[4,4,128,1024]{3,2,1,0:T(8,128)(2,1)} %attention_grads.4), channel_id=1, source_target_pairs={{0,16},{1,9},{8,24},{9,1},{16,0},{17,25},{24,8},{25,17},{2,18},{3,... | collective-permute-start | bytes 12582920 | tf_op jit(solution)/shard_map/ppermute | solution.py:105
  887.8 60.9 %collective-permute-start.69 = (bf16[4,4,128,1024]{3,2,1,0:T(8,128)(2,1)}, bf16[4,4,128,1024]{3,2,1,0:T(8,128)(2,1)}, u32[]{:S(2)}, u32[]{:S(2)}) collective-permute-start(bf16[4,4,128,1024]{3,2,1,0:T(8,128)(2,1)} %attention_grads.5), channel_id=1, source_target_pairs={{0,16},{1,9},{8,24},{9,1},{16,0},{17,25},{24,8},{25,17},{2,18},{3,... | collective-permute-start | bytes 12582920 | tf_op jit(solution)/shard_map/ppermute | solution.py:105
  904.3 52.8 %collective-permute-start.64 = (bf16[1,256,4096]{2,1,0:T(8,128)(2,1)}, bf16[1,256,4096]{2,1,0:T(8,128)(2,1)}, u32[]{:S(2)}, u32[]{:S(2)}) collective-permute-start(bf16[1,256,4096]{2,1,0:T(8,128)(2,1)} %collective-permute-done.55.refs_2_), channel_id=1, source_target_pairs={{4,6},{5,7},{12,14},{13,15},{20,22},{21,23},{28,30},{29,31}} | collective-permute-start | bytes 6291464 | tf_op jit(solution)/shard_map/ppermute | solution.py:171
  960.6 62.9 %collective-permute-start.70 = (bf16[1,256,4096]{2,1,0:T(8,128)(2,1)S(1)}, bf16[1,256,4096]{2,1,0:T(8,128)(2,1)}, u32[]{:S(2)}, u32[]{:S(2)}) collective-permute-start(bf16[1,256,4096]{2,1,0:T(8,128)(2,1)S(1)} %bitcast.303), channel_id=1, source_target_pairs={{0,2},{2,4},{4,6},{1,3},{3,5},{5,7},{8,10},{10,12},{12,14},{9,11},... | collective-permute-start | bytes 6291464 | tf_op jit(solution)/shard_map/ppermute | solution.py:171
  1031.2 54.1 %collective-permute-start.74 = (bf16[1,256,4096]{2,1,0:T(8,128)(2,1)}, bf16[1,256,4096]{2,1,0:T(8,128)(2,1)}, u32[]{:S(2)}, u32[]{:S(2)}) collective-permute-start(bf16[1,256,4096]{2,1,0:T(8,128)(2,1)} %collective-permute-done.71.refs_6_), channel_id=1, source_target_pairs={{2,0},{4,2},{3,1},{5,3},{10,8},{12,10},{11,9},{13,11},{18,16},{20,... | collective-permute-start | bytes 6291464 | tf_op jit(solution)/shard_map/ppermute | solution.py:172
  1143.7 71.7 %collective-permute-start.83 = (bf16[8,128,1024]{2,1,0:T(8,128)(2,1)}, bf16[8,128,1024]{2,1,0:T(8,128)(2,1)}, u32[]{:S(2)}, u32[]{:S(2)}) collective-permute-start(bf16[8,128,1024]{2,1,0:T(8,128)(2,1)} %get-tuple-element.407), channel_id=1, source_target_pairs={{0,2},{2,4},{4,6},{1,3},{3,5},{5,7},{8,10},{10,12},{12,14},{9,11},... | collective-permute-start | bytes 6291464 | tf_op jit(solution)/shard_map/ppermute | solution.py:208
  1146.5 68.9 %collective-permute-start.84 = (bf16[8,128,1024]{2,1,0:T(8,128)(2,1)}, bf16[8,128,1024]{2,1,0:T(8,128)(2,1)}, u32[]{:S(2)}, u32[]{:S(2)}) collective-permute-start(bf16[8,128,1024]{2,1,0:T(8,128)(2,1)} %get-tuple-element.408), channel_id=1, source_target_pairs={{6,4},{4,2},{2,0},{7,5},{5,3},{3,1},{14,12},{12,10},{10,8},{15,13}... | collective-permute-start | bytes 6291464 | tf_op jit(solution)/shard_map/ppermute | solution.py:209
  1152.8 57.2 %collective-permute-start.81 = (bf16[1,512,1024]{2,1,0:T(8,128)(2,1)}, bf16[1,512,1024]{2,1,0:T(8,128)(2,1)}, u32[]{:S(2)}, u32[]{:S(2)}) collective-permute-start(bf16[1,512,1024]{2,1,0:T(8,128)(2,1)} %get-tuple-element.401), channel_id=1, source_target_pairs={{0,2},{2,4},{4,6},{1,3},{3,5},{5,7},{8,10},{10,12},{12,14},{9,11},... | collective-permute-start | bytes 3145736 | tf_op jit(solution)/shard_map/ppermute | solution.py:208
  1158.4 57.0 %collective-permute-start.82 = (bf16[1,512,1024]{2,1,0:T(8,128)(2,1)}, bf16[1,512,1024]{2,1,0:T(8,128)(2,1)}, u32[]{:S(2)}, u32[]{:S(2)}) collective-permute-start(bf16[1,512,1024]{2,1,0:T(8,128)(2,1)} %get-tuple-element.402), channel_id=1, source_target_pairs={{6,4},{4,2},{2,0},{7,5},{5,3},{3,1},{14,12},{12,10},{10,8},{15,13}... | collective-permute-start | bytes 3145736 | tf_op jit(solution)/shard_map/ppermute | solution.py:209
  (180 other events, 2902.6 us)
Sparse Core Ops, SparseCore 0:
  20.3 89.7 all-gather.4
  336.9 50.1 all-gather.6
  411.2 35.9 all-gather.8
  635.3 33.7 all-gather.10

commit v5 on v4

--- a/solution.py
+++ b/solution.py
@@ -209,6 +209,35 @@
         self.down = lax.ppermute(goes_down, "depth", down_pairs)
         return later
 
+    def step_with(self, line, *later):
+        size, here = line_size()
+        lead, _, tall, wide = self.terms.shape
+        shape = line.up[0].shape
+        if (
+            len(line.up) != self.at + 2
+            or self.at + 2 > size - 1
+            or math.prod(shape) != lead * tall * wide
+            or shape[2] != wide
+        ):
+            line.step()
+            return self.step(*later)
+        self.at += 1
+        goes = hop_sums(
+            self.terms,
+            jnp.minimum(size - self.at + here, size - 1),
+            jnp.maximum(here - size + self.at, 0),
+            self.up,
+            self.down,
+            [v[-1].reshape(lead, tall, wide) for v in (line.up, line.down)],
+            [here < self.at, here > size - 1 - self.at],
+        )
+        goes, *later = fence(goes, *later)
+        self.up = lax.ppermute(goes[0], "depth", [(i, i + 1) for i in range(size - 1)])
+        self.down = lax.ppermute(goes[1], "depth", [(i, i - 1) for i in range(1, size)])
+        line.up.append(self.up.reshape(shape))
+        line.down.append(self.down.reshape(shape))
+        return later
+
     def hold(self, *others):
         (self.up, self.down), *rest = fence((self.up, self.down), *others)
         return rest
@@ -410,16 +439,29 @@
     )(places, own, other, own, other)
 
 
-def hop_kernel(at_ref, *refs):
-    ins, outs = refs[:-2], refs[-2:]
+def hop_kernel(has_sums, has_blocks, at_ref, *refs):
+    ins, outs = list(refs[:-2]), refs[-2:]
+    terms, ins = ins[:2], ins[2:]
+    sums, ins = (ins[:2], ins[2:]) if has_sums else (None, ins)
+
+    def send_sum(way):
+        term = terms[way][0, 0].astype(f32)
+        if sums is not None:
+            term = term + sums[way][0].astype(f32)
+        outs[way][0] = term.astype(bf16)
+
     for way in range(2):
-        term = ins[way][0, 0].astype(f32)
-        if len(ins) > 2:
-            term = term + ins[2 + way][0].astype(f32)
-        outs[way][0] = term.astype(bf16)
-
-
-def hop_sums(terms, up_at, down_at, up, down):
+        if not has_blocks:
+            send_sum(way)
+            continue
+        pl.when(at_ref[2 + way] == 1)(functools.partial(send_sum, way))
+
+        @pl.when(at_ref[2 + way] == 0)
+        def _(way=way):
+            outs[way][0] = ins[way][0]
+
+
+def hop_sums(terms, up_at, down_at, up, down, blocks=None, first=None):
     lead, _, tall, wide = terms.shape
     rows = chunk_of(tall, wide)
     block = pl.BlockSpec((1, rows, wide), lambda l, i, m: (l, i, 0))
@@ -428,11 +470,16 @@
         pl.BlockSpec((1, 1, rows, wide), lambda l, i, m: (l, m[1], i, 0)),
     ]
     operands = [terms, terms]
+    where = [up_at, down_at]
     if up is not None:
         in_specs += [block, block]
         operands += [up, down]
-    return pl.pallas_call(
-        hop_kernel,
+    if blocks is not None:
+        in_specs += [block, block]
+        operands += list(blocks)
+        where += list(first)
+    return pl.pallas_call(
+        functools.partial(hop_kernel, up is not None, blocks is not None),
         grid_spec=pltpu.PrefetchScalarGridSpec(
             num_scalar_prefetch=1,
             grid=(lead, tall // rows),
@@ -444,7 +491,7 @@
             flops=2 * lead * tall * wide, bytes_accessed=12 * lead * tall * wide, transcendentals=0
         ),
         name="hop_sums",
-    )(jnp.stack([up_at, down_at]).astype(jnp.int32), *operands)
+    )(jnp.stack(where).astype(jnp.int32), *operands)
 
 
 def end_kernel(at_ref, term_ref, up_ref, down_ref, out_ref):
@@ -588,7 +635,7 @@
                     term = weights[:, s * slots + k : s * slots + k + 1] * state
                     sums[s] = term if sums[s] is None else sums[s] + term
             for s in range(STREAMS):
-                out_ref[pl.ds(r0, 16), s * width + c0 : s * width + c0 + part] = sums[s].astype(bf16)
+                out_ref[s, pl.ds(r0, 16), c0 : c0 + part] = sums[s].astype(bf16)
         return carry
 
     lax.fori_loop(0, rows // 16, step, 0)
@@ -609,8 +656,8 @@
             pl.BlockSpec((rows, slot_mix.shape[1]), lambda i: (row_block(i), 0)),
             pl.BlockSpec((slots, rows, width), lambda i: (0, row_block(i), 0)),
         ],
-        out_specs=pl.BlockSpec((rows, STREAMS * width), lambda i: (i, 0)),
-        out_shape=jax.ShapeDtypeStruct((depth_count * rows_mb, STREAMS * width), bf16),
+        out_specs=pl.BlockSpec((STREAMS, rows, width), lambda i: (0, i, 0)),
+        out_shape=jax.ShapeDtypeStruct((STREAMS, depth_count * rows_mb, width), bf16),
         cost_estimate=spent(
             flops=2 * slots * STREAMS * depth_count * rows_mb * width,
             bytes_accessed=2 * (slots + STREAMS) * depth_count * rows_mb * width,
@@ -631,7 +678,7 @@
         totals = [None] * (STREAMS * slots)
         for c0 in range(0, width, part):
             grads = [
-                grad_ref[pl.ds(r0, 16), s * width + c0 : s * width + c0 + part].astype(f32)
+                grad_ref[s, pl.ds(r0, 16), c0 : c0 + part].astype(f32)
                 for s in range(STREAMS)
             ]
             for k in range(slots):
@@ -669,7 +716,7 @@
     in_specs = [
         pl.BlockSpec((rows, slot_mix.shape[1]), lambda i: (row_block(i), 0)),
         pl.BlockSpec((slots, rows, width), lambda i: (0, row_block(i), 0)),
-        pl.BlockSpec((rows, STREAMS * width), lambda i: (i, 0)),
+        pl.BlockSpec((STREAMS, rows, width), lambda i: (0, i, 0)),
     ]
     operands = [slot_mix, history, grads]
     aliases = {}
@@ -765,8 +812,8 @@
     current = cur_ref[...].astype(f32)
     for s in range(STREAMS):
         lanes = slice(s * width, (s + 1) * width)
-        total = part_ref[0, 0, :, lanes].astype(f32)
-        total = total + up_ref[0, :, lanes].astype(f32) + down_ref[0, :, lanes].astype(f32)
+        total = part_ref[s, 0].astype(f32)
+        total = total + up_ref[s].astype(f32) + down_ref[s].astype(f32)
         total = total + last_ref[:, s : s + 1] * current
         if s == STREAMS - 1:
             resid_ref[...] = total
@@ -774,8 +821,8 @@
 
 
 def total_streams(sums, current_half, last, depth_at):
-    _, _, tall, wide = sums.terms.shape
-    width = wide // STREAMS
+    _, _, tall, width = sums.terms.shape
+    wide = STREAMS * width
     rows = min(64, tall)
     row = lambda i, d: (i, 0)
     return pl.pallas_call(
@@ -784,9 +831,9 @@
             num_scalar_prefetch=1,
             grid=(tall // rows,),
             in_specs=[
-                pl.BlockSpec((1, 1, rows, wide), lambda i, d: (0, d[0], i, 0)),
-                pl.BlockSpec((1, rows, wide), lambda i, d: (0, i, 0)),
-                pl.BlockSpec((1, rows, wide), lambda i, d: (0, i, 0)),
+                pl.BlockSpec((STREAMS, 1, rows, width), lambda i, d: (0, d[0], i, 0)),
+                pl.BlockSpec((STREAMS, rows, width), lambda i, d: (0, i, 0)),
+                pl.BlockSpec((STREAMS, rows, width), lambda i, d: (0, i, 0)),
                 pl.BlockSpec((rows, width), row),
                 pl.BlockSpec((rows, 128), row),
             ],
@@ -1215,7 +1262,7 @@
         if s == STREAMS - 1:
             grad = grad + cot_ref[...].astype(f32)
         grad = grad.astype(bf16)
-        grad_ref[:, lanes] = grad
+        grad_ref[s] = grad
         grad = grad.astype(f32)
         term = last_ref[:, s : s + 1] * grad
         mixed = term if mixed is None else mixed + term
@@ -1243,12 +1290,12 @@
             pl.BlockSpec((rows, 128), row),
         ],
         out_specs=[
-            pl.BlockSpec((rows, wide), row),
+            pl.BlockSpec((STREAMS, rows, width), lambda i: (0, i, 0)),
             pl.BlockSpec((rows, width), row),
             pl.BlockSpec((rows, 128), row),
         ],
         out_shape=[
-            jax.ShapeDtypeStruct((tall, wide), bf16),
+            jax.ShapeDtypeStruct((STREAMS, tall, width), bf16),
             jax.ShapeDtypeStruct((tall, width), f32),
             jax.ShapeDtypeStruct((tall, 128), f32),
         ],
@@ -1357,7 +1404,7 @@
 
     def mix_part(micro_at, slot_mix):
         partial = mix_streams(slot_mix, history, micro_at, depth_count, rows_mb)
-        return partial.reshape(1, depth_count, rows_mb, STREAMS * width)
+        return partial.reshape(STREAMS, depth_count, rows_mb, width)
 
     slot_mix, ff_rows, cotangent, places_all = fence(slot_mix, ff_rows, cotangent, places_all)
     partial = mix_part(0, slot_mix)
@@ -1373,8 +1420,7 @@
     cots = None
     sums, sums_next = LineScatter(partial), LineScatter(partial_next)
     for hop in range(1, depth_count):
-        sums.step()
-        weights_line.step()
+        sums.step_with(weights_line)
         last_hop = hop == depth_count - 1
         for place in range(placed, len(pieces)):
             weights = place_block(weights, pieces[place][None], place_index(place), dp_count)
@@ -1527,7 +1573,7 @@
         target = place - (1 << at)
         pieces[target] = pieces[target].astype(f32) + arrived.astype(f32)
 
-    grad_line = LineGather(grad_low[None])
+    grad_line = LineGather(grad_low)
     grad_line.step()
     answer = attention(1, by_head)
     kept, ff_parts = hidden_units(1, group_normed)
@@ -1542,8 +1588,7 @@
     answer, near, ff_products = fence(answer, near, ff_products)
 
     ff_sums = LineScatter(ff_products)
-    grad_line.step()
-    (answer,) = ff_sums.step(answer)
+    (answer,) = ff_sums.step_with(grad_line, answer)
     own, got, flat = back(second, answer)
     ff_sum = group_back_rest(near)
     second["flat"] = flat
@@ -1554,12 +1599,10 @@
     )
     ff_sums.up, ff_sums.down, own, got, second["flat"], ff_sum, far_grads, arrived = state
     while len(grad_line.up) < depth_count - 1:
-        grad_line.step()
-        ff_sums.step()
+        ff_sums.step_with(grad_line)
         (state,) = grad_line.hold((ff_sums.up, ff_sums.down))
         ff_sums.up, ff_sums.down = state
-    grad_line.step()
-    (ff_sum,) = ff_sums.step(ff_sum)
+    (ff_sum,) = ff_sums.step_with(grad_line, ff_sum)
     grad_low = leave(1, second, own, got, ff_sum)
     pieces = {p: place_grads(p, f32) for p in range(half)}
     pieces[0] = pieces[0] + arrived.astype(f32)
@@ -1568,16 +1611,20 @@
     (state,) = grad_line.hold((ff_sums.up, ff_sums.down, grad_low, pieces))
     ff_sums.up, ff_sums.down, grad_low, pieces = state
 
-    last_line = LineGather(grad_low[None])
+    last_line = LineGather(grad_low)
     last_line.step()
+    ff_sums.step()
     while hops_left:
         sums_hop()
-    grad_first = grad_line.placed().reshape(length, -1)
+    grad_first = grad_line.placed().reshape(STREAMS, length, width)
     history_grad, slot_part = unmix_streams(
         slot_mix, history, grad_first, 0, depth_count, rows_mb, None
     )
     slot_parts = [slot_part.reshape(depth_count, 1, rows_mb, 128)]
-    pieces, history_grad = last_line.hold(pieces, history_grad)
+    pieces, history_grad, state = last_line.hold(
+        pieces, history_grad, (ff_sums.up, ff_sums.down)
+    )
+    ff_sums.up, ff_sums.down = state
     out_sums = LineScatter(pieces[0].reshape(1, depth_count, 4 * own_rows, heads_width))
     for hop in range(2, depth_count):
         last_line.step()
@@ -1585,23 +1632,21 @@
         (state,) = last_line.hold((out_sums.up, out_sums.down, ff_sums.up, ff_sums.down))
         out_sums.up, out_sums.down, ff_sums.up, ff_sums.down = state
     out_sums.step()
-    ff_sums.step()
-    last_grads = last_line.placed().reshape(length, -1)
-    history_grad, slot_part = unmix_streams(
-        slot_mix, history, last_grads, 1, depth_count, rows_mb, history_grad
-    )
-    slot_parts.append(slot_part.reshape(depth_count, 1, rows_mb, 128))
-
-    slot_grads = jnp.concatenate(slot_parts, axis=1).reshape(-1, 128)[:, : STREAMS * slots]
-    mix_grads = dot_exact(slot_grads, pick.T).reshape(depth_count, MB * rows_mb, STREAMS * MIX)
-    (state,) = out_sums.hold((mix_grads, ff_sums.up, ff_sums.down))
-    mix_grads, ff_sums.up, ff_sums.down = state
-    grad_mixing = scatter_small(mix_grads, ("depth",))
     ff_grads = end_sums(ff_sums, bf16).reshape(2, dp_count, own_rows, ff_part)
     ff_pieces = [
         lax.dynamic_index_in_dim(ff_grads, partners[m], 1, keepdims=False) for m in range(dp_count)
     ]
     ff_pieces = [ff_pieces[0]] + [swap_mask(ff_pieces[m], "dp", m) for m in range(1, dp_count)]
+    last_grads = last_line.placed().reshape(STREAMS, length, width)
+    history_grad, slot_part = unmix_streams(
+        slot_mix, history, last_grads, 1, depth_count, rows_mb, history_grad
+    )
+    slot_parts.append(slot_part.reshape(depth_count, 1, rows_mb, 128))
+
+    slot_grads = jnp.concatenate(slot_parts, axis=1).reshape(-1, 128)[:, : STREAMS * slots]
+    mix_grads = dot_exact(slot_grads, pick.T).reshape(depth_count, MB * rows_mb, STREAMS * MIX)
+    mix_grads, ff_pieces = out_sums.hold(mix_grads, ff_pieces)
+    grad_mixing = scatter_small(mix_grads, ("depth",))
     up_grad, down_grad = ff_join(jnp.stack(ff_pieces), partners)
     last_dots = rows_of("last_dot")
     grad_mixing = grad_mixing + dot_exact(last_dots, pick_last.astype(f32).T)

time: 1320 us -> 1310 us (level)
  starting transfers between devices: 232 us -> 173 us
  waiting for transfers between devices: 451 us -> 484 us
    ppermute x0 -> x8, waiting for transfers between devices: none -> 103 us  [the longest x4 83.6 us: step_with(): lax.ppermute(goes[0], 'depth', [(i, i + 1) for i in range(size - 1)])]
    ppermute x9 -> x5, waiting for transfers between devices: 121 us -> 40.5 us  [step(): self.down.append(lax.ppermute(self.down[-1], 'depth', down_pairs))]
    ppermute x12 -> x8, starting transfers between devices: 89.1 us -> 49.9 us  [step(): self.up = lax.ppermute(goes_up, 'depth', up_pairs)]
    ppermute x9 -> x5, starting transfers between devices: 40.2 us -> 13.6 us  [step(): self.up.append(lax.ppermute(self.up[-1], 'depth', up_pairs))]
    ppermute x0 -> x8, starting transfers between devices: none -> 16.2 us  [the longest x4 11.1 us: step_with(): lax.ppermute(goes[0], 'depth', [(i, i + 1) for i in range(size - 1)])]
    ppermute x12 -> x8, waiting for transfers between devices: 168 us -> 163 us  [step(): self.up = lax.ppermute(goes_up, 'depth', up_pairs)]
    unnamed x186 -> x204, local copies, waits for them, and re-layouts: 45.3 us -> 49 us
  transfers between devices with their start and end apart: 113 -> 105, of which waited for: 52 -> 48; matrix products, arithmetic and copies ran while one was open for 8% -> 8% of each run, Pallas kernels for 33% -> 33%
where the time goes in v5:
time: 1310 us; the launch traced here: 1300 us
  waiting for transfers between devices  484 us (37%)
  Pallas kernels  461 us (35%)
  starting transfers between devices  173 us (13%)
  local copies, waits for them, and re-layouts  80.1 us (6%)
  other arithmetic  74 us (6%)
  between operations  15.9 us (1%)
    ppermute x8, waiting for transfers between devices, step(): self.up = lax.ppermute(goes_up, 'depth', up_pairs)  163 us
    ppermute x4, waiting for transfers between devices, step_with(): lax.ppermute(goes[0], 'depth', [(i, i + 1) for i in range(size - 1)])  83.6 us
    pallas_call x12, Pallas kernels, hop_sums(): pl.pallas_call(functools.partial(hop_kernel, up is not None, blocks is no...  82.6 us
    ppermute x53, waiting for transfers between devices, swap_mask(): return lax.ppermute(values, axis, [(i, i ^ mask) for i in range(size)])  80.1 us
    ppermute x8, starting transfers between devices, step(): self.up = lax.ppermute(goes_up, 'depth', up_pairs)  49.9 us
    unnamed x204, local copies, waits for them, and re-layouts  49 us
    pallas_call x2, Pallas kernels, feed_forward(): pl.pallas_call(ff_kernel, grid_spec=pltpu.PrefetchScalarGridSpec(num_scal...  48.1 us
    ppermute x53, starting transfers between devices, swap_mask(): return lax.ppermute(values, axis, [(i, i ^ mask) for i in range(size)])  43.1 us
  transfers between devices with their start and end apart: 105, of which 48 were waited for; matrix products, arithmetic and copies ran while one was open for 8% of the time, Pallas kernels for 33%

profile of v5, /device:TPU:0, one launch (start us, length us, event | category | flops | bytes accessed | tf_op | source)
XLA Modules:
  0.0 1299.0 jit_solution(3629283259617478898)
XLA Ops:
  102.2 14.4 %mix_streams.2 = bf16[4,1024,1024]{2,1,0:T(8,128)(2,1)} custom-call(f32[2048,20]{1,0:T(8,128)} %copy.94.mix_ref, bf16[5,2048,1024]{2,1,0:T(8,128)(2,1)} %hist_ref.7), custom_call_target="tpu_custom_call" | custom-call | flops 2097152 | bytes 943718 | tf_op jit(solution)/shard_map/mix_streams/pallas_call | solution.py:652
  116.6 14.4 %mix_streams.3 = bf16[4,1024,1024]{2,1,0:T(8,128)(2,1)} custom-call(f32[2048,20]{1,0:T(8,128)} %copy.94.mix_ref, bf16[5,2048,1024]{2,1,0:T(8,128)(2,1)} %hist_ref.7), custom_call_target="tpu_custom_call" | custom-call | flops 2097152 | bytes 943718 | tf_op jit(solution)/shard_map/mix_streams/pallas_call | solution.py:652
  130.9 16.9 %collective-permute-done.21.refs_1_ = bf16[8,128,1024]{2,1,0:T(8,128)(2,1)S(1)} collective-permute-done((bf16[8,128,1024]{2,1,0:T(8,128)(2,1)}, bf16[8,128,1024]{2,1,0:T(8,128)(2,1)S(1)}, u32[]{:S(2)}, u32[]{:S(2)}) %collective-permute-start.21) | collective-permute-done | bytes 2097184 | tf_op jit(solution)/shard_map/ppermute | solution.py:171
  171.5 37.3 %collective-permute-done.23.refs_2_ = bf16[4,256,1024]{2,1,0:T(8,128)(2,1)S(1)} collective-permute-done((bf16[4,256,1024]{2,1,0:T(8,128)(2,1)}, bf16[4,256,1024]{2,1,0:T(8,128)(2,1)S(1)}, u32[]{:S(2)}, u32[]{:S(2)}) %collective-permute-start.23) | collective-permute-done | bytes 2097184 | tf_op jit(solution)/shard_map/ppermute | solution.py:235
  232.9 36.7 %collective-permute-done.26.refs_2_ = bf16[4,256,1024]{2,1,0:T(8,128)(2,1)S(1)} collective-permute-done((bf16[4,256,1024]{2,1,0:T(8,128)(2,1)}, bf16[4,256,1024]{2,1,0:T(8,128)(2,1)S(1)}, u32[]{:S(2)}, u32[]{:S(2)}) %collective-permute-start.26) | collective-permute-done | bytes 2097184 | tf_op jit(solution)/shard_map/ppermute | solution.py:235
  313.3 13.5 %collective-permute-done.29.up_ref = bf16[4,256,1024]{2,1,0:T(8,128)(2,1)} collective-permute-done((bf16[4,256,1024]{2,1,0:T(8,128)(2,1)}, bf16[4,256,1024]{2,1,0:T(8,128)(2,1)}, u32[]{:S(2)}, u32[]{:S(2)}) %collective-permute-start.29) | collective-permute-done | bytes 2097184 | tf_op jit(solution)/shard_map/ppermute | solution.py:208
  379.8 14.7 %collective-permute-done.33.refs_2_ = bf16[4,256,1024]{2,1,0:T(8,128)(2,1)} collective-permute-done((bf16[4,256,1024]{2,1,0:T(8,128)(2,1)}, bf16[4,256,1024]{2,1,0:T(8,128)(2,1)}, u32[]{:S(2)}, u32[]{:S(2)}) %collective-permute-start.33) | collective-permute-done | bytes 2097184 | tf_op jit(solution)/shard_map/ppermute | solution.py:208
  423.2 62.7 %collective-permute-done.36.refs_2_ = bf16[4,256,1024]{2,1,0:T(8,128)(2,1)} collective-permute-done((bf16[4,256,1024]{2,1,0:T(8,128)(2,1)}, bf16[4,256,1024]{2,1,0:T(8,128)(2,1)}, u32[]{:S(2)}, u32[]{:S(2)}) %collective-permute-start.36) | collective-permute-done | bytes 2097184 | tf_op jit(solution)/shard_map/ppermute | solution.py:208
  492.5 18.1 %collective-permute-start.39 = (bf16[4,256,1024]{2,1,0:T(8,128)(2,1)}, bf16[4,256,1024]{2,1,0:T(8,128)(2,1)}, u32[]{:S(2)}, u32[]{:S(2)}) collective-permute-start(bf16[4,256,1024]{2,1,0:T(8,128)(2,1)} %get-tuple-element.289), channel_id=1, source_target_pairs={{0,2},{2,4},{4,6},{1,3},{3,5},{5,7},{8,10},{10,12},{12,14},{9,11},... | collective-permute-start | bytes 6291464 | tf_op jit(solution)/shard_map/ppermute | solution.py:208
  519.9 11.1 attend.2
  537.1 24.0 %feed_forward.2 = (bf16[1024,1024]{1,0:T(8,128)(2,1)S(1)}, bf16[1024,1024]{1,0:T(8,128)(2,1)S(1)}, f32[2,1024,1024]{2,1,0:T(8,128)}, bf16[2,1024,1024]{2,1,0:T(8,128)(2,1)}) custom-call(s32[1]{0:T(128)} %bitcast.73.model_ref.half_ref, bf16[1024,2048]{1,0:T(8,128)(2,1)} %join_halves.6.x_ref.x0_ref, bf16[4,2,256,2048]{3,2,1,0:T(8,128)(2,1)} %bitcast.376, ...), custom_call_target="tpu_custom_call" | custom-call | flops 858993472 | bytes 2097152 | tf_op jit(solution)/shard_map/feed_forward/pallas_call | solution.py:1083
  591.0 14.8 %collective-permute-done.44 = bf16[2,2,256,1024]{3,2,1,0:T(8,128)(2,1)} collective-permute-done((bf16[2,2,256,1024]{3,2,1,0:T(8,128)(2,1)}, bf16[2,2,256,1024]{3,2,1,0:T(8,128)(2,1)}, u32[]{:S(2)}, u32[]{:S(2)}) %collective-permute-start.44) | collective-permute-done | bytes 2097184 | tf_op jit(solution)/shard_map/ppermute | solution.py:105
  646.0 24.7 %all-gather.11.cloned.1.call-done.own_ref = bf16[1024,1024]{1,0:T(8,128)(2,1)} async-done(((bf16[256,1024]{1,0:T(8,128)(2,1)}), bf16[1024,1024]{1,0:T(8,128)(2,1)}) %all-gather.11.cloned.1.call-update) | async-done | bytes 2097168 | tf_op jit(solution)/shard_map/all_gather | solution.py:1477
  708.5 10.9 attend.3
  720.8 24.1 %feed_forward.3 = (bf16[1024,1024]{1,0:T(8,128)(2,1)S(1)}, bf16[1024,1024]{1,0:T(8,128)(2,1)S(1)}, f32[2,1024,1024]{2,1,0:T(8,128)}, bf16[2,1024,1024]{2,1,0:T(8,128)(2,1)}) custom-call(s32[1]{0:T(128)} %bitcast.73.model_ref.half_ref, bf16[1024,2048]{1,0:T(8,128)(2,1)} %join_halves.7.x_ref.x1_ref, bf16[4,2,256,2048]{3,2,1,0:T(8,128)(2,1)} %bitcast.377, ...), custom_call_target="tpu_custom_call" | custom-call | flops 858993472 | bytes 2097152 | tf_op jit(solution)/shard_map/feed_forward/pallas_call | solution.py:1083
  774.0 24.3 %hidden_grads.1.refs_0_.refs_1_.term_ref = f32[8,4,128,1024]{3,2,1,0:T(8,128)} custom-call(bf16[1024,2048]{1,0:T(8,128)(2,1)} %join_halves.6.x_ref.x0_ref, bf16[1024,2048]{1,0:T(8,128)(2,1)} %join_halves.7.x_ref.x1_ref, bf16[4,2,256,2048]{3,2,1,0:T(8,128)(2,1)} %bitcast.378, bf16[4,2,256,2048]{3,2,1,0:T(8,128)(2,1)} %bitcast.379, ...), custom_call_target="tpu_custom_call" | custom-call | flops 858993472 | bytes 838860 | tf_op jit(solution)/shard_map/hidden_grads/pallas_call | solution.py:600
  845.4 21.0 %collective-permute-done.56 = bf16[1,2,256,1024]{3,2,1,0:T(8,128)(2,1)S(1)} collective-permute-done((bf16[1,2,256,1024]{3,2,1,0:T(8,128)(2,1)S(1)}, bf16[1,2,256,1024]{3,2,1,0:T(8,128)(2,1)S(1)}, u32[]{:S(2)}, u32[]{:S(2)}) %collective-permute-start.56) | collective-permute-done | bytes 1048608 | tf_op jit(solution)/shard_map/ppermute | solution.py:105
  989.5 19.5 %unmix_streams.2 = (bf16[5,2048,1024]{2,1,0:T(8,128)(2,1)}, f32[1024,128]{1,0:T(8,128)}) custom-call(f32[2048,20]{1,0:T(8,128)} %copy.94.mix_ref, bf16[5,2048,1024]{2,1,0:T(8,128)(2,1)} %hist_ref.7, bf16[4,1024,1024]{2,1,0:T(8,128)(2,1)} %bitcast.385), custom_call_target="tpu_custom_call" | custom-call | flops 4194304 | bytes 1468006 | tf_op jit(solution)/shard_map/unmix_streams/pallas_call | solution.py:727
  1019.1 32.4 %collective-permute-done.65.up_ref = bf16[8,128,1024]{2,1,0:T(8,128)(2,1)} collective-permute-done((bf16[8,128,1024]{2,1,0:T(8,128)(2,1)}, bf16[8,128,1024]{2,1,0:T(8,128)(2,1)}, u32[]{:S(2)}, u32[]{:S(2)}) %collective-permute-start.65) | collective-permute-done | bytes 2097184 | tf_op jit(solution)/shard_map/ppermute | solution.py:208
  1069.8 21.0 %collective-permute-done.69.refs_2_ = bf16[1,512,1024]{2,1,0:T(8,128)(2,1)S(1)} collective-permute-done((bf16[1,512,1024]{2,1,0:T(8,128)(2,1)}, bf16[1,512,1024]{2,1,0:T(8,128)(2,1)S(1)}, u32[]{:S(2)}, u32[]{:S(2)}) %collective-permute-start.69) | collective-permute-done | bytes 1048608 | tf_op jit(solution)/shard_map/ppermute | solution.py:208
  1091.8 16.0 %collective-permute-done.68.refs_5_ = bf16[4,256,1024]{2,1,0:T(8,128)(2,1)} collective-permute-done((bf16[4,256,1024]{2,1,0:T(8,128)(2,1)}, bf16[4,256,1024]{2,1,0:T(8,128)(2,1)}, u32[]{:S(2)}, u32[]{:S(2)}) %collective-permute-start.68) | collective-permute-done | bytes 2097184 | tf_op jit(solution)/shard_map/ppermute | solution.py:172
  1123.7 19.1 %collective-permute-done.73.refs_2_ = bf16[1,512,1024]{2,1,0:T(8,128)(2,1)S(1)} collective-permute-done((bf16[1,512,1024]{2,1,0:T(8,128)(2,1)}, bf16[1,512,1024]{2,1,0:T(8,128)(2,1)S(1)}, u32[]{:S(2)}, u32[]{:S(2)}) %collective-permute-start.73) | collective-permute-done | bytes 1048608 | tf_op jit(solution)/shard_map/ppermute | solution.py:208
  1142.8 15.0 %collective-permute-done.72.refs_4_ = bf16[4,256,1024]{2,1,0:T(8,128)(2,1)} collective-permute-done((bf16[4,256,1024]{2,1,0:T(8,128)(2,1)}, bf16[4,256,1024]{2,1,0:T(8,128)(2,1)}, u32[]{:S(2)}, u32[]{:S(2)}) %collective-permute-start.72) | collective-permute-done | bytes 2097184 | tf_op jit(solution)/shard_map/ppermute | solution.py:172
  1194.3 19.6 %unmix_streams.3 = (bf16[5,2048,1024]{2,1,0:T(8,128)(2,1)}, f32[1024,128]{1,0:T(8,128)}) custom-call(f32[2048,20]{1,0:T(8,128)} %copy.94.mix_ref, bf16[5,2048,1024]{2,1,0:T(8,128)(2,1)} %hist_ref.7, bf16[4,1024,1024]{2,1,0:T(8,128)(2,1)} %bitcast.384, bf16[5,2048,1024]{2,1,0:T(8,128)(2,1)} %get-tuple-element.403.rest_0_), custom_call_target="tpu_custom_call", output_to_operand_aliasing={{0}: (3, {})} | custom-call | flops 4194304 | bytes 1468006 | tf_op jit(solution)/shard_map/unmix_streams/pallas_call | solution.py:727
  (613 shorter events, 757.0 us)
Async XLA Ops:
  7.2 146.0 %all-gather.5.cloned.1.call-start = ((), (), s32[]{:S(2)}) async-start(), calls=%async_computation.4 | async-start | bytes 5242880 | tf_op jit(solution)/shard_map/all_gather | solution.py:1379
  20.1 374.3 %all-gather.7.cloned.1.call-start = ((), (), s32[]{:S(2)}) async-start(), calls=%async_computation.5 | async-start | bytes 5242880 | tf_op jit(solution)/shard_map/all_gather | solution.py:1517
  99.6 53.6 %collective-permute-start.22 = (bf16[8,128,1024]{2,1,0:T(8,128)(2,1)}, bf16[8,128,1024]{2,1,0:T(8,128)(2,1)}, u32[]{:S(2)}, u32[]{:S(2)}) collective-permute-start(bf16[8,128,1024]{2,1,0:T(8,128)(2,1)} %bitcast.319), channel_id=1, source_target_pairs={{2,0},{4,2},{6,4},{3,1},{5,3},{7,5},{10,8},{12,10},{14,12},{11,9},... | collective-permute-start | bytes 6291464 | tf_op jit(solution)/shard_map/ppermute | solution.py:172
  153.1 59.9 %collective-permute-start.25 = (bf16[2048,1024]{1,0:T(8,128)(2,1)}, bf16[2048,1024]{1,0:T(8,128)(2,1)}, u32[]{:S(2)}, u32[]{:S(2)}) collective-permute-start(bf16[2048,1024]{1,0:T(8,128)(2,1)} %all-gather.5.cloned.1.call-done), channel_id=1, source_target_pairs={{0,8},{1,17},{8,0},{9,25},{16,24},{17,1},{24,16},{25,9},{2,10},{3,... | collective-permute-start | bytes 12582920 | tf_op jit(solution)/shard_map/ppermute | solution.py:105
  213.0 60.8 %collective-permute-start.28 = (bf16[2048,1024]{1,0:T(8,128)(2,1)}, bf16[2048,1024]{1,0:T(8,128)(2,1)}, u32[]{:S(2)}, u32[]{:S(2)}) collective-permute-start(bf16[2048,1024]{1,0:T(8,128)(2,1)} %all-gather.5.cloned.1.call-done), channel_id=1, source_target_pairs={{0,16},{1,9},{8,24},{9,1},{16,0},{17,25},{24,8},{25,17},{2,18},{3,... | collective-permute-start | bytes 12582920 | tf_op jit(solution)/shard_map/ppermute | solution.py:105
  273.9 58.4 %collective-permute-start.31 = (bf16[2048,1024]{1,0:T(8,128)(2,1)}, bf16[2048,1024]{1,0:T(8,128)(2,1)}, u32[]{:S(2)}, u32[]{:S(2)}) collective-permute-start(bf16[2048,1024]{1,0:T(8,128)(2,1)} %collective-permute-done.25), channel_id=1, source_target_pairs={{0,16},{1,9},{8,24},{9,1},{16,0},{17,25},{24,8},{25,17},{2,18},{3,... | collective-permute-start | bytes 12582920 | tf_op jit(solution)/shard_map/ppermute | solution.py:105
  400.9 85.0 %all-to-all-start = ((bf16[4,256,1024]{2,1,0:T(8,128)(2,1)}), bf16[4,256,1024]{2,1,0:T(8,128)(2,1)S(1)}, u32[]{:S(2)}, u32[]{:S(2)}) async-start(bf16[4,256,1024]{2,1,0:T(8,128)(2,1)} %project_heads.2), calls=%async_computation | async-start | bytes 4194304 | tf_op jit(solution)/shard_map/all_to_all | solution.py:1403
  406.3 79.6 %all-gather.9.cloned.1.call-start = ((), (), s32[]{:S(2)}) async-start(), calls=%async_computation.6 | async-start | bytes 2621440 | tf_op jit(solution)/shard_map/all_gather | solution.py:1477
  407.0 78.9 %collective-permute-start.36 = (bf16[4,256,1024]{2,1,0:T(8,128)(2,1)}, bf16[4,256,1024]{2,1,0:T(8,128)(2,1)}, u32[]{:S(2)}, u32[]{:S(2)}) collective-permute-start(bf16[4,256,1024]{2,1,0:T(8,128)(2,1)} %get-tuple-element.278), channel_id=1, source_target_pairs={{0,2},{2,4},{1,3},{3,5},{8,10},{10,12},{9,11},{11,13},{16,18},{18,... | collective-permute-start | bytes 6291464 | tf_op jit(solution)/shard_map/ppermute | solution.py:208
  412.3 73.6 %collective-permute-start.37 = (bf16[4,256,1024]{2,1,0:T(8,128)(2,1)}, bf16[4,256,1024]{2,1,0:T(8,128)(2,1)}, u32[]{:S(2)}, u32[]{:S(2)}) collective-permute-start(bf16[4,256,1024]{2,1,0:T(8,128)(2,1)} %get-tuple-element.279), channel_id=1, source_target_pairs={{6,4},{4,2},{7,5},{5,3},{14,12},{12,10},{15,13},{13,11},{22,20},{2... | collective-permute-start | bytes 6291464 | tf_op jit(solution)/shard_map/ppermute | solution.py:209
  492.5 71.2 %collective-permute-start.39 = (bf16[4,256,1024]{2,1,0:T(8,128)(2,1)}, bf16[4,256,1024]{2,1,0:T(8,128)(2,1)}, u32[]{:S(2)}, u32[]{:S(2)}) collective-permute-start(bf16[4,256,1024]{2,1,0:T(8,128)(2,1)} %get-tuple-element.289), channel_id=1, source_target_pairs={{0,2},{2,4},{4,6},{1,3},{3,5},{5,7},{8,10},{10,12},{12,14},{9,11},... | collective-permute-start | bytes 6291464 | tf_op jit(solution)/shard_map/ppermute | solution.py:208
  581.6 53.8 %all-to-all-start.1 = ((bf16[4,256,1024]{2,1,0:T(8,128)(2,1)}), bf16[4,256,1024]{2,1,0:T(8,128)(2,1)S(1)}, u32[]{:S(2)}, u32[]{:S(2)}) async-start(bf16[4,256,1024]{2,1,0:T(8,128)(2,1)} %bitcast.321), calls=%async_computation.1 | async-start | bytes 4194304 | tf_op jit(solution)/shard_map/all_to_all | solution.py:1403
  585.5 85.2 %all-gather.11.cloned.1.call-start = ((), (), s32[]{:S(2)}) async-start(), calls=%async_computation.7 | async-start | bytes 2621440 | tf_op jit(solution)/shard_map/all_gather | solution.py:1477
  635.4 65.2 %all-to-all-start.2 = ((bf16[4,256,1024]{2,1,0:T(8,128)(2,1)}), bf16[4,256,1024]{2,1,0:T(8,128)(2,1)}, u32[]{:S(2)}, u32[]{:S(2)}) async-start(bf16[4,256,1024]{2,1,0:T(8,128)(2,1)} %copy-done.29), calls=%async_computation.2 | async-start | bytes 4194304 | tf_op jit(solution)/shard_map/all_to_all | solution.py:1403
  753.9 53.1 %all-to-all-start.3 = ((bf16[4,256,1024]{2,1,0:T(8,128)(2,1)}), bf16[4,256,1024]{2,1,0:T(8,128)(2,1)S(1)}, u32[]{:S(2)}, u32[]{:S(2)}) async-start(bf16[4,256,1024]{2,1,0:T(8,128)(2,1)} %bitcast.322), calls=%async_computation.3 | async-start | bytes 4194304 | tf_op jit(solution)/shard_map/all_to_all | solution.py:1403
  829.6 60.1 %collective-permute-start.57 = (bf16[4,4,128,1024]{3,2,1,0:T(8,128)(2,1)}, bf16[4,4,128,1024]{3,2,1,0:T(8,128)(2,1)}, u32[]{:S(2)}, u32[]{:S(2)}) collective-permute-start(bf16[4,4,128,1024]{3,2,1,0:T(8,128)(2,1)} %attention_grads.4), channel_id=1, source_target_pairs={{0,16},{1,9},{8,24},{9,1},{16,0},{17,25},{24,8},{25,17},{2,18},{3,... | collective-permute-start | bytes 12582920 | tf_op jit(solution)/shard_map/ppermute | solution.py:105
  889.7 57.7 %collective-permute-start.61 = (bf16[4,4,128,1024]{3,2,1,0:T(8,128)(2,1)}, bf16[4,4,128,1024]{3,2,1,0:T(8,128)(2,1)}, u32[]{:S(2)}, u32[]{:S(2)}) collective-permute-start(bf16[4,4,128,1024]{3,2,1,0:T(8,128)(2,1)} %attention_grads.5), channel_id=1, source_target_pairs={{0,16},{1,9},{8,24},{9,1},{16,0},{17,25},{24,8},{25,17},{2,18},{3,... | collective-permute-start | bytes 12582920 | tf_op jit(solution)/shard_map/ppermute | solution.py:105
  901.6 54.0 %collective-permute-start.58 = (bf16[8,128,1024]{2,1,0:T(8,128)(2,1)}, bf16[8,128,1024]{2,1,0:T(8,128)(2,1)}, u32[]{:S(2)}, u32[]{:S(2)}) collective-permute-start(bf16[8,128,1024]{2,1,0:T(8,128)(2,1)} %get-tuple-element.356), channel_id=1, source_target_pairs={{0,2},{2,4},{4,6},{1,3},{3,5},{5,7},{8,10},{10,12},{12,14},{9,11},... | collective-permute-start | bytes 6291464 | tf_op jit(solution)/shard_map/ppermute | solution.py:235
  955.5 53.5 %collective-permute-start.64 = (bf16[4,4,128,1024]{3,2,1,0:T(8,128)(2,1)}, bf16[4,4,128,1024]{3,2,1,0:T(8,128)(2,1)}, u32[]{:S(2)}, u32[]{:S(2)}) collective-permute-start(bf16[4,4,128,1024]{3,2,1,0:T(8,128)(2,1)} %convert_add_fusion.1), channel_id=1, source_target_pairs={{0,8},{1,17},{8,0},{9,25},{16,24},{17,1},{24,16},{25,9},{2,10},{3,... | collective-permute-start | bytes 12582920 | tf_op jit(solution)/shard_map/ppermute | solution.py:105
  956.5 62.7 %collective-permute-start.62 = (bf16[4,256,1024]{2,1,0:T(8,128)(2,1)}, bf16[4,256,1024]{2,1,0:T(8,128)(2,1)}, u32[]{:S(2)}, u32[]{:S(2)}) collective-permute-start(bf16[4,256,1024]{2,1,0:T(8,128)(2,1)} %get-tuple-element.366.refs_0_), channel_id=1, source_target_pairs={{0,2},{2,4},{4,6},{1,3},{3,5},{5,7},{8,10},{10,12},{12,14},{9,11},... | collective-permute-start | bytes 6291464 | tf_op jit(solution)/shard_map/ppermute | solution.py:171
  962.3 56.8 %collective-permute-start.63 = (bf16[4,256,1024]{2,1,0:T(8,128)(2,1)}, bf16[4,256,1024]{2,1,0:T(8,128)(2,1)}, u32[]{:S(2)}, u32[]{:S(2)}) collective-permute-start(bf16[4,256,1024]{2,1,0:T(8,128)(2,1)} %get-tuple-element.366.refs_0_), channel_id=1, source_target_pairs={{2,0},{4,2},{6,4},{3,1},{5,3},{7,5},{10,8},{12,10},{14,12},{11,9},... | collective-permute-start | bytes 6291464 | tf_op jit(solution)/shard_map/ppermute | solution.py:172
  972.7 78.9 %collective-permute-start.65 = (bf16[8,128,1024]{2,1,0:T(8,128)(2,1)}, bf16[8,128,1024]{2,1,0:T(8,128)(2,1)}, u32[]{:S(2)}, u32[]{:S(2)}) collective-permute-start(bf16[8,128,1024]{2,1,0:T(8,128)(2,1)} %get-tuple-element.378), channel_id=1, source_target_pairs={{0,2},{2,4},{4,6},{1,3},{3,5},{5,7},{8,10},{10,12},{12,14},{9,11},... | collective-permute-start | bytes 6291464 | tf_op jit(solution)/shard_map/ppermute | solution.py:208
  978.6 78.4 %collective-permute-start.66 = (bf16[8,128,1024]{2,1,0:T(8,128)(2,1)}, bf16[8,128,1024]{2,1,0:T(8,128)(2,1)}, u32[]{:S(2)}, u32[]{:S(2)}) collective-permute-start(bf16[8,128,1024]{2,1,0:T(8,128)(2,1)} %get-tuple-element.379), channel_id=1, source_target_pairs={{6,4},{4,2},{2,0},{7,5},{5,3},{3,1},{14,12},{12,10},{10,8},{15,13}... | collective-permute-start | bytes 6291464 | tf_op jit(solution)/shard_map/ppermute | solution.py:209
  1162.8 53.6 %collective-permute-start.75 = (bf16[1,512,1024]{2,1,0:T(8,128)(2,1)}, bf16[1,512,1024]{2,1,0:T(8,128)(2,1)}, u32[]{:S(2)}, u32[]{:S(2)}) collective-permute-start(bf16[1,512,1024]{2,1,0:T(8,128)(2,1)} %get-tuple-element.409), channel_id=1, source_target_pairs={{0,2},{2,4},{4,6},{1,3},{3,5},{5,7},{8,10},{10,12},{12,14},{9,11},... | collective-permute-start | bytes 3145736 | tf_op jit(solution)/shard_map/ppermute | solution.py:208
  (181 other events, 2674.7 us)
Sparse Core Ops, SparseCore 0:
  20.3 93.4 all-gather.4
  332.4 52.1 all-gather.6
  409.5 37.8 all-gather.8
  635.5 35.1 all-gather.10

commit v6 on v5

--- a/solution.py
+++ b/solution.py
@@ -1412,13 +1412,21 @@
 
     weights_line = LineGather(ff_rows)
     weights_line.step()
-    over_depth, partial, partial_next = weights_line.hold(over_depth, partial, partial_next)
+    cot_pieces = lax.all_gather(cotangent, "dp", axis=0, tiled=True)
+    over_depth, partial, partial_next, cot_pieces = weights_line.hold(
+        over_depth, partial, partial_next, cot_pieces
+    )
     pieces = [over_depth]
     weights = place_block(None, pieces[0][None], place_index(0), dp_count)
     hops_left = [(p, at) for at in range(len(dp_bits)) for p in range(1 << at)]
     placed = 1
     cots = None
     sums, sums_next = LineScatter(partial), LineScatter(partial_next)
+    own_tables = turning_tables(positions)
+    tables = [
+        turning_tables(places_all[:, m * rows_mb : (m + 1) * rows_mb].reshape(length))
+        for m in range(MB)
+    ]
     for hop in range(1, depth_count):
         sums.step_with(weights_line)
         last_hop = hop == depth_count - 1
@@ -1433,17 +1441,18 @@
         if last_hop:
             cot_full = join_halves(cotangent, other_core(cotangent), model_at)
             ff_weights = weights_line.placed()
-            cots = cot_full, cotangent, ff_weights
-        (state,) = weights_line.hold((sums.up, sums.down, pieces, weights, cots))
-        sums.up, sums.down, pieces, weights, cots = state
-    cot_full, cotangent, ff_weights = cots
+            cots = cot_full, cotangent, cot_pieces, ff_weights
+        (state,) = weights_line.hold(
+            (sums.up, sums.down, pieces, weights, cots, own_tables, tables)
+        )
+        sums.up, sums.down, pieces, weights, cots, own_tables, tables = state
+    cot_full, cotangent, cot_pieces, ff_weights = cots
     for place in range(placed, len(pieces)):
         weights = place_block(weights, pieces[place][None], place_index(place), dp_count)
     weights = weights.reshape(dp_count, depth_count, 4, own_rows, heads_width)
     ff_weights = ff_weights.reshape(2, dp_count, depth_count, own_rows, ff_part)
 
     document_view = doc_ids.reshape(depth_count, MB, rows_mb)
-    own_tables = turning_tables(positions)
     which = model_at.astype(jnp.int32)[None]
     depth_at = lax.axis_index("depth").astype(jnp.int32)[None]
     gains = gain_float
@@ -1464,11 +1473,9 @@
         )
 
     def attention(micro_at, by_head):
-        span = slice(micro_at * rows_mb, (micro_at + 1) * rows_mb)
         documents = document_view[:, micro_at].reshape(length)
-        seq_places = places_all[:, span].reshape(length)
         by_head = by_head.reshape(length, 4 * heads_each * HDIM)
-        answer = attend(by_head, documents, turning_tables(seq_places), heads_each)
+        answer = attend(by_head, documents, tables[micro_at], heads_each)
         return answer.reshape(depth_count, rows_mb, 4 * heads_each * HDIM)
 
     place_list = jnp.stack([place_index(p) for p in range(dp_count)]).astype(jnp.int32)
@@ -1514,34 +1521,34 @@
 
     ((sums.up, sums.down),) = sums_next.step((sums.up, sums.down))
     first = enter(0, sums)
-    cot_mine = lax.all_gather(cotangent, "dp", axis=0, tiled=True)
-    packed, ff_normed, cot_mine = sums_next.hold(first["packed"], first["ff_normed"], cot_mine)
+    mine = group_rows(first["ff_normed"])
+    packed, mine, cot_pieces = sums_next.hold(first["packed"], mine, cot_pieces)
     while sums_next.at < depth_count - 3:
         sums_next.step()
         sums_next.hold()
-    packed, ff_normed = sums_next.step(packed, ff_normed)
+    packed, mine, cot_pieces = sums_next.step(packed, mine, cot_pieces)
     by_head = over_depth_swap(packed)
-    cot_group = join_halves(cot_mine, other_core(cot_mine), model_at)
+    cot_group = join_halves(cot_pieces, other_core(cot_pieces), model_at)
     cot_group = cot_group.reshape(dp_count, MB, rows_mb, model)
-    by_head, mine, cot_group = sums_next.hold(by_head, group_rows(ff_normed), cot_group)
-    by_head, mine = sums_next.step(by_head, mine)
     kept, ff_parts = hidden_units(0, group_joined(mine))
     first.update(kept)
+    by_head, ff_parts, cot_group = sums_next.hold(by_head, ff_parts, cot_group)
+    by_head, ff_parts = sums_next.step(by_head, ff_parts)
     answer = attention(0, by_head)
-    answer, ff_parts = sums_next.hold(answer, ff_parts)
+    near, far = group_split(ff_parts[0], other_core(ff_parts[1]), place_list)
+    near = near + core_hop(far, len(dp_bits) - 1).astype(f32)
+    answer, near = sums_next.hold(answer, near)
 
     answer = over_depth_swap(answer)
     second = enter(1, sums_next)
-    ff_sum = group_back(ff_parts[0], other_core(ff_parts[1]))
     answer, packed, ff_normed, ff_sum = fence(
-        answer, second["packed"], second["ff_normed"], ff_sum
+        answer, second["packed"], second["ff_normed"], group_back_rest(near)
     )
     by_head = over_depth_swap(packed)
+    mine = group_rows(ff_normed)
     own, got, first["flat"] = back(first, answer)
     grad_low = leave(0, first, own, got, ff_sum)
-    by_head, grad_low, group_normed = fence(
-        by_head, grad_low, group_joined(group_rows(ff_normed))
-    )
+    by_head, grad_low, mine = fence(by_head, grad_low, mine)
     saved = [first, second]
 
     def each(name):
@@ -1576,7 +1583,7 @@
     grad_line = LineGather(grad_low)
     grad_line.step()
     answer = attention(1, by_head)
-    kept, ff_parts = hidden_units(1, group_normed)
+    kept, ff_parts = hidden_units(1, group_joined(mine))
     second.update(kept)
     answer, ff_parts = grad_line.hold(answer, ff_parts)
     answer = over_depth_swap(answer)
@@ -1592,51 +1599,51 @@
     own, got, flat = back(second, answer)
     ff_sum = group_back_rest(near)
     second["flat"] = flat
-    far_grads = [place_grads(p, bf16) for p in range(half, dp_count)]
-    arrived = core_hop(far_grads[0], hops_left.pop(0)[1])
-    (state,) = grad_line.hold(
-        (ff_sums.up, ff_sums.down, own, got, flat, ff_sum, far_grads, arrived)
-    )
-    ff_sums.up, ff_sums.down, own, got, second["flat"], ff_sum, far_grads, arrived = state
+    (state,) = grad_line.hold((ff_sums.up, ff_sums.down, own, got, flat, ff_sum))
+    ff_sums.up, ff_sums.down, own, got, second["flat"], ff_sum = state
     while len(grad_line.up) < depth_count - 1:
         ff_sums.step_with(grad_line)
         (state,) = grad_line.hold((ff_sums.up, ff_sums.down))
         ff_sums.up, ff_sums.down = state
     (ff_sum,) = ff_sums.step_with(grad_line, ff_sum)
     grad_low = leave(1, second, own, got, ff_sum)
-    pieces = {p: place_grads(p, f32) for p in range(half)}
-    pieces[0] = pieces[0] + arrived.astype(f32)
-    pieces.update({half + at: far_grads[at] for at in range(1, half)})
+    pieces = {p: place_grads(p, bf16 if p >= half else f32) for p in range(dp_count)}
     sums_hop()
     (state,) = grad_line.hold((ff_sums.up, ff_sums.down, grad_low, pieces))
     ff_sums.up, ff_sums.down, grad_low, pieces = state
 
     last_line = LineGather(grad_low)
     last_line.step()
-    ff_sums.step()
-    while hops_left:
+    if hops_left:
         sums_hop()
     grad_first = grad_line.placed().reshape(STREAMS, length, width)
     history_grad, slot_part = unmix_streams(
         slot_mix, history, grad_first, 0, depth_count, rows_mb, None
     )
     slot_parts = [slot_part.reshape(depth_count, 1, rows_mb, 128)]
-    pieces, history_grad, state = last_line.hold(
-        pieces, history_grad, (ff_sums.up, ff_sums.down)
-    )
-    ff_sums.up, ff_sums.down = state
+    pieces, history_grad = last_line.hold(pieces, history_grad)
+    (pieces,) = ff_sums.step(pieces)
+    while hops_left:
+        sums_hop()
+    (pieces,) = ff_sums.hold(pieces)
     out_sums = LineScatter(pieces[0].reshape(1, depth_count, 4 * own_rows, heads_width))
     for hop in range(2, depth_count):
         last_line.step()
         out_sums.step()
+        if hop == depth_count - 1:
+            ff_grads = end_sums(ff_sums, bf16).reshape(2, dp_count, own_rows, ff_part)
+            ff_pieces = [
+                lax.dynamic_index_in_dim(ff_grads, partners[m], 1, keepdims=False)
+                for m in range(dp_count)
+            ]
+            ff_pieces = ff_pieces[:1] + [
+                swap_mask(ff_pieces[m], "dp", m) for m in range(1, dp_count)
+            ]
+            ff_sums.up = ff_sums.down = ff_pieces
         (state,) = last_line.hold((out_sums.up, out_sums.down, ff_sums.up, ff_sums.down))
         out_sums.up, out_sums.down, ff_sums.up, ff_sums.down = state
     out_sums.step()
-    ff_grads = end_sums(ff_sums, bf16).reshape(2, dp_count, own_rows, ff_part)
-    ff_pieces = [
-        lax.dynamic_index_in_dim(ff_grads, partners[m], 1, keepdims=False) for m in range(dp_count)
-    ]
-    ff_pieces = [ff_pieces[0]] + [swap_mask(ff_pieces[m], "dp", m) for m in range(1, dp_count)]
+    ff_pieces = ff_sums.up
     last_grads = last_line.placed().reshape(STREAMS, length, width)
     history_grad, slot_part = unmix_streams(
         slot_mix, history, last_grads, 1, depth_count, rows_mb, history_grad

time: 1310 us -> 1270 us (0.969)
  waiting for transfers between devices: 484 us -> 445 us
    ppermute x8, waiting for transfers between devices: 163 us -> 91.5 us  [step(): self.up = lax.ppermute(goes_up, 'depth', up_pairs)]
    ppermute x10, waiting for transfers between devices: 36.2 us -> 61 us  [core_hop(): return lax.ppermute(values, ('dp', 'mp'), pairs)]
    all_gather x2, waiting for transfers between devices: 24.7 us -> 0.01 us  [group_rows(): return lax.all_gather(ff_normed, 'dp', axis=0, tiled=True)]
    all_to_all x4, waiting for transfers between devices: 5.74 us -> 27 us  [over_depth_swap(): return lax.all_to_all(values, 'depth', 0, 0, tiled=True)]
    add x2 -> x0, other arithmetic: 13.8 us -> none  [the longest x1 10.2 us: local(): pieces[0] = pieces[0] + arrived.astype(f32)]
    unnamed x204 -> x194, local copies, waits for them, and re-layouts: 49 us -> 48.7 us
  transfers between devices with their start and end apart: 105 -> 105, of which waited for: 48 -> 52; matrix products, arithmetic and copies ran while one was open for 8% -> 8% of each run, Pallas kernels for 33% -> 32%
where the time goes in v6:
time: 1270 us; the launch traced here: 1260 us
  Pallas kernels  459 us (36%)
  waiting for transfers between devices  445 us (35%)
  starting transfers between devices  180 us (14%)
  local copies, waits for them, and re-layouts  74.2 us (6%)
  other arithmetic  72.4 us (6%)
  between operations  16 us (1%)
    ppermute x8, waiting for transfers between devices, step(): self.up = lax.ppermute(goes_up, 'depth', up_pairs)  91.5 us
    ppermute x53, waiting for transfers between devices, swap_mask(): return lax.ppermute(values, axis, [(i, i ^ mask) for i in range(size)])  87.2 us
    ppermute x4, waiting for transfers between devices, step_with(): lax.ppermute(goes[0], 'depth', [(i, i + 1) for i in range(size - 1)])  84.3 us
    pallas_call x12, Pallas kernels, hop_sums(): pl.pallas_call(functools.partial(hop_kernel, up is not None, blocks is no...  82.3 us
    ppermute x10, waiting for transfers between devices, core_hop(): return lax.ppermute(values, ('dp', 'mp'), pairs)  61 us
    ppermute x8, starting transfers between devices, step(): self.up = lax.ppermute(goes_up, 'depth', up_pairs)  51 us
    unnamed x194, local copies, waits for them, and re-layouts  48.7 us
    ppermute x53, starting transfers between devices, swap_mask(): return lax.ppermute(values, axis, [(i, i ^ mask) for i in range(size)])  48.6 us
  transfers between devices with their start and end apart: 105, of which 52 were waited for; matrix products, arithmetic and copies ran while one was open for 8% of the time, Pallas kernels for 32%

profile of v6, /device:TPU:0, one launch (start us, length us, event | category | flops | bytes accessed | tf_op | source)
XLA Modules:
  0.0 1258.6 jit_solution(16660891436867823766)
XLA Ops:
  99.7 14.4 %mix_streams.2 = bf16[4,1024,1024]{2,1,0:T(8,128)(2,1)} custom-call(f32[2048,20]{1,0:T(8,128)} %copy.94.mix_ref, bf16[5,2048,1024]{2,1,0:T(8,128)(2,1)} %hist_ref.7), custom_call_target="tpu_custom_call" | custom-call | flops 2097152 | bytes 943718 | tf_op jit(solution)/shard_map/mix_streams/pallas_call | solution.py:652
  114.1 14.4 %mix_streams.3 = bf16[4,1024,1024]{2,1,0:T(8,128)(2,1)} custom-call(f32[2048,20]{1,0:T(8,128)} %copy.94.mix_ref, bf16[5,2048,1024]{2,1,0:T(8,128)(2,1)} %hist_ref.7), custom_call_target="tpu_custom_call" | custom-call | flops 2097152 | bytes 943718 | tf_op jit(solution)/shard_map/mix_streams/pallas_call | solution.py:652
  128.5 13.1 %collective-permute-done.21.refs_1_ = bf16[8,128,1024]{2,1,0:T(8,128)(2,1)S(1)} collective-permute-done((bf16[8,128,1024]{2,1,0:T(8,128)(2,1)}, bf16[8,128,1024]{2,1,0:T(8,128)(2,1)S(1)}, u32[]{:S(2)}, u32[]{:S(2)}) %collective-permute-start.21) | collective-permute-done | bytes 2097184 | tf_op jit(solution)/shard_map/ppermute | solution.py:171
  146.7 12.0 all-gather.7.cloned.1.call-done.own_ref
  186.8 27.9 %collective-permute-done.23.refs_2_ = bf16[4,256,1024]{2,1,0:T(8,128)(2,1)S(1)} collective-permute-done((bf16[4,256,1024]{2,1,0:T(8,128)(2,1)}, bf16[4,256,1024]{2,1,0:T(8,128)(2,1)S(1)}, u32[]{:S(2)}, u32[]{:S(2)}) %collective-permute-start.23) | collective-permute-done | bytes 2097184 | tf_op jit(solution)/shard_map/ppermute | solution.py:235
  239.2 36.0 %collective-permute-done.26.refs_2_ = bf16[4,256,1024]{2,1,0:T(8,128)(2,1)S(1)} collective-permute-done((bf16[4,256,1024]{2,1,0:T(8,128)(2,1)}, bf16[4,256,1024]{2,1,0:T(8,128)(2,1)S(1)}, u32[]{:S(2)}, u32[]{:S(2)}) %collective-permute-start.26) | collective-permute-done | bytes 2097184 | tf_op jit(solution)/shard_map/ppermute | solution.py:235
  378.7 24.3 %collective-permute-done.33.refs_2_ = bf16[4,256,1024]{2,1,0:T(8,128)(2,1)} collective-permute-done((bf16[4,256,1024]{2,1,0:T(8,128)(2,1)}, bf16[4,256,1024]{2,1,0:T(8,128)(2,1)}, u32[]{:S(2)}, u32[]{:S(2)}) %collective-permute-start.33) | collective-permute-done | bytes 2097184 | tf_op jit(solution)/shard_map/ppermute | solution.py:208
  435.3 24.1 %feed_forward.2 = (bf16[1024,1024]{1,0:T(8,128)(2,1)S(1)}, bf16[1024,1024]{1,0:T(8,128)(2,1)S(1)}, f32[2,1024,1024]{2,1,0:T(8,128)}, bf16[2,1024,1024]{2,1,0:T(8,128)(2,1)}) custom-call(s32[1]{0:T(128)} %bitcast.73.model_ref.half_ref, bf16[1024,2048]{1,0:T(8,128)(2,1)} %join_halves.5.x_ref.x0_ref, bf16[4,2,256,2048]{3,2,1,0:T(8,128)(2,1)} %bitcast.377, ...), custom_call_target="tpu_custom_call" | custom-call | flops 858993472 | bytes 2097152 | tf_op jit(solution)/shard_map/feed_forward/pallas_call | solution.py:1083
  462.1 32.1 %collective-permute-done.36.refs_2_ = bf16[4,256,1024]{2,1,0:T(8,128)(2,1)} collective-permute-done((bf16[4,256,1024]{2,1,0:T(8,128)(2,1)}, bf16[4,256,1024]{2,1,0:T(8,128)(2,1)}, u32[]{:S(2)}, u32[]{:S(2)}) %collective-permute-start.36) | collective-permute-done | bytes 2097184 | tf_op jit(solution)/shard_map/ppermute | solution.py:208
  516.8 18.1 %collective-permute-start.40 = (bf16[4,256,1024]{2,1,0:T(8,128)(2,1)}, bf16[4,256,1024]{2,1,0:T(8,128)(2,1)}, u32[]{:S(2)}, u32[]{:S(2)}) collective-permute-start(bf16[4,256,1024]{2,1,0:T(8,128)(2,1)} %get-tuple-element.355), channel_id=1, source_target_pairs={{0,2},{2,4},{4,6},{1,3},{3,5},{5,7},{8,10},{10,12},{12,14},{9,11},... | collective-permute-start | bytes 6291464 | tf_op jit(solution)/shard_map/ppermute | solution.py:208
  536.9 10.9 attend.2
  553.2 25.5 %collective-permute-done.40.up_ref = bf16[4,256,1024]{2,1,0:T(8,128)(2,1)} collective-permute-done((bf16[4,256,1024]{2,1,0:T(8,128)(2,1)}, bf16[4,256,1024]{2,1,0:T(8,128)(2,1)}, u32[]{:S(2)}, u32[]{:S(2)}) %collective-permute-start.40) | collective-permute-done | bytes 2097184 | tf_op jit(solution)/shard_map/ppermute | solution.py:208
  596.5 13.3 %collective-permute-done.45 = bf16[1,2,256,1024]{3,2,1,0:T(8,128)(2,1)S(1)} collective-permute-done((bf16[1,2,256,1024]{3,2,1,0:T(8,128)(2,1)S(1)}, bf16[1,2,256,1024]{3,2,1,0:T(8,128)(2,1)S(1)}, u32[]{:S(2)}, u32[]{:S(2)}) %collective-permute-start.45) | collective-permute-done | bytes 1048608 | tf_op jit(solution)/shard_map/ppermute | solution.py:105
  671.6 15.6 %all-to-all-done.2 = bf16[4,256,1024]{2,1,0:T(8,128)(2,1)} async-done(((bf16[4,256,1024]{2,1,0:T(8,128)(2,1)}), bf16[4,256,1024]{2,1,0:T(8,128)(2,1)}, u32[]{:S(2)}, u32[]{:S(2)}) %all-to-all-start.2) | async-done | bytes 2097184 | tf_op jit(solution)/shard_map/all_to_all | solution.py:1403
  693.1 10.7 attend.3
  709.8 24.0 %feed_forward.3 = (bf16[1024,1024]{1,0:T(8,128)(2,1)S(1)}, bf16[1024,1024]{1,0:T(8,128)(2,1)S(1)}, f32[2,1024,1024]{2,1,0:T(8,128)}, bf16[2,1024,1024]{2,1,0:T(8,128)(2,1)}) custom-call(s32[1]{0:T(128)} %bitcast.73.model_ref.half_ref, bf16[1024,2048]{1,0:T(8,128)(2,1)} %join_halves.7.x_ref.x1_ref, bf16[4,2,256,2048]{3,2,1,0:T(8,128)(2,1)} %bitcast.378, ...), custom_call_target="tpu_custom_call" | custom-call | flops 858993472 | bytes 2097152 | tf_op jit(solution)/shard_map/feed_forward/pallas_call | solution.py:1083
  759.1 24.3 %hidden_grads.1.refs_0_.refs_1_.term_ref = f32[8,4,128,1024]{3,2,1,0:T(8,128)} custom-call(bf16[1024,2048]{1,0:T(8,128)(2,1)} %join_halves.5.x_ref.x0_ref, bf16[1024,2048]{1,0:T(8,128)(2,1)} %join_halves.7.x_ref.x1_ref, bf16[4,2,256,2048]{3,2,1,0:T(8,128)(2,1)} %bitcast.379, bf16[4,2,256,2048]{3,2,1,0:T(8,128)(2,1)} %bitcast.380, ...), custom_call_target="tpu_custom_call" | custom-call | flops 858993472 | bytes 838860 | tf_op jit(solution)/shard_map/hidden_grads/pallas_call | solution.py:600
  828.6 20.4 %collective-permute-done.53.refs_2_ = bf16[8,128,1024]{2,1,0:T(8,128)(2,1)S(1)} collective-permute-done((bf16[8,128,1024]{2,1,0:T(8,128)(2,1)}, bf16[8,128,1024]{2,1,0:T(8,128)(2,1)S(1)}, u32[]{:S(2)}, u32[]{:S(2)}) %collective-permute-start.53) | collective-permute-done | bytes 2097184 | tf_op jit(solution)/shard_map/ppermute | solution.py:235
  859.3 10.3 hop_sums.19
  911.0 10.1 convert_add_fusion.2
  948.7 19.5 %unmix_streams.2 = (bf16[5,2048,1024]{2,1,0:T(8,128)(2,1)}, f32[1024,128]{1,0:T(8,128)}) custom-call(f32[2048,20]{1,0:T(8,128)} %copy.94.mix_ref, bf16[5,2048,1024]{2,1,0:T(8,128)(2,1)} %hist_ref.7, bf16[4,1024,1024]{2,1,0:T(8,128)(2,1)} %bitcast.386), custom_call_target="tpu_custom_call" | custom-call | flops 4194304 | bytes 1468006 | tf_op jit(solution)/shard_map/unmix_streams/pallas_call | solution.py:727
  986.1 39.7 %collective-permute-done.68 = bf16[4,4,128,1024]{3,2,1,0:T(8,128)(2,1)S(1)} collective-permute-done((bf16[4,4,128,1024]{3,2,1,0:T(8,128)(2,1)S(1)}, bf16[4,4,128,1024]{3,2,1,0:T(8,128)(2,1)S(1)}, u32[]{:S(2)}, u32[]{:S(2)}) %collective-permute-start.68) | collective-permute-done | bytes 4194336 | tf_op jit(solution)/shard_map/ppermute | solution.py:105
  1043.4 32.8 %collective-permute-done.65.refs_5_ = bf16[4,256,1024]{2,1,0:T(8,128)(2,1)} collective-permute-done((bf16[4,256,1024]{2,1,0:T(8,128)(2,1)}, bf16[4,256,1024]{2,1,0:T(8,128)(2,1)}, u32[]{:S(2)}, u32[]{:S(2)}) %collective-permute-start.65) | collective-permute-done | bytes 2097184 | tf_op jit(solution)/shard_map/ppermute | solution.py:172
  1154.8 19.6 %unmix_streams.3 = (bf16[5,2048,1024]{2,1,0:T(8,128)(2,1)}, f32[1024,128]{1,0:T(8,128)}) custom-call(f32[2048,20]{1,0:T(8,128)} %copy.94.mix_ref, bf16[5,2048,1024]{2,1,0:T(8,128)(2,1)} %hist_ref.7, bf16[4,1024,1024]{2,1,0:T(8,128)(2,1)} %bitcast.385, bf16[5,2048,1024]{2,1,0:T(8,128)(2,1)} %get-tuple-element.477.rest_0_), custom_call_target="tpu_custom_call", output_to_operand_aliasing={{0}: (3, {})} | custom-call | flops 4194304 | bytes 1468006 | tf_op jit(solution)/shard_map/unmix_streams/pallas_call | solution.py:727
  (604 shorter events, 749.4 us)
Async XLA Ops:
  7.2 139.5 %all-gather.5.cloned.1.call-start = ((), (), s32[]{:S(2)}) async-start(), calls=%async_computation.4 | async-start | bytes 5242880 | tf_op jit(solution)/shard_map/all_gather | solution.py:1379
  10.5 148.1 %all-gather.7.cloned.1.call-start = ((), (), s32[]{:S(2)}) async-start(), calls=%async_computation.5 | async-start | bytes 5242880 | tf_op jit(solution)/shard_map/all_gather | solution.py:1415
  95.6 307.5 %all-gather.9.cloned.1.call-start = ((), (), s32[]{:S(2)}) async-start(), calls=%async_computation.6 | async-start | bytes 2621440 | tf_op jit(solution)/shard_map/all_gather | solution.py:1484
  97.0 49.6 %collective-permute-start.22 = (bf16[8,128,1024]{2,1,0:T(8,128)(2,1)}, bf16[8,128,1024]{2,1,0:T(8,128)(2,1)}, u32[]{:S(2)}, u32[]{:S(2)}) collective-permute-start(bf16[8,128,1024]{2,1,0:T(8,128)(2,1)} %bitcast.320), channel_id=1, source_target_pairs={{2,0},{4,2},{6,4},{3,1},{5,3},{7,5},{10,8},{12,10},{14,12},{11,9},... | collective-permute-start | bytes 6291464 | tf_op jit(solution)/shard_map/ppermute | solution.py:172
  158.7 60.3 %collective-permute-start.25 = (bf16[2048,1024]{1,0:T(8,128)(2,1)}, bf16[2048,1024]{1,0:T(8,128)(2,1)}, u32[]{:S(2)}, u32[]{:S(2)}) collective-permute-start(bf16[2048,1024]{1,0:T(8,128)(2,1)} %all-gather.5.cloned.1.call-done), channel_id=1, source_target_pairs={{0,8},{1,17},{8,0},{9,25},{16,24},{17,1},{24,16},{25,9},{2,10},{3,... | collective-permute-start | bytes 12582920 | tf_op jit(solution)/shard_map/ppermute | solution.py:105
  219.0 60.5 %collective-permute-start.28 = (bf16[2048,1024]{1,0:T(8,128)(2,1)}, bf16[2048,1024]{1,0:T(8,128)(2,1)}, u32[]{:S(2)}, u32[]{:S(2)}) collective-permute-start(bf16[2048,1024]{1,0:T(8,128)(2,1)} %all-gather.5.cloned.1.call-done), channel_id=1, source_target_pairs={{0,16},{1,9},{8,24},{9,1},{16,0},{17,25},{24,8},{25,17},{2,18},{3,... | collective-permute-start | bytes 12582920 | tf_op jit(solution)/shard_map/ppermute | solution.py:105
  279.5 59.4 %collective-permute-start.31 = (bf16[2048,1024]{1,0:T(8,128)(2,1)}, bf16[2048,1024]{1,0:T(8,128)(2,1)}, u32[]{:S(2)}, u32[]{:S(2)}) collective-permute-start(bf16[2048,1024]{1,0:T(8,128)(2,1)} %collective-permute-done.25), channel_id=1, source_target_pairs={{0,16},{1,9},{8,24},{9,1},{16,0},{17,25},{24,8},{25,17},{2,18},{3,... | collective-permute-start | bytes 12582920 | tf_op jit(solution)/shard_map/ppermute | solution.py:105
  409.5 84.6 %all-to-all-start = ((bf16[4,256,1024]{2,1,0:T(8,128)(2,1)}), bf16[4,256,1024]{2,1,0:T(8,128)(2,1)S(1)}, u32[]{:S(2)}, u32[]{:S(2)}) async-start(bf16[4,256,1024]{2,1,0:T(8,128)(2,1)} %project_heads.2), calls=%async_computation | async-start | bytes 4194304 | tf_op jit(solution)/shard_map/all_to_all | solution.py:1403
  414.8 79.4 %collective-permute-start.36 = (bf16[4,256,1024]{2,1,0:T(8,128)(2,1)}, bf16[4,256,1024]{2,1,0:T(8,128)(2,1)}, u32[]{:S(2)}, u32[]{:S(2)}) collective-permute-start(bf16[4,256,1024]{2,1,0:T(8,128)(2,1)} %get-tuple-element.340), channel_id=1, source_target_pairs={{0,2},{2,4},{1,3},{3,5},{8,10},{10,12},{9,11},{11,13},{16,18},{18,... | collective-permute-start | bytes 6291464 | tf_op jit(solution)/shard_map/ppermute | solution.py:208
  419.8 74.3 %collective-permute-start.37 = (bf16[4,256,1024]{2,1,0:T(8,128)(2,1)}, bf16[4,256,1024]{2,1,0:T(8,128)(2,1)}, u32[]{:S(2)}, u32[]{:S(2)}) collective-permute-start(bf16[4,256,1024]{2,1,0:T(8,128)(2,1)} %get-tuple-element.341), channel_id=1, source_target_pairs={{6,4},{4,2},{7,5},{5,3},{14,12},{12,10},{15,13},{13,11},{22,20},{2... | collective-permute-start | bytes 6291464 | tf_op jit(solution)/shard_map/ppermute | solution.py:209
  516.8 61.9 %collective-permute-start.40 = (bf16[4,256,1024]{2,1,0:T(8,128)(2,1)}, bf16[4,256,1024]{2,1,0:T(8,128)(2,1)}, u32[]{:S(2)}, u32[]{:S(2)}) collective-permute-start(bf16[4,256,1024]{2,1,0:T(8,128)(2,1)} %get-tuple-element.355), channel_id=1, source_target_pairs={{0,2},{2,4},{4,6},{1,3},{3,5},{5,7},{8,10},{10,12},{12,14},{9,11},... | collective-permute-start | bytes 6291464 | tf_op jit(solution)/shard_map/ppermute | solution.py:208
  534.9 49.3 %collective-permute-start.41 = (bf16[4,256,1024]{2,1,0:T(8,128)(2,1)}, bf16[4,256,1024]{2,1,0:T(8,128)(2,1)}, u32[]{:S(2)}, u32[]{:S(2)}) collective-permute-start(bf16[4,256,1024]{2,1,0:T(8,128)(2,1)} %get-tuple-element.356), channel_id=1, source_target_pairs={{6,4},{4,2},{2,0},{7,5},{5,3},{3,1},{14,12},{12,10},{10,8},{15,13}... | collective-permute-start | bytes 6291464 | tf_op jit(solution)/shard_map/ppermute | solution.py:209
  584.2 50.9 %all-to-all-start.1 = ((bf16[4,256,1024]{2,1,0:T(8,128)(2,1)}), bf16[4,256,1024]{2,1,0:T(8,128)(2,1)S(1)}, u32[]{:S(2)}, u32[]{:S(2)}) async-start(bf16[4,256,1024]{2,1,0:T(8,128)(2,1)} %bitcast.322), calls=%async_computation.1 | async-start | bytes 4194304 | tf_op jit(solution)/shard_map/all_to_all | solution.py:1403
  635.0 52.2 %all-to-all-start.2 = ((bf16[4,256,1024]{2,1,0:T(8,128)(2,1)}), bf16[4,256,1024]{2,1,0:T(8,128)(2,1)}, u32[]{:S(2)}, u32[]{:S(2)}) async-start(bf16[4,256,1024]{2,1,0:T(8,128)(2,1)} %copy-done.25), calls=%async_computation.2 | async-start | bytes 4194304 | tf_op jit(solution)/shard_map/all_to_all | solution.py:1403
  688.7 50.3 %collective-permute-start.49 = (bf16[4,256,1024]{2,1,0:T(8,128)(2,1)}, bf16[4,256,1024]{2,1,0:T(8,128)(2,1)}, u32[]{:S(2)}, u32[]{:S(2)}) collective-permute-start(bf16[4,256,1024]{2,1,0:T(8,128)(2,1)} %get-tuple-element.383.refs_0_), channel_id=1, source_target_pairs={{2,0},{4,2},{6,4},{3,1},{5,3},{7,5},{10,8},{12,10},{14,12},{11,9},... | collective-permute-start | bytes 6291464 | tf_op jit(solution)/shard_map/ppermute | solution.py:172
  738.9 54.8 %all-to-all-start.3 = ((bf16[4,256,1024]{2,1,0:T(8,128)(2,1)}), bf16[4,256,1024]{2,1,0:T(8,128)(2,1)S(1)}, u32[]{:S(2)}, u32[]{:S(2)}) async-start(bf16[4,256,1024]{2,1,0:T(8,128)(2,1)} %bitcast.323), calls=%async_computation.3 | async-start | bytes 4194304 | tf_op jit(solution)/shard_map/all_to_all | solution.py:1403
  857.7 53.3 %collective-permute-start.60 = (bf16[4,4,128,1024]{3,2,1,0:T(8,128)(2,1)}, bf16[4,4,128,1024]{3,2,1,0:T(8,128)(2,1)}, u32[]{:S(2)}, u32[]{:S(2)}) collective-permute-start(bf16[4,4,128,1024]{3,2,1,0:T(8,128)(2,1)} %attention_grads.5), channel_id=1, source_target_pairs={{0,16},{1,9},{8,24},{9,1},{16,0},{17,25},{24,8},{25,17},{2,18},{3,... | collective-permute-start | bytes 12582920 | tf_op jit(solution)/shard_map/ppermute | solution.py:105
  869.6 51.5 %collective-permute-start.57 = (bf16[8,128,1024]{2,1,0:T(8,128)(2,1)}, bf16[8,128,1024]{2,1,0:T(8,128)(2,1)}, u32[]{:S(2)}, u32[]{:S(2)}) collective-permute-start(bf16[8,128,1024]{2,1,0:T(8,128)(2,1)} %get-tuple-element.424), channel_id=1, source_target_pairs={{0,2},{2,4},{4,6},{1,3},{3,5},{5,7},{8,10},{10,12},{12,14},{9,11},... | collective-permute-start | bytes 6291464 | tf_op jit(solution)/shard_map/ppermute | solution.py:235
  921.7 54.6 %collective-permute-start.61 = (bf16[4,256,1024]{2,1,0:T(8,128)(2,1)}, bf16[4,256,1024]{2,1,0:T(8,128)(2,1)}, u32[]{:S(2)}, u32[]{:S(2)}) collective-permute-start(bf16[4,256,1024]{2,1,0:T(8,128)(2,1)} %get-tuple-element.433.refs_0_), channel_id=1, source_target_pairs={{0,2},{2,4},{4,6},{1,3},{3,5},{5,7},{8,10},{10,12},{12,14},{9,11},... | collective-permute-start | bytes 6291464 | tf_op jit(solution)/shard_map/ppermute | solution.py:171
  927.6 49.7 %collective-permute-start.62 = (bf16[4,256,1024]{2,1,0:T(8,128)(2,1)}, bf16[4,256,1024]{2,1,0:T(8,128)(2,1)}, u32[]{:S(2)}, u32[]{:S(2)}) collective-permute-start(bf16[4,256,1024]{2,1,0:T(8,128)(2,1)} %get-tuple-element.433.refs_0_), channel_id=1, source_target_pairs={{2,0},{4,2},{6,4},{3,1},{5,3},{7,5},{10,8},{12,10},{14,12},{11,9},... | collective-permute-start | bytes 6291464 | tf_op jit(solution)/shard_map/ppermute | solution.py:172
  978.7 56.0 %collective-permute-start.66 = (bf16[8,128,1024]{2,1,0:T(8,128)(2,1)}, bf16[8,128,1024]{2,1,0:T(8,128)(2,1)}, u32[]{:S(2)}, u32[]{:S(2)}) collective-permute-start(bf16[8,128,1024]{2,1,0:T(8,128)(2,1)} %get-tuple-element.452), channel_id=1, source_target_pairs={{0,2},{2,4},{4,6},{1,3},{3,5},{5,7},{8,10},{10,12},{12,14},{9,11},... | collective-permute-start | bytes 6291464 | tf_op jit(solution)/shard_map/ppermute | solution.py:208
  982.7 52.0 %collective-permute-start.67 = (bf16[8,128,1024]{2,1,0:T(8,128)(2,1)S(1)}, bf16[8,128,1024]{2,1,0:T(8,128)(2,1)}, u32[]{:S(2)}, u32[]{:S(2)}) collective-permute-start(bf16[8,128,1024]{2,1,0:T(8,128)(2,1)S(1)} %copy-done.94), channel_id=1, source_target_pairs={{6,4},{4,2},{2,0},{7,5},{5,3},{3,1},{14,12},{12,10},{10,8},{15,13}... | collective-permute-start | bytes 6291464 | tf_op jit(solution)/shard_map/ppermute | solution.py:209
  984.0 59.4 %collective-permute-start.64 = (bf16[4,256,1024]{2,1,0:T(8,128)(2,1)}, bf16[4,256,1024]{2,1,0:T(8,128)(2,1)S(1)}, u32[]{:S(2)}, u32[]{:S(2)}) collective-permute-start(bf16[4,256,1024]{2,1,0:T(8,128)(2,1)} %collective-permute-done.61.refs_1_), channel_id=1, source_target_pairs={{2,4},{4,6},{3,5},{5,7},{10,12},{12,14},{11,13},{13,15},{18,20},{2... | collective-permute-start | bytes 6291464 | tf_op jit(solution)/shard_map/ppermute | solution.py:171
  984.8 91.4 %collective-permute-start.65 = (bf16[4,256,1024]{2,1,0:T(8,128)(2,1)}, bf16[4,256,1024]{2,1,0:T(8,128)(2,1)}, u32[]{:S(2)}, u32[]{:S(2)}) collective-permute-start(bf16[4,256,1024]{2,1,0:T(8,128)(2,1)} %collective-permute-done.62.refs_6_), channel_id=1, source_target_pairs={{2,0},{4,2},{3,1},{5,3},{10,8},{12,10},{11,9},{13,11},{18,16},{20,... | collective-permute-start | bytes 6291464 | tf_op jit(solution)/shard_map/ppermute | solution.py:172
  (176 other events, 2701.4 us)
Sparse Core Ops, SparseCore 0:
  10.7 91.4 all-gather.4
  104.0 54.6 all-gather.6
  356.1 32.5 all-gather.8
  642.4 35.8 all-gather.10

commit v7 on v6

--- a/solution.py
+++ b/solution.py
@@ -176,6 +176,20 @@
         (up, down), rest = kept[0], kept[1:]
         self.up, self.down = self.up[:1] + list(up), self.down[:1] + list(down)
         return rest
+
+    def placed_early(self):
+        size, here = line_size()
+        steps = jnp.arange(size)
+        index = lax.rem(here - steps + size, size)
+        own = self.up[0]
+        blocks = self.up[: size - 1] + [own]
+        instead = [own] + self.down[1 : size - 1][::-1]
+        return place_line(index, here >= steps, blocks, instead)
+
+    def farthest(self, early):
+        size, here = line_size()
+        last = jnp.where(here == size - 1, self.up[size - 1], early[:, 0])
+        return jnp.where(here == 0, self.down[size - 1], last), jnp.where(here == 0, size - 1, 0)
 
     def placed(self):
         size, here = line_size()
@@ -744,6 +758,47 @@
         ),
         name="unmix_streams",
     )(*operands)
+
+
+def unmix_one(slot_mix, history, grads, micro_at, index, rows_mb, earlier):
+    slots, tokens, width = history.shape
+    rows = min(128, rows_mb)
+    per = rows_mb // rows
+
+    def row_block(i, m):
+        return (m[0] * MB + micro_at) * per + i
+
+    def kernel(at_ref, *refs):
+        unmix_kernel(slots, *refs)
+
+    return pl.pallas_call(
+        kernel,
+        grid_spec=pltpu.PrefetchScalarGridSpec(
+            num_scalar_prefetch=1,
+            grid=(per,),
+            in_specs=[
+                pl.BlockSpec((rows, slot_mix.shape[1]), lambda i, m: (row_block(i, m), 0)),
+                pl.BlockSpec((slots, rows, width), lambda i, m: (0, row_block(i, m), 0)),
+                pl.BlockSpec((STREAMS, rows, width), lambda i, m: (0, i, 0)),
+                pl.BlockSpec(memory_space=pl.ANY),
+            ],
+            out_specs=[
+                pl.BlockSpec((slots, rows, width), lambda i, m: (0, row_block(i, m), 0)),
+                pl.BlockSpec((rows, 128), lambda i, m: (i, 0)),
+            ],
+        ),
+        out_shape=[
+            jax.ShapeDtypeStruct((slots, tokens, width), bf16),
+            jax.ShapeDtypeStruct((rows_mb, 128), f32),
+        ],
+        input_output_aliases={4: 0},
+        cost_estimate=spent(
+            flops=4 * slots * STREAMS * rows_mb * width,
+            bytes_accessed=2 * (2 * slots + STREAMS) * rows_mb * width,
+            transcendentals=0,
+        ),
+        name="unmix_one",
+    )(index.astype(jnp.int32)[None], slot_mix, history, grads, earlier)
 
 
 def own_spans(model_ref, width):
@@ -1413,9 +1468,7 @@
     weights_line = LineGather(ff_rows)
     weights_line.step()
     cot_pieces = lax.all_gather(cotangent, "dp", axis=0, tiled=True)
-    over_depth, partial, partial_next, cot_pieces = weights_line.hold(
-        over_depth, partial, partial_next, cot_pieces
-    )
+    over_depth, partial, partial_next = weights_line.hold(over_depth, partial, partial_next)
     pieces = [over_depth]
     weights = place_block(None, pieces[0][None], place_index(0), dp_count)
     hops_left = [(p, at) for at in range(len(dp_bits)) for p in range(1 << at)]
@@ -1441,12 +1494,12 @@
         if last_hop:
             cot_full = join_halves(cotangent, other_core(cotangent), model_at)
             ff_weights = weights_line.placed()
-            cots = cot_full, cotangent, cot_pieces, ff_weights
+            cots = cot_full, cotangent, ff_weights
         (state,) = weights_line.hold(
-            (sums.up, sums.down, pieces, weights, cots, own_tables, tables)
+            (sums.up, sums.down, pieces, weights, cots, own_tables, tables, cot_pieces)
         )
-        sums.up, sums.down, pieces, weights, cots, own_tables, tables = state
-    cot_full, cotangent, cot_pieces, ff_weights = cots
+        sums.up, sums.down, pieces, weights, cots, own_tables, tables, cot_pieces = state
+    cot_full, cotangent, ff_weights = cots
     for place in range(placed, len(pieces)):
         weights = place_block(weights, pieces[place][None], place_index(place), dp_count)
     weights = weights.reshape(dp_count, depth_count, 4, own_rows, heads_width)
@@ -1535,20 +1588,22 @@
     by_head, ff_parts, cot_group = sums_next.hold(by_head, ff_parts, cot_group)
     by_head, ff_parts = sums_next.step(by_head, ff_parts)
     answer = attention(0, by_head)
+    answer, ff_parts = sums_next.hold(answer, ff_parts)
+
+    answer = over_depth_swap(answer)
+    second = enter(1, sums_next)
     near, far = group_split(ff_parts[0], other_core(ff_parts[1]), place_list)
     near = near + core_hop(far, len(dp_bits) - 1).astype(f32)
-    answer, near = sums_next.hold(answer, near)
-
-    answer = over_depth_swap(answer)
-    second = enter(1, sums_next)
-    answer, packed, ff_normed, ff_sum = fence(
-        answer, second["packed"], second["ff_normed"], group_back_rest(near)
+    answer, packed, ff_normed, near = fence(
+        answer, second["packed"], second["ff_normed"], near
     )
     by_head = over_depth_swap(packed)
     mine = group_rows(ff_normed)
     own, got, first["flat"] = back(first, answer)
-    grad_low = leave(0, first, own, got, ff_sum)
-    by_head, grad_low, mine = fence(by_head, grad_low, mine)
+    grad_low = leave(0, first, own, got, group_back_rest(near))
+    by_head, grad_low, mine, first["layer_rows"] = fence(
+        by_head, grad_low, mine, first["layer_rows"]
+    )
     saved = [first, second]
 
     def each(name):
@@ -1609,8 +1664,8 @@
     grad_low = leave(1, second, own, got, ff_sum)
     pieces = {p: place_grads(p, bf16 if p >= half else f32) for p in range(dp_count)}
     sums_hop()
-    (state,) = grad_line.hold((ff_sums.up, ff_sums.down, grad_low, pieces))
-    ff_sums.up, ff_sums.down, grad_low, pieces = state
+    (state,) = grad_line.hold((ff_sums.up, ff_sums.down, grad_low, pieces, second["layer_rows"]))
+    ff_sums.up, ff_sums.down, grad_low, pieces, second["layer_rows"] = state
 
     last_line = LineGather(grad_low)
     last_line.step()
@@ -1640,15 +1695,29 @@
                 swap_mask(ff_pieces[m], "dp", m) for m in range(1, dp_count)
             ]
             ff_sums.up = ff_sums.down = ff_pieces
-        (state,) = last_line.hold((out_sums.up, out_sums.down, ff_sums.up, ff_sums.down))
-        out_sums.up, out_sums.down, ff_sums.up, ff_sums.down = state
+            early = last_line.placed_early()
+            history_grad, slot_part = unmix_streams(
+                slot_mix,
+                history,
+                early.reshape(STREAMS, length, width),
+                1,
+                depth_count,
+                rows_mb,
+                history_grad,
+            )
+        (state,) = last_line.hold(
+            (out_sums.up, out_sums.down, ff_sums.up, ff_sums.down, history_grad, slot_part)
+        )
+        out_sums.up, out_sums.down, ff_sums.up, ff_sums.down, history_grad, slot_part = state
     out_sums.step()
     ff_pieces = ff_sums.up
-    last_grads = last_line.placed().reshape(STREAMS, length, width)
-    history_grad, slot_part = unmix_streams(
-        slot_mix, history, last_grads, 1, depth_count, rows_mb, history_grad
+    far_grads, far_index = last_line.farthest(early)
+    history_grad, far_part = unmix_one(
+        slot_mix, history, far_grads, 1, far_index, rows_mb, history_grad
     )
-    slot_parts.append(slot_part.reshape(depth_count, 1, rows_mb, 128))
+    slot_part = slot_part.reshape(depth_count, rows_mb, 128)
+    slot_part = lax.dynamic_update_index_in_dim(slot_part, far_part, far_index, 0)
+    slot_parts.append(slot_part[:, None])
 
     slot_grads = jnp.concatenate(slot_parts, axis=1).reshape(-1, 128)[:, : STREAMS * slots]
     mix_grads = dot_exact(slot_grads, pick.T).reshape(depth_count, MB * rows_mb, STREAMS * MIX)

time: 1270 us -> 1250 us (0.984)
  waiting for transfers between devices: 445 us -> 407 us
    ppermute x53, waiting for transfers between devices: 87.2 us -> 64.7 us  [swap_mask(): return lax.ppermute(values, axis, [(i, i ^ mask) for i in range(size)])]
    all_to_all x4, waiting for transfers between devices: 27 us -> 13.6 us  [over_depth_swap(): return lax.all_to_all(values, 'depth', 0, 0, tiled=True)]
    unnamed x194 -> x200, local copies, waits for them, and re-layouts: 48.7 us -> 47.5 us
  transfers between devices with their start and end apart: 105 -> 105, of which waited for: 52 -> 47; matrix products, arithmetic and copies ran while one was open for 8% -> 8% of each run, Pallas kernels for 32% -> 35%
where the time goes in v7:
time: 1250 us; the launch traced here: 1230 us
  Pallas kernels  465 us (37%)
  waiting for transfers between devices  407 us (33%)
  starting transfers between devices  185 us (15%)
  other arithmetic  74.3 us (6%)
  local copies, waits for them, and re-layouts  72.3 us (6%)
  between operations  15.9 us (1%)
    ppermute x8, waiting for transfers between devices, step(): self.up = lax.ppermute(goes_up, 'depth', up_pairs)  101 us
    ppermute x4, waiting for transfers between devices, step_with(): lax.ppermute(goes[0], 'depth', [(i, i + 1) for i in range(size - 1)])  83.7 us
    pallas_call x12, Pallas kernels, hop_sums(): pl.pallas_call(functools.partial(hop_kernel, up is not None, blocks is no...  82.8 us
    ppermute x53, waiting for transfers between devices, swap_mask(): return lax.ppermute(values, axis, [(i, i ^ mask) for i in range(size)])  64.7 us
    ppermute x10, waiting for transfers between devices, core_hop(): return lax.ppermute(values, ('dp', 'mp'), pairs)  62.3 us
    ppermute x8, starting transfers between devices, step(): self.up = lax.ppermute(goes_up, 'depth', up_pairs)  53.9 us
    ppermute x53, starting transfers between devices, swap_mask(): return lax.ppermute(values, axis, [(i, i ^ mask) for i in range(size)])  48.5 us
    pallas_call x2, Pallas kernels, feed_forward(): pl.pallas_call(ff_kernel, grid_spec=pltpu.PrefetchScalarGridSpec(num_scal...  48.2 us
  transfers between devices with their start and end apart: 105, of which 47 were waited for; matrix products, arithmetic and copies ran while one was open for 8% of the time, Pallas kernels for 35%

profile of v7, /device:TPU:0, one launch (start us, length us, event | category | flops | bytes accessed | tf_op | source)
XLA Modules:
  0.0 1232.3 jit_solution(4477083545011296852)
XLA Ops:
  99.7 14.4 %mix_streams.2 = bf16[4,1024,1024]{2,1,0:T(8,128)(2,1)} custom-call(f32[2048,20]{1,0:T(8,128)} %copy.101.mix_ref.refs_0_, bf16[5,2048,1024]{2,1,0:T(8,128)(2,1)} %refs_1_.1), custom_call_target="tpu_custom_call" | custom-call | flops 2097152 | bytes 943718 | tf_op jit(solution)/shard_map/mix_streams/pallas_call | solution.py:666
  114.0 14.4 %mix_streams.3 = bf16[4,1024,1024]{2,1,0:T(8,128)(2,1)} custom-call(f32[2048,20]{1,0:T(8,128)} %copy.101.mix_ref.refs_0_, bf16[5,2048,1024]{2,1,0:T(8,128)(2,1)} %refs_1_.1), custom_call_target="tpu_custom_call" | custom-call | flops 2097152 | bytes 943718 | tf_op jit(solution)/shard_map/mix_streams/pallas_call | solution.py:666
  128.4 13.0 %collective-permute-done.21.refs_1_ = bf16[8,128,1024]{2,1,0:T(8,128)(2,1)S(1)} collective-permute-done((bf16[8,128,1024]{2,1,0:T(8,128)(2,1)}, bf16[8,128,1024]{2,1,0:T(8,128)(2,1)S(1)}, u32[]{:S(2)}, u32[]{:S(2)}) %collective-permute-start.21) | collective-permute-done | bytes 2097184 | tf_op jit(solution)/shard_map/ppermute | solution.py:171
  173.8 26.5 %collective-permute-done.23.refs_2_ = bf16[4,256,1024]{2,1,0:T(8,128)(2,1)S(1)} collective-permute-done((bf16[4,256,1024]{2,1,0:T(8,128)(2,1)}, bf16[4,256,1024]{2,1,0:T(8,128)(2,1)S(1)}, u32[]{:S(2)}, u32[]{:S(2)}) %collective-permute-start.23) | collective-permute-done | bytes 2097184 | tf_op jit(solution)/shard_map/ppermute | solution.py:249
  225.6 36.8 %collective-permute-done.26.refs_2_ = bf16[4,256,1024]{2,1,0:T(8,128)(2,1)S(1)} collective-permute-done((bf16[4,256,1024]{2,1,0:T(8,128)(2,1)}, bf16[4,256,1024]{2,1,0:T(8,128)(2,1)S(1)}, u32[]{:S(2)}, u32[]{:S(2)}) %collective-permute-start.26) | collective-permute-done | bytes 2097184 | tf_op jit(solution)/shard_map/ppermute | solution.py:249
  356.9 10.0 project_heads.2
  366.9 24.2 %collective-permute-done.33.refs_2_ = bf16[4,256,1024]{2,1,0:T(8,128)(2,1)} collective-permute-done((bf16[4,256,1024]{2,1,0:T(8,128)(2,1)}, bf16[4,256,1024]{2,1,0:T(8,128)(2,1)}, u32[]{:S(2)}, u32[]{:S(2)}) %collective-permute-start.33) | collective-permute-done | bytes 2097184 | tf_op jit(solution)/shard_map/ppermute | solution.py:222
  423.9 24.1 %feed_forward.2 = (bf16[1024,1024]{1,0:T(8,128)(2,1)S(1)}, bf16[1024,1024]{1,0:T(8,128)(2,1)S(1)}, f32[2,1024,1024]{2,1,0:T(8,128)}, bf16[2,1024,1024]{2,1,0:T(8,128)(2,1)}) custom-call(s32[1]{0:T(128)} %bitcast.72.model_ref.half_ref, bf16[1024,2048]{1,0:T(8,128)(2,1)} %join_halves.5.x_ref.x0_ref, bf16[4,2,256,2048]{3,2,1,0:T(8,128)(2,1)} %bitcast.391, ...), custom_call_target="tpu_custom_call" | custom-call | flops 858993472 | bytes 2097152 | tf_op jit(solution)/shard_map/feed_forward/pallas_call | solution.py:1138
  450.6 32.0 %collective-permute-done.36.refs_2_ = bf16[4,256,1024]{2,1,0:T(8,128)(2,1)} collective-permute-done((bf16[4,256,1024]{2,1,0:T(8,128)(2,1)}, bf16[4,256,1024]{2,1,0:T(8,128)(2,1)}, u32[]{:S(2)}, u32[]{:S(2)}) %collective-permute-start.36) | collective-permute-done | bytes 2097184 | tf_op jit(solution)/shard_map/ppermute | solution.py:222
  490.6 18.1 %collective-permute-start.40 = (bf16[4,256,1024]{2,1,0:T(8,128)(2,1)}, bf16[4,256,1024]{2,1,0:T(8,128)(2,1)}, u32[]{:S(2)}, u32[]{:S(2)}) collective-permute-start(bf16[4,256,1024]{2,1,0:T(8,128)(2,1)} %get-tuple-element.360), channel_id=1, source_target_pairs={{0,2},{2,4},{4,6},{1,3},{3,5},{5,7},{8,10},{10,12},{12,14},{9,11},... | collective-permute-start | bytes 6291464 | tf_op jit(solution)/shard_map/ppermute | solution.py:222
  510.3 10.7 attend.2
  522.4 29.7 %collective-permute-done.40.up_ref = bf16[4,256,1024]{2,1,0:T(8,128)(2,1)} collective-permute-done((bf16[4,256,1024]{2,1,0:T(8,128)(2,1)}, bf16[4,256,1024]{2,1,0:T(8,128)(2,1)}, u32[]{:S(2)}, u32[]{:S(2)}) %collective-permute-start.40) | collective-permute-done | bytes 2097184 | tf_op jit(solution)/shard_map/ppermute | solution.py:222
  630.8 10.7 collective-permute-done.46
  671.2 10.7 attend.3
  688.0 24.1 %feed_forward.3 = (bf16[1024,1024]{1,0:T(8,128)(2,1)S(1)}, bf16[1024,1024]{1,0:T(8,128)(2,1)S(1)}, f32[2,1024,1024]{2,1,0:T(8,128)}, bf16[2,1024,1024]{2,1,0:T(8,128)(2,1)}) custom-call(s32[1]{0:T(128)} %bitcast.72.model_ref.half_ref, bf16[1024,2048]{1,0:T(8,128)(2,1)} %join_halves.7.x_ref.x1_ref, bf16[4,2,256,2048]{3,2,1,0:T(8,128)(2,1)} %bitcast.392, ...), custom_call_target="tpu_custom_call" | custom-call | flops 858993472 | bytes 2097152 | tf_op jit(solution)/shard_map/feed_forward/pallas_call | solution.py:1138
  735.4 24.3 %hidden_grads.1.refs_0_.refs_1_.term_ref = f32[8,4,128,1024]{3,2,1,0:T(8,128)} custom-call(bf16[1024,2048]{1,0:T(8,128)(2,1)} %join_halves.5.x_ref.x0_ref, bf16[1024,2048]{1,0:T(8,128)(2,1)} %join_halves.7.x_ref.x1_ref, bf16[4,2,256,2048]{3,2,1,0:T(8,128)(2,1)} %bitcast.393, bf16[4,2,256,2048]{3,2,1,0:T(8,128)(2,1)} %bitcast.394, ...), custom_call_target="tpu_custom_call" | custom-call | flops 858993472 | bytes 838860 | tf_op jit(solution)/shard_map/hidden_grads/pallas_call | solution.py:614
  806.1 20.4 %collective-permute-done.53.refs_2_ = bf16[8,128,1024]{2,1,0:T(8,128)(2,1)S(1)} collective-permute-done((bf16[8,128,1024]{2,1,0:T(8,128)(2,1)}, bf16[8,128,1024]{2,1,0:T(8,128)(2,1)S(1)}, u32[]{:S(2)}, u32[]{:S(2)}) %collective-permute-start.53) | collective-permute-done | bytes 2097184 | tf_op jit(solution)/shard_map/ppermute | solution.py:249
  836.0 10.8 hop_sums.19
  889.3 10.2 convert_add_fusion.2
  908.1 9.0 hop_sums.20
  929.4 19.5 %unmix_streams.2 = (bf16[5,2048,1024]{2,1,0:T(8,128)(2,1)}, f32[1024,128]{1,0:T(8,128)}) custom-call(f32[2048,20]{1,0:T(8,128)} %copy.101.mix_ref.refs_0_, bf16[5,2048,1024]{2,1,0:T(8,128)(2,1)} %refs_1_.1, bf16[4,1024,1024]{2,1,0:T(8,128)(2,1)} %bitcast.400), custom_call_target="tpu_custom_call" | custom-call | flops 4194304 | bytes 1468006 | tf_op jit(solution)/shard_map/unmix_streams/pallas_call | solution.py:741
  967.3 38.0 %collective-permute-done.68 = bf16[4,4,128,1024]{3,2,1,0:T(8,128)(2,1)S(1)} collective-permute-done((bf16[4,4,128,1024]{3,2,1,0:T(8,128)(2,1)S(1)}, bf16[4,4,128,1024]{3,2,1,0:T(8,128)(2,1)S(1)}, u32[]{:S(2)}, u32[]{:S(2)}) %collective-permute-start.68) | collective-permute-done | bytes 4194336 | tf_op jit(solution)/shard_map/ppermute | solution.py:105
  1024.3 31.9 %collective-permute-done.65.refs_5_ = bf16[4,256,1024]{2,1,0:T(8,128)(2,1)} collective-permute-done((bf16[4,256,1024]{2,1,0:T(8,128)(2,1)}, bf16[4,256,1024]{2,1,0:T(8,128)(2,1)}, u32[]{:S(2)}, u32[]{:S(2)}) %collective-permute-start.65) | collective-permute-done | bytes 2097184 | tf_op jit(solution)/shard_map/ppermute | solution.py:172
  1093.9 19.5 %unmix_streams.3 = (bf16[5,2048,1024]{2,1,0:T(8,128)(2,1)}, f32[1024,128]{1,0:T(8,128)}) custom-call(f32[2048,20]{1,0:T(8,128)} %copy.101.mix_ref.refs_0_, bf16[5,2048,1024]{2,1,0:T(8,128)(2,1)} %refs_1_.1, bf16[4,1024,1024]{2,1,0:T(8,128)(2,1)} %bitcast.399, bf16[5,2048,1024]{2,1,0:T(8,128)(2,1)} %get-tuple-element.482.rest_0_), custom_call_target="tpu_custom_call", output_to_operand_aliasing={{0}: (3, {})} | custom-call | flops 4194304 | bytes 1468006 | tf_op jit(solution)/shard_map/unmix_streams/pallas_call | solution.py:741
  (613 shorter events, 733.1 us)
Async XLA Ops:
  7.2 139.5 %all-gather.5.cloned.1.call-start = ((), (), s32[]{:S(2)}) async-start(), calls=%async_computation.4 | async-start | bytes 5242880 | tf_op jit(solution)/shard_map/all_gather | solution.py:1434
  10.5 163.3 %all-gather.7.cloned.1.call-start = ((), (), s32[]{:S(2)}) async-start(), calls=%async_computation.5 | async-start | bytes 5242880 | tf_op jit(solution)/shard_map/all_gather | solution.py:1470
  98.3 292.8 %all-gather.9.cloned.1.call-start = ((), (), s32[]{:S(2)}) async-start(), calls=%async_computation.6 | async-start | bytes 2621440 | tf_op jit(solution)/shard_map/all_gather | solution.py:1537
  146.7 57.9 %collective-permute-start.25 = (bf16[2048,1024]{1,0:T(8,128)(2,1)}, bf16[2048,1024]{1,0:T(8,128)(2,1)}, u32[]{:S(2)}, u32[]{:S(2)}) collective-permute-start(bf16[2048,1024]{1,0:T(8,128)(2,1)} %all-gather.5.cloned.1.call-done), channel_id=1, source_target_pairs={{0,8},{1,17},{8,0},{9,25},{16,24},{17,1},{24,16},{25,9},{2,10},{3,... | collective-permute-start | bytes 12582920 | tf_op jit(solution)/shard_map/ppermute | solution.py:105
  204.6 62.1 %collective-permute-start.28 = (bf16[2048,1024]{1,0:T(8,128)(2,1)}, bf16[2048,1024]{1,0:T(8,128)(2,1)}, u32[]{:S(2)}, u32[]{:S(2)}) collective-permute-start(bf16[2048,1024]{1,0:T(8,128)(2,1)} %all-gather.5.cloned.1.call-done), channel_id=1, source_target_pairs={{0,16},{1,9},{8,24},{9,1},{16,0},{17,25},{24,8},{25,17},{2,18},{3,... | collective-permute-start | bytes 12582920 | tf_op jit(solution)/shard_map/ppermute | solution.py:105
  266.6 58.8 %collective-permute-start.31 = (bf16[2048,1024]{1,0:T(8,128)(2,1)}, bf16[2048,1024]{1,0:T(8,128)(2,1)}, u32[]{:S(2)}, u32[]{:S(2)}) collective-permute-start(bf16[2048,1024]{1,0:T(8,128)(2,1)} %collective-permute-done.25), channel_id=1, source_target_pairs={{0,16},{1,9},{8,24},{9,1},{16,0},{17,25},{24,8},{25,17},{2,18},{3,... | collective-permute-start | bytes 12582920 | tf_op jit(solution)/shard_map/ppermute | solution.py:105
  397.6 85.1 %all-to-all-start = ((bf16[4,256,1024]{2,1,0:T(8,128)(2,1)}), bf16[4,256,1024]{2,1,0:T(8,128)(2,1)S(1)}, u32[]{:S(2)}, u32[]{:S(2)}) async-start(bf16[4,256,1024]{2,1,0:T(8,128)(2,1)} %project_heads.2), calls=%async_computation | async-start | bytes 4194304 | tf_op jit(solution)/shard_map/all_to_all | solution.py:1458
  403.3 79.4 %collective-permute-start.36 = (bf16[4,256,1024]{2,1,0:T(8,128)(2,1)}, bf16[4,256,1024]{2,1,0:T(8,128)(2,1)}, u32[]{:S(2)}, u32[]{:S(2)}) collective-permute-start(bf16[4,256,1024]{2,1,0:T(8,128)(2,1)} %get-tuple-element.345), channel_id=1, source_target_pairs={{0,2},{2,4},{1,3},{3,5},{8,10},{10,12},{9,11},{11,13},{16,18},{18,... | collective-permute-start | bytes 6291464 | tf_op jit(solution)/shard_map/ppermute | solution.py:222
  408.3 74.4 %collective-permute-start.37 = (bf16[4,256,1024]{2,1,0:T(8,128)(2,1)}, bf16[4,256,1024]{2,1,0:T(8,128)(2,1)}, u32[]{:S(2)}, u32[]{:S(2)}) collective-permute-start(bf16[4,256,1024]{2,1,0:T(8,128)(2,1)} %get-tuple-element.346), channel_id=1, source_target_pairs={{6,4},{4,2},{7,5},{5,3},{14,12},{12,10},{15,13},{13,11},{22,20},{2... | collective-permute-start | bytes 6291464 | tf_op jit(solution)/shard_map/ppermute | solution.py:223
  490.6 61.5 %collective-permute-start.40 = (bf16[4,256,1024]{2,1,0:T(8,128)(2,1)}, bf16[4,256,1024]{2,1,0:T(8,128)(2,1)}, u32[]{:S(2)}, u32[]{:S(2)}) collective-permute-start(bf16[4,256,1024]{2,1,0:T(8,128)(2,1)} %get-tuple-element.360), channel_id=1, source_target_pairs={{0,2},{2,4},{4,6},{1,3},{3,5},{5,7},{8,10},{10,12},{12,14},{9,11},... | collective-permute-start | bytes 6291464 | tf_op jit(solution)/shard_map/ppermute | solution.py:222
  557.6 52.9 %all-to-all-start.1 = ((bf16[4,256,1024]{2,1,0:T(8,128)(2,1)}), bf16[4,256,1024]{2,1,0:T(8,128)(2,1)S(1)}, u32[]{:S(2)}, u32[]{:S(2)}) async-start(bf16[4,256,1024]{2,1,0:T(8,128)(2,1)} %bitcast.336), calls=%async_computation.1 | async-start | bytes 4194304 | tf_op jit(solution)/shard_map/all_to_all | solution.py:1458
  610.5 52.9 %all-to-all-start.2 = ((bf16[4,256,1024]{2,1,0:T(8,128)(2,1)}), bf16[4,256,1024]{2,1,0:T(8,128)(2,1)}, u32[]{:S(2)}, u32[]{:S(2)}) async-start(bf16[4,256,1024]{2,1,0:T(8,128)(2,1)} %copy-done.26), calls=%async_computation.2 | async-start | bytes 4194304 | tf_op jit(solution)/shard_map/all_to_all | solution.py:1458
  663.4 51.4 %collective-permute-start.48 = (bf16[4,256,1024]{2,1,0:T(8,128)(2,1)}, bf16[4,256,1024]{2,1,0:T(8,128)(2,1)S(1)}, u32[]{:S(2)}, u32[]{:S(2)}) collective-permute-start(bf16[4,256,1024]{2,1,0:T(8,128)(2,1)} %get-tuple-element.390.refs_0_), channel_id=1, source_target_pairs={{0,2},{2,4},{4,6},{1,3},{3,5},{5,7},{8,10},{10,12},{12,14},{9,11},... | collective-permute-start | bytes 6291464 | tf_op jit(solution)/shard_map/ppermute | solution.py:171
  716.1 55.1 %all-to-all-start.3 = ((bf16[4,256,1024]{2,1,0:T(8,128)(2,1)}), bf16[4,256,1024]{2,1,0:T(8,128)(2,1)S(1)}, u32[]{:S(2)}, u32[]{:S(2)}) async-start(bf16[4,256,1024]{2,1,0:T(8,128)(2,1)} %bitcast.337), calls=%async_computation.3 | async-start | bytes 4194304 | tf_op jit(solution)/shard_map/all_to_all | solution.py:1458
  835.3 54.1 %collective-permute-start.60 = (bf16[4,4,128,1024]{3,2,1,0:T(8,128)(2,1)}, bf16[4,4,128,1024]{3,2,1,0:T(8,128)(2,1)}, u32[]{:S(2)}, u32[]{:S(2)}) collective-permute-start(bf16[4,4,128,1024]{3,2,1,0:T(8,128)(2,1)} %attention_grads.5), channel_id=1, source_target_pairs={{0,16},{1,9},{8,24},{9,1},{16,0},{17,25},{24,8},{25,17},{2,18},{3,... | collective-permute-start | bytes 12582920 | tf_op jit(solution)/shard_map/ppermute | solution.py:105
  846.9 52.7 %collective-permute-start.57 = (bf16[8,128,1024]{2,1,0:T(8,128)(2,1)}, bf16[8,128,1024]{2,1,0:T(8,128)(2,1)}, u32[]{:S(2)}, u32[]{:S(2)}) collective-permute-start(bf16[8,128,1024]{2,1,0:T(8,128)(2,1)} %get-tuple-element.428), channel_id=1, source_target_pairs={{0,2},{2,4},{4,6},{1,3},{3,5},{5,7},{8,10},{10,12},{12,14},{9,11},... | collective-permute-start | bytes 6291464 | tf_op jit(solution)/shard_map/ppermute | solution.py:249
  900.9 54.4 %collective-permute-start.61 = (bf16[4,256,1024]{2,1,0:T(8,128)(2,1)S(1)}, bf16[4,256,1024]{2,1,0:T(8,128)(2,1)}, u32[]{:S(2)}, u32[]{:S(2)}) collective-permute-start(bf16[4,256,1024]{2,1,0:T(8,128)(2,1)S(1)} %copy-done.13), channel_id=1, source_target_pairs={{0,2},{2,4},{4,6},{1,3},{3,5},{5,7},{8,10},{10,12},{12,14},{9,11},... | collective-permute-start | bytes 6291464 | tf_op jit(solution)/shard_map/ppermute | solution.py:171
  906.8 50.0 %collective-permute-start.62 = (bf16[4,256,1024]{2,1,0:T(8,128)(2,1)S(1)}, bf16[4,256,1024]{2,1,0:T(8,128)(2,1)}, u32[]{:S(2)}, u32[]{:S(2)}) collective-permute-start(bf16[4,256,1024]{2,1,0:T(8,128)(2,1)S(1)} %copy-done.13), channel_id=1, source_target_pairs={{2,0},{4,2},{6,4},{3,1},{5,3},{7,5},{10,8},{12,10},{14,12},{11,9},... | collective-permute-start | bytes 6291464 | tf_op jit(solution)/shard_map/ppermute | solution.py:172
  957.0 57.1 %collective-permute-start.66 = (bf16[8,128,1024]{2,1,0:T(8,128)(2,1)}, bf16[8,128,1024]{2,1,0:T(8,128)(2,1)}, u32[]{:S(2)}, u32[]{:S(2)}) collective-permute-start(bf16[8,128,1024]{2,1,0:T(8,128)(2,1)} %get-tuple-element.461), channel_id=1, source_target_pairs={{0,2},{2,4},{4,6},{1,3},{3,5},{5,7},{8,10},{10,12},{12,14},{9,11},... | collective-permute-start | bytes 6291464 | tf_op jit(solution)/shard_map/ppermute | solution.py:222
  962.7 51.4 %collective-permute-start.67 = (bf16[8,128,1024]{2,1,0:T(8,128)(2,1)S(1)}, bf16[8,128,1024]{2,1,0:T(8,128)(2,1)}, u32[]{:S(2)}, u32[]{:S(2)}) collective-permute-start(bf16[8,128,1024]{2,1,0:T(8,128)(2,1)S(1)} %copy-done.97), channel_id=1, source_target_pairs={{6,4},{4,2},{2,0},{7,5},{5,3},{3,1},{14,12},{12,10},{10,8},{15,13}... | collective-permute-start | bytes 6291464 | tf_op jit(solution)/shard_map/ppermute | solution.py:223
  964.0 60.3 %collective-permute-start.64 = (bf16[4,256,1024]{2,1,0:T(8,128)(2,1)}, bf16[4,256,1024]{2,1,0:T(8,128)(2,1)}, u32[]{:S(2)}, u32[]{:S(2)}) collective-permute-start(bf16[4,256,1024]{2,1,0:T(8,128)(2,1)} %collective-permute-done.61.refs_1_), channel_id=1, source_target_pairs={{2,4},{4,6},{3,5},{5,7},{10,12},{12,14},{11,13},{13,15},{18,20},{2... | collective-permute-start | bytes 6291464 | tf_op jit(solution)/shard_map/ppermute | solution.py:171
  966.0 90.3 %collective-permute-start.65 = (bf16[4,256,1024]{2,1,0:T(8,128)(2,1)}, bf16[4,256,1024]{2,1,0:T(8,128)(2,1)}, u32[]{:S(2)}, u32[]{:S(2)}) collective-permute-start(bf16[4,256,1024]{2,1,0:T(8,128)(2,1)} %collective-permute-done.62.refs_6_), channel_id=1, source_target_pairs={{2,0},{4,2},{3,1},{5,3},{10,8},{12,10},{11,9},{13,11},{18,16},{20,... | collective-permute-start | bytes 6291464 | tf_op jit(solution)/shard_map/ppermute | solution.py:172
  1056.3 57.2 %collective-permute-start.71 = (bf16[4,256,1024]{2,1,0:T(8,128)(2,1)}, bf16[4,256,1024]{2,1,0:T(8,128)(2,1)}, u32[]{:S(2)}, u32[]{:S(2)}) collective-permute-start(bf16[4,256,1024]{2,1,0:T(8,128)(2,1)} %collective-permute-done.64.refs_2_), channel_id=1, source_target_pairs={{4,6},{5,7},{12,14},{13,15},{20,22},{21,23},{28,30},{29,31}} | collective-permute-start | bytes 6291464 | tf_op jit(solution)/shard_map/ppermute | solution.py:171
  1058.3 55.2 %collective-permute-start.72 = (bf16[4,256,1024]{2,1,0:T(8,128)(2,1)}, bf16[4,256,1024]{2,1,0:T(8,128)(2,1)}, u32[]{:S(2)}, u32[]{:S(2)}) collective-permute-start(bf16[4,256,1024]{2,1,0:T(8,128)(2,1)} %collective-permute-done.65.refs_5_), channel_id=1, source_target_pairs={{2,0},{3,1},{10,8},{11,9},{18,16},{19,17},{26,24},{27,25}} | collective-permute-start | bytes 6291464 | tf_op jit(solution)/shard_map/ppermute | solution.py:172
  (179 other events, 2703.8 us)
Sparse Core Ops, SparseCore 0:
  10.7 91.4 all-gather.4
  104.0 59.6 all-gather.6
  342.6 33.6 all-gather.8
  617.9 39.0 all-gather.10

commit v8 on v7

--- a/solution.py
+++ b/solution.py
@@ -592,7 +592,7 @@
 
 def hidden_grad_kernel(x0_ref, x1_ref, c0_ref, c1_ref, u0_ref, u1_ref, h0_ref, h1_ref, out_ref):
     def store(total):
-        out_ref[...] = total.reshape(out_ref.shape)
+        out_ref[...] = total.reshape(out_ref.shape).astype(bf16)
 
     @pl.when(pl.program_id(0) == 0)
     def _():
@@ -624,7 +624,7 @@
             (1, depth_count, block // depth_count, part), lambda k, n: (k * dp_count + n, 0, 0, 0)
         ),
         out_shape=jax.ShapeDtypeStruct(
-            (2 * dp_count, depth_count, block // depth_count, part), f32
+            (2 * dp_count, depth_count, block // depth_count, part), bf16
         ),
         compiler_params=pltpu.CompilerParams(vmem_limit_bytes=48 << 20),
         cost_estimate=spent(
@@ -1662,10 +1662,10 @@
         ff_sums.up, ff_sums.down = state
     (ff_sum,) = ff_sums.step_with(grad_line, ff_sum)
     grad_low = leave(1, second, own, got, ff_sum)
-    pieces = {p: place_grads(p, bf16 if p >= half else f32) for p in range(dp_count)}
+    pieces = {p: place_grads(p, bf16) for p in range(dp_count)}
     sums_hop()
-    (state,) = grad_line.hold((ff_sums.up, ff_sums.down, grad_low, pieces, second["layer_rows"]))
-    ff_sums.up, ff_sums.down, grad_low, pieces, second["layer_rows"] = state
+    (state,) = grad_line.hold((ff_sums.up, ff_sums.down, grad_low, pieces))
+    ff_sums.up, ff_sums.down, grad_low, pieces = state
 
     last_line = LineGather(grad_low)
     last_line.step()
@@ -1676,7 +1676,9 @@
         slot_mix, history, grad_first, 0, depth_count, rows_mb, None
     )
     slot_parts = [slot_part.reshape(depth_count, 1, rows_mb, 128)]
-    pieces, history_grad = last_line.hold(pieces, history_grad)
+    pieces, history_grad, second["layer_rows"] = last_line.hold(
+        pieces, history_grad, second["layer_rows"]
+    )
     (pieces,) = ff_sums.step(pieces)
     while hops_left:
         sums_hop()
@@ -1684,17 +1686,9 @@
     out_sums = LineScatter(pieces[0].reshape(1, depth_count, 4 * own_rows, heads_width))
     for hop in range(2, depth_count):
         last_line.step()
-        out_sums.step()
+        ((ff_sums.up, ff_sums.down),) = out_sums.step((ff_sums.up, ff_sums.down))
         if hop == depth_count - 1:
-            ff_grads = end_sums(ff_sums, bf16).reshape(2, dp_count, own_rows, ff_part)
-            ff_pieces = [
-                lax.dynamic_index_in_dim(ff_grads, partners[m], 1, keepdims=False)
-                for m in range(dp_count)
-            ]
-            ff_pieces = ff_pieces[:1] + [
-                swap_mask(ff_pieces[m], "dp", m) for m in range(1, dp_count)
-            ]
-            ff_sums.up = ff_sums.down = ff_pieces
+            ff_sums.up = ff_sums.down = end_sums(ff_sums, bf16)
             early = last_line.placed_early()
             history_grad, slot_part = unmix_streams(
                 slot_mix,
@@ -1709,8 +1703,12 @@
             (out_sums.up, out_sums.down, ff_sums.up, ff_sums.down, history_grad, slot_part)
         )
         out_sums.up, out_sums.down, ff_sums.up, ff_sums.down, history_grad, slot_part = state
-    out_sums.step()
-    ff_pieces = ff_sums.up
+    early, ff_grads = out_sums.step(early, ff_sums.up)
+    ff_grads = ff_grads.reshape(2, dp_count, own_rows, ff_part)
+    ff_pieces = [
+        lax.dynamic_index_in_dim(ff_grads, partners[m], 1, keepdims=False) for m in range(dp_count)
+    ]
+    ff_pieces = ff_pieces[:1] + [swap_mask(ff_pieces[m], "dp", m) for m in range(1, dp_count)]
     far_grads, far_index = last_line.farthest(early)
     history_grad, far_part = unmix_one(
         slot_mix, history, far_grads, 1, far_index, rows_mb, history_grad

time: 1250 us -> 1230 us (0.984)
    unnamed x200 -> x212, local copies, waits for them, and re-layouts: 47.5 us -> 48.9 us
  transfers between devices with their start and end apart: 105 -> 105, of which waited for: 47 -> 45; matrix products, arithmetic and copies ran while one was open for 8% -> 8% of each run, Pallas kernels for 35% -> 34%
where the time goes in v8:
time: 1230 us; the launch traced here: 1220 us
  Pallas kernels  461 us (37%)
  waiting for transfers between devices  402 us (33%)
  starting transfers between devices  180 us (15%)
  local copies, waits for them, and re-layouts  73.7 us (6%)
  other arithmetic  73.2 us (6%)
  between operations  16 us (1%)
  matrix products  12.3 us (1%)
    ppermute x8, waiting for transfers between devices, step(): self.up = lax.ppermute(goes_up, 'depth', up_pairs)  93.7 us
    ppermute x4, waiting for transfers between devices, step_with(): lax.ppermute(goes[0], 'depth', [(i, i + 1) for i in range(size - 1)])  89.6 us
    pallas_call x12, Pallas kernels, hop_sums(): pl.pallas_call(functools.partial(hop_kernel, up is not None, blocks is no...  80 us
    ppermute x10, waiting for transfers between devices, core_hop(): return lax.ppermute(values, ('dp', 'mp'), pairs)  63.4 us
    ppermute x53, waiting for transfers between devices, swap_mask(): return lax.ppermute(values, axis, [(i, i ^ mask) for i in range(size)])  57.6 us
    ppermute x8, starting transfers between devices, step(): self.up = lax.ppermute(goes_up, 'depth', up_pairs)  50 us
    unnamed x212, local copies, waits for them, and re-layouts  48.9 us
    ppermute x53, starting transfers between devices, swap_mask(): return lax.ppermute(values, axis, [(i, i ^ mask) for i in range(size)])  48.6 us
  transfers between devices with their start and end apart: 105, of which 45 were waited for; matrix products, arithmetic and copies ran while one was open for 8% of the time, Pallas kernels for 34%

profile of v8, /device:TPU:0, one launch (start us, length us, event | category | flops | bytes accessed | tf_op | source)
XLA Modules:
  0.0 1217.2 jit_solution(2805437057699130232)
XLA Ops:
  99.6 14.3 %mix_streams.2 = bf16[4,1024,1024]{2,1,0:T(8,128)(2,1)} custom-call(f32[2048,20]{1,0:T(8,128)} %copy.101.mix_ref.refs_0_, bf16[5,2048,1024]{2,1,0:T(8,128)(2,1)} %refs_1_.1), custom_call_target="tpu_custom_call" | custom-call | flops 2097152 | bytes 943718 | tf_op jit(solution)/shard_map/mix_streams/pallas_call | solution.py:666
  113.9 14.4 %mix_streams.3 = bf16[4,1024,1024]{2,1,0:T(8,128)(2,1)} custom-call(f32[2048,20]{1,0:T(8,128)} %copy.101.mix_ref.refs_0_, bf16[5,2048,1024]{2,1,0:T(8,128)(2,1)} %refs_1_.1), custom_call_target="tpu_custom_call" | custom-call | flops 2097152 | bytes 943718 | tf_op jit(solution)/shard_map/mix_streams/pallas_call | solution.py:666
  128.3 12.8 %collective-permute-done.21.refs_1_ = bf16[8,128,1024]{2,1,0:T(8,128)(2,1)S(1)} collective-permute-done((bf16[8,128,1024]{2,1,0:T(8,128)(2,1)}, bf16[8,128,1024]{2,1,0:T(8,128)(2,1)S(1)}, u32[]{:S(2)}, u32[]{:S(2)}) %collective-permute-start.21) | collective-permute-done | bytes 2097184 | tf_op jit(solution)/shard_map/ppermute | solution.py:171
  174.4 25.9 %collective-permute-done.23.refs_2_ = bf16[4,256,1024]{2,1,0:T(8,128)(2,1)S(1)} collective-permute-done((bf16[4,256,1024]{2,1,0:T(8,128)(2,1)}, bf16[4,256,1024]{2,1,0:T(8,128)(2,1)S(1)}, u32[]{:S(2)}, u32[]{:S(2)}) %collective-permute-start.23) | collective-permute-done | bytes 2097184 | tf_op jit(solution)/shard_map/ppermute | solution.py:249
  225.6 36.8 %collective-permute-done.26.refs_2_ = bf16[4,256,1024]{2,1,0:T(8,128)(2,1)S(1)} collective-permute-done((bf16[4,256,1024]{2,1,0:T(8,128)(2,1)}, bf16[4,256,1024]{2,1,0:T(8,128)(2,1)S(1)}, u32[]{:S(2)}, u32[]{:S(2)}) %collective-permute-start.26) | collective-permute-done | bytes 2097184 | tf_op jit(solution)/shard_map/ppermute | solution.py:249
  356.5 10.0 project_heads.2
  366.6 24.1 %collective-permute-done.33.refs_2_ = bf16[4,256,1024]{2,1,0:T(8,128)(2,1)} collective-permute-done((bf16[4,256,1024]{2,1,0:T(8,128)(2,1)}, bf16[4,256,1024]{2,1,0:T(8,128)(2,1)}, u32[]{:S(2)}, u32[]{:S(2)}) %collective-permute-start.33) | collective-permute-done | bytes 2097184 | tf_op jit(solution)/shard_map/ppermute | solution.py:222
  423.5 24.1 %feed_forward.2 = (bf16[1024,1024]{1,0:T(8,128)(2,1)S(1)}, bf16[1024,1024]{1,0:T(8,128)(2,1)S(1)}, f32[2,1024,1024]{2,1,0:T(8,128)}, bf16[2,1024,1024]{2,1,0:T(8,128)(2,1)}) custom-call(s32[1]{0:T(128)} %bitcast.72.model_ref.half_ref, bf16[1024,2048]{1,0:T(8,128)(2,1)} %join_halves.5.x_ref.x0_ref, bf16[4,2,256,2048]{3,2,1,0:T(8,128)(2,1)} %bitcast.385, ...), custom_call_target="tpu_custom_call" | custom-call | flops 858993472 | bytes 2097152 | tf_op jit(solution)/shard_map/feed_forward/pallas_call | solution.py:1138
  450.2 32.0 %collective-permute-done.36.refs_2_ = bf16[4,256,1024]{2,1,0:T(8,128)(2,1)} collective-permute-done((bf16[4,256,1024]{2,1,0:T(8,128)(2,1)}, bf16[4,256,1024]{2,1,0:T(8,128)(2,1)}, u32[]{:S(2)}, u32[]{:S(2)}) %collective-permute-start.36) | collective-permute-done | bytes 2097184 | tf_op jit(solution)/shard_map/ppermute | solution.py:222
  490.3 18.1 %collective-permute-start.40 = (bf16[4,256,1024]{2,1,0:T(8,128)(2,1)}, bf16[4,256,1024]{2,1,0:T(8,128)(2,1)}, u32[]{:S(2)}, u32[]{:S(2)}) collective-permute-start(bf16[4,256,1024]{2,1,0:T(8,128)(2,1)} %get-tuple-element.369), channel_id=1, source_target_pairs={{0,2},{2,4},{4,6},{1,3},{3,5},{5,7},{8,10},{10,12},{12,14},{9,11},... | collective-permute-start | bytes 6291464 | tf_op jit(solution)/shard_map/ppermute | solution.py:222
  510.0 10.7 attend.2
  522.0 29.7 %collective-permute-done.40.up_ref = bf16[4,256,1024]{2,1,0:T(8,128)(2,1)} collective-permute-done((bf16[4,256,1024]{2,1,0:T(8,128)(2,1)}, bf16[4,256,1024]{2,1,0:T(8,128)(2,1)}, u32[]{:S(2)}, u32[]{:S(2)}) %collective-permute-start.40) | collective-permute-done | bytes 2097184 | tf_op jit(solution)/shard_map/ppermute | solution.py:222
  584.4 8.9 project_heads.3
  630.6 10.5 collective-permute-done.46
  670.7 10.7 attend.3
  687.4 24.1 %feed_forward.3 = (bf16[1024,1024]{1,0:T(8,128)(2,1)S(1)}, bf16[1024,1024]{1,0:T(8,128)(2,1)S(1)}, f32[2,1024,1024]{2,1,0:T(8,128)}, bf16[2,1024,1024]{2,1,0:T(8,128)(2,1)}) custom-call(s32[1]{0:T(128)} %bitcast.72.model_ref.half_ref, bf16[1024,2048]{1,0:T(8,128)(2,1)} %join_halves.7.x_ref.x1_ref, bf16[4,2,256,2048]{3,2,1,0:T(8,128)(2,1)} %bitcast.386, ...), custom_call_target="tpu_custom_call" | custom-call | flops 858993472 | bytes 2097152 | tf_op jit(solution)/shard_map/feed_forward/pallas_call | solution.py:1138
  735.3 24.0 %hidden_grads.1.refs_0_.refs_1_.term_ref = bf16[8,4,128,1024]{3,2,1,0:T(8,128)(2,1)} custom-call(bf16[1024,2048]{1,0:T(8,128)(2,1)} %join_halves.5.x_ref.x0_ref, bf16[1024,2048]{1,0:T(8,128)(2,1)} %join_halves.7.x_ref.x1_ref, bf16[4,2,256,2048]{3,2,1,0:T(8,128)(2,1)} %bitcast.387, bf16[4,2,256,2048]{3,2,1,0:T(8,128)(2,1)} %bitcast.388, ...), custom_call_target="tpu_custom_call" | custom-call | flops 858993472 | bytes 838860 | tf_op jit(solution)/shard_map/hidden_grads/pallas_call | solution.py:614
  804.7 26.9 %collective-permute-done.53.refs_2_ = bf16[8,128,1024]{2,1,0:T(8,128)(2,1)S(1)} collective-permute-done((bf16[8,128,1024]{2,1,0:T(8,128)(2,1)}, bf16[8,128,1024]{2,1,0:T(8,128)(2,1)S(1)}, u32[]{:S(2)}, u32[]{:S(2)}) %collective-permute-start.53) | collective-permute-done | bytes 2097184 | tf_op jit(solution)/shard_map/ppermute | solution.py:249
  841.3 9.4 hop_sums.19
  890.8 8.9 convert_add_fusion.2
  932.4 19.5 %unmix_streams.2 = (bf16[5,2048,1024]{2,1,0:T(8,128)(2,1)}, f32[1024,128]{1,0:T(8,128)}) custom-call(f32[2048,20]{1,0:T(8,128)} %copy.101.mix_ref.refs_0_, bf16[5,2048,1024]{2,1,0:T(8,128)(2,1)} %refs_1_.1, bf16[4,1024,1024]{2,1,0:T(8,128)(2,1)} %bitcast.398), custom_call_target="tpu_custom_call" | custom-call | flops 4194304 | bytes 1468006 | tf_op jit(solution)/shard_map/unmix_streams/pallas_call | solution.py:741
  968.8 38.6 %collective-permute-done.68 = bf16[4,4,128,1024]{3,2,1,0:T(8,128)(2,1)S(1)} collective-permute-done((bf16[4,4,128,1024]{3,2,1,0:T(8,128)(2,1)S(1)}, bf16[4,4,128,1024]{3,2,1,0:T(8,128)(2,1)S(1)}, u32[]{:S(2)}, u32[]{:S(2)}) %collective-permute-start.68) | collective-permute-done | bytes 4194336 | tf_op jit(solution)/shard_map/ppermute | solution.py:105
  1026.6 30.2 %collective-permute-done.65.refs_5_ = bf16[4,256,1024]{2,1,0:T(8,128)(2,1)} collective-permute-done((bf16[4,256,1024]{2,1,0:T(8,128)(2,1)}, bf16[4,256,1024]{2,1,0:T(8,128)(2,1)}, u32[]{:S(2)}, u32[]{:S(2)}) %collective-permute-start.65) | collective-permute-done | bytes 2097184 | tf_op jit(solution)/shard_map/ppermute | solution.py:172
  1088.6 19.5 %unmix_streams.3 = (bf16[5,2048,1024]{2,1,0:T(8,128)(2,1)}, f32[1024,128]{1,0:T(8,128)}) custom-call(f32[2048,20]{1,0:T(8,128)} %copy.101.mix_ref.refs_0_, bf16[5,2048,1024]{2,1,0:T(8,128)(2,1)} %refs_1_.1, bf16[4,1024,1024]{2,1,0:T(8,128)(2,1)} %bitcast.397, bf16[5,2048,1024]{2,1,0:T(8,128)(2,1)} %get-tuple-element.499.rest_0_), custom_call_target="tpu_custom_call", output_to_operand_aliasing={{0}: (3, {})} | custom-call | flops 4194304 | bytes 1468006 | tf_op jit(solution)/shard_map/unmix_streams/pallas_call | solution.py:741
  (625 shorter events, 716.8 us)
Async XLA Ops:
  7.2 139.5 %all-gather.5.cloned.1.call-start = ((), (), s32[]{:S(2)}) async-start(), calls=%async_computation.4 | async-start | bytes 5242880 | tf_op jit(solution)/shard_map/all_gather | solution.py:1434
  10.5 163.9 %all-gather.7.cloned.1.call-start = ((), (), s32[]{:S(2)}) async-start(), calls=%async_computation.5 | async-start | bytes 5242880 | tf_op jit(solution)/shard_map/all_gather | solution.py:1470
  96.9 49.8 %collective-permute-start.22 = (bf16[8,128,1024]{2,1,0:T(8,128)(2,1)}, bf16[8,128,1024]{2,1,0:T(8,128)(2,1)}, u32[]{:S(2)}, u32[]{:S(2)}) collective-permute-start(bf16[8,128,1024]{2,1,0:T(8,128)(2,1)} %bitcast.332), channel_id=1, source_target_pairs={{2,0},{4,2},{6,4},{3,1},{5,3},{7,5},{10,8},{12,10},{14,12},{11,9},... | collective-permute-start | bytes 6291464 | tf_op jit(solution)/shard_map/ppermute | solution.py:172
  98.2 292.5 %all-gather.9.cloned.1.call-start = ((), (), s32[]{:S(2)}) async-start(), calls=%async_computation.6 | async-start | bytes 2621440 | tf_op jit(solution)/shard_map/all_gather | solution.py:1537
  146.7 57.9 %collective-permute-start.25 = (bf16[2048,1024]{1,0:T(8,128)(2,1)}, bf16[2048,1024]{1,0:T(8,128)(2,1)}, u32[]{:S(2)}, u32[]{:S(2)}) collective-permute-start(bf16[2048,1024]{1,0:T(8,128)(2,1)} %all-gather.5.cloned.1.call-done), channel_id=1, source_target_pairs={{0,8},{1,17},{8,0},{9,25},{16,24},{17,1},{24,16},{25,9},{2,10},{3,... | collective-permute-start | bytes 12582920 | tf_op jit(solution)/shard_map/ppermute | solution.py:105
  204.6 62.1 %collective-permute-start.28 = (bf16[2048,1024]{1,0:T(8,128)(2,1)}, bf16[2048,1024]{1,0:T(8,128)(2,1)}, u32[]{:S(2)}, u32[]{:S(2)}) collective-permute-start(bf16[2048,1024]{1,0:T(8,128)(2,1)} %all-gather.5.cloned.1.call-done), channel_id=1, source_target_pairs={{0,16},{1,9},{8,24},{9,1},{16,0},{17,25},{24,8},{25,17},{2,18},{3,... | collective-permute-start | bytes 12582920 | tf_op jit(solution)/shard_map/ppermute | solution.py:105
  266.7 58.8 %collective-permute-start.31 = (bf16[2048,1024]{1,0:T(8,128)(2,1)}, bf16[2048,1024]{1,0:T(8,128)(2,1)}, u32[]{:S(2)}, u32[]{:S(2)}) collective-permute-start(bf16[2048,1024]{1,0:T(8,128)(2,1)} %collective-permute-done.25), channel_id=1, source_target_pairs={{0,16},{1,9},{8,24},{9,1},{16,0},{17,25},{24,8},{25,17},{2,18},{3,... | collective-permute-start | bytes 12582920 | tf_op jit(solution)/shard_map/ppermute | solution.py:105
  397.2 85.1 %all-to-all-start = ((bf16[4,256,1024]{2,1,0:T(8,128)(2,1)}), bf16[4,256,1024]{2,1,0:T(8,128)(2,1)S(1)}, u32[]{:S(2)}, u32[]{:S(2)}) async-start(bf16[4,256,1024]{2,1,0:T(8,128)(2,1)} %project_heads.2), calls=%async_computation | async-start | bytes 4194304 | tf_op jit(solution)/shard_map/all_to_all | solution.py:1458
  402.9 79.4 %collective-permute-start.36 = (bf16[4,256,1024]{2,1,0:T(8,128)(2,1)}, bf16[4,256,1024]{2,1,0:T(8,128)(2,1)}, u32[]{:S(2)}, u32[]{:S(2)}) collective-permute-start(bf16[4,256,1024]{2,1,0:T(8,128)(2,1)} %get-tuple-element.354), channel_id=1, source_target_pairs={{0,2},{2,4},{1,3},{3,5},{8,10},{10,12},{9,11},{11,13},{16,18},{18,... | collective-permute-start | bytes 6291464 | tf_op jit(solution)/shard_map/ppermute | solution.py:222
  407.9 74.4 %collective-permute-start.37 = (bf16[4,256,1024]{2,1,0:T(8,128)(2,1)}, bf16[4,256,1024]{2,1,0:T(8,128)(2,1)}, u32[]{:S(2)}, u32[]{:S(2)}) collective-permute-start(bf16[4,256,1024]{2,1,0:T(8,128)(2,1)} %get-tuple-element.355), channel_id=1, source_target_pairs={{6,4},{4,2},{7,5},{5,3},{14,12},{12,10},{15,13},{13,11},{22,20},{2... | collective-permute-start | bytes 6291464 | tf_op jit(solution)/shard_map/ppermute | solution.py:223
  490.3 61.5 %collective-permute-start.40 = (bf16[4,256,1024]{2,1,0:T(8,128)(2,1)}, bf16[4,256,1024]{2,1,0:T(8,128)(2,1)}, u32[]{:S(2)}, u32[]{:S(2)}) collective-permute-start(bf16[4,256,1024]{2,1,0:T(8,128)(2,1)} %get-tuple-element.369), channel_id=1, source_target_pairs={{0,2},{2,4},{4,6},{1,3},{3,5},{5,7},{8,10},{10,12},{12,14},{9,11},... | collective-permute-start | bytes 6291464 | tf_op jit(solution)/shard_map/ppermute | solution.py:222
  557.2 52.9 %all-to-all-start.1 = ((bf16[4,256,1024]{2,1,0:T(8,128)(2,1)}), bf16[4,256,1024]{2,1,0:T(8,128)(2,1)S(1)}, u32[]{:S(2)}, u32[]{:S(2)}) async-start(bf16[4,256,1024]{2,1,0:T(8,128)(2,1)} %bitcast.334), calls=%async_computation.1 | async-start | bytes 4194304 | tf_op jit(solution)/shard_map/all_to_all | solution.py:1458
  610.1 52.9 %all-to-all-start.2 = ((bf16[4,256,1024]{2,1,0:T(8,128)(2,1)}), bf16[4,256,1024]{2,1,0:T(8,128)(2,1)}, u32[]{:S(2)}, u32[]{:S(2)}) async-start(bf16[4,256,1024]{2,1,0:T(8,128)(2,1)} %copy-done.26), calls=%async_computation.2 | async-start | bytes 4194304 | tf_op jit(solution)/shard_map/all_to_all | solution.py:1458
  663.0 51.2 %collective-permute-start.48 = (bf16[4,256,1024]{2,1,0:T(8,128)(2,1)}, bf16[4,256,1024]{2,1,0:T(8,128)(2,1)S(1)}, u32[]{:S(2)}, u32[]{:S(2)}) collective-permute-start(bf16[4,256,1024]{2,1,0:T(8,128)(2,1)} %get-tuple-element.399.refs_0_), channel_id=1, source_target_pairs={{0,2},{2,4},{4,6},{1,3},{3,5},{5,7},{8,10},{10,12},{12,14},{9,11},... | collective-permute-start | bytes 6291464 | tf_op jit(solution)/shard_map/ppermute | solution.py:171
  715.6 55.1 %all-to-all-start.3 = ((bf16[4,256,1024]{2,1,0:T(8,128)(2,1)}), bf16[4,256,1024]{2,1,0:T(8,128)(2,1)S(1)}, u32[]{:S(2)}, u32[]{:S(2)}) async-start(bf16[4,256,1024]{2,1,0:T(8,128)(2,1)} %bitcast.335), calls=%async_computation.3 | async-start | bytes 4194304 | tf_op jit(solution)/shard_map/all_to_all | solution.py:1458
  785.6 50.2 %collective-permute-start.54 = (bf16[8,128,1024]{2,1,0:T(8,128)(2,1)}, bf16[8,128,1024]{2,1,0:T(8,128)(2,1)}, u32[]{:S(2)}, u32[]{:S(2)}) collective-permute-start(bf16[8,128,1024]{2,1,0:T(8,128)(2,1)} %get-tuple-element.424), channel_id=1, source_target_pairs={{2,0},{4,2},{6,4},{3,1},{5,3},{7,5},{10,8},{12,10},{14,12},{11,9},... | collective-permute-start | bytes 6291464 | tf_op jit(solution)/shard_map/ppermute | solution.py:250
  840.3 50.5 %collective-permute-start.60 = (bf16[4,4,128,1024]{3,2,1,0:T(8,128)(2,1)}, bf16[4,4,128,1024]{3,2,1,0:T(8,128)(2,1)}, u32[]{:S(2)}, u32[]{:S(2)}) collective-permute-start(bf16[4,4,128,1024]{3,2,1,0:T(8,128)(2,1)} %attention_grads.5), channel_id=1, source_target_pairs={{0,16},{1,9},{8,24},{9,1},{16,0},{17,25},{24,8},{25,17},{2,18},{3,... | collective-permute-start | bytes 12582920 | tf_op jit(solution)/shard_map/ppermute | solution.py:105
  905.5 53.4 %collective-permute-start.61 = (bf16[4,256,1024]{2,1,0:T(8,128)(2,1)S(1)}, bf16[4,256,1024]{2,1,0:T(8,128)(2,1)}, u32[]{:S(2)}, u32[]{:S(2)}) collective-permute-start(bf16[4,256,1024]{2,1,0:T(8,128)(2,1)S(1)} %copy-done.13), channel_id=1, source_target_pairs={{0,2},{2,4},{4,6},{1,3},{3,5},{5,7},{8,10},{10,12},{12,14},{9,11},... | collective-permute-start | bytes 6291464 | tf_op jit(solution)/shard_map/ppermute | solution.py:171
  908.8 50.1 %collective-permute-start.62 = (bf16[4,256,1024]{2,1,0:T(8,128)(2,1)S(1)}, bf16[4,256,1024]{2,1,0:T(8,128)(2,1)}, u32[]{:S(2)}, u32[]{:S(2)}) collective-permute-start(bf16[4,256,1024]{2,1,0:T(8,128)(2,1)S(1)} %copy-done.13), channel_id=1, source_target_pairs={{2,0},{4,2},{6,4},{3,1},{5,3},{7,5},{10,8},{12,10},{14,12},{11,9},... | collective-permute-start | bytes 6291464 | tf_op jit(solution)/shard_map/ppermute | solution.py:172
  959.3 57.0 %collective-permute-start.66 = (bf16[8,128,1024]{2,1,0:T(8,128)(2,1)S(1)}, bf16[8,128,1024]{2,1,0:T(8,128)(2,1)}, u32[]{:S(2)}, u32[]{:S(2)}) collective-permute-start(bf16[8,128,1024]{2,1,0:T(8,128)(2,1)S(1)} %copy-done.103), channel_id=1, source_target_pairs={{0,2},{2,4},{4,6},{1,3},{3,5},{5,7},{8,10},{10,12},{12,14},{9,11},... | collective-permute-start | bytes 6291464 | tf_op jit(solution)/shard_map/ppermute | solution.py:222
  964.0 52.2 %collective-permute-start.67 = (bf16[8,128,1024]{2,1,0:T(8,128)(2,1)S(1)}, bf16[8,128,1024]{2,1,0:T(8,128)(2,1)}, u32[]{:S(2)}, u32[]{:S(2)}) collective-permute-start(bf16[8,128,1024]{2,1,0:T(8,128)(2,1)S(1)} %copy-done.102), channel_id=1, source_target_pairs={{6,4},{4,2},{2,0},{7,5},{5,3},{3,1},{14,12},{12,10},{10,8},{15,13}... | collective-permute-start | bytes 6291464 | tf_op jit(solution)/shard_map/ppermute | solution.py:223
  965.3 61.3 %collective-permute-start.64 = (bf16[4,256,1024]{2,1,0:T(8,128)(2,1)}, bf16[4,256,1024]{2,1,0:T(8,128)(2,1)}, u32[]{:S(2)}, u32[]{:S(2)}) collective-permute-start(bf16[4,256,1024]{2,1,0:T(8,128)(2,1)} %collective-permute-done.61.refs_1_), channel_id=1, source_target_pairs={{2,4},{4,6},{3,5},{5,7},{10,12},{12,14},{11,13},{13,15},{18,20},{2... | collective-permute-start | bytes 6291464 | tf_op jit(solution)/shard_map/ppermute | solution.py:171
  967.3 89.4 %collective-permute-start.65 = (bf16[4,256,1024]{2,1,0:T(8,128)(2,1)}, bf16[4,256,1024]{2,1,0:T(8,128)(2,1)}, u32[]{:S(2)}, u32[]{:S(2)}) collective-permute-start(bf16[4,256,1024]{2,1,0:T(8,128)(2,1)} %collective-permute-done.62.refs_6_), channel_id=1, source_target_pairs={{2,0},{4,2},{3,1},{5,3},{10,8},{12,10},{11,9},{13,11},{18,16},{20,... | collective-permute-start | bytes 6291464 | tf_op jit(solution)/shard_map/ppermute | solution.py:172
  1056.8 51.3 %collective-permute-start.71 = (bf16[4,256,1024]{2,1,0:T(8,128)(2,1)}, bf16[4,256,1024]{2,1,0:T(8,128)(2,1)}, u32[]{:S(2)}, u32[]{:S(2)}) collective-permute-start(bf16[4,256,1024]{2,1,0:T(8,128)(2,1)} %collective-permute-done.64.refs_2_), channel_id=1, source_target_pairs={{4,6},{5,7},{12,14},{13,15},{20,22},{21,23},{28,30},{29,31}} | collective-permute-start | bytes 6291464 | tf_op jit(solution)/shard_map/ppermute | solution.py:171
  (185 other events, 2719.1 us)
Sparse Core Ops, SparseCore 0:
  10.7 91.8 all-gather.4
  104.4 59.1 all-gather.6
  342.7 33.3 all-gather.8
  617.5 39.3 all-gather.10

commit v9 on v8

--- a/solution.py
+++ b/solution.py
@@ -215,6 +215,7 @@
             jnp.maximum(here - size + self.at, 0),
             self.up,
             self.down,
+            [here < self.at, here > size - 1 - self.at],
         )
         (goes_up, goes_down), *later = fence((goes_up, goes_down), *later)
         up_pairs = [(i, i + 1) for i in range(min(self.at, size - 1))]
@@ -242,8 +243,8 @@
             jnp.maximum(here - size + self.at, 0),
             self.up,
             self.down,
+            [here < self.at, here > size - 1 - self.at],
             [v[-1].reshape(lead, tall, wide) for v in (line.up, line.down)],
-            [here < self.at, here > size - 1 - self.at],
         )
         goes, *later = fence(goes, *later)
         self.up = lax.ppermute(goes[0], "depth", [(i, i + 1) for i in range(size - 1)])
@@ -475,23 +476,31 @@
             outs[way][0] = ins[way][0]
 
 
-def hop_sums(terms, up_at, down_at, up, down, blocks=None, first=None):
+def hop_sums(terms, up_at, down_at, up, down, sends, blocks=None):
     lead, _, tall, wide = terms.shape
     rows = chunk_of(tall, wide)
     block = pl.BlockSpec((1, rows, wide), lambda l, i, m: (l, i, 0))
-    in_specs = [
-        pl.BlockSpec((1, 1, rows, wide), lambda l, i, m: (l, m[0], i, 0)),
-        pl.BlockSpec((1, 1, rows, wide), lambda l, i, m: (l, m[1], i, 0)),
-    ]
+
+    def term_spec(way):
+        return pl.BlockSpec(
+            (1, 1, rows, wide), lambda l, i, m: (l * m[2 + way], m[way], i * m[2 + way], 0)
+        )
+
+    def block_spec(way, sign):
+        def index(l, i, m):
+            need = m[2 + way] if sign else 1 - m[2 + way]
+            return (l * need, i * need, 0)
+
+        return pl.BlockSpec((1, rows, wide), index)
+
+    in_specs = [term_spec(0), term_spec(1)]
     operands = [terms, terms]
-    where = [up_at, down_at]
     if up is not None:
-        in_specs += [block, block]
+        in_specs += [block_spec(0, True), block_spec(1, True)]
         operands += [up, down]
     if blocks is not None:
-        in_specs += [block, block]
+        in_specs += [block_spec(0, False), block_spec(1, False)]
         operands += list(blocks)
-        where += list(first)
     return pl.pallas_call(
         functools.partial(hop_kernel, up is not None, blocks is not None),
         grid_spec=pltpu.PrefetchScalarGridSpec(
@@ -505,7 +514,7 @@
             flops=2 * lead * tall * wide, bytes_accessed=12 * lead * tall * wide, transcendentals=0
         ),
         name="hop_sums",
-    )(jnp.stack(where).astype(jnp.int32), *operands)
+    )(jnp.stack([up_at, down_at, *sends]).astype(jnp.int32), *operands)
 
 
 def end_kernel(at_ref, term_ref, up_ref, down_ref, out_ref):
@@ -1631,9 +1640,9 @@
 
     def sums_hop():
         place, at = hops_left.pop(0)
-        arrived = core_hop(pieces.pop(place).astype(bf16), at)
+        arrived = core_hop(pieces.pop(place), at)
         target = place - (1 << at)
-        pieces[target] = pieces[target].astype(f32) + arrived.astype(f32)
+        pieces[target] = (pieces[target].astype(f32) + arrived.astype(f32)).astype(bf16)
 
     grad_line = LineGather(grad_low)
     grad_line.step()

time: 1230 us -> 1220 us (level)
    add x3 -> x0, other arithmetic: 23.4 us -> none  [sums_hop(): pieces[target] = pieces[target].astype(f32) + arrived.astype(f32)]
    convert_element_type x0 -> x3, other arithmetic: none -> 18 us  [sums_hop(): (pieces[target].astype(f32) + arrived.astype(f32)).astype(bf16)]
    unnamed x212 -> x214, local copies, waits for them, and re-layouts: 48.9 us -> 48.7 us
  transfers between devices with their start and end apart: 105 -> 105, of which waited for: 45 -> 47; matrix products, arithmetic and copies ran while one was open for 8% -> 8% of each run, Pallas kernels for 34% -> 34%
where the time goes in v9:
time: 1220 us; the launch traced here: 1210 us
  Pallas kernels  452 us (37%)
  waiting for transfers between devices  403 us (33%)
  starting transfers between devices  185 us (15%)
  local copies, waits for them, and re-layouts  73.5 us (6%)
  other arithmetic  67.3 us (6%)
  between operations  16 us (1%)
  matrix products  12.4 us (1%)
    ppermute x8, waiting for transfers between devices, step(): self.up = lax.ppermute(goes_up, 'depth', up_pairs)  94.5 us
    ppermute x4, waiting for transfers between devices, step_with(): lax.ppermute(goes[0], 'depth', [(i, i + 1) for i in range(size - 1)])  91.3 us
    pallas_call x12, Pallas kernels, hop_sums(): pl.pallas_call(functools.partial(hop_kernel, up is not None, blocks is no...  71.1 us
    ppermute x10, waiting for transfers between devices, core_hop(): return lax.ppermute(values, ('dp', 'mp'), pairs)  62.5 us
    ppermute x53, waiting for transfers between devices, swap_mask(): return lax.ppermute(values, axis, [(i, i ^ mask) for i in range(size)])  54.2 us
    ppermute x53, starting transfers between devices, swap_mask(): return lax.ppermute(values, axis, [(i, i ^ mask) for i in range(size)])  52.2 us
    ppermute x8, starting transfers between devices, step(): self.up = lax.ppermute(goes_up, 'depth', up_pairs)  51.4 us
    unnamed x214, local copies, waits for them, and re-layouts  48.7 us
  transfers between devices with their start and end apart: 105, of which 47 were waited for; matrix products, arithmetic and copies ran while one was open for 8% of the time, Pallas kernels for 34%

profile of v9, /device:TPU:0, one launch (start us, length us, event | category | flops | bytes accessed | tf_op | source)
XLA Modules:
  0.0 1209.0 jit_solution(7265398075285986552)
XLA Ops:
  99.7 14.3 %mix_streams.2 = bf16[4,1024,1024]{2,1,0:T(8,128)(2,1)} custom-call(f32[2048,20]{1,0:T(8,128)} %copy.101.mix_ref.refs_0_, bf16[5,2048,1024]{2,1,0:T(8,128)(2,1)} %refs_1_.1), custom_call_target="tpu_custom_call" | custom-call | flops 2097152 | bytes 943718 | tf_op jit(solution)/shard_map/mix_streams/pallas_call | solution.py:675
  114.0 14.4 %mix_streams.3 = bf16[4,1024,1024]{2,1,0:T(8,128)(2,1)} custom-call(f32[2048,20]{1,0:T(8,128)} %copy.101.mix_ref.refs_0_, bf16[5,2048,1024]{2,1,0:T(8,128)(2,1)} %refs_1_.1), custom_call_target="tpu_custom_call" | custom-call | flops 2097152 | bytes 943718 | tf_op jit(solution)/shard_map/mix_streams/pallas_call | solution.py:675
  128.4 13.1 %collective-permute-done.21.refs_1_ = bf16[8,128,1024]{2,1,0:T(8,128)(2,1)S(1)} collective-permute-done((bf16[8,128,1024]{2,1,0:T(8,128)(2,1)}, bf16[8,128,1024]{2,1,0:T(8,128)(2,1)S(1)}, u32[]{:S(2)}, u32[]{:S(2)}) %collective-permute-start.21) | collective-permute-done | bytes 2097184 | tf_op jit(solution)/shard_map/ppermute | solution.py:171
  174.5 25.8 %collective-permute-done.23.refs_2_ = bf16[4,256,1024]{2,1,0:T(8,128)(2,1)S(1)} collective-permute-done((bf16[4,256,1024]{2,1,0:T(8,128)(2,1)}, bf16[4,256,1024]{2,1,0:T(8,128)(2,1)S(1)}, u32[]{:S(2)}, u32[]{:S(2)}) %collective-permute-start.23) | collective-permute-done | bytes 2097184 | tf_op jit(solution)/shard_map/ppermute | solution.py:250
  222.9 37.4 %collective-permute-done.26.refs_2_ = bf16[4,256,1024]{2,1,0:T(8,128)(2,1)S(1)} collective-permute-done((bf16[4,256,1024]{2,1,0:T(8,128)(2,1)}, bf16[4,256,1024]{2,1,0:T(8,128)(2,1)S(1)}, u32[]{:S(2)}, u32[]{:S(2)}) %collective-permute-start.26) | collective-permute-done | bytes 2097184 | tf_op jit(solution)/shard_map/ppermute | solution.py:250
  355.3 10.0 project_heads.2
  365.3 23.6 %collective-permute-done.33.refs_2_ = bf16[4,256,1024]{2,1,0:T(8,128)(2,1)} collective-permute-done((bf16[4,256,1024]{2,1,0:T(8,128)(2,1)}, bf16[4,256,1024]{2,1,0:T(8,128)(2,1)}, u32[]{:S(2)}, u32[]{:S(2)}) %collective-permute-start.33) | collective-permute-done | bytes 2097184 | tf_op jit(solution)/shard_map/ppermute | solution.py:223
  412.3 8.9 join_halves.6
  421.2 24.0 %feed_forward.2 = (bf16[1024,1024]{1,0:T(8,128)(2,1)S(1)}, bf16[1024,1024]{1,0:T(8,128)(2,1)S(1)}, f32[2,1024,1024]{2,1,0:T(8,128)}, bf16[2,1024,1024]{2,1,0:T(8,128)(2,1)}) custom-call(s32[1]{0:T(128)} %bitcast.74.model_ref.half_ref, bf16[1024,2048]{1,0:T(8,128)(2,1)} %join_halves.5.x_ref.x0_ref, bf16[4,2,256,2048]{3,2,1,0:T(8,128)(2,1)} %bitcast.387, ...), custom_call_target="tpu_custom_call" | custom-call | flops 858993472 | bytes 2097152 | tf_op jit(solution)/shard_map/feed_forward/pallas_call | solution.py:1147
  447.8 32.1 %collective-permute-done.36.refs_2_ = bf16[4,256,1024]{2,1,0:T(8,128)(2,1)} collective-permute-done((bf16[4,256,1024]{2,1,0:T(8,128)(2,1)}, bf16[4,256,1024]{2,1,0:T(8,128)(2,1)}, u32[]{:S(2)}, u32[]{:S(2)}) %collective-permute-start.36) | collective-permute-done | bytes 2097184 | tf_op jit(solution)/shard_map/ppermute | solution.py:223
  487.2 18.7 %collective-permute-start.40 = (bf16[4,256,1024]{2,1,0:T(8,128)(2,1)}, bf16[4,256,1024]{2,1,0:T(8,128)(2,1)}, u32[]{:S(2)}, u32[]{:S(2)}) collective-permute-start(bf16[4,256,1024]{2,1,0:T(8,128)(2,1)} %get-tuple-element.369), channel_id=1, source_target_pairs={{0,2},{2,4},{4,6},{1,3},{3,5},{5,7},{8,10},{10,12},{12,14},{9,11},... | collective-permute-start | bytes 6291464 | tf_op jit(solution)/shard_map/ppermute | solution.py:223
  507.5 10.7 attend.2
  519.6 29.8 %collective-permute-done.40.up_ref = bf16[4,256,1024]{2,1,0:T(8,128)(2,1)} collective-permute-done((bf16[4,256,1024]{2,1,0:T(8,128)(2,1)}, bf16[4,256,1024]{2,1,0:T(8,128)(2,1)}, u32[]{:S(2)}, u32[]{:S(2)}) %collective-permute-start.40) | collective-permute-done | bytes 2097184 | tf_op jit(solution)/shard_map/ppermute | solution.py:223
  581.3 8.9 project_heads.3
  627.5 11.2 collective-permute-done.46
  668.4 10.7 attend.3
  685.2 24.0 %feed_forward.3 = (bf16[1024,1024]{1,0:T(8,128)(2,1)S(1)}, bf16[1024,1024]{1,0:T(8,128)(2,1)S(1)}, f32[2,1024,1024]{2,1,0:T(8,128)}, bf16[2,1024,1024]{2,1,0:T(8,128)(2,1)}) custom-call(s32[1]{0:T(128)} %bitcast.74.model_ref.half_ref, bf16[1024,2048]{1,0:T(8,128)(2,1)} %join_halves.7.x_ref.x1_ref, bf16[4,2,256,2048]{3,2,1,0:T(8,128)(2,1)} %bitcast.388, ...), custom_call_target="tpu_custom_call" | custom-call | flops 858993472 | bytes 2097152 | tf_op jit(solution)/shard_map/feed_forward/pallas_call | solution.py:1147
  732.2 24.0 %hidden_grads.1.refs_0_.refs_1_.term_ref = bf16[8,4,128,1024]{3,2,1,0:T(8,128)(2,1)} custom-call(bf16[1024,2048]{1,0:T(8,128)(2,1)} %join_halves.5.x_ref.x0_ref, bf16[1024,2048]{1,0:T(8,128)(2,1)} %join_halves.7.x_ref.x1_ref, bf16[4,2,256,2048]{3,2,1,0:T(8,128)(2,1)} %bitcast.389, bf16[4,2,256,2048]{3,2,1,0:T(8,128)(2,1)} %bitcast.390, ...), custom_call_target="tpu_custom_call" | custom-call | flops 858993472 | bytes 838860 | tf_op jit(solution)/shard_map/hidden_grads/pallas_call | solution.py:623
  759.2 9.1 all-to-all-done.3.ans_ref
  801.5 26.9 %collective-permute-done.53.refs_2_ = bf16[8,128,1024]{2,1,0:T(8,128)(2,1)S(1)} collective-permute-done((bf16[8,128,1024]{2,1,0:T(8,128)(2,1)}, bf16[8,128,1024]{2,1,0:T(8,128)(2,1)S(1)}, u32[]{:S(2)}, u32[]{:S(2)}) %collective-permute-start.53) | collective-permute-done | bytes 2097184 | tf_op jit(solution)/shard_map/ppermute | solution.py:250
  926.4 19.5 %unmix_streams.2 = (bf16[5,2048,1024]{2,1,0:T(8,128)(2,1)}, f32[1024,128]{1,0:T(8,128)}) custom-call(f32[2048,20]{1,0:T(8,128)} %copy.101.mix_ref.refs_0_, bf16[5,2048,1024]{2,1,0:T(8,128)(2,1)} %refs_1_.1, bf16[4,1024,1024]{2,1,0:T(8,128)(2,1)} %bitcast.400), custom_call_target="tpu_custom_call" | custom-call | flops 4194304 | bytes 1468006 | tf_op jit(solution)/shard_map/unmix_streams/pallas_call | solution.py:750
  963.6 36.8 %collective-permute-done.68 = bf16[4,4,128,1024]{3,2,1,0:T(8,128)(2,1)S(1)} collective-permute-done((bf16[4,4,128,1024]{3,2,1,0:T(8,128)(2,1)S(1)}, bf16[4,4,128,1024]{3,2,1,0:T(8,128)(2,1)S(1)}, u32[]{:S(2)}, u32[]{:S(2)}) %collective-permute-start.68) | collective-permute-done | bytes 4194336 | tf_op jit(solution)/shard_map/ppermute | solution.py:105
  1017.3 32.9 %collective-permute-done.65.refs_5_ = bf16[4,256,1024]{2,1,0:T(8,128)(2,1)} collective-permute-done((bf16[4,256,1024]{2,1,0:T(8,128)(2,1)}, bf16[4,256,1024]{2,1,0:T(8,128)(2,1)}, u32[]{:S(2)}, u32[]{:S(2)}) %collective-permute-start.65) | collective-permute-done | bytes 2097184 | tf_op jit(solution)/shard_map/ppermute | solution.py:172
  1081.5 19.5 %unmix_streams.3 = (bf16[5,2048,1024]{2,1,0:T(8,128)(2,1)}, f32[1024,128]{1,0:T(8,128)}) custom-call(f32[2048,20]{1,0:T(8,128)} %copy.101.mix_ref.refs_0_, bf16[5,2048,1024]{2,1,0:T(8,128)(2,1)} %refs_1_.1, bf16[4,1024,1024]{2,1,0:T(8,128)(2,1)} %bitcast.399, bf16[5,2048,1024]{2,1,0:T(8,128)(2,1)} %get-tuple-element.499.rest_0_), custom_call_target="tpu_custom_call", output_to_operand_aliasing={{0}: (3, {})} | custom-call | flops 4194304 | bytes 1468006 | tf_op jit(solution)/shard_map/unmix_streams/pallas_call | solution.py:750
  (626 shorter events, 706.6 us)
Async XLA Ops:
  7.2 139.5 %all-gather.5.cloned.1.call-start = ((), (), s32[]{:S(2)}) async-start(), calls=%async_computation.4 | async-start | bytes 5242880 | tf_op jit(solution)/shard_map/all_gather | solution.py:1443
  10.5 164.0 %all-gather.7.cloned.1.call-start = ((), (), s32[]{:S(2)}) async-start(), calls=%async_computation.5 | async-start | bytes 5242880 | tf_op jit(solution)/shard_map/all_gather | solution.py:1479
  97.0 49.7 %collective-permute-start.22 = (bf16[8,128,1024]{2,1,0:T(8,128)(2,1)}, bf16[8,128,1024]{2,1,0:T(8,128)(2,1)}, u32[]{:S(2)}, u32[]{:S(2)}) collective-permute-start(bf16[8,128,1024]{2,1,0:T(8,128)(2,1)} %bitcast.334), channel_id=1, source_target_pairs={{2,0},{4,2},{6,4},{3,1},{5,3},{7,5},{10,8},{12,10},{14,12},{11,9},... | collective-permute-start | bytes 6291464 | tf_op jit(solution)/shard_map/ppermute | solution.py:172
  98.3 290.6 %all-gather.9.cloned.1.call-start = ((), (), s32[]{:S(2)}) async-start(), calls=%async_computation.6 | async-start | bytes 2621440 | tf_op jit(solution)/shard_map/all_gather | solution.py:1546
  146.7 57.9 %collective-permute-start.25 = (bf16[2048,1024]{1,0:T(8,128)(2,1)}, bf16[2048,1024]{1,0:T(8,128)(2,1)}, u32[]{:S(2)}, u32[]{:S(2)}) collective-permute-start(bf16[2048,1024]{1,0:T(8,128)(2,1)} %all-gather.5.cloned.1.call-done), channel_id=1, source_target_pairs={{0,8},{1,17},{8,0},{9,25},{16,24},{17,1},{24,16},{25,9},{2,10},{3,... | collective-permute-start | bytes 12582920 | tf_op jit(solution)/shard_map/ppermute | solution.py:105
  204.6 60.0 %collective-permute-start.28 = (bf16[2048,1024]{1,0:T(8,128)(2,1)}, bf16[2048,1024]{1,0:T(8,128)(2,1)}, u32[]{:S(2)}, u32[]{:S(2)}) collective-permute-start(bf16[2048,1024]{1,0:T(8,128)(2,1)} %all-gather.5.cloned.1.call-done), channel_id=1, source_target_pairs={{0,16},{1,9},{8,24},{9,1},{16,0},{17,25},{24,8},{25,17},{2,18},{3,... | collective-permute-start | bytes 12582920 | tf_op jit(solution)/shard_map/ppermute | solution.py:105
  264.6 58.8 %collective-permute-start.31 = (bf16[2048,1024]{1,0:T(8,128)(2,1)}, bf16[2048,1024]{1,0:T(8,128)(2,1)}, u32[]{:S(2)}, u32[]{:S(2)}) collective-permute-start(bf16[2048,1024]{1,0:T(8,128)(2,1)} %collective-permute-done.25), channel_id=1, source_target_pairs={{0,16},{1,9},{8,24},{9,1},{16,0},{17,25},{24,8},{25,17},{2,18},{3,... | collective-permute-start | bytes 12582920 | tf_op jit(solution)/shard_map/ppermute | solution.py:105
  394.8 85.1 %all-to-all-start = ((bf16[4,256,1024]{2,1,0:T(8,128)(2,1)}), bf16[4,256,1024]{2,1,0:T(8,128)(2,1)S(1)}, u32[]{:S(2)}, u32[]{:S(2)}) async-start(bf16[4,256,1024]{2,1,0:T(8,128)(2,1)} %project_heads.2), calls=%async_computation | async-start | bytes 4194304 | tf_op jit(solution)/shard_map/all_to_all | solution.py:1467
  400.5 79.4 %collective-permute-start.36 = (bf16[4,256,1024]{2,1,0:T(8,128)(2,1)}, bf16[4,256,1024]{2,1,0:T(8,128)(2,1)}, u32[]{:S(2)}, u32[]{:S(2)}) collective-permute-start(bf16[4,256,1024]{2,1,0:T(8,128)(2,1)} %get-tuple-element.354), channel_id=1, source_target_pairs={{0,2},{2,4},{1,3},{3,5},{8,10},{10,12},{9,11},{11,13},{16,18},{18,... | collective-permute-start | bytes 6291464 | tf_op jit(solution)/shard_map/ppermute | solution.py:223
  405.6 74.3 %collective-permute-start.37 = (bf16[4,256,1024]{2,1,0:T(8,128)(2,1)}, bf16[4,256,1024]{2,1,0:T(8,128)(2,1)}, u32[]{:S(2)}, u32[]{:S(2)}) collective-permute-start(bf16[4,256,1024]{2,1,0:T(8,128)(2,1)} %get-tuple-element.355), channel_id=1, source_target_pairs={{6,4},{4,2},{7,5},{5,3},{14,12},{12,10},{15,13},{13,11},{22,20},{2... | collective-permute-start | bytes 6291464 | tf_op jit(solution)/shard_map/ppermute | solution.py:224
  487.2 62.2 %collective-permute-start.40 = (bf16[4,256,1024]{2,1,0:T(8,128)(2,1)}, bf16[4,256,1024]{2,1,0:T(8,128)(2,1)}, u32[]{:S(2)}, u32[]{:S(2)}) collective-permute-start(bf16[4,256,1024]{2,1,0:T(8,128)(2,1)} %get-tuple-element.369), channel_id=1, source_target_pairs={{0,2},{2,4},{4,6},{1,3},{3,5},{5,7},{8,10},{10,12},{12,14},{9,11},... | collective-permute-start | bytes 6291464 | tf_op jit(solution)/shard_map/ppermute | solution.py:223
  554.8 52.9 %all-to-all-start.1 = ((bf16[4,256,1024]{2,1,0:T(8,128)(2,1)}), bf16[4,256,1024]{2,1,0:T(8,128)(2,1)S(1)}, u32[]{:S(2)}, u32[]{:S(2)}) async-start(bf16[4,256,1024]{2,1,0:T(8,128)(2,1)} %bitcast.336), calls=%async_computation.1 | async-start | bytes 4194304 | tf_op jit(solution)/shard_map/all_to_all | solution.py:1467
  607.7 52.9 %all-to-all-start.2 = ((bf16[4,256,1024]{2,1,0:T(8,128)(2,1)}), bf16[4,256,1024]{2,1,0:T(8,128)(2,1)}, u32[]{:S(2)}, u32[]{:S(2)}) async-start(bf16[4,256,1024]{2,1,0:T(8,128)(2,1)} %copy-done.26), calls=%async_computation.2 | async-start | bytes 4194304 | tf_op jit(solution)/shard_map/all_to_all | solution.py:1467
  660.6 51.2 %collective-permute-start.48 = (bf16[4,256,1024]{2,1,0:T(8,128)(2,1)}, bf16[4,256,1024]{2,1,0:T(8,128)(2,1)S(1)}, u32[]{:S(2)}, u32[]{:S(2)}) collective-permute-start(bf16[4,256,1024]{2,1,0:T(8,128)(2,1)} %get-tuple-element.399.refs_0_), channel_id=1, source_target_pairs={{0,2},{2,4},{4,6},{1,3},{3,5},{5,7},{8,10},{10,12},{12,14},{9,11},... | collective-permute-start | bytes 6291464 | tf_op jit(solution)/shard_map/ppermute | solution.py:171
  713.3 55.0 %all-to-all-start.3 = ((bf16[4,256,1024]{2,1,0:T(8,128)(2,1)}), bf16[4,256,1024]{2,1,0:T(8,128)(2,1)S(1)}, u32[]{:S(2)}, u32[]{:S(2)}) async-start(bf16[4,256,1024]{2,1,0:T(8,128)(2,1)} %bitcast.337), calls=%async_computation.3 | async-start | bytes 4194304 | tf_op jit(solution)/shard_map/all_to_all | solution.py:1467
  782.4 50.2 %collective-permute-start.54 = (bf16[8,128,1024]{2,1,0:T(8,128)(2,1)}, bf16[8,128,1024]{2,1,0:T(8,128)(2,1)}, u32[]{:S(2)}, u32[]{:S(2)}) collective-permute-start(bf16[8,128,1024]{2,1,0:T(8,128)(2,1)} %get-tuple-element.424), channel_id=1, source_target_pairs={{2,0},{4,2},{6,4},{3,1},{5,3},{7,5},{10,8},{12,10},{14,12},{11,9},... | collective-permute-start | bytes 6291464 | tf_op jit(solution)/shard_map/ppermute | solution.py:251
  837.2 50.4 %collective-permute-start.60 = (bf16[4,4,128,1024]{3,2,1,0:T(8,128)(2,1)}, bf16[4,4,128,1024]{3,2,1,0:T(8,128)(2,1)}, u32[]{:S(2)}, u32[]{:S(2)}) collective-permute-start(bf16[4,4,128,1024]{3,2,1,0:T(8,128)(2,1)} %attention_grads.5), channel_id=1, source_target_pairs={{0,16},{1,9},{8,24},{9,1},{16,0},{17,25},{24,8},{25,17},{2,18},{3,... | collective-permute-start | bytes 12582920 | tf_op jit(solution)/shard_map/ppermute | solution.py:105
  845.7 49.7 %collective-permute-start.58 = (bf16[8,128,1024]{2,1,0:T(8,128)(2,1)}, bf16[8,128,1024]{2,1,0:T(8,128)(2,1)}, u32[]{:S(2)}, u32[]{:S(2)}) collective-permute-start(bf16[8,128,1024]{2,1,0:T(8,128)(2,1)} %get-tuple-element.439), channel_id=1, source_target_pairs={{2,0},{4,2},{6,4},{3,1},{5,3},{7,5},{10,8},{12,10},{14,12},{11,9},... | collective-permute-start | bytes 6291464 | tf_op jit(solution)/shard_map/ppermute | solution.py:251
  897.8 54.0 %collective-permute-start.61 = (bf16[4,256,1024]{2,1,0:T(8,128)(2,1)S(1)}, bf16[4,256,1024]{2,1,0:T(8,128)(2,1)}, u32[]{:S(2)}, u32[]{:S(2)}) collective-permute-start(bf16[4,256,1024]{2,1,0:T(8,128)(2,1)S(1)} %copy-done.13), channel_id=1, source_target_pairs={{0,2},{2,4},{4,6},{1,3},{3,5},{5,7},{8,10},{10,12},{12,14},{9,11},... | collective-permute-start | bytes 6291464 | tf_op jit(solution)/shard_map/ppermute | solution.py:171
  952.6 52.2 %collective-permute-start.66 = (bf16[8,128,1024]{2,1,0:T(8,128)(2,1)S(1)}, bf16[8,128,1024]{2,1,0:T(8,128)(2,1)}, u32[]{:S(2)}, u32[]{:S(2)}) collective-permute-start(bf16[8,128,1024]{2,1,0:T(8,128)(2,1)S(1)} %copy-done.104), channel_id=1, source_target_pairs={{0,2},{2,4},{4,6},{1,3},{3,5},{5,7},{8,10},{10,12},{12,14},{9,11},... | collective-permute-start | bytes 6291464 | tf_op jit(solution)/shard_map/ppermute | solution.py:223
  958.8 50.6 %collective-permute-start.67 = (bf16[8,128,1024]{2,1,0:T(8,128)(2,1)S(1)}, bf16[8,128,1024]{2,1,0:T(8,128)(2,1)}, u32[]{:S(2)}, u32[]{:S(2)}) collective-permute-start(bf16[8,128,1024]{2,1,0:T(8,128)(2,1)S(1)} %copy-done.103), channel_id=1, source_target_pairs={{6,4},{4,2},{2,0},{7,5},{5,3},{3,1},{14,12},{12,10},{10,8},{15,13}... | collective-permute-start | bytes 6291464 | tf_op jit(solution)/shard_map/ppermute | solution.py:224
  960.1 57.1 %collective-permute-start.64 = (bf16[4,256,1024]{2,1,0:T(8,128)(2,1)}, bf16[4,256,1024]{2,1,0:T(8,128)(2,1)}, u32[]{:S(2)}, u32[]{:S(2)}) collective-permute-start(bf16[4,256,1024]{2,1,0:T(8,128)(2,1)} %collective-permute-done.61.refs_1_), channel_id=1, source_target_pairs={{2,4},{4,6},{3,5},{5,7},{10,12},{12,14},{11,13},{13,15},{18,20},{2... | collective-permute-start | bytes 6291464 | tf_op jit(solution)/shard_map/ppermute | solution.py:171
  962.1 88.0 %collective-permute-start.65 = (bf16[4,256,1024]{2,1,0:T(8,128)(2,1)}, bf16[4,256,1024]{2,1,0:T(8,128)(2,1)}, u32[]{:S(2)}, u32[]{:S(2)}) collective-permute-start(bf16[4,256,1024]{2,1,0:T(8,128)(2,1)} %collective-permute-done.62.refs_6_), channel_id=1, source_target_pairs={{2,0},{4,2},{3,1},{5,3},{10,8},{12,10},{11,9},{13,11},{18,16},{20,... | collective-permute-start | bytes 6291464 | tf_op jit(solution)/shard_map/ppermute | solution.py:172
  1050.2 50.9 %collective-permute-start.71 = (bf16[4,256,1024]{2,1,0:T(8,128)(2,1)}, bf16[4,256,1024]{2,1,0:T(8,128)(2,1)}, u32[]{:S(2)}, u32[]{:S(2)}) collective-permute-start(bf16[4,256,1024]{2,1,0:T(8,128)(2,1)} %collective-permute-done.64.refs_2_), channel_id=1, source_target_pairs={{4,6},{5,7},{12,14},{13,15},{20,22},{21,23},{28,30},{29,31}} | collective-permute-start | bytes 6291464 | tf_op jit(solution)/shard_map/ppermute | solution.py:171
  (186 other events, 2772.4 us)
Sparse Core Ops, SparseCore 0:
  10.7 91.4 all-gather.4
  104.0 59.7 all-gather.6
  340.6 33.0 all-gather.8
  615.1 38.5 all-gather.10

commit v10 on v9

--- a/solution.py
+++ b/solution.py
@@ -295,9 +295,9 @@
     )
 
 
-def chunk_of(tall, wide):
+def chunk_of(tall, wide, most=1 << 19):
     rows = tall
-    while rows * wide > 1 << 19 and rows % 32 == 0:
+    while rows * wide > most and rows % 32 == 0:
         rows //= 2
     return rows
 
@@ -478,7 +478,7 @@
 
 def hop_sums(terms, up_at, down_at, up, down, sends, blocks=None):
     lead, _, tall, wide = terms.shape
-    rows = chunk_of(tall, wide)
+    rows = chunk_of(tall, wide, 1 << 17)
     block = pl.BlockSpec((1, rows, wide), lambda l, i, m: (l, i, 0))
 
     def term_spec(way):
@@ -1423,15 +1423,15 @@
 
     partners = jnp.stack([dp_at ^ m for m in range(dp_count)]).astype(jnp.int32)
     ff_local = ff_split(up_weight, down_weight, partners)
-    ff_rows = [ff_local[0]] + [swap_mask(ff_local[m], "dp", m) for m in range(1, dp_count)]
-    ff_rows = place_many(partners, ff_rows).reshape(2 * dp_count, own_rows, ff_part)
-
     small_cols = jnp.concatenate(
         [generator_in, norm_gains.T, jnp.zeros((own_rows, 128 - GEN - 5), bf16)], axis=1
     )
     small_all = gather_small(small_cols, both).reshape(model, 128)
     gen_first = small_all[:, :GEN]
-    gen_first, ff_rows = fence(gen_first, ff_rows)
+    gen_first, ff_local = fence(gen_first, ff_local)
+    ff_rows = [ff_local[0]] + [swap_mask(ff_local[m], "dp", m) for m in range(1, dp_count)]
+    ff_rows = place_many(partners, ff_rows).reshape(2 * dp_count, own_rows, ff_part)
+
     gain_float = small_all[:, GEN : GEN + 5].astype(f32).T
     second_rows = generator_out.shape[0]
     second_pad = -second_rows % 128

time: 1220 us -> 1230 us (level)
    unnamed x214 -> x206, local copies, waits for them, and re-layouts: 48.7 us -> 45.3 us
  transfers between devices with their start and end apart: 105 -> 105, of which waited for: 47 -> 45; matrix products, arithmetic and copies ran while one was open for 8% -> 8% of each run, Pallas kernels for 34% -> 34%
where the time goes in v10:
time: 1230 us; the launch traced here: 1220 us
  Pallas kernels  464 us (38%)
  waiting for transfers between devices  393 us (32%)
  starting transfers between devices  194 us (16%)
  local copies, waits for them, and re-layouts  71.5 us (6%)
  other arithmetic  67.3 us (5%)
  between operations  15.9 us (1%)
  matrix products  12.3 us (1%)
    ppermute x8, waiting for transfers between devices, step(): self.up = lax.ppermute(goes_up, 'depth', up_pairs)  94.3 us
    ppermute x4, waiting for transfers between devices, step_with(): lax.ppermute(goes[0], 'depth', [(i, i + 1) for i in range(size - 1)])  91.1 us
    pallas_call x12, Pallas kernels, hop_sums(): pl.pallas_call(functools.partial(hop_kernel, up is not None, blocks is no...  82.1 us
    ppermute x10, waiting for transfers between devices, core_hop(): return lax.ppermute(values, ('dp', 'mp'), pairs)  62.1 us
    ppermute x53, starting transfers between devices, swap_mask(): return lax.ppermute(values, axis, [(i, i ^ mask) for i in range(size)])  54.7 us
    ppermute x8, starting transfers between devices, step(): self.up = lax.ppermute(goes_up, 'depth', up_pairs)  51 us
    pallas_call x2, Pallas kernels, feed_forward(): pl.pallas_call(ff_kernel, grid_spec=pltpu.PrefetchScalarGridSpec(num_scal...  48 us
    ppermute x53, waiting for transfers between devices, swap_mask(): return lax.ppermute(values, axis, [(i, i ^ mask) for i in range(size)])  46 us
  transfers between devices with their start and end apart: 105, of which 45 were waited for; matrix products, arithmetic and copies ran while one was open for 8% of the time, Pallas kernels for 34%

profile of v10, /device:TPU:0, one launch (start us, length us, event | category | flops | bytes accessed | tf_op | source)
XLA Modules:
  0.0 1218.8 jit_solution(761487244329160990)
XLA Ops:
  95.7 14.3 %mix_streams.2 = bf16[4,1024,1024]{2,1,0:T(8,128)(2,1)} custom-call(f32[2048,20]{1,0:T(8,128)} %copy.101.mix_ref.refs_0_, bf16[5,2048,1024]{2,1,0:T(8,128)(2,1)} %refs_1_.1), custom_call_target="tpu_custom_call" | custom-call | flops 2097152 | bytes 943718 | tf_op jit(solution)/shard_map/mix_streams/pallas_call | solution.py:675
  110.0 14.5 %mix_streams.3 = bf16[4,1024,1024]{2,1,0:T(8,128)(2,1)} custom-call(f32[2048,20]{1,0:T(8,128)} %copy.101.mix_ref.refs_0_, bf16[5,2048,1024]{2,1,0:T(8,128)(2,1)} %refs_1_.1), custom_call_target="tpu_custom_call" | custom-call | flops 2097152 | bytes 943718 | tf_op jit(solution)/shard_map/mix_streams/pallas_call | solution.py:675
  124.5 16.2 %collective-permute-done.21.refs_1_ = bf16[8,128,1024]{2,1,0:T(8,128)(2,1)S(1)} collective-permute-done((bf16[8,128,1024]{2,1,0:T(8,128)(2,1)}, bf16[8,128,1024]{2,1,0:T(8,128)(2,1)S(1)}, u32[]{:S(2)}, u32[]{:S(2)}) %collective-permute-start.21) | collective-permute-done | bytes 2097184 | tf_op jit(solution)/shard_map/ppermute | solution.py:171
  176.2 25.8 %collective-permute-done.23.refs_2_ = bf16[4,256,1024]{2,1,0:T(8,128)(2,1)S(1)} collective-permute-done((bf16[4,256,1024]{2,1,0:T(8,128)(2,1)}, bf16[4,256,1024]{2,1,0:T(8,128)(2,1)S(1)}, u32[]{:S(2)}, u32[]{:S(2)}) %collective-permute-start.23) | collective-permute-done | bytes 2097184 | tf_op jit(solution)/shard_map/ppermute | solution.py:250
  226.8 37.4 %collective-permute-done.26.refs_2_ = bf16[4,256,1024]{2,1,0:T(8,128)(2,1)S(1)} collective-permute-done((bf16[4,256,1024]{2,1,0:T(8,128)(2,1)}, bf16[4,256,1024]{2,1,0:T(8,128)(2,1)S(1)}, u32[]{:S(2)}, u32[]{:S(2)}) %collective-permute-start.26) | collective-permute-done | bytes 2097184 | tf_op jit(solution)/shard_map/ppermute | solution.py:250
  306.7 9.6 place_line.5
  360.8 9.9 project_heads.2
  370.7 24.1 %collective-permute-done.33.refs_2_ = bf16[4,256,1024]{2,1,0:T(8,128)(2,1)} collective-permute-done((bf16[4,256,1024]{2,1,0:T(8,128)(2,1)}, bf16[4,256,1024]{2,1,0:T(8,128)(2,1)}, u32[]{:S(2)}, u32[]{:S(2)}) %collective-permute-start.33) | collective-permute-done | bytes 2097184 | tf_op jit(solution)/shard_map/ppermute | solution.py:223
  420.0 8.9 join_halves.6
  428.9 24.0 %feed_forward.2 = (bf16[1024,1024]{1,0:T(8,128)(2,1)S(1)}, bf16[1024,1024]{1,0:T(8,128)(2,1)S(1)}, f32[2,1024,1024]{2,1,0:T(8,128)}, bf16[2,1024,1024]{2,1,0:T(8,128)(2,1)}) custom-call(s32[1]{0:T(128)} %bitcast.74.model_ref.half_ref, bf16[1024,2048]{1,0:T(8,128)(2,1)} %join_halves.5.x_ref.x0_ref, bf16[4,2,256,2048]{3,2,1,0:T(8,128)(2,1)} %bitcast.384, ...), custom_call_target="tpu_custom_call" | custom-call | flops 858993472 | bytes 2097152 | tf_op jit(solution)/shard_map/feed_forward/pallas_call | solution.py:1147
  455.6 31.8 %collective-permute-done.36.refs_2_ = bf16[4,256,1024]{2,1,0:T(8,128)(2,1)} collective-permute-done((bf16[4,256,1024]{2,1,0:T(8,128)(2,1)}, bf16[4,256,1024]{2,1,0:T(8,128)(2,1)}, u32[]{:S(2)}, u32[]{:S(2)}) %collective-permute-start.36) | collective-permute-done | bytes 2097184 | tf_op jit(solution)/shard_map/ppermute | solution.py:223
  496.2 18.8 %collective-permute-start.40 = (bf16[4,256,1024]{2,1,0:T(8,128)(2,1)}, bf16[4,256,1024]{2,1,0:T(8,128)(2,1)}, u32[]{:S(2)}, u32[]{:S(2)}) collective-permute-start(bf16[4,256,1024]{2,1,0:T(8,128)(2,1)} %get-tuple-element.369), channel_id=1, source_target_pairs={{0,2},{2,4},{4,6},{1,3},{3,5},{5,7},{8,10},{10,12},{12,14},{9,11},... | collective-permute-start | bytes 6291464 | tf_op jit(solution)/shard_map/ppermute | solution.py:223
  516.6 10.7 attend.2
  528.7 29.8 %collective-permute-done.40.up_ref = bf16[4,256,1024]{2,1,0:T(8,128)(2,1)} collective-permute-done((bf16[4,256,1024]{2,1,0:T(8,128)(2,1)}, bf16[4,256,1024]{2,1,0:T(8,128)(2,1)}, u32[]{:S(2)}, u32[]{:S(2)}) %collective-permute-start.40) | collective-permute-done | bytes 2097184 | tf_op jit(solution)/shard_map/ppermute | solution.py:223
  590.7 8.9 project_heads.3
  636.6 11.2 collective-permute-done.46
  677.5 10.7 attend.3
  694.2 24.0 %feed_forward.3 = (bf16[1024,1024]{1,0:T(8,128)(2,1)S(1)}, bf16[1024,1024]{1,0:T(8,128)(2,1)S(1)}, f32[2,1024,1024]{2,1,0:T(8,128)}, bf16[2,1024,1024]{2,1,0:T(8,128)(2,1)}) custom-call(s32[1]{0:T(128)} %bitcast.74.model_ref.half_ref, bf16[1024,2048]{1,0:T(8,128)(2,1)} %join_halves.7.x_ref.x1_ref, bf16[4,2,256,2048]{3,2,1,0:T(8,128)(2,1)} %bitcast.385, ...), custom_call_target="tpu_custom_call" | custom-call | flops 858993472 | bytes 2097152 | tf_op jit(solution)/shard_map/feed_forward/pallas_call | solution.py:1147
  741.5 24.0 %hidden_grads.1.refs_0_.refs_1_.term_ref = bf16[8,4,128,1024]{3,2,1,0:T(8,128)(2,1)} custom-call(bf16[1024,2048]{1,0:T(8,128)(2,1)} %join_halves.5.x_ref.x0_ref, bf16[1024,2048]{1,0:T(8,128)(2,1)} %join_halves.7.x_ref.x1_ref, bf16[4,2,256,2048]{3,2,1,0:T(8,128)(2,1)} %bitcast.386, bf16[4,2,256,2048]{3,2,1,0:T(8,128)(2,1)} %bitcast.387, ...), custom_call_target="tpu_custom_call" | custom-call | flops 858993472 | bytes 838860 | tf_op jit(solution)/shard_map/hidden_grads/pallas_call | solution.py:623
  810.5 26.9 %collective-permute-done.53.refs_2_ = bf16[8,128,1024]{2,1,0:T(8,128)(2,1)S(1)} collective-permute-done((bf16[8,128,1024]{2,1,0:T(8,128)(2,1)}, bf16[8,128,1024]{2,1,0:T(8,128)(2,1)S(1)}, u32[]{:S(2)}, u32[]{:S(2)}) %collective-permute-start.53) | collective-permute-done | bytes 2097184 | tf_op jit(solution)/shard_map/ppermute | solution.py:250
  935.5 19.5 %unmix_streams.2 = (bf16[5,2048,1024]{2,1,0:T(8,128)(2,1)}, f32[1024,128]{1,0:T(8,128)}) custom-call(f32[2048,20]{1,0:T(8,128)} %copy.101.mix_ref.refs_0_, bf16[5,2048,1024]{2,1,0:T(8,128)(2,1)} %refs_1_.1, bf16[4,1024,1024]{2,1,0:T(8,128)(2,1)} %bitcast.397), custom_call_target="tpu_custom_call" | custom-call | flops 4194304 | bytes 1468006 | tf_op jit(solution)/shard_map/unmix_streams/pallas_call | solution.py:750
  973.0 36.5 %collective-permute-done.68 = bf16[4,4,128,1024]{3,2,1,0:T(8,128)(2,1)S(1)} collective-permute-done((bf16[4,4,128,1024]{3,2,1,0:T(8,128)(2,1)S(1)}, bf16[4,4,128,1024]{3,2,1,0:T(8,128)(2,1)S(1)}, u32[]{:S(2)}, u32[]{:S(2)}) %collective-permute-start.68) | collective-permute-done | bytes 4194336 | tf_op jit(solution)/shard_map/ppermute | solution.py:105
  1027.0 32.2 %collective-permute-done.65.refs_5_ = bf16[4,256,1024]{2,1,0:T(8,128)(2,1)} collective-permute-done((bf16[4,256,1024]{2,1,0:T(8,128)(2,1)}, bf16[4,256,1024]{2,1,0:T(8,128)(2,1)}, u32[]{:S(2)}, u32[]{:S(2)}) %collective-permute-start.65) | collective-permute-done | bytes 2097184 | tf_op jit(solution)/shard_map/ppermute | solution.py:172
  1090.8 19.5 %unmix_streams.3 = (bf16[5,2048,1024]{2,1,0:T(8,128)(2,1)}, f32[1024,128]{1,0:T(8,128)}) custom-call(f32[2048,20]{1,0:T(8,128)} %copy.101.mix_ref.refs_0_, bf16[5,2048,1024]{2,1,0:T(8,128)(2,1)} %refs_1_.1, bf16[4,1024,1024]{2,1,0:T(8,128)(2,1)} %bitcast.396, bf16[5,2048,1024]{2,1,0:T(8,128)(2,1)} %get-tuple-element.499.rest_0_), custom_call_target="tpu_custom_call", output_to_operand_aliasing={{0}: (3, {})} | custom-call | flops 4194304 | bytes 1468006 | tf_op jit(solution)/shard_map/unmix_streams/pallas_call | solution.py:750
  (618 shorter events, 713.6 us)
Async XLA Ops:
  7.2 135.3 %all-gather.5.cloned.1.call-start = ((), (), s32[]{:S(2)}) async-start(), calls=%async_computation.4 | async-start | bytes 5242880 | tf_op jit(solution)/shard_map/all_gather | solution.py:1443
  10.7 165.5 %all-gather.7.cloned.1.call-start = ((), (), s32[]{:S(2)}) async-start(), calls=%async_computation.5 | async-start | bytes 5242880 | tf_op jit(solution)/shard_map/all_gather | solution.py:1479
  89.7 50.9 %collective-permute-start.21 = (bf16[8,128,1024]{2,1,0:T(8,128)(2,1)}, bf16[8,128,1024]{2,1,0:T(8,128)(2,1)S(1)}, u32[]{:S(2)}, u32[]{:S(2)}) collective-permute-start(bf16[8,128,1024]{2,1,0:T(8,128)(2,1)} %bitcast.43.refs_0_), channel_id=1, source_target_pairs={{0,2},{2,4},{4,6},{1,3},{3,5},{5,7},{8,10},{10,12},{12,14},{9,11},... | collective-permute-start | bytes 6291464 | tf_op jit(solution)/shard_map/ppermute | solution.py:171
  94.3 300.4 %all-gather.9.cloned.1.call-start = ((), (), s32[]{:S(2)}) async-start(), calls=%async_computation.6 | async-start | bytes 2621440 | tf_op jit(solution)/shard_map/all_gather | solution.py:1546
  142.5 63.7 %collective-permute-start.25 = (bf16[2048,1024]{1,0:T(8,128)(2,1)}, bf16[2048,1024]{1,0:T(8,128)(2,1)}, u32[]{:S(2)}, u32[]{:S(2)}) collective-permute-start(bf16[2048,1024]{1,0:T(8,128)(2,1)} %all-gather.5.cloned.1.call-done), channel_id=1, source_target_pairs={{0,8},{1,17},{8,0},{9,25},{16,24},{17,1},{24,16},{25,9},{2,10},{3,... | collective-permute-start | bytes 12582920 | tf_op jit(solution)/shard_map/ppermute | solution.py:105
  152.1 49.8 %collective-permute-start.23 = (bf16[4,256,1024]{2,1,0:T(8,128)(2,1)}, bf16[4,256,1024]{2,1,0:T(8,128)(2,1)S(1)}, u32[]{:S(2)}, u32[]{:S(2)}) collective-permute-start(bf16[4,256,1024]{2,1,0:T(8,128)(2,1)} %get-tuple-element.282), channel_id=1, source_target_pairs={{0,2},{2,4},{4,6},{1,3},{3,5},{5,7},{8,10},{10,12},{12,14},{9,11},... | collective-permute-start | bytes 6291464 | tf_op jit(solution)/shard_map/ppermute | solution.py:250
  206.2 62.2 %collective-permute-start.28 = (bf16[2048,1024]{1,0:T(8,128)(2,1)}, bf16[2048,1024]{1,0:T(8,128)(2,1)}, u32[]{:S(2)}, u32[]{:S(2)}) collective-permute-start(bf16[2048,1024]{1,0:T(8,128)(2,1)} %all-gather.5.cloned.1.call-done), channel_id=1, source_target_pairs={{0,16},{1,9},{8,24},{9,1},{16,0},{17,25},{24,8},{25,17},{2,18},{3,... | collective-permute-start | bytes 12582920 | tf_op jit(solution)/shard_map/ppermute | solution.py:105
  268.5 61.6 %collective-permute-start.31 = (bf16[2048,1024]{1,0:T(8,128)(2,1)}, bf16[2048,1024]{1,0:T(8,128)(2,1)}, u32[]{:S(2)}, u32[]{:S(2)}) collective-permute-start(bf16[2048,1024]{1,0:T(8,128)(2,1)} %collective-permute-done.25), channel_id=1, source_target_pairs={{0,16},{1,9},{8,24},{9,1},{16,0},{17,25},{24,8},{25,17},{2,18},{3,... | collective-permute-start | bytes 12582920 | tf_op jit(solution)/shard_map/ppermute | solution.py:105
  402.2 85.1 %all-to-all-start = ((bf16[4,256,1024]{2,1,0:T(8,128)(2,1)}), bf16[4,256,1024]{2,1,0:T(8,128)(2,1)S(1)}, u32[]{:S(2)}, u32[]{:S(2)}) async-start(bf16[4,256,1024]{2,1,0:T(8,128)(2,1)} %project_heads.2), calls=%async_computation | async-start | bytes 4194304 | tf_op jit(solution)/shard_map/all_to_all | solution.py:1467
  407.9 79.4 %collective-permute-start.36 = (bf16[4,256,1024]{2,1,0:T(8,128)(2,1)}, bf16[4,256,1024]{2,1,0:T(8,128)(2,1)}, u32[]{:S(2)}, u32[]{:S(2)}) collective-permute-start(bf16[4,256,1024]{2,1,0:T(8,128)(2,1)} %get-tuple-element.354), channel_id=1, source_target_pairs={{0,2},{2,4},{1,3},{3,5},{8,10},{10,12},{9,11},{11,13},{16,18},{18,... | collective-permute-start | bytes 6291464 | tf_op jit(solution)/shard_map/ppermute | solution.py:223
  413.4 74.0 %collective-permute-start.37 = (bf16[4,256,1024]{2,1,0:T(8,128)(2,1)}, bf16[4,256,1024]{2,1,0:T(8,128)(2,1)}, u32[]{:S(2)}, u32[]{:S(2)}) collective-permute-start(bf16[4,256,1024]{2,1,0:T(8,128)(2,1)} %get-tuple-element.355), channel_id=1, source_target_pairs={{6,4},{4,2},{7,5},{5,3},{14,12},{12,10},{15,13},{13,11},{22,20},{2... | collective-permute-start | bytes 6291464 | tf_op jit(solution)/shard_map/ppermute | solution.py:224
  496.2 62.2 %collective-permute-start.40 = (bf16[4,256,1024]{2,1,0:T(8,128)(2,1)}, bf16[4,256,1024]{2,1,0:T(8,128)(2,1)}, u32[]{:S(2)}, u32[]{:S(2)}) collective-permute-start(bf16[4,256,1024]{2,1,0:T(8,128)(2,1)} %get-tuple-element.369), channel_id=1, source_target_pairs={{0,2},{2,4},{4,6},{1,3},{3,5},{5,7},{8,10},{10,12},{12,14},{9,11},... | collective-permute-start | bytes 6291464 | tf_op jit(solution)/shard_map/ppermute | solution.py:223
  563.9 52.9 %all-to-all-start.1 = ((bf16[4,256,1024]{2,1,0:T(8,128)(2,1)}), bf16[4,256,1024]{2,1,0:T(8,128)(2,1)S(1)}, u32[]{:S(2)}, u32[]{:S(2)}) async-start(bf16[4,256,1024]{2,1,0:T(8,128)(2,1)} %bitcast.333), calls=%async_computation.1 | async-start | bytes 4194304 | tf_op jit(solution)/shard_map/all_to_all | solution.py:1467
  616.8 52.9 %all-to-all-start.2 = ((bf16[4,256,1024]{2,1,0:T(8,128)(2,1)}), bf16[4,256,1024]{2,1,0:T(8,128)(2,1)}, u32[]{:S(2)}, u32[]{:S(2)}) async-start(bf16[4,256,1024]{2,1,0:T(8,128)(2,1)} %copy-done.24), calls=%async_computation.2 | async-start | bytes 4194304 | tf_op jit(solution)/shard_map/all_to_all | solution.py:1467
  669.7 51.1 %collective-permute-start.48 = (bf16[4,256,1024]{2,1,0:T(8,128)(2,1)}, bf16[4,256,1024]{2,1,0:T(8,128)(2,1)S(1)}, u32[]{:S(2)}, u32[]{:S(2)}) collective-permute-start(bf16[4,256,1024]{2,1,0:T(8,128)(2,1)} %get-tuple-element.399.refs_0_), channel_id=1, source_target_pairs={{0,2},{2,4},{4,6},{1,3},{3,5},{5,7},{8,10},{10,12},{12,14},{9,11},... | collective-permute-start | bytes 6291464 | tf_op jit(solution)/shard_map/ppermute | solution.py:171
  722.4 54.9 %all-to-all-start.3 = ((bf16[4,256,1024]{2,1,0:T(8,128)(2,1)}), bf16[4,256,1024]{2,1,0:T(8,128)(2,1)S(1)}, u32[]{:S(2)}, u32[]{:S(2)}) async-start(bf16[4,256,1024]{2,1,0:T(8,128)(2,1)} %bitcast.334), calls=%async_computation.3 | async-start | bytes 4194304 | tf_op jit(solution)/shard_map/all_to_all | solution.py:1467
  791.4 50.2 %collective-permute-start.54 = (bf16[8,128,1024]{2,1,0:T(8,128)(2,1)}, bf16[8,128,1024]{2,1,0:T(8,128)(2,1)}, u32[]{:S(2)}, u32[]{:S(2)}) collective-permute-start(bf16[8,128,1024]{2,1,0:T(8,128)(2,1)} %get-tuple-element.424), channel_id=1, source_target_pairs={{2,0},{4,2},{6,4},{3,1},{5,3},{7,5},{10,8},{12,10},{14,12},{11,9},... | collective-permute-start | bytes 6291464 | tf_op jit(solution)/shard_map/ppermute | solution.py:251
  846.2 50.7 %collective-permute-start.60 = (bf16[4,4,128,1024]{3,2,1,0:T(8,128)(2,1)}, bf16[4,4,128,1024]{3,2,1,0:T(8,128)(2,1)}, u32[]{:S(2)}, u32[]{:S(2)}) collective-permute-start(bf16[4,4,128,1024]{3,2,1,0:T(8,128)(2,1)} %attention_grads.5), channel_id=1, source_target_pairs={{0,16},{1,9},{8,24},{9,1},{16,0},{17,25},{24,8},{25,17},{2,18},{3,... | collective-permute-start | bytes 12582920 | tf_op jit(solution)/shard_map/ppermute | solution.py:105
  906.8 54.1 %collective-permute-start.61 = (bf16[4,256,1024]{2,1,0:T(8,128)(2,1)S(1)}, bf16[4,256,1024]{2,1,0:T(8,128)(2,1)}, u32[]{:S(2)}, u32[]{:S(2)}) collective-permute-start(bf16[4,256,1024]{2,1,0:T(8,128)(2,1)S(1)} %copy-done.13), channel_id=1, source_target_pairs={{0,2},{2,4},{4,6},{1,3},{3,5},{5,7},{8,10},{10,12},{12,14},{9,11},... | collective-permute-start | bytes 6291464 | tf_op jit(solution)/shard_map/ppermute | solution.py:171
  961.6 52.3 %collective-permute-start.66 = (bf16[8,128,1024]{2,1,0:T(8,128)(2,1)S(1)}, bf16[8,128,1024]{2,1,0:T(8,128)(2,1)}, u32[]{:S(2)}, u32[]{:S(2)}) collective-permute-start(bf16[8,128,1024]{2,1,0:T(8,128)(2,1)S(1)} %copy-done.100), channel_id=1, source_target_pairs={{0,2},{2,4},{4,6},{1,3},{3,5},{5,7},{8,10},{10,12},{12,14},{9,11},... | collective-permute-start | bytes 6291464 | tf_op jit(solution)/shard_map/ppermute | solution.py:223
  968.2 50.6 %collective-permute-start.67 = (bf16[8,128,1024]{2,1,0:T(8,128)(2,1)S(1)}, bf16[8,128,1024]{2,1,0:T(8,128)(2,1)}, u32[]{:S(2)}, u32[]{:S(2)}) collective-permute-start(bf16[8,128,1024]{2,1,0:T(8,128)(2,1)S(1)} %copy-done.99), channel_id=1, source_target_pairs={{6,4},{4,2},{2,0},{7,5},{5,3},{3,1},{14,12},{12,10},{10,8},{15,13}... | collective-permute-start | bytes 6291464 | tf_op jit(solution)/shard_map/ppermute | solution.py:224
  969.5 57.6 %collective-permute-start.64 = (bf16[4,256,1024]{2,1,0:T(8,128)(2,1)}, bf16[4,256,1024]{2,1,0:T(8,128)(2,1)}, u32[]{:S(2)}, u32[]{:S(2)}) collective-permute-start(bf16[4,256,1024]{2,1,0:T(8,128)(2,1)} %collective-permute-done.61.refs_1_), channel_id=1, source_target_pairs={{2,4},{4,6},{3,5},{5,7},{10,12},{12,14},{11,13},{13,15},{18,20},{2... | collective-permute-start | bytes 6291464 | tf_op jit(solution)/shard_map/ppermute | solution.py:171
  971.5 87.8 %collective-permute-start.65 = (bf16[4,256,1024]{2,1,0:T(8,128)(2,1)}, bf16[4,256,1024]{2,1,0:T(8,128)(2,1)}, u32[]{:S(2)}, u32[]{:S(2)}) collective-permute-start(bf16[4,256,1024]{2,1,0:T(8,128)(2,1)} %collective-permute-done.62.refs_6_), channel_id=1, source_target_pairs={{2,0},{4,2},{3,1},{5,3},{10,8},{12,10},{11,9},{13,11},{18,16},{20,... | collective-permute-start | bytes 6291464 | tf_op jit(solution)/shard_map/ppermute | solution.py:172
  1059.3 51.1 %collective-permute-start.71 = (bf16[4,256,1024]{2,1,0:T(8,128)(2,1)}, bf16[4,256,1024]{2,1,0:T(8,128)(2,1)}, u32[]{:S(2)}, u32[]{:S(2)}) collective-permute-start(bf16[4,256,1024]{2,1,0:T(8,128)(2,1)} %collective-permute-done.64.refs_2_), channel_id=1, source_target_pairs={{4,6},{5,7},{12,14},{13,15},{20,22},{21,23},{28,30},{29,31}} | collective-permute-start | bytes 6291464 | tf_op jit(solution)/shard_map/ppermute | solution.py:171
  (182 other events, 2695.3 us)
Sparse Core Ops, SparseCore 0:
  10.8 96.6 all-gather.4
  109.3 62.2 all-gather.6
  347.3 32.5 all-gather.8
  624.2 38.5 all-gather.10

commit v11 on v10

--- a/solution.py
+++ b/solution.py
@@ -295,9 +295,9 @@
     )
 
 
-def chunk_of(tall, wide, most=1 << 19):
+def chunk_of(tall, wide):
     rows = tall
-    while rows * wide > most and rows % 32 == 0:
+    while rows * wide > 1 << 19 and rows % 32 == 0:
         rows //= 2
     return rows
 
@@ -460,10 +460,10 @@
     sums, ins = (ins[:2], ins[2:]) if has_sums else (None, ins)
 
     def send_sum(way):
-        term = terms[way][0, 0].astype(f32)
+        term = terms[way][:, 0].astype(f32)
         if sums is not None:
-            term = term + sums[way][0].astype(f32)
-        outs[way][0] = term.astype(bf16)
+            term = term + sums[way][...].astype(f32)
+        outs[way][...] = term.astype(bf16)
 
     for way in range(2):
         if not has_blocks:
@@ -473,17 +473,20 @@
 
         @pl.when(at_ref[2 + way] == 0)
         def _(way=way):
-            outs[way][0] = ins[way][0]
+            outs[way][...] = ins[way][...]
 
 
 def hop_sums(terms, up_at, down_at, up, down, sends, blocks=None):
     lead, _, tall, wide = terms.shape
-    rows = chunk_of(tall, wide, 1 << 17)
-    block = pl.BlockSpec((1, rows, wide), lambda l, i, m: (l, i, 0))
+    rows = chunk_of(tall, wide)
+    deep = lead
+    while deep * rows * wide > 1 << 19 and deep % 2 == 0:
+        deep //= 2
+    block = pl.BlockSpec((deep, rows, wide), lambda l, i, m: (l, i, 0))
 
     def term_spec(way):
         return pl.BlockSpec(
-            (1, 1, rows, wide), lambda l, i, m: (l * m[2 + way], m[way], i * m[2 + way], 0)
+            (deep, 1, rows, wide), lambda l, i, m: (l * m[2 + way], m[way], i * m[2 + way], 0)
         )
 
     def block_spec(way, sign):
@@ -491,7 +494,7 @@
             need = m[2 + way] if sign else 1 - m[2 + way]
             return (l * need, i * need, 0)
 
-        return pl.BlockSpec((1, rows, wide), index)
+        return pl.BlockSpec((deep, rows, wide), index)
 
     in_specs = [term_spec(0), term_spec(1)]
     operands = [terms, terms]
@@ -505,7 +508,7 @@
         functools.partial(hop_kernel, up is not None, blocks is not None),
         grid_spec=pltpu.PrefetchScalarGridSpec(
             num_scalar_prefetch=1,
-            grid=(lead, tall // rows),
+            grid=(lead // deep, tall // rows),
             in_specs=in_specs,
             out_specs=[block, block],
         ),
@@ -513,6 +516,7 @@
         cost_estimate=spent(
             flops=2 * lead * tall * wide, bytes_accessed=12 * lead * tall * wide, transcendentals=0
         ),
+        compiler_params=pltpu.CompilerParams(vmem_limit_bytes=40 << 20),
         name="hop_sums",
     )(jnp.stack([up_at, down_at, *sends]).astype(jnp.int32), *operands)
 

time: 1230 us -> 1210 us (0.984)
  Pallas kernels: 464 us -> 428 us
  local copies, waits for them, and re-layouts: 71.5 us -> 84.9 us
    pallas_call x12, Pallas kernels: 82.1 us -> 45.4 us  [hop_sums(): pl.pallas_call(functools.partial(hop_kernel, up is not None, blocks is no...]
    unnamed x206 -> x228, local copies, waits for them, and re-layouts: 45.3 us -> 56.3 us
  transfers between devices with their start and end apart: 105 -> 105, of which waited for: 45 -> 48; matrix products, arithmetic and copies ran while one was open for 8% -> 8% of each run, Pallas kernels for 34% -> 33%
where the time goes in v11:
time: 1210 us; the launch traced here: 1200 us
  Pallas kernels  428 us (35%)
  waiting for transfers between devices  405 us (33%)
  starting transfers between devices  183 us (15%)
  local copies, waits for them, and re-layouts  84.9 us (7%)
  other arithmetic  68 us (6%)
  between operations  16.1 us (1%)
  matrix products  12.3 us (1%)
    ppermute x8, waiting for transfers between devices, step(): self.up = lax.ppermute(goes_up, 'depth', up_pairs)  94.4 us
    ppermute x4, waiting for transfers between devices, step_with(): lax.ppermute(goes[0], 'depth', [(i, i + 1) for i in range(size - 1)])  84.8 us
    ppermute x10, waiting for transfers between devices, core_hop(): return lax.ppermute(values, ('dp', 'mp'), pairs)  67.9 us
    unnamed x228, local copies, waits for them, and re-layouts  56.3 us
    ppermute x53, waiting for transfers between devices, swap_mask(): return lax.ppermute(values, axis, [(i, i ^ mask) for i in range(size)])  53.5 us
    ppermute x53, starting transfers between devices, swap_mask(): return lax.ppermute(values, axis, [(i, i ^ mask) for i in range(size)])  50.5 us
    pallas_call x2, Pallas kernels, feed_forward(): pl.pallas_call(ff_kernel, grid_spec=pltpu.PrefetchScalarGridSpec(num_scal...  48 us
    ppermute x8, starting transfers between devices, step(): self.up = lax.ppermute(goes_up, 'depth', up_pairs)  46.9 us
  transfers between devices with their start and end apart: 105, of which 48 were waited for; matrix products, arithmetic and copies ran while one was open for 8% of the time, Pallas kernels for 33%

profile of v11, /device:TPU:0, one launch (start us, length us, event | category | flops | bytes accessed | tf_op | source)
XLA Modules:
  0.0 1196.7 jit_solution(8845241547055590312)
XLA Ops:
  101.5 14.4 %mix_streams.2 = bf16[4,1024,1024]{2,1,0:T(8,128)(2,1)} custom-call(f32[2048,20]{1,0:T(8,128)} %copy.101.mix_ref.refs_0_, bf16[5,2048,1024]{2,1,0:T(8,128)(2,1)} %refs_1_.1), custom_call_target="tpu_custom_call" | custom-call | flops 2097152 | bytes 943718 | tf_op jit(solution)/shard_map/mix_streams/pallas_call | solution.py:679
  116.0 14.3 %mix_streams.3 = bf16[4,1024,1024]{2,1,0:T(8,128)(2,1)} custom-call(f32[2048,20]{1,0:T(8,128)} %copy.101.mix_ref.refs_0_, bf16[5,2048,1024]{2,1,0:T(8,128)(2,1)} %refs_1_.1), custom_call_target="tpu_custom_call" | custom-call | flops 2097152 | bytes 943718 | tf_op jit(solution)/shard_map/mix_streams/pallas_call | solution.py:679
  130.2 12.1 %collective-permute-done.21.refs_1_ = bf16[8,128,1024]{2,1,0:T(8,128)(2,1)S(1)} collective-permute-done((bf16[8,128,1024]{2,1,0:T(8,128)(2,1)}, bf16[8,128,1024]{2,1,0:T(8,128)(2,1)S(1)}, u32[]{:S(2)}, u32[]{:S(2)}) %collective-permute-start.21) | collective-permute-done | bytes 2097184 | tf_op jit(solution)/shard_map/ppermute | solution.py:171
  173.5 23.8 %collective-permute-done.23.refs_2_ = bf16[4,256,1024]{2,1,0:T(8,128)(2,1)S(1)} collective-permute-done((bf16[4,256,1024]{2,1,0:T(8,128)(2,1)}, bf16[4,256,1024]{2,1,0:T(8,128)(2,1)S(1)}, u32[]{:S(2)}, u32[]{:S(2)}) %collective-permute-start.23) | collective-permute-done | bytes 2097184 | tf_op jit(solution)/shard_map/ppermute | solution.py:250
  220.7 36.6 %collective-permute-done.26.refs_2_ = bf16[4,256,1024]{2,1,0:T(8,128)(2,1)} collective-permute-done((bf16[4,256,1024]{2,1,0:T(8,128)(2,1)}, bf16[4,256,1024]{2,1,0:T(8,128)(2,1)}, u32[]{:S(2)}, u32[]{:S(2)}) %collective-permute-start.26) | collective-permute-done | bytes 2097184 | tf_op jit(solution)/shard_map/ppermute | solution.py:250
  294.7 10.0 place_line.5
  304.6 9.9 collective-permute-done.29.up_ref
  351.4 9.9 project_heads.2
  361.3 23.7 %collective-permute-done.33.refs_2_ = bf16[4,256,1024]{2,1,0:T(8,128)(2,1)} collective-permute-done((bf16[4,256,1024]{2,1,0:T(8,128)(2,1)}, bf16[4,256,1024]{2,1,0:T(8,128)(2,1)}, u32[]{:S(2)}, u32[]{:S(2)}) %collective-permute-start.33) | collective-permute-done | bytes 2097184 | tf_op jit(solution)/shard_map/ppermute | solution.py:223
  416.8 24.0 %feed_forward.2 = (bf16[1024,1024]{1,0:T(8,128)(2,1)S(1)}, bf16[1024,1024]{1,0:T(8,128)(2,1)S(1)}, f32[2,1024,1024]{2,1,0:T(8,128)}, bf16[2,1024,1024]{2,1,0:T(8,128)(2,1)}) custom-call(s32[1]{0:T(128)} %bitcast.74.model_ref.half_ref, bf16[1024,2048]{1,0:T(8,128)(2,1)} %join_halves.5.x_ref.x0_ref, bf16[4,2,256,2048]{3,2,1,0:T(8,128)(2,1)} %bitcast.383, ...), custom_call_target="tpu_custom_call" | custom-call | flops 858993472 | bytes 2097152 | tf_op jit(solution)/shard_map/feed_forward/pallas_call | solution.py:1151
  443.4 33.3 %collective-permute-done.36.refs_2_ = bf16[4,256,1024]{2,1,0:T(8,128)(2,1)S(1)} collective-permute-done((bf16[4,256,1024]{2,1,0:T(8,128)(2,1)}, bf16[4,256,1024]{2,1,0:T(8,128)(2,1)S(1)}, u32[]{:S(2)}, u32[]{:S(2)}) %collective-permute-start.36) | collective-permute-done | bytes 2097184 | tf_op jit(solution)/shard_map/ppermute | solution.py:223
  481.4 19.1 %collective-permute-start.40 = (bf16[4,256,1024]{2,1,0:T(8,128)(2,1)}, bf16[4,256,1024]{2,1,0:T(8,128)(2,1)}, u32[]{:S(2)}, u32[]{:S(2)}) collective-permute-start(bf16[4,256,1024]{2,1,0:T(8,128)(2,1)} %get-tuple-element.369), channel_id=1, source_target_pairs={{0,2},{2,4},{4,6},{1,3},{3,5},{5,7},{8,10},{10,12},{12,14},{9,11},... | collective-permute-start | bytes 6291464 | tf_op jit(solution)/shard_map/ppermute | solution.py:223
  505.3 10.7 attend.2
  517.3 27.2 %collective-permute-done.40.up_ref = bf16[4,256,1024]{2,1,0:T(8,128)(2,1)} collective-permute-done((bf16[4,256,1024]{2,1,0:T(8,128)(2,1)}, bf16[4,256,1024]{2,1,0:T(8,128)(2,1)}, u32[]{:S(2)}, u32[]{:S(2)}) %collective-permute-start.40) | collective-permute-done | bytes 2097184 | tf_op jit(solution)/shard_map/ppermute | solution.py:223
  622.7 11.1 collective-permute-done.46
  663.6 10.7 attend.3
  680.3 24.0 %feed_forward.3 = (bf16[1024,1024]{1,0:T(8,128)(2,1)S(1)}, bf16[1024,1024]{1,0:T(8,128)(2,1)S(1)}, f32[2,1024,1024]{2,1,0:T(8,128)}, bf16[2,1024,1024]{2,1,0:T(8,128)(2,1)}) custom-call(s32[1]{0:T(128)} %bitcast.74.model_ref.half_ref, bf16[1024,2048]{1,0:T(8,128)(2,1)} %join_halves.7.x_ref.x1_ref, bf16[4,2,256,2048]{3,2,1,0:T(8,128)(2,1)} %bitcast.384, ...), custom_call_target="tpu_custom_call" | custom-call | flops 858993472 | bytes 2097152 | tf_op jit(solution)/shard_map/feed_forward/pallas_call | solution.py:1151
  727.4 24.0 %hidden_grads.1.refs_0_.refs_1_.term_ref = bf16[8,4,128,1024]{3,2,1,0:T(8,128)(2,1)} custom-call(bf16[1024,2048]{1,0:T(8,128)(2,1)} %join_halves.5.x_ref.x0_ref, bf16[1024,2048]{1,0:T(8,128)(2,1)} %join_halves.7.x_ref.x1_ref, bf16[4,2,256,2048]{3,2,1,0:T(8,128)(2,1)} %bitcast.385, bf16[4,2,256,2048]{3,2,1,0:T(8,128)(2,1)} %bitcast.386, ...), custom_call_target="tpu_custom_call" | custom-call | flops 858993472 | bytes 838860 | tf_op jit(solution)/shard_map/hidden_grads/pallas_call | solution.py:627
  754.4 10.1 all-to-all-done.3.ans_ref
  798.2 23.3 %collective-permute-done.53.refs_2_ = bf16[8,128,1024]{2,1,0:T(8,128)(2,1)S(1)} collective-permute-done((bf16[8,128,1024]{2,1,0:T(8,128)(2,1)S(1)}, bf16[8,128,1024]{2,1,0:T(8,128)(2,1)S(1)}, u32[]{:S(2)}, u32[]{:S(2)}) %collective-permute-start.53) | collective-permute-done | bytes 2097184 | tf_op jit(solution)/shard_map/ppermute | solution.py:250
  914.0 19.5 %unmix_streams.2 = (bf16[5,2048,1024]{2,1,0:T(8,128)(2,1)}, f32[1024,128]{1,0:T(8,128)}) custom-call(f32[2048,20]{1,0:T(8,128)} %copy.101.mix_ref.refs_0_, bf16[5,2048,1024]{2,1,0:T(8,128)(2,1)} %refs_1_.1, bf16[4,1024,1024]{2,1,0:T(8,128)(2,1)} %bitcast.392), custom_call_target="tpu_custom_call" | custom-call | flops 4194304 | bytes 1468006 | tf_op jit(solution)/shard_map/unmix_streams/pallas_call | solution.py:754
  954.0 38.0 %collective-permute-done.68 = bf16[4,4,128,1024]{3,2,1,0:T(8,128)(2,1)S(1)} collective-permute-done((bf16[4,4,128,1024]{3,2,1,0:T(8,128)(2,1)S(1)}, bf16[4,4,128,1024]{3,2,1,0:T(8,128)(2,1)S(1)}, u32[]{:S(2)}, u32[]{:S(2)}) %collective-permute-start.68) | collective-permute-done | bytes 4194336 | tf_op jit(solution)/shard_map/ppermute | solution.py:105
  1004.6 35.9 %collective-permute-done.65.refs_5_ = bf16[4,256,1024]{2,1,0:T(8,128)(2,1)} collective-permute-done((bf16[4,256,1024]{2,1,0:T(8,128)(2,1)}, bf16[4,256,1024]{2,1,0:T(8,128)(2,1)}, u32[]{:S(2)}, u32[]{:S(2)}) %collective-permute-start.65) | collective-permute-done | bytes 2097184 | tf_op jit(solution)/shard_map/ppermute | solution.py:172
  1068.7 19.5 %unmix_streams.3 = (bf16[5,2048,1024]{2,1,0:T(8,128)(2,1)}, f32[1024,128]{1,0:T(8,128)}) custom-call(f32[2048,20]{1,0:T(8,128)} %copy.101.mix_ref.refs_0_, bf16[5,2048,1024]{2,1,0:T(8,128)(2,1)} %refs_1_.1, bf16[4,1024,1024]{2,1,0:T(8,128)(2,1)} %bitcast.391, bf16[5,2048,1024]{2,1,0:T(8,128)(2,1)} %get-tuple-element.499.rest_0_), custom_call_target="tpu_custom_call", output_to_operand_aliasing={{0}: (3, {})} | custom-call | flops 4194304 | bytes 1468006 | tf_op jit(solution)/shard_map/unmix_streams/pallas_call | solution.py:754
  (640 shorter events, 695.4 us)
Async XLA Ops:
  7.2 139.6 %all-gather.5.cloned.1.call-start = ((), (), s32[]{:S(2)}) async-start(), calls=%async_computation.4 | async-start | bytes 5242880 | tf_op jit(solution)/shard_map/all_gather | solution.py:1447
  10.7 162.8 %all-gather.7.cloned.1.call-start = ((), (), s32[]{:S(2)}) async-start(), calls=%async_computation.5 | async-start | bytes 5242880 | tf_op jit(solution)/shard_map/all_gather | solution.py:1483
  100.1 284.9 %all-gather.9.cloned.1.call-start = ((), (), s32[]{:S(2)}) async-start(), calls=%async_computation.6 | async-start | bytes 2621440 | tf_op jit(solution)/shard_map/all_gather | solution.py:1550
  146.9 54.8 %collective-permute-start.25 = (bf16[2048,1024]{1,0:T(8,128)(2,1)}, bf16[2048,1024]{1,0:T(8,128)(2,1)}, u32[]{:S(2)}, u32[]{:S(2)}) collective-permute-start(bf16[2048,1024]{1,0:T(8,128)(2,1)} %all-gather.5.cloned.1.call-done), channel_id=1, source_target_pairs={{0,8},{1,17},{8,0},{9,25},{16,24},{17,1},{24,16},{25,9},{2,10},{3,... | collective-permute-start | bytes 12582920 | tf_op jit(solution)/shard_map/ppermute | solution.py:105
  201.7 61.0 %collective-permute-start.28 = (bf16[2048,1024]{1,0:T(8,128)(2,1)}, bf16[2048,1024]{1,0:T(8,128)(2,1)}, u32[]{:S(2)}, u32[]{:S(2)}) collective-permute-start(bf16[2048,1024]{1,0:T(8,128)(2,1)} %all-gather.5.cloned.1.call-done), channel_id=1, source_target_pairs={{0,16},{1,9},{8,24},{9,1},{16,0},{17,25},{24,8},{25,17},{2,18},{3,... | collective-permute-start | bytes 12582920 | tf_op jit(solution)/shard_map/ppermute | solution.py:105
  262.7 57.2 %collective-permute-start.31 = (bf16[2048,1024]{1,0:T(8,128)(2,1)}, bf16[2048,1024]{1,0:T(8,128)(2,1)}, u32[]{:S(2)}, u32[]{:S(2)}) collective-permute-start(bf16[2048,1024]{1,0:T(8,128)(2,1)} %collective-permute-done.25), channel_id=1, source_target_pairs={{0,16},{1,9},{8,24},{9,1},{16,0},{17,25},{24,8},{25,17},{2,18},{3,... | collective-permute-start | bytes 12582920 | tf_op jit(solution)/shard_map/ppermute | solution.py:105
  391.6 85.2 %all-to-all-start = ((bf16[4,256,1024]{2,1,0:T(8,128)(2,1)}), bf16[4,256,1024]{2,1,0:T(8,128)(2,1)}, u32[]{:S(2)}, u32[]{:S(2)}) async-start(bf16[4,256,1024]{2,1,0:T(8,128)(2,1)} %project_heads.2), calls=%async_computation | async-start | bytes 4194304 | tf_op jit(solution)/shard_map/all_to_all | solution.py:1471
  397.3 79.4 %collective-permute-start.36 = (bf16[4,256,1024]{2,1,0:T(8,128)(2,1)}, bf16[4,256,1024]{2,1,0:T(8,128)(2,1)S(1)}, u32[]{:S(2)}, u32[]{:S(2)}) collective-permute-start(bf16[4,256,1024]{2,1,0:T(8,128)(2,1)} %copy-done.55), channel_id=1, source_target_pairs={{0,2},{2,4},{1,3},{3,5},{8,10},{10,12},{9,11},{11,13},{16,18},{18,... | collective-permute-start | bytes 6291464 | tf_op jit(solution)/shard_map/ppermute | solution.py:223
  401.2 75.6 %collective-permute-start.37 = (bf16[4,256,1024]{2,1,0:T(8,128)(2,1)}, bf16[4,256,1024]{2,1,0:T(8,128)(2,1)}, u32[]{:S(2)}, u32[]{:S(2)}) collective-permute-start(bf16[4,256,1024]{2,1,0:T(8,128)(2,1)} %copy-done.54), channel_id=1, source_target_pairs={{6,4},{4,2},{7,5},{5,3},{14,12},{12,10},{15,13},{13,11},{22,20},{2... | collective-permute-start | bytes 6291464 | tf_op jit(solution)/shard_map/ppermute | solution.py:224
  481.4 63.1 %collective-permute-start.40 = (bf16[4,256,1024]{2,1,0:T(8,128)(2,1)}, bf16[4,256,1024]{2,1,0:T(8,128)(2,1)}, u32[]{:S(2)}, u32[]{:S(2)}) collective-permute-start(bf16[4,256,1024]{2,1,0:T(8,128)(2,1)} %get-tuple-element.369), channel_id=1, source_target_pairs={{0,2},{2,4},{4,6},{1,3},{3,5},{5,7},{8,10},{10,12},{12,14},{9,11},... | collective-permute-start | bytes 6291464 | tf_op jit(solution)/shard_map/ppermute | solution.py:223
  550.0 52.9 %all-to-all-start.1 = ((bf16[4,256,1024]{2,1,0:T(8,128)(2,1)}), bf16[4,256,1024]{2,1,0:T(8,128)(2,1)S(1)}, u32[]{:S(2)}, u32[]{:S(2)}) async-start(bf16[4,256,1024]{2,1,0:T(8,128)(2,1)} %bitcast.346), calls=%async_computation.1 | async-start | bytes 4194304 | tf_op jit(solution)/shard_map/all_to_all | solution.py:1471
  602.9 52.9 %all-to-all-start.2 = ((bf16[4,256,1024]{2,1,0:T(8,128)(2,1)}), bf16[4,256,1024]{2,1,0:T(8,128)(2,1)}, u32[]{:S(2)}, u32[]{:S(2)}) async-start(bf16[4,256,1024]{2,1,0:T(8,128)(2,1)} %copy-done.25), calls=%async_computation.2 | async-start | bytes 4194304 | tf_op jit(solution)/shard_map/all_to_all | solution.py:1471
  655.8 51.2 %collective-permute-start.48 = (bf16[4,256,1024]{2,1,0:T(8,128)(2,1)}, bf16[4,256,1024]{2,1,0:T(8,128)(2,1)S(1)}, u32[]{:S(2)}, u32[]{:S(2)}) collective-permute-start(bf16[4,256,1024]{2,1,0:T(8,128)(2,1)} %get-tuple-element.399.refs_0_), channel_id=1, source_target_pairs={{0,2},{2,4},{4,6},{1,3},{3,5},{5,7},{8,10},{10,12},{12,14},{9,11},... | collective-permute-start | bytes 6291464 | tf_op jit(solution)/shard_map/ppermute | solution.py:171
  659.0 49.5 %collective-permute-start.49 = (bf16[4,256,1024]{2,1,0:T(8,128)(2,1)}, bf16[4,256,1024]{2,1,0:T(8,128)(2,1)}, u32[]{:S(2)}, u32[]{:S(2)}) collective-permute-start(bf16[4,256,1024]{2,1,0:T(8,128)(2,1)} %get-tuple-element.399.refs_0_), channel_id=1, source_target_pairs={{2,0},{4,2},{6,4},{3,1},{5,3},{7,5},{10,8},{12,10},{14,12},{11,9},... | collective-permute-start | bytes 6291464 | tf_op jit(solution)/shard_map/ppermute | solution.py:172
  708.5 56.0 %all-to-all-start.3 = ((bf16[4,256,1024]{2,1,0:T(8,128)(2,1)}), bf16[4,256,1024]{2,1,0:T(8,128)(2,1)S(1)}, u32[]{:S(2)}, u32[]{:S(2)}) async-start(bf16[4,256,1024]{2,1,0:T(8,128)(2,1)} %bitcast.347), calls=%async_computation.3 | async-start | bytes 4194304 | tf_op jit(solution)/shard_map/all_to_all | solution.py:1471
  775.8 50.0 %collective-permute-start.54 = (bf16[8,128,1024]{2,1,0:T(8,128)(2,1)S(1)}, bf16[8,128,1024]{2,1,0:T(8,128)(2,1)}, u32[]{:S(2)}, u32[]{:S(2)}) collective-permute-start(bf16[8,128,1024]{2,1,0:T(8,128)(2,1)S(1)} %get-tuple-element.424), channel_id=1, source_target_pairs={{2,0},{4,2},{6,4},{3,1},{5,3},{7,5},{10,8},{12,10},{14,12},{11,9},... | collective-permute-start | bytes 6291464 | tf_op jit(solution)/shard_map/ppermute | solution.py:251
  830.3 49.5 %collective-permute-start.60 = (bf16[4,4,128,1024]{3,2,1,0:T(8,128)(2,1)}, bf16[4,4,128,1024]{3,2,1,0:T(8,128)(2,1)}, u32[]{:S(2)}, u32[]{:S(2)}) collective-permute-start(bf16[4,4,128,1024]{3,2,1,0:T(8,128)(2,1)} %attention_grads.5), channel_id=1, source_target_pairs={{0,16},{1,9},{8,24},{9,1},{16,0},{17,25},{24,8},{25,17},{2,18},{3,... | collective-permute-start | bytes 12582920 | tf_op jit(solution)/shard_map/ppermute | solution.py:105
  837.9 49.7 %collective-permute-start.58 = (bf16[8,128,1024]{2,1,0:T(8,128)(2,1)}, bf16[8,128,1024]{2,1,0:T(8,128)(2,1)}, u32[]{:S(2)}, u32[]{:S(2)}) collective-permute-start(bf16[8,128,1024]{2,1,0:T(8,128)(2,1)} %get-tuple-element.439), channel_id=1, source_target_pairs={{2,0},{4,2},{6,4},{3,1},{5,3},{7,5},{10,8},{12,10},{14,12},{11,9},... | collective-permute-start | bytes 6291464 | tf_op jit(solution)/shard_map/ppermute | solution.py:251
  839.2 49.6 %collective-permute-start.57 = (bf16[8,128,1024]{2,1,0:T(8,128)(2,1)}, bf16[8,128,1024]{2,1,0:T(8,128)(2,1)}, u32[]{:S(2)}, u32[]{:S(2)}) collective-permute-start(bf16[8,128,1024]{2,1,0:T(8,128)(2,1)} %get-tuple-element.437), channel_id=1, source_target_pairs={{0,2},{2,4},{4,6},{1,3},{3,5},{5,7},{8,10},{10,12},{12,14},{9,11},... | collective-permute-start | bytes 6291464 | tf_op jit(solution)/shard_map/ppermute | solution.py:250
  890.0 53.5 %collective-permute-start.61 = (bf16[4,256,1024]{2,1,0:T(8,128)(2,1)S(1)}, bf16[4,256,1024]{2,1,0:T(8,128)(2,1)}, u32[]{:S(2)}, u32[]{:S(2)}) collective-permute-start(bf16[4,256,1024]{2,1,0:T(8,128)(2,1)S(1)} %copy-done.16), channel_id=1, source_target_pairs={{0,2},{2,4},{4,6},{1,3},{3,5},{5,7},{8,10},{10,12},{12,14},{9,11},... | collective-permute-start | bytes 6291464 | tf_op jit(solution)/shard_map/ppermute | solution.py:171
  944.7 49.6 %collective-permute-start.66 = (bf16[8,128,1024]{2,1,0:T(8,128)(2,1)S(1)}, bf16[8,128,1024]{2,1,0:T(8,128)(2,1)S(1)}, u32[]{:S(2)}, u32[]{:S(2)}) collective-permute-start(bf16[8,128,1024]{2,1,0:T(8,128)(2,1)S(1)} %copy-done.53), channel_id=1, source_target_pairs={{0,2},{2,4},{4,6},{1,3},{3,5},{5,7},{8,10},{10,12},{12,14},{9,11},... | collective-permute-start | bytes 6291464 | tf_op jit(solution)/shard_map/ppermute | solution.py:223
  949.2 50.6 %collective-permute-start.67 = (bf16[8,128,1024]{2,1,0:T(8,128)(2,1)S(1)}, bf16[8,128,1024]{2,1,0:T(8,128)(2,1)}, u32[]{:S(2)}, u32[]{:S(2)}) collective-permute-start(bf16[8,128,1024]{2,1,0:T(8,128)(2,1)S(1)} %copy-done.51), channel_id=1, source_target_pairs={{6,4},{4,2},{2,0},{7,5},{5,3},{3,1},{14,12},{12,10},{10,8},{15,13}... | collective-permute-start | bytes 6291464 | tf_op jit(solution)/shard_map/ppermute | solution.py:224
  950.5 54.0 %collective-permute-start.64 = (bf16[4,256,1024]{2,1,0:T(8,128)(2,1)}, bf16[4,256,1024]{2,1,0:T(8,128)(2,1)}, u32[]{:S(2)}, u32[]{:S(2)}) collective-permute-start(bf16[4,256,1024]{2,1,0:T(8,128)(2,1)} %collective-permute-done.61.refs_1_), channel_id=1, source_target_pairs={{2,4},{4,6},{3,5},{5,7},{10,12},{12,14},{11,13},{13,15},{18,20},{2... | collective-permute-start | bytes 6291464 | tf_op jit(solution)/shard_map/ppermute | solution.py:171
  952.5 88.0 %collective-permute-start.65 = (bf16[4,256,1024]{2,1,0:T(8,128)(2,1)}, bf16[4,256,1024]{2,1,0:T(8,128)(2,1)}, u32[]{:S(2)}, u32[]{:S(2)}) collective-permute-start(bf16[4,256,1024]{2,1,0:T(8,128)(2,1)} %collective-permute-done.62.refs_6_), channel_id=1, source_target_pairs={{2,0},{4,2},{3,1},{5,3},{10,8},{12,10},{11,9},{13,11},{18,16},{20,... | collective-permute-start | bytes 6291464 | tf_op jit(solution)/shard_map/ppermute | solution.py:172
  (193 other events, 3235.6 us)
Sparse Core Ops, SparseCore 0:
  10.8 91.5 all-gather.4
  104.2 57.5 all-gather.6
  337.3 32.8 all-gather.8
  610.3 38.5 all-gather.10

commit v12 on v11

--- a/solution.py
+++ b/solution.py
@@ -891,7 +891,7 @@
 def total_streams(sums, current_half, last, depth_at):
     _, _, tall, width = sums.terms.shape
     wide = STREAMS * width
-    rows = min(64, tall)
+    rows = min(128, tall)
     row = lambda i, d: (i, 0)
     return pl.pallas_call(
         total_kernel,
@@ -912,6 +912,7 @@
             jax.ShapeDtypeStruct((tall, width), f32),
         ],
         cost_estimate=spent(flops=5 * tall * wide, bytes_accessed=9 * tall * wide, transcendentals=0),
+        compiler_params=pltpu.CompilerParams(vmem_limit_bytes=40 << 20),
         name="total_streams",
     )(depth_at, sums.terms, sums.up, sums.down, current_half, last)
 
@@ -950,7 +951,7 @@
 def norm_streams(low, low_other, gains, which):
     tall, wide = low.shape
     width = wide // STREAMS
-    rows = min(64, tall)
+    rows = min(128, tall)
     row = lambda i, m: (i, 0)
     return pl.pallas_call(
         norm_kernel,
@@ -976,6 +977,7 @@
         cost_estimate=spent(
             flops=20 * tall * wide, bytes_accessed=8 * tall * wide, transcendentals=0
         ),
+        compiler_params=pltpu.CompilerParams(vmem_limit_bytes=40 << 20),
         name="norm_streams",
     )(which, low, low_other, gains)
 
@@ -1274,7 +1276,7 @@
 def norm_slopes(own, got, ff_grad, low, stats, gains, which):
     tall, wide = low.shape
     width = wide // STREAMS
-    rows = min(64, tall)
+    rows = min(128, tall)
     row = lambda i, m: (i, 0)
     cube = pl.BlockSpec((4, rows, width), lambda i, m: (0, i, 0))
     return pl.pallas_call(
@@ -1304,6 +1306,7 @@
         cost_estimate=spent(
             flops=12 * tall * wide, bytes_accessed=12 * tall * wide, transcendentals=0
         ),
+        compiler_params=pltpu.CompilerParams(vmem_limit_bytes=40 << 20),
         name="norm_slopes",
     )(which, own, got, ff_grad, low, stats, gains)
 
@@ -1342,7 +1345,7 @@
 def stream_grads(scaled, mine, theirs, low, stats, cot, current_half, last):
     tall, wide = low.shape
     width = wide // STREAMS
-    rows = min(64, tall)
+    rows = min(128, tall)
     row = lambda i: (i, 0)
     return pl.pallas_call(
         grads_kernel,
@@ -1370,6 +1373,7 @@
         cost_estimate=spent(
             flops=12 * tall * wide, bytes_accessed=10 * tall * wide, transcendentals=0
         ),
+        compiler_params=pltpu.CompilerParams(vmem_limit_bytes=40 << 20),
         name="stream_grads",
     )(scaled, mine, theirs, low, stats, cot, current_half, last)
 

time: 1210 us -> 1220 us (level)
  Pallas kernels: 428 us -> 410 us
  local copies, waits for them, and re-layouts: 84.9 us -> 100 us
    ppermute x10, waiting for transfers between devices: 67.9 us -> 82.6 us  [core_hop(): return lax.ppermute(values, ('dp', 'mp'), pairs)]
    unnamed x228 -> x240, local copies, waits for them, and re-layouts: 56.3 us -> 60.4 us
  transfers between devices with their start and end apart: 105 -> 105, of which waited for: 48 -> 44; matrix products, arithmetic and copies ran while one was open for 8% -> 9% of each run, Pallas kernels for 33% -> 31%
where the time goes in v12:
time: 1220 us; the launch traced here: 1210 us
  waiting for transfers between devices  411 us (34%)
  Pallas kernels  410 us (34%)
  starting transfers between devices  191 us (16%)
  local copies, waits for them, and re-layouts  100 us (8%)
  other arithmetic  68.7 us (6%)
  between operations  16.2 us (1%)
  matrix products  14.9 us (1%)
    ppermute x8, waiting for transfers between devices, step(): self.up = lax.ppermute(goes_up, 'depth', up_pairs)  86.4 us
    ppermute x4, waiting for transfers between devices, step_with(): lax.ppermute(goes[0], 'depth', [(i, i + 1) for i in range(size - 1)])  85.5 us
    ppermute x10, waiting for transfers between devices, core_hop(): return lax.ppermute(values, ('dp', 'mp'), pairs)  82.6 us
    unnamed x240, local copies, waits for them, and re-layouts  60.4 us
    ppermute x53, starting transfers between devices, swap_mask(): return lax.ppermute(values, axis, [(i, i ^ mask) for i in range(size)])  54.2 us
    ppermute x53, waiting for transfers between devices, swap_mask(): return lax.ppermute(values, axis, [(i, i ^ mask) for i in range(size)])  50.3 us
    ppermute x8, starting transfers between devices, step(): self.up = lax.ppermute(goes_up, 'depth', up_pairs)  48.9 us
    pallas_call x2, Pallas kernels, feed_forward(): pl.pallas_call(ff_kernel, grid_spec=pltpu.PrefetchScalarGridSpec(num_scal...  48.1 us
  transfers between devices with their start and end apart: 105, of which 44 were waited for; matrix products, arithmetic and copies ran while one was open for 9% of the time, Pallas kernels for 31%

profile of v12, /device:TPU:0, one launch (start us, length us, event | category | flops | bytes accessed | tf_op | source)
XLA Modules:
  0.0 1211.4 jit_solution(13580055309980673238)
XLA Ops:
  95.6 14.3 %mix_streams.2 = bf16[4,1024,1024]{2,1,0:T(8,128)(2,1)} custom-call(f32[2048,20]{1,0:T(8,128)} %copy.101.mix_ref.refs_0_, bf16[5,2048,1024]{2,1,0:T(8,128)(2,1)} %refs_1_.1), custom_call_target="tpu_custom_call" | custom-call | flops 2097152 | bytes 943718 | tf_op jit(solution)/shard_map/mix_streams/pallas_call | solution.py:679
  109.9 14.6 %mix_streams.3 = bf16[4,1024,1024]{2,1,0:T(8,128)(2,1)} custom-call(f32[2048,20]{1,0:T(8,128)} %copy.101.mix_ref.refs_0_, bf16[5,2048,1024]{2,1,0:T(8,128)(2,1)} %refs_1_.1), custom_call_target="tpu_custom_call" | custom-call | flops 2097152 | bytes 943718 | tf_op jit(solution)/shard_map/mix_streams/pallas_call | solution.py:679
  124.5 16.2 %collective-permute-done.21.refs_1_ = bf16[8,128,1024]{2,1,0:T(8,128)(2,1)S(1)} collective-permute-done((bf16[8,128,1024]{2,1,0:T(8,128)(2,1)}, bf16[8,128,1024]{2,1,0:T(8,128)(2,1)S(1)}, u32[]{:S(2)}, u32[]{:S(2)}) %collective-permute-start.21) | collective-permute-done | bytes 2097184 | tf_op jit(solution)/shard_map/ppermute | solution.py:171
  172.9 25.7 %collective-permute-done.23.refs_2_ = bf16[4,256,1024]{2,1,0:T(8,128)(2,1)S(1)} collective-permute-done((bf16[4,256,1024]{2,1,0:T(8,128)(2,1)}, bf16[4,256,1024]{2,1,0:T(8,128)(2,1)S(1)}, u32[]{:S(2)}, u32[]{:S(2)}) %collective-permute-start.23) | collective-permute-done | bytes 2097184 | tf_op jit(solution)/shard_map/ppermute | solution.py:250
  225.4 36.3 %collective-permute-done.26.refs_2_ = bf16[4,256,1024]{2,1,0:T(8,128)(2,1)} collective-permute-done((bf16[4,256,1024]{2,1,0:T(8,128)(2,1)}, bf16[4,256,1024]{2,1,0:T(8,128)(2,1)}, u32[]{:S(2)}, u32[]{:S(2)}) %collective-permute-start.26) | collective-permute-done | bytes 2097184 | tf_op jit(solution)/shard_map/ppermute | solution.py:250
  298.3 10.0 place_line.5
  308.3 11.2 collective-permute-done.29.up_ref
  367.7 18.1 %collective-permute-done.33.refs_2_ = bf16[4,256,1024]{2,1,0:T(8,128)(2,1)} collective-permute-done((bf16[4,256,1024]{2,1,0:T(8,128)(2,1)}, bf16[4,256,1024]{2,1,0:T(8,128)(2,1)}, u32[]{:S(2)}, u32[]{:S(2)}) %collective-permute-start.33) | collective-permute-done | bytes 2097184 | tf_op jit(solution)/shard_map/ppermute | solution.py:223
  419.2 24.1 %feed_forward.2 = (bf16[1024,1024]{1,0:T(8,128)(2,1)S(1)}, bf16[1024,1024]{1,0:T(8,128)(2,1)S(1)}, f32[2,1024,1024]{2,1,0:T(8,128)}, bf16[2,1024,1024]{2,1,0:T(8,128)(2,1)}) custom-call(s32[1]{0:T(128)} %bitcast.74.model_ref.half_ref, bf16[1024,2048]{1,0:T(8,128)(2,1)} %join_halves.5.x_ref.x0_ref, bf16[4,2,256,2048]{3,2,1,0:T(8,128)(2,1)} %bitcast.384, ...), custom_call_target="tpu_custom_call" | custom-call | flops 858993472 | bytes 2097152 | tf_op jit(solution)/shard_map/feed_forward/pallas_call | solution.py:1153
  446.0 31.9 %collective-permute-done.36.refs_2_ = bf16[4,256,1024]{2,1,0:T(8,128)(2,1)} collective-permute-done((bf16[4,256,1024]{2,1,0:T(8,128)(2,1)}, bf16[4,256,1024]{2,1,0:T(8,128)(2,1)}, u32[]{:S(2)}, u32[]{:S(2)}) %collective-permute-start.36) | collective-permute-done | bytes 2097184 | tf_op jit(solution)/shard_map/ppermute | solution.py:223
  483.1 19.4 %collective-permute-start.40 = (bf16[4,256,1024]{2,1,0:T(8,128)(2,1)}, bf16[4,256,1024]{2,1,0:T(8,128)(2,1)}, u32[]{:S(2)}, u32[]{:S(2)}) collective-permute-start(bf16[4,256,1024]{2,1,0:T(8,128)(2,1)} %get-tuple-element.369), channel_id=1, source_target_pairs={{0,2},{2,4},{4,6},{1,3},{3,5},{5,7},{8,10},{10,12},{12,14},{9,11},... | collective-permute-start | bytes 6291464 | tf_op jit(solution)/shard_map/ppermute | solution.py:223
  509.2 10.7 attend.2
  521.3 25.2 %collective-permute-done.40.up_ref = bf16[4,256,1024]{2,1,0:T(8,128)(2,1)} collective-permute-done((bf16[4,256,1024]{2,1,0:T(8,128)(2,1)}, bf16[4,256,1024]{2,1,0:T(8,128)(2,1)}, u32[]{:S(2)}, u32[]{:S(2)}) %collective-permute-start.40) | collective-permute-done | bytes 2097184 | tf_op jit(solution)/shard_map/ppermute | solution.py:223
  577.4 10.2 project_heads.3
  589.0 9.2 collective-permute-done.44
  627.9 10.5 collective-permute-done.46
  667.8 10.7 attend.3
  684.6 24.1 %feed_forward.3 = (bf16[1024,1024]{1,0:T(8,128)(2,1)S(1)}, bf16[1024,1024]{1,0:T(8,128)(2,1)S(1)}, f32[2,1024,1024]{2,1,0:T(8,128)}, bf16[2,1024,1024]{2,1,0:T(8,128)(2,1)}) custom-call(s32[1]{0:T(128)} %bitcast.74.model_ref.half_ref, bf16[1024,2048]{1,0:T(8,128)(2,1)} %join_halves.7.x_ref.x1_ref, bf16[4,2,256,2048]{3,2,1,0:T(8,128)(2,1)} %bitcast.385, ...), custom_call_target="tpu_custom_call" | custom-call | flops 858993472 | bytes 2097152 | tf_op jit(solution)/shard_map/feed_forward/pallas_call | solution.py:1153
  730.6 24.0 %hidden_grads.1.refs_0_.refs_1_.term_ref = bf16[8,4,128,1024]{3,2,1,0:T(8,128)(2,1)} custom-call(bf16[1024,2048]{1,0:T(8,128)(2,1)} %join_halves.5.x_ref.x0_ref, bf16[1024,2048]{1,0:T(8,128)(2,1)} %join_halves.7.x_ref.x1_ref, bf16[4,2,256,2048]{3,2,1,0:T(8,128)(2,1)} %bitcast.386, bf16[4,2,256,2048]{3,2,1,0:T(8,128)(2,1)} %bitcast.387, ...), custom_call_target="tpu_custom_call" | custom-call | flops 858993472 | bytes 838860 | tf_op jit(solution)/shard_map/hidden_grads/pallas_call | solution.py:627
  801.4 23.6 %collective-permute-done.53.refs_2_ = bf16[8,128,1024]{2,1,0:T(8,128)(2,1)S(1)} collective-permute-done((bf16[8,128,1024]{2,1,0:T(8,128)(2,1)}, bf16[8,128,1024]{2,1,0:T(8,128)(2,1)S(1)}, u32[]{:S(2)}, u32[]{:S(2)}) %collective-permute-start.53) | collective-permute-done | bytes 2097184 | tf_op jit(solution)/shard_map/ppermute | solution.py:250
  915.7 19.5 %unmix_streams.2 = (bf16[5,2048,1024]{2,1,0:T(8,128)(2,1)}, f32[1024,128]{1,0:T(8,128)}) custom-call(f32[2048,20]{1,0:T(8,128)} %copy.101.mix_ref.refs_0_, bf16[5,2048,1024]{2,1,0:T(8,128)(2,1)} %refs_1_.1, bf16[4,1024,1024]{2,1,0:T(8,128)(2,1)} %bitcast.393), custom_call_target="tpu_custom_call" | custom-call | flops 4194304 | bytes 1468006 | tf_op jit(solution)/shard_map/unmix_streams/pallas_call | solution.py:754
  955.5 39.2 %collective-permute-done.68 = bf16[4,4,128,1024]{3,2,1,0:T(8,128)(2,1)S(1)} collective-permute-done((bf16[4,4,128,1024]{3,2,1,0:T(8,128)(2,1)S(1)}, bf16[4,4,128,1024]{3,2,1,0:T(8,128)(2,1)S(1)}, u32[]{:S(2)}, u32[]{:S(2)}) %collective-permute-start.68) | collective-permute-done | bytes 4194336 | tf_op jit(solution)/shard_map/ppermute | solution.py:105
  1006.5 35.7 %collective-permute-done.65.refs_5_ = bf16[4,256,1024]{2,1,0:T(8,128)(2,1)} collective-permute-done((bf16[4,256,1024]{2,1,0:T(8,128)(2,1)}, bf16[4,256,1024]{2,1,0:T(8,128)(2,1)}, u32[]{:S(2)}, u32[]{:S(2)}) %collective-permute-start.65) | collective-permute-done | bytes 2097184 | tf_op jit(solution)/shard_map/ppermute | solution.py:172
  1070.6 19.5 %unmix_streams.3 = (bf16[5,2048,1024]{2,1,0:T(8,128)(2,1)}, f32[1024,128]{1,0:T(8,128)}) custom-call(f32[2048,20]{1,0:T(8,128)} %copy.101.mix_ref.refs_0_, bf16[5,2048,1024]{2,1,0:T(8,128)(2,1)} %refs_1_.1, bf16[4,1024,1024]{2,1,0:T(8,128)(2,1)} %bitcast.392, bf16[5,2048,1024]{2,1,0:T(8,128)(2,1)} %get-tuple-element.499.rest_0_), custom_call_target="tpu_custom_call", output_to_operand_aliasing={{0}: (3, {})} | custom-call | flops 4194304 | bytes 1468006 | tf_op jit(solution)/shard_map/unmix_streams/pallas_call | solution.py:754
  (652 shorter events, 711.3 us)
Async XLA Ops:
  7.2 135.3 %all-gather.5.cloned.1.call-start = ((), (), s32[]{:S(2)}) async-start(), calls=%async_computation.4 | async-start | bytes 5242880 | tf_op jit(solution)/shard_map/all_gather | solution.py:1451
  10.7 162.2 %all-gather.7.cloned.1.call-start = ((), (), s32[]{:S(2)}) async-start(), calls=%async_computation.5 | async-start | bytes 5242880 | tf_op jit(solution)/shard_map/all_gather | solution.py:1487
  89.8 50.9 %collective-permute-start.21 = (bf16[8,128,1024]{2,1,0:T(8,128)(2,1)}, bf16[8,128,1024]{2,1,0:T(8,128)(2,1)S(1)}, u32[]{:S(2)}, u32[]{:S(2)}) collective-permute-start(bf16[8,128,1024]{2,1,0:T(8,128)(2,1)} %bitcast.43.refs_0_), channel_id=1, source_target_pairs={{0,2},{2,4},{4,6},{1,3},{3,5},{5,7},{8,10},{10,12},{12,14},{9,11},... | collective-permute-start | bytes 6291464 | tf_op jit(solution)/shard_map/ppermute | solution.py:171
  94.2 291.6 %all-gather.9.cloned.1.call-start = ((), (), s32[]{:S(2)}) async-start(), calls=%async_computation.6 | async-start | bytes 2621440 | tf_op jit(solution)/shard_map/all_gather | solution.py:1554
  142.5 63.7 %collective-permute-start.25 = (bf16[2048,1024]{1,0:T(8,128)(2,1)}, bf16[2048,1024]{1,0:T(8,128)(2,1)}, u32[]{:S(2)}, u32[]{:S(2)}) collective-permute-start(bf16[2048,1024]{1,0:T(8,128)(2,1)} %all-gather.5.cloned.1.call-done), channel_id=1, source_target_pairs={{0,8},{1,17},{8,0},{9,25},{16,24},{17,1},{24,16},{25,9},{2,10},{3,... | collective-permute-start | bytes 12582920 | tf_op jit(solution)/shard_map/ppermute | solution.py:105
  206.2 60.9 %collective-permute-start.28 = (bf16[2048,1024]{1,0:T(8,128)(2,1)}, bf16[2048,1024]{1,0:T(8,128)(2,1)}, u32[]{:S(2)}, u32[]{:S(2)}) collective-permute-start(bf16[2048,1024]{1,0:T(8,128)(2,1)} %all-gather.5.cloned.1.call-done), channel_id=1, source_target_pairs={{0,16},{1,9},{8,24},{9,1},{16,0},{17,25},{24,8},{25,17},{2,18},{3,... | collective-permute-start | bytes 12582920 | tf_op jit(solution)/shard_map/ppermute | solution.py:105
  267.1 57.7 %collective-permute-start.31 = (bf16[2048,1024]{1,0:T(8,128)(2,1)}, bf16[2048,1024]{1,0:T(8,128)(2,1)}, u32[]{:S(2)}, u32[]{:S(2)}) collective-permute-start(bf16[2048,1024]{1,0:T(8,128)(2,1)} %collective-permute-done.25), channel_id=1, source_target_pairs={{0,16},{1,9},{8,24},{9,1},{16,0},{17,25},{24,8},{25,17},{2,18},{3,... | collective-permute-start | bytes 12582920 | tf_op jit(solution)/shard_map/ppermute | solution.py:105
  392.4 85.6 %all-to-all-start = ((bf16[4,256,1024]{2,1,0:T(8,128)(2,1)}), bf16[4,256,1024]{2,1,0:T(8,128)(2,1)}, u32[]{:S(2)}, u32[]{:S(2)}) async-start(bf16[4,256,1024]{2,1,0:T(8,128)(2,1)} %copy-done.22), calls=%async_computation | async-start | bytes 4194304 | tf_op jit(solution)/shard_map/all_to_all | solution.py:1475
  398.5 79.4 %collective-permute-start.36 = (bf16[4,256,1024]{2,1,0:T(8,128)(2,1)}, bf16[4,256,1024]{2,1,0:T(8,128)(2,1)}, u32[]{:S(2)}, u32[]{:S(2)}) collective-permute-start(bf16[4,256,1024]{2,1,0:T(8,128)(2,1)} %copy-done.85), channel_id=1, source_target_pairs={{0,2},{2,4},{1,3},{3,5},{8,10},{10,12},{9,11},{11,13},{16,18},{18,... | collective-permute-start | bytes 6291464 | tf_op jit(solution)/shard_map/ppermute | solution.py:223
  403.6 74.3 %collective-permute-start.37 = (bf16[4,256,1024]{2,1,0:T(8,128)(2,1)}, bf16[4,256,1024]{2,1,0:T(8,128)(2,1)}, u32[]{:S(2)}, u32[]{:S(2)}) collective-permute-start(bf16[4,256,1024]{2,1,0:T(8,128)(2,1)} %copy-done.84), channel_id=1, source_target_pairs={{6,4},{4,2},{7,5},{5,3},{14,12},{12,10},{15,13},{13,11},{22,20},{2... | collective-permute-start | bytes 6291464 | tf_op jit(solution)/shard_map/ppermute | solution.py:224
  483.1 63.4 %collective-permute-start.40 = (bf16[4,256,1024]{2,1,0:T(8,128)(2,1)}, bf16[4,256,1024]{2,1,0:T(8,128)(2,1)}, u32[]{:S(2)}, u32[]{:S(2)}) collective-permute-start(bf16[4,256,1024]{2,1,0:T(8,128)(2,1)} %get-tuple-element.369), channel_id=1, source_target_pairs={{0,2},{2,4},{4,6},{1,3},{3,5},{5,7},{8,10},{10,12},{12,14},{9,11},... | collective-permute-start | bytes 6291464 | tf_op jit(solution)/shard_map/ppermute | solution.py:223
  551.9 53.7 %all-to-all-start.1 = ((bf16[4,256,1024]{2,1,0:T(8,128)(2,1)}), bf16[4,256,1024]{2,1,0:T(8,128)(2,1)}, u32[]{:S(2)}, u32[]{:S(2)}) async-start(bf16[4,256,1024]{2,1,0:T(8,128)(2,1)} %bitcast.347), calls=%async_computation.1 | async-start | bytes 4194304 | tf_op jit(solution)/shard_map/all_to_all | solution.py:1475
  605.6 52.9 %all-to-all-start.2 = ((bf16[4,256,1024]{2,1,0:T(8,128)(2,1)}), bf16[4,256,1024]{2,1,0:T(8,128)(2,1)}, u32[]{:S(2)}, u32[]{:S(2)}) async-start(bf16[4,256,1024]{2,1,0:T(8,128)(2,1)} %copy-done.21), calls=%async_computation.2 | async-start | bytes 4194304 | tf_op jit(solution)/shard_map/all_to_all | solution.py:1475
  658.5 52.8 %collective-permute-start.48 = (bf16[4,256,1024]{2,1,0:T(8,128)(2,1)}, bf16[4,256,1024]{2,1,0:T(8,128)(2,1)}, u32[]{:S(2)}, u32[]{:S(2)}) collective-permute-start(bf16[4,256,1024]{2,1,0:T(8,128)(2,1)} %copy-done.37), channel_id=1, source_target_pairs={{0,2},{2,4},{4,6},{1,3},{3,5},{5,7},{8,10},{10,12},{12,14},{9,11},... | collective-permute-start | bytes 6291464 | tf_op jit(solution)/shard_map/ppermute | solution.py:171
  661.1 50.3 %collective-permute-start.49 = (bf16[4,256,1024]{2,1,0:T(8,128)(2,1)}, bf16[4,256,1024]{2,1,0:T(8,128)(2,1)}, u32[]{:S(2)}, u32[]{:S(2)}) collective-permute-start(bf16[4,256,1024]{2,1,0:T(8,128)(2,1)} %copy-done.37), channel_id=1, source_target_pairs={{2,0},{4,2},{6,4},{3,1},{5,3},{7,5},{10,8},{12,10},{14,12},{11,9},... | collective-permute-start | bytes 6291464 | tf_op jit(solution)/shard_map/ppermute | solution.py:172
  711.9 54.9 %all-to-all-start.3 = ((bf16[4,256,1024]{2,1,0:T(8,128)(2,1)}), bf16[4,256,1024]{2,1,0:T(8,128)(2,1)}, u32[]{:S(2)}, u32[]{:S(2)}) async-start(bf16[4,256,1024]{2,1,0:T(8,128)(2,1)} %bitcast.348), calls=%async_computation.3 | async-start | bytes 4194304 | tf_op jit(solution)/shard_map/all_to_all | solution.py:1475
  779.0 50.1 %collective-permute-start.54 = (bf16[8,128,1024]{2,1,0:T(8,128)(2,1)}, bf16[8,128,1024]{2,1,0:T(8,128)(2,1)S(1)}, u32[]{:S(2)}, u32[]{:S(2)}) collective-permute-start(bf16[8,128,1024]{2,1,0:T(8,128)(2,1)} %get-tuple-element.424), channel_id=1, source_target_pairs={{2,0},{4,2},{6,4},{3,1},{5,3},{7,5},{10,8},{12,10},{14,12},{11,9},... | collective-permute-start | bytes 6291464 | tf_op jit(solution)/shard_map/ppermute | solution.py:251
  839.9 51.6 %collective-permute-start.58 = (bf16[8,128,1024]{2,1,0:T(8,128)(2,1)}, bf16[8,128,1024]{2,1,0:T(8,128)(2,1)}, u32[]{:S(2)}, u32[]{:S(2)}) collective-permute-start(bf16[8,128,1024]{2,1,0:T(8,128)(2,1)} %get-tuple-element.439), channel_id=1, source_target_pairs={{2,0},{4,2},{6,4},{3,1},{5,3},{7,5},{10,8},{12,10},{14,12},{11,9},... | collective-permute-start | bytes 6291464 | tf_op jit(solution)/shard_map/ppermute | solution.py:251
  841.2 50.4 %collective-permute-start.57 = (bf16[8,128,1024]{2,1,0:T(8,128)(2,1)}, bf16[8,128,1024]{2,1,0:T(8,128)(2,1)}, u32[]{:S(2)}, u32[]{:S(2)}) collective-permute-start(bf16[8,128,1024]{2,1,0:T(8,128)(2,1)} %get-tuple-element.437), channel_id=1, source_target_pairs={{0,2},{2,4},{4,6},{1,3},{3,5},{5,7},{8,10},{10,12},{12,14},{9,11},... | collective-permute-start | bytes 6291464 | tf_op jit(solution)/shard_map/ppermute | solution.py:250
  892.1 54.0 %collective-permute-start.61 = (bf16[4,256,1024]{2,1,0:T(8,128)(2,1)S(1)}, bf16[4,256,1024]{2,1,0:T(8,128)(2,1)}, u32[]{:S(2)}, u32[]{:S(2)}) collective-permute-start(bf16[4,256,1024]{2,1,0:T(8,128)(2,1)S(1)} %get-tuple-element.449.refs_0_.refs_3_.refs_4_), channel_id=1, source_target_pairs={{0,2},{2,4},{4,6},{1,3},{3,5},{5,7},{8,10},{10,12},{12,14},{9,11},... | collective-permute-start | bytes 6291464 | tf_op jit(solution)/shard_map/ppermute | solution.py:171
  947.1 49.9 %collective-permute-start.66 = (bf16[8,128,1024]{2,1,0:T(8,128)(2,1)S(1)}, bf16[8,128,1024]{2,1,0:T(8,128)(2,1)S(1)}, u32[]{:S(2)}, u32[]{:S(2)}) collective-permute-start(bf16[8,128,1024]{2,1,0:T(8,128)(2,1)S(1)} %copy-done.83), channel_id=1, source_target_pairs={{0,2},{2,4},{4,6},{1,3},{3,5},{5,7},{8,10},{10,12},{12,14},{9,11},... | collective-permute-start | bytes 6291464 | tf_op jit(solution)/shard_map/ppermute | solution.py:223
  950.9 50.6 %collective-permute-start.67 = (bf16[8,128,1024]{2,1,0:T(8,128)(2,1)S(1)}, bf16[8,128,1024]{2,1,0:T(8,128)(2,1)}, u32[]{:S(2)}, u32[]{:S(2)}) collective-permute-start(bf16[8,128,1024]{2,1,0:T(8,128)(2,1)S(1)} %copy-done.81), channel_id=1, source_target_pairs={{6,4},{4,2},{2,0},{7,5},{5,3},{3,1},{14,12},{12,10},{10,8},{15,13}... | collective-permute-start | bytes 6291464 | tf_op jit(solution)/shard_map/ppermute | solution.py:224
  952.2 54.3 %collective-permute-start.64 = (bf16[4,256,1024]{2,1,0:T(8,128)(2,1)}, bf16[4,256,1024]{2,1,0:T(8,128)(2,1)}, u32[]{:S(2)}, u32[]{:S(2)}) collective-permute-start(bf16[4,256,1024]{2,1,0:T(8,128)(2,1)} %collective-permute-done.61.refs_1_), channel_id=1, source_target_pairs={{2,4},{4,6},{3,5},{5,7},{10,12},{12,14},{11,13},{13,15},{18,20},{2... | collective-permute-start | bytes 6291464 | tf_op jit(solution)/shard_map/ppermute | solution.py:171
  954.2 88.0 %collective-permute-start.65 = (bf16[4,256,1024]{2,1,0:T(8,128)(2,1)}, bf16[4,256,1024]{2,1,0:T(8,128)(2,1)}, u32[]{:S(2)}, u32[]{:S(2)}) collective-permute-start(bf16[4,256,1024]{2,1,0:T(8,128)(2,1)} %collective-permute-done.62.refs_6_), channel_id=1, source_target_pairs={{2,0},{4,2},{3,1},{5,3},{10,8},{12,10},{11,9},{13,11},{18,16},{20,... | collective-permute-start | bytes 6291464 | tf_op jit(solution)/shard_map/ppermute | solution.py:172
  (199 other events, 3583.6 us)
Sparse Core Ops, SparseCore 0:
  10.8 96.5 all-gather.4
  109.3 62.4 all-gather.6
  338.3 32.5 all-gather.8
  613.0 38.5 all-gather.10
